TPU v7x, 32 devices: a whole 2x2x4 slice. The times are simulated.
32 devices in a mesh: modes: 8 (over z, y), grid: 4 (over x, core).
Axes of the slice: x: 2, y: 2, z: 4, core: 2. Of those that a mesh axis runs over, the one named last changes fastest.
Arguments:
- u_modes: float32 [8, 2, 64, 1024], P('modes', None, 'grid'), may hold values from -5 to 5
- v_modes: float32 [8, 2, 64, 1024], P('modes', None, 'grid'), may hold values from -0.85 to 0.85
- potential: float32 [64, 1024], P('grid'), may hold values from -1.5 to 0
- pairing: float32 [2, 64, 1024], P(None, 'grid'), may hold values from -1 to 1
Outputs:
- u_next: float32 [8, 2, 64, 1024], P('modes', None, 'grid')
- v_next: float32 [8, 2, 64, 1024], P('modes', None, 'grid')
- fields: float32 [4, 64, 1024], P(None, 'grid')
All inputs are finite; a program needn't handle non-finite values.
Results may differ from a plain program's by a relative error of at most 0.00035.
Values sent between devices are 32-bit elements; how exact they have to be, the bound alone decides.
No kernel may reach another device: no remote copies, remote signals or barrier semaphores. Data moves between devices by JAX's collectives and lax.ppermute only.
A program may use at most 64 MiB of HBM per device.

v0:
```python
import functools

import jax
import jax.numpy as jnp
import numpy as np
from jax import lax
from jax.experimental import pallas as pl
from jax.experimental.pallas import tpu as pltpu
from jax.sharding import PartitionSpec as P

NX = 32
NY = 32

stencil_coef = (-205.0 / 72.0, 8.0 / 5.0, -1.0 / 5.0, 8.0 / 315.0, -1.0 / 560.0)
alpha_coef = 1.14
beta_coef = -0.553
gamma_coef = -11.11
time_step = 0.18
epsilon = 1e-06

REACH = 4
LANES = 128
BLOCK = 256
WINDOW = BLOCK + 2 * LANES


def in_plane_matrix():
    rows_out = BLOCK // NX
    mat = np.zeros((WINDOW, BLOCK), np.float64)
    for y in range(rows_out):
        for x in range(NX):
            out = y * NX + x
            for k in range(1, REACH + 1):
                for sign in (-1, 1):
                    mat[(y + REACH) * NX + (x + sign * k) % NX, out] += stencil_coef[k]
                    mat[(y + REACH + sign * k) * NX + x, out] += stencil_coef[k]
    mat = mat.astype(np.float32)
    high = mat.astype(jnp.bfloat16)
    low = (mat - high.astype(np.float32)).astype(jnp.bfloat16)
    return np.concatenate([high, high, low], axis=0)


def up16(n):
    return -(-n // 16) * 16


def laplace_in_plane(read, rows, w_ref, hi_ref, lo_ref, xy_ref):
    for c in range(4):
        for j in range(8):
            value = read(c, j)
            high = value.astype(jnp.bfloat16)
            low = (value - high.astype(jnp.float32)).astype(jnp.bfloat16)
            if j % 2 == 0:
                places = ((j // 2, 1), ((j // 2 + 3) % 4, 3))
            else:
                places = ((j // 2, 2), ((j // 2 + 1) % 4, 0))
            for big, part in places:
                hi_ref[big, c, :rows, part * LANES : (part + 1) * LANES] = high
                lo_ref[big, c, :rows, part * LANES : (part + 1) * LANES] = low
    high = hi_ref[:, :, :rows, :].reshape(16 * rows, WINDOW)
    low = lo_ref[:, :, :rows, :].reshape(16 * rows, WINDOW)
    total = jnp.dot(
        jnp.concatenate([high, low, high], axis=1),
        w_ref[...],
        preferred_element_type=jnp.float32,
    )
    xy_ref[:, :, :rows, :] = total.reshape(4, 4, rows, BLOCK)


def z_part(ref, c, j, start, count):
    centre = ref[c, j, pl.ds(start, count), :]
    total = (3.0 * stencil_coef[0]) * centre
    for k in range(1, REACH + 1):
        total = total + stencil_coef[k] * (
            ref[c, j, pl.ds(start + k, count), :] + ref[c, j, pl.ds(start - k, count), :]
        )
    return centre, total


def slope(f, lap, pot, pr, pi):
    kin = [-0.5 * alpha_coef * lap[c] + pot * f[c] for c in range(4)]
    upper_re = kin[0] + pr * f[2] - pi * f[3]
    upper_im = kin[1] + pr * f[3] + pi * f[2]
    lower_re = pr * f[0] + pi * f[1] - kin[2]
    lower_im = pr * f[1] - pi * f[0] - kin[3]
    return upper_im, -upper_re, lower_im, -lower_re


def chunks(rows, size=16):
    return [(r, min(size, rows - r)) for r in range(0, rows, size)]


def stages_kernel(pieces, planes, low_bits, *refs):
    n = len(pieces)
    parts = refs[:n]
    w_ref = refs[n]
    psi1_ref, lap1_ref, sums_ref = refs[n + 1 : n + 4]
    b0, b1, b2, b3, b4, pd, hi, lo, xy = refs[n + 4 :]
    odd = lax.rem(lax.axis_index("grid"), 2)
    quarter = lax.rem(lax.axis_index("modes"), low_bits)

    for ref, (channels, moves) in zip(parts, pieces):
        for src, count, dst_even, dst_odd in moves:
            if dst_even == dst_odd:
                dst = dst_even
                dst_pd = dst_even - 8
            else:
                dst = pl.multiple_of(dst_even + odd * (dst_odd - dst_even), 8)
                dst_pd = pl.multiple_of(dst - 8, 8)
            for c in range(channels):
                for j in range(8):
                    value = ref[c, src : src + count, j * LANES : (j + 1) * LANES]
                    if c < 4:
                        b0[c, j, pl.ds(dst, count), :] = value
                    else:
                        pd[c - 4, j, pl.ds(dst_pd, count), :] = value

    def run(src, start, rows, store):
        tall = up16(rows)
        laplace_in_plane(
            lambda c, j: src[c, j, pl.ds(start, tall), :], tall, w_ref, hi, lo, xy
        )
        margin = (planes + 32 - rows) // 2

        def body(big, carry):
            for half in range(2):
                j = big * 2 + half
                for r, count in chunks(rows):
                    centre, lap = [], []
                    for c in range(4):
                        f, z = z_part(src, c, j, start + r, count)
                        centre.append(f)
                        lap.append(
                            z + xy[big, c, pl.ds(r, count), half * LANES : (half + 1) * LANES]
                        )
                    store(big, half, j, r, count, margin + r, centre, lap)
            return carry

        lax.fori_loop(0, 4, body, 0)

    def fields_at(j, row, count):
        return [pd[i, j, pl.ds(row, count), :] for i in range(3)]

    def stage(dst, factor):
        def store(big, half, j, r, count, row, centre, lap):
            k = slope(centre, lap, *fields_at(j, row, count))
            for c in range(4):
                dst[c, j, pl.ds(r, count), :] = b0[c, j, pl.ds(row + 8, count), :] + factor * k[c]

        return store

    run(b0, 8, planes + 32, stage(b1, 0.5 * time_step))
    run(b1, 4, planes + 24, stage(b2, 0.5 * time_step))
    run(b2, 4, planes + 16, stage(b3, time_step))

    def last(big, half, j, r, count, row, centre, lap):
        k = slope(centre, lap, *fields_at(j, row, count))
        for c in range(4):
            early = (
                b1[c, j, pl.ds(r + 12, count), :]
                - b0[c, j, pl.ds(r + 20, count), :]
                + 2.0 * b2[c, j, pl.ds(r + 8, count), :]
                + centre[c]
            )
            b4[c, j, pl.ds(r, count), :] = early * (1.0 / 3.0) + (time_step / 6.0) * k[c]

    run(b3, 4, planes + 8, last)

    def finish(big, half, j, r, count, row, f, lap):
        for c in range(4):
            psi1_ref[c, j, pl.ds(r, count), :] = f[c]
            lap1_ref[c, j, pl.ds(r, count), :] = lap[c]
        sums = (
            f[2] * f[2] + f[3] * f[3],
            f[2] * lap[2] + f[3] * lap[3],
            f[0] * f[2] + f[1] * f[3],
            f[1] * f[2] - f[0] * f[3],
        )
        place = lax.bitwise_xor(big, quarter) if low_bits == 4 else big
        for s in range(4):
            sums_ref[place, half, s, pl.ds(r, count), :] = sums[s]

    run(b4, 4, planes, finish)


def field_reader(parts, low_bits):
    stack, = parts

    def read(big, half, i):
        return stack[big, half, i]

    return read


def middle_kernel(paired, planes, low_bits, *refs):
    count = len(refs) - 6 - 2
    pieces = refs[:low_bits]
    psi1, lap1 = refs[low_bits : low_bits + 2]
    mid, first_send, second_send, fields_out, fields_flat = refs[low_bits + 2 :]
    even = lax.rem(lax.axis_index("grid"), 2) == 0
    quarter = lax.rem(lax.axis_index("modes"), low_bits)
    per = 4 // low_bits
    for k in range(low_bits):
        for t in range(per):
            place = lax.bitwise_xor(quarter, k) * per + t
            for half in range(2):
                for i in range(4):
                    fields_flat[place, half, i] = pieces[k][t, half, i]

    for j in range(8):
        big, half = j // 2, j % 2
        now = [fields_flat[big, half, i] for i in range(4)]
        for i in range(4):
            fields_out[i, :, j * LANES : (j + 1) * LANES] = now[i]
        f = [psi1[c, j] for c in range(4)]
        q = slope(f, [lap1[c, j] for c in range(4)], now[0], now[1], now[2])
        for c in range(4):
            m = f[c] + (0.5 * time_step) * q[c]
            mid[c, j] = m
            top, bottom = m[:REACH], m[planes - REACH :]
            if paired:
                a, b = jnp.where(even, top, bottom), jnp.where(even, bottom, top)
            else:
                a, b = top, bottom
            first_send[j, c * REACH : (c + 1) * REACH, :] = a
            second_send[j, c * REACH : (c + 1) * REACH, :] = b


def inner_kernel(planes, *refs):
    psi1, lap1, mid, fields_flat, w_ref, part_ref, pad, hi, lo, xy = refs
    tall = up16(planes)
    zero = jnp.zeros((8, LANES), jnp.float32)
    for c in range(4):
        for j in range(8):
            pad[c, j, 0:8, :] = zero
            pad[c, j, 8 : 8 + planes, :] = mid[c, j]
            for r in range(8 + planes, pad.shape[2], 8):
                pad[c, j, r : r + 8, :] = zero
    laplace_in_plane(lambda c, j: pad[c, j, 8 : 8 + tall, :], tall, w_ref, hi, lo, xy)

    def body(big, carry):
        for half in range(2):
            j = big * 2 + half
            for r, count in chunks(planes):
                field = [fields_flat[big, half, i, pl.ds(r, count), :] for i in range(3)]
                f = [psi1[c, j, pl.ds(r, count), :] for c in range(4)]
                q1 = slope(f, [lap1[c, j, pl.ds(r, count), :] for c in range(4)], *field)
                m, lap = [], []
                for c in range(4):
                    centre, z = z_part(pad, c, j, 8 + r, count)
                    m.append(centre)
                    lap.append(z + xy[big, c, pl.ds(r, count), half * LANES : (half + 1) * LANES])
                q2 = slope(m, lap, *field)
                for c in range(4):
                    part_ref[c, j, pl.ds(r, count), :] = f[c] + (time_step / 6.0) * (
                        q1[c] + 2.0 * q2[c]
                    )
        return carry

    lax.fori_loop(0, 4, body, 0)


def edge_kernel(paired, planes, *refs):
    part, first, second, u_ref, v_ref = refs
    even = lax.rem(lax.axis_index("grid"), 2) == 0
    scale = -0.5 * alpha_coef * 2.0 * time_step / 6.0
    terms = ((0, 1, 1.0), (1, 0, -1.0), (2, 3, -1.0), (3, 2, 1.0))
    for j in range(8):
        a, b = first[j], second[j]
        if paired:
            before, after = jnp.where(even, a, b), jnp.where(even, b, a)
        else:
            before, after = b, a
        for out, src, sign in terms:
            lo_rows = before[src * REACH : (src + 1) * REACH]
            hi_rows = after[src * REACH : (src + 1) * REACH]
            lead, tail = [], []
            for r in range(REACH):
                lead.append(
                    sum(
                        stencil_coef[k] * lo_rows[r - k + REACH : r - k + REACH + 1]
                        for k in range(r + 1, REACH + 1)
                    )
                )
                tail.append(
                    sum(
                        stencil_coef[k] * hi_rows[r + k - REACH : r + k - REACH + 1]
                        for k in range(REACH - r, REACH + 1)
                    )
                )
            value = part[out, j]
            parts = [value[:REACH] + (sign * scale) * jnp.concatenate(lead, axis=0)]
            if planes > 2 * REACH:
                parts.append(value[REACH : planes - REACH])
            parts.append(value[planes - REACH :] + (sign * scale) * jnp.concatenate(tail, axis=0))
            ref = u_ref if out < 2 else v_ref
            ref[0, out % 2, :, j * LANES : (j + 1) * LANES] = jnp.concatenate(parts, axis=0)


def potentials(raw, modes_total):
    density = 2.0 * raw[:, :, 0] / modes_total
    kinetic = -2.0 * raw[:, :, 1] / modes_total
    anomal_re = raw[:, :, 2] / modes_total
    anomal_im = raw[:, :, 3] / modes_total
    dense_safe = density + epsilon
    fermi = 0.5 * jnp.power(3.0 * jnp.pi**2 * dense_safe, 2.0 / 3.0)
    anomal_sq = anomal_re * anomal_re + anomal_im * anomal_im
    third_root = jnp.power(dense_safe, -1.0 / 3.0)
    field_pot = beta_coef * fermi - gamma_coef / 3.0 * anomal_sq * third_root / dense_safe
    pair_re = -gamma_coef * anomal_re * third_root
    pair_im = -gamma_coef * anomal_im * third_root
    energy = (
        alpha_coef * kinetic / 2.0
        + 0.6 * beta_coef * dense_safe * fermi
        + gamma_coef * anomal_sq * third_root
    )
    return jnp.stack([field_pot, pair_re, pair_im, energy], axis=2)


def call(kernel, outs, scratch, args, name):
    vmem = pl.BlockSpec(memory_space=pltpu.VMEM)
    flops = 2 * sum(int(np.prod(s)) for s in outs)
    return pl.pallas_call(
        kernel,
        out_shape=tuple(jax.ShapeDtypeStruct(s, jnp.float32) for s in outs),
        in_specs=[vmem] * len(args),
        out_specs=tuple([vmem] * len(outs)),
        scratch_shapes=[pltpu.VMEM(s, d) for s, d in scratch],
        compiler_params=pltpu.CompilerParams(vmem_limit_bytes=48 << 20),
        cost_estimate=pl.CostEstimate(flops=1000 * flops, bytes_accessed=4 * flops, transcendentals=0),
        name=name,
    )(*args)


def exchange_xor(x, axis, bits, count):
    return lax.ppermute(x, axis, [(i, i ^ bits) for i in range(count)])


def local(u_modes, v_modes, potential, pairing):
    planes = u_modes.shape[2]
    slabs = lax.axis_size("grid")
    modes = lax.axis_size("modes")
    paired = slabs == 4 and planes == 16
    f32, bf16 = jnp.float32, jnp.bfloat16
    weights = jnp.asarray(in_plane_matrix())
    own = jnp.concatenate([u_modes[0], v_modes[0], potential[None], pairing], axis=0)

    cross = [(i, (i - 1 if i % 2 == 0 else i + 1) % slabs) for i in range(slabs)]
    up = [(i, (i + 1) % slabs) for i in range(slabs)]
    down = [(j, i) for i, j in up]
    base = 24
    pieces, arrays = [(7, [(0, planes, base, base)])], [own]
    if paired:
        far_slab = lax.ppermute(own, "grid", cross)
        near_slab = exchange_xor(own, "grid", 1, slabs)
        both = jnp.concatenate([far_slab[:4, :REACH], far_slab[:4, planes - REACH :]], axis=1)
        relayed = exchange_xor(both, "grid", 1, slabs)
        pieces += [
            (7, [(0, planes, base - planes, base + planes)]),
            (7, [(0, planes, base + planes, base - planes)]),
            (4, [(0, REACH, base + 2 * planes, base + 2 * planes), (REACH, REACH, base - planes - REACH, base - planes - REACH)]),
        ]
        arrays += [far_slab, near_slab, relayed]
    else:
        reach, step = 0, 0
        while reach < 5 * REACH:
            step += 1
            count = min(planes, 5 * REACH - reach)
            wide = 7 if reach < 4 * REACH else 4
            before = lax.ppermute(
                own[:wide, planes - count :], "grid", [(i, (i + step) % slabs) for i in range(slabs)]
            )
            after = lax.ppermute(
                own[:wide, :count], "grid", [((i + step) % slabs, i) for i in range(slabs)]
            )
            lead, tail = base - reach - count, base + planes + reach
            pieces += [(wide, [(0, count, lead, lead)]), (wide, [(0, count, tail, tail)])]
            arrays += [before, after]
            reach += count

    low_bits = 4 if modes % 4 == 0 else 1
    tall = up16(planes + 32)
    state = (4, 8, planes, LANES)
    psi1, lap1, sums = call(
        functools.partial(stages_kernel, pieces, planes, low_bits),
        [state, state, (4, 2, 4, planes, LANES)],
        [
            ((4, 8, tall + 24, LANES), f32),
            ((4, 8, tall + 8, LANES), f32),
            ((4, 8, tall + 8, LANES), f32),
            ((4, 8, tall + 8, LANES), f32),
            ((4, 8, tall + 8, LANES), f32),
            ((3, 8, tall + 8, LANES), f32),
            ((4, 4, tall, WINDOW), bf16),
            ((4, 4, tall, WINDOW), bf16),
            ((4, 4, tall, BLOCK), f32),
        ],
        arrays + [weights],
        "stages",
    )

    if low_bits == 4:
        total = sums[0:1]
        for k in (1, 2, 3):
            total = total + exchange_xor(sums[k : k + 1], "modes", k, modes)
    else:
        total = sums
    bits = low_bits
    while bits < modes:
        total = total + exchange_xor(total, "modes", bits, modes)
        bits *= 2
    quarter = potentials(total, float(u_modes.shape[0] * modes))
    got = [quarter] + [exchange_xor(quarter, "modes", k, modes) for k in range(1, low_bits)]

    edge = (8, 4 * REACH, LANES)
    mid, first, second, fields, fields_flat = call(
        functools.partial(middle_kernel, paired, planes, low_bits),
        [state, edge, edge, (4, planes, NX * NY), (4, 2, 4, planes, LANES)],
        [],
        got + [psi1, lap1],
        "middle",
    )
    if paired:
        first = lax.ppermute(first, "grid", cross)
        second = exchange_xor(second, "grid", 1, slabs)
    else:
        first = lax.ppermute(first, "grid", down)
        second = lax.ppermute(second, "grid", up)
    flat = up16(planes)
    (part,) = call(
        functools.partial(inner_kernel, planes),
        [state],
        [
            ((4, 8, flat + 16, LANES), f32),
            ((4, 4, flat, WINDOW), bf16),
            ((4, 4, flat, WINDOW), bf16),
            ((4, 4, flat, BLOCK), f32),
        ],
        [psi1, lap1, mid, fields_flat, weights],
        "inner",
    )
    u_next, v_next = call(
        functools.partial(edge_kernel, paired, planes),
        [u_modes.shape, v_modes.shape],
        [],
        [part, first, second],
        "edges",
    )
    return u_next, v_next, fields


def solution(mesh):
    wide = P("modes", None, "grid", None)
    return jax.shard_map(
        local,
        mesh=mesh,
        in_specs=(wide, wide, P("grid", None), P(None, "grid", None)),
        out_specs=(wide, wide, P(None, "grid", None)),
        check_vma=False,
    )
```

profile of v0, /device:TPU:0, one launch (start us, length us, event | category | flops | bytes accessed | tf_op | source)
XLA Modules:
  0.0 51.8 jit_solution(9733882187808171507)
XLA Ops:
  0.6 0.0 copy-start
  0.6 1.2 %pad_maximum_fusion.refs_0_ = f32[7,16,1024]{2,1,0:T(8,128)S(1)} fusion(f32[2,16,1024]{2,1,0:T(8,128)} %param.8, f32[1,16,1024]{2,1,0:T(8,128)} %bitcast.5, f32[2,16,1024]{2,1,0:T(8,128)} %bitcast.3, f32[2,16,1024]{2,1,0:T(8,128)} %bitcast.4), kind=kLoop, calls=%fused_computation | loop fusion | flops 344064 | bytes 917504 | tf_op jit(solution)/shard_map/concatenate | solution.py:346
  1.8 2.5 %collective-permute-start = (f32[7,16,1024]{2,1,0:T(8,128)S(1)}, f32[7,16,1024]{2,1,0:T(8,128)S(1)}, u32[]{:S(2)}, u32[]{:S(2)}) collective-permute-start(f32[7,16,1024]{2,1,0:T(8,128)S(1)} %pad_maximum_fusion.refs_0_), channel_id=1, source_target_pairs={{0,3},{1,2},{2,1},{3,0},{4,7},{5,6},{6,5},{7,4},{8,11},{9,10},{10,... | collective-permute-start | bytes 1376264 | tf_op jit(solution)/shard_map/ppermute | solution.py:354
  4.3 0.7 %collective-permute-start.1 = (f32[7,16,1024]{2,1,0:T(8,128)S(1)}, f32[7,16,1024]{2,1,0:T(8,128)S(1)}, u32[]{:S(2)}, u32[]{:S(2)}) collective-permute-start(f32[7,16,1024]{2,1,0:T(8,128)S(1)} %pad_maximum_fusion.refs_0_), channel_id=1, source_target_pairs={{0,1},{1,0},{2,3},{3,2},{4,5},{5,4},{6,7},{7,6},{8,9},{9,8},{10,11... | collective-permute-start | bytes 1376264 | tf_op jit(solution)/shard_map/ppermute | solution.py:336
  5.0 10.2 %collective-permute-done.refs_1_ = f32[7,16,1024]{2,1,0:T(8,128)S(1)} collective-permute-done((f32[7,16,1024]{2,1,0:T(8,128)S(1)}, f32[7,16,1024]{2,1,0:T(8,128)S(1)}, u32[]{:S(2)}, u32[]{:S(2)}) %collective-permute-start) | collective-permute-done | bytes 458784 | tf_op jit(solution)/shard_map/ppermute | solution.py:354
  15.3 0.2 collective-permute-start.2
  15.4 0.0 collective-permute-done.1.refs_2_
  15.4 1.3 %collective-permute-done.2.refs_3_ = f32[4,8,1024]{2,1,0:T(8,128)S(1)} collective-permute-done((f32[4,8,1024]{2,1,0:T(8,128)S(1)}, f32[4,8,1024]{2,1,0:T(8,128)S(1)}, u32[]{:S(2)}, u32[]{:S(2)}) %collective-permute-start.2) | collective-permute-done | bytes 131104 | tf_op jit(solution)/shard_map/ppermute | solution.py:336
  16.7 0.0 copy-done
  16.7 7.5 %stages.1 = (f32[4,8,16,128]{3,2,1,0:T(8,128)S(1)}, f32[4,8,16,128]{3,2,1,0:T(8,128)S(1)}, f32[4,2,4,16,128]{4,3,2,1,0:T(8,128)S(1)}) custom-call(f32[7,16,1024]{2,1,0:T(8,128)S(1)} %pad_maximum_fusion.refs_0_, f32[7,16,1024]{2,1,0:T(8,128)S(1)} %collective-permute-done.refs_1_, f32[7,16,1024]{2,1,0:T(8,128)S(1)} %collective-permute-done.1.refs_2_, ...), custom_call_target="tpu_custom_call" | custom-call | flops 393216000 | bytes 1572864 | tf_op jit(solution)/shard_map/stages/pallas_call | solution.py:323
  24.2 2.5 %collective-permute-start.3 = (f32[1,2,4,16,128]{4,3,2,1,0:T(8,128)S(1)}, f32[1,2,4,16,128]{4,3,2,1,0:T(8,128)S(1)}, u32[]{:S(2)}, u32[]{:S(2)}) collective-permute-start(f32[1,2,4,16,128]{4,3,2,1,0:T(8,128)S(1)} %get-tuple-element.25), channel_id=1, source_target_pairs={{0,4},{4,0},{8,12},{12,8},{16,20},{20,16},{24,28},{28,24},{1,5},{5... | collective-permute-start | bytes 196616 | tf_op jit(solution)/shard_map/ppermute | solution.py:336
  26.7 1.5 %collective-permute-start.5 = (f32[1,2,4,16,128]{4,3,2,1,0:T(8,128)S(1)}, f32[1,2,4,16,128]{4,3,2,1,0:T(8,128)S(1)}, u32[]{:S(2)}, u32[]{:S(2)}) collective-permute-start(f32[1,2,4,16,128]{4,3,2,1,0:T(8,128)S(1)} %get-tuple-element.26), channel_id=1, source_target_pairs={{0,12},{4,8},{8,4},{12,0},{16,28},{20,24},{24,20},{28,16},{1,13},{... | collective-permute-start | bytes 196616 | tf_op jit(solution)/shard_map/ppermute | solution.py:336
  28.2 0.1 collective-permute-start.4
  28.3 1.6 %collective-permute-done.3 = f32[1,2,4,16,128]{4,3,2,1,0:T(8,128)S(1)} collective-permute-done((f32[1,2,4,16,128]{4,3,2,1,0:T(8,128)S(1)}, f32[1,2,4,16,128]{4,3,2,1,0:T(8,128)S(1)}, u32[]{:S(2)}, u32[]{:S(2)}) %collective-permute-start.3) | collective-permute-done | bytes 65568 | tf_op jit(solution)/shard_map/ppermute | solution.py:336
  29.9 2.4 %collective-permute-done.5 = f32[1,2,4,16,128]{4,3,2,1,0:T(8,128)S(1)} collective-permute-done((f32[1,2,4,16,128]{4,3,2,1,0:T(8,128)S(1)}, f32[1,2,4,16,128]{4,3,2,1,0:T(8,128)S(1)}, u32[]{:S(2)}, u32[]{:S(2)}) %collective-permute-start.5) | collective-permute-done | bytes 65568 | tf_op jit(solution)/shard_map/ppermute | solution.py:336
  32.3 0.1 collective-permute-done.4
  32.5 2.7 %collective-permute-start.6 = (f32[1,2,4,16,128]{4,3,2,1,0:T(8,128)S(1)}, f32[1,2,4,16,128]{4,3,2,1,0:T(8,128)S(1)}, u32[]{:S(2)}, u32[]{:S(2)}) collective-permute-start(f32[1,2,4,16,128]{4,3,2,1,0:T(8,128)S(1)} %add_add_fusion), channel_id=1, source_target_pairs={{0,16},{4,20},{8,24},{12,28},{16,0},{20,4},{24,8},{28,12},{1,17},{... | collective-permute-start | bytes 196616 | tf_op jit(solution)/shard_map/ppermute | solution.py:336
  35.1 2.6 %collective-permute-done.6 = f32[1,2,4,16,128]{4,3,2,1,0:T(8,128)S(1)} collective-permute-done((f32[1,2,4,16,128]{4,3,2,1,0:T(8,128)S(1)}, f32[1,2,4,16,128]{4,3,2,1,0:T(8,128)S(1)}, u32[]{:S(2)}, u32[]{:S(2)}) %collective-permute-start.6) | collective-permute-done | bytes 65568 | tf_op jit(solution)/shard_map/ppermute | solution.py:336
  37.7 0.1 divide_subtract_fusion
  37.8 2.1 %collective-permute-start.9 = (f32[1,2,4,16,128]{4,3,2,1,0:T(8,128)S(1)}, f32[1,2,4,16,128]{4,3,2,1,0:T(8,128)S(1)}, u32[]{:S(2)}, u32[]{:S(2)}) collective-permute-start(f32[1,2,4,16,128]{4,3,2,1,0:T(8,128)S(1)} %pad_maximum_fusion.2.refs_0_), channel_id=1, source_target_pairs={{0,12},{4,8},{8,4},{12,0},{16,28},{20,24},{24,20},{28,16},{1,13},{... | collective-permute-start | bytes 196616 | tf_op jit(solution)/shard_map/ppermute | solution.py:336
  40.0 1.6 %collective-permute-start.8 = (f32[1,2,4,16,128]{4,3,2,1,0:T(8,128)S(1)}, f32[1,2,4,16,128]{4,3,2,1,0:T(8,128)S(1)}, u32[]{:S(2)}, u32[]{:S(2)}) collective-permute-start(f32[1,2,4,16,128]{4,3,2,1,0:T(8,128)S(1)} %pad_maximum_fusion.2.refs_0_), channel_id=1, source_target_pairs={{0,8},{4,12},{8,0},{12,4},{16,24},{20,28},{24,16},{28,20},{1,9},{5... | collective-permute-start | bytes 196616 | tf_op jit(solution)/shard_map/ppermute | solution.py:336
  41.6 0.0 collective-permute-start.7
  41.6 1.5 %collective-permute-done.9.refs_3_ = f32[1,2,4,16,128]{4,3,2,1,0:T(8,128)S(1)} collective-permute-done((f32[1,2,4,16,128]{4,3,2,1,0:T(8,128)S(1)}, f32[1,2,4,16,128]{4,3,2,1,0:T(8,128)S(1)}, u32[]{:S(2)}, u32[]{:S(2)}) %collective-permute-start.9) | collective-permute-done | bytes 65568 | tf_op jit(solution)/shard_map/ppermute | solution.py:336
  43.0 1.5 %collective-permute-done.8.refs_2_ = f32[1,2,4,16,128]{4,3,2,1,0:T(8,128)S(1)} collective-permute-done((f32[1,2,4,16,128]{4,3,2,1,0:T(8,128)S(1)}, f32[1,2,4,16,128]{4,3,2,1,0:T(8,128)S(1)}, u32[]{:S(2)}, u32[]{:S(2)}) %collective-permute-start.8) | collective-permute-done | bytes 65568 | tf_op jit(solution)/shard_map/ppermute | solution.py:336
  44.5 1.3 %collective-permute-done.7.refs_1_ = f32[1,2,4,16,128]{4,3,2,1,0:T(8,128)S(1)} collective-permute-done((f32[1,2,4,16,128]{4,3,2,1,0:T(8,128)S(1)}, f32[1,2,4,16,128]{4,3,2,1,0:T(8,128)S(1)}, u32[]{:S(2)}, u32[]{:S(2)}) %collective-permute-start.7) | collective-permute-done | bytes 65568 | tf_op jit(solution)/shard_map/ppermute | solution.py:336
  45.8 0.8 %middle.1 = (f32[4,8,16,128]{3,2,1,0:T(8,128)S(1)}, f32[8,16,128]{2,1,0:T(8,128)S(1)}, f32[8,16,128]{2,1,0:T(8,128)S(1)}, f32[4,16,1024]{2,1,0:T(8,128)}, f32[4,2,4,16,128]{4,3,2,1,0:T(8,128)S(1)}) custom-call(f32[1,2,4,16,128]{4,3,2,1,0:T(8,128)S(1)} %pad_maximum_fusion.2.refs_0_, f32[1,2,4,16,128]{4,3,2,1,0:T(8,128)S(1)} %collective-permute-done.7.refs_1_, ...), custom_call_target="tpu_custom_call" | custom-call | flops 458752000 | bytes 1835008 | tf_op jit(solution)/shard_map/middle/pallas_call | solution.py:323
  46.6 0.0 collective-permute-start.10
  46.6 1.6 %collective-permute-start.11 = (f32[8,16,128]{2,1,0:T(8,128)S(1)}, f32[8,16,128]{2,1,0:T(8,128)S(1)}, u32[]{:S(2)}, u32[]{:S(2)}) collective-permute-start(f32[8,16,128]{2,1,0:T(8,128)S(1)} %get-tuple-element.19), channel_id=1, source_target_pairs={{0,1},{1,0},{2,3},{3,2},{4,5},{5,4},{6,7},{7,6},{8,9},{9,8},{10,11... | collective-permute-start | bytes 196616 | tf_op jit(solution)/shard_map/ppermute | solution.py:336
  48.2 0.7 %inner.1.refs_0_ = f32[4,8,16,128]{3,2,1,0:T(8,128)S(1)} custom-call(f32[4,8,16,128]{3,2,1,0:T(8,128)S(1)} %get-tuple-element.13.refs_4_.refs_0_, f32[4,8,16,128]{3,2,1,0:T(8,128)S(1)} %get-tuple-element.14.refs_5_.refs_1_, f32[4,8,16,128]{3,2,1,0:T(8,128)S(1)} %get-tuple-element.16.refs_2_, f32[4,2,4,16,128]{4,3,2,1,0:T(8,128)S(1)} %get-tuple-element.17.refs_3_, ...), custom_call_target="tpu_custom_call" | custom-call | flops 131072000 | bytes 524288 | tf_op jit(solution)/shard_map/inner/pallas_call | solution.py:323
  49.0 1.9 %collective-permute-done.10.refs_1_ = f32[8,16,128]{2,1,0:T(8,128)S(1)} collective-permute-done((f32[8,16,128]{2,1,0:T(8,128)S(1)}, f32[8,16,128]{2,1,0:T(8,128)S(1)}, u32[]{:S(2)}, u32[]{:S(2)}) %collective-permute-start.10) | collective-permute-done | bytes 65568 | tf_op jit(solution)/shard_map/ppermute | solution.py:424
  50.9 0.0 collective-permute-done.11.refs_2_
  50.9 0.9 %edges.1 = (f32[1,2,16,1024]{3,2,1,0:T(8,128)}, f32[1,2,16,1024]{3,2,1,0:T(8,128)}) custom-call(f32[4,8,16,128]{3,2,1,0:T(8,128)S(1)} %inner.1.refs_0_, f32[8,16,128]{2,1,0:T(8,128)S(1)} %collective-permute-done.10.refs_1_, f32[8,16,128]{2,1,0:T(8,128)S(1)} %collective-permute-done.11.refs_2_), custom_call_target="tpu_custom_call" | custom-call | flops 131072000 | bytes 524288 | tf_op jit(solution)/shard_map/edges/pallas_call | solution.py:323
  (6 shorter events, 0.1 us)
Async XLA Ops:
  0.6 16.1 %copy-start = (bf16[1536,256]{1,0:T(8,128)(2,1)S(1)}, bf16[1536,256]{1,0:T(8,128)(2,1)}, u32[]{:S(2)}) copy-start(bf16[1536,256]{1,0:T(8,128)(2,1)} %constant.44.clone.refs_4_) | copy-start | bytes 2359300
  1.8 13.4 %collective-permute-start = (f32[7,16,1024]{2,1,0:T(8,128)S(1)}, f32[7,16,1024]{2,1,0:T(8,128)S(1)}, u32[]{:S(2)}, u32[]{:S(2)}) collective-permute-start(f32[7,16,1024]{2,1,0:T(8,128)S(1)} %pad_maximum_fusion.refs_0_), channel_id=1, source_target_pairs={{0,3},{1,2},{2,1},{3,0},{4,7},{5,6},{6,5},{7,4},{8,11},{9,10},{10,... | collective-permute-start | bytes 1376264 | tf_op jit(solution)/shard_map/ppermute | solution.py:354
  4.3 11.1 %collective-permute-start.1 = (f32[7,16,1024]{2,1,0:T(8,128)S(1)}, f32[7,16,1024]{2,1,0:T(8,128)S(1)}, u32[]{:S(2)}, u32[]{:S(2)}) collective-permute-start(f32[7,16,1024]{2,1,0:T(8,128)S(1)} %pad_maximum_fusion.refs_0_), channel_id=1, source_target_pairs={{0,1},{1,0},{2,3},{3,2},{4,5},{5,4},{6,7},{7,6},{8,9},{9,8},{10,11... | collective-permute-start | bytes 1376264 | tf_op jit(solution)/shard_map/ppermute | solution.py:336
  15.3 1.4 %collective-permute-start.2 = (f32[4,8,1024]{2,1,0:T(8,128)S(1)}, f32[4,8,1024]{2,1,0:T(8,128)S(1)}, u32[]{:S(2)}, u32[]{:S(2)}) collective-permute-start(f32[4,8,1024]{2,1,0:T(8,128)S(1)} %pad_maximum_fusion.1), channel_id=1, source_target_pairs={{0,1},{1,0},{2,3},{3,2},{4,5},{5,4},{6,7},{7,6},{8,9},{9,8},{10,11... | collective-permute-start | bytes 393224 | tf_op jit(solution)/shard_map/ppermute | solution.py:336
  24.2 5.7 %collective-permute-start.3 = (f32[1,2,4,16,128]{4,3,2,1,0:T(8,128)S(1)}, f32[1,2,4,16,128]{4,3,2,1,0:T(8,128)S(1)}, u32[]{:S(2)}, u32[]{:S(2)}) collective-permute-start(f32[1,2,4,16,128]{4,3,2,1,0:T(8,128)S(1)} %get-tuple-element.25), channel_id=1, source_target_pairs={{0,4},{4,0},{8,12},{12,8},{16,20},{20,16},{24,28},{28,24},{1,5},{5... | collective-permute-start | bytes 196616 | tf_op jit(solution)/shard_map/ppermute | solution.py:336
  26.7 5.7 %collective-permute-start.5 = (f32[1,2,4,16,128]{4,3,2,1,0:T(8,128)S(1)}, f32[1,2,4,16,128]{4,3,2,1,0:T(8,128)S(1)}, u32[]{:S(2)}, u32[]{:S(2)}) collective-permute-start(f32[1,2,4,16,128]{4,3,2,1,0:T(8,128)S(1)} %get-tuple-element.26), channel_id=1, source_target_pairs={{0,12},{4,8},{8,4},{12,0},{16,28},{20,24},{24,20},{28,16},{1,13},{... | collective-permute-start | bytes 196616 | tf_op jit(solution)/shard_map/ppermute | solution.py:336
  28.2 4.3 %collective-permute-start.4 = (f32[1,2,4,16,128]{4,3,2,1,0:T(8,128)S(1)}, f32[1,2,4,16,128]{4,3,2,1,0:T(8,128)S(1)}, u32[]{:S(2)}, u32[]{:S(2)}) collective-permute-start(f32[1,2,4,16,128]{4,3,2,1,0:T(8,128)S(1)} %get-tuple-element.27), channel_id=1, source_target_pairs={{0,8},{4,12},{8,0},{12,4},{16,24},{20,28},{24,16},{28,20},{1,9},{5... | collective-permute-start | bytes 196616 | tf_op jit(solution)/shard_map/ppermute | solution.py:336
  32.5 5.2 %collective-permute-start.6 = (f32[1,2,4,16,128]{4,3,2,1,0:T(8,128)S(1)}, f32[1,2,4,16,128]{4,3,2,1,0:T(8,128)S(1)}, u32[]{:S(2)}, u32[]{:S(2)}) collective-permute-start(f32[1,2,4,16,128]{4,3,2,1,0:T(8,128)S(1)} %add_add_fusion), channel_id=1, source_target_pairs={{0,16},{4,20},{8,24},{12,28},{16,0},{20,4},{24,8},{28,12},{1,17},{... | collective-permute-start | bytes 196616 | tf_op jit(solution)/shard_map/ppermute | solution.py:336
  37.8 5.2 %collective-permute-start.9 = (f32[1,2,4,16,128]{4,3,2,1,0:T(8,128)S(1)}, f32[1,2,4,16,128]{4,3,2,1,0:T(8,128)S(1)}, u32[]{:S(2)}, u32[]{:S(2)}) collective-permute-start(f32[1,2,4,16,128]{4,3,2,1,0:T(8,128)S(1)} %pad_maximum_fusion.2.refs_0_), channel_id=1, source_target_pairs={{0,12},{4,8},{8,4},{12,0},{16,28},{20,24},{24,20},{28,16},{1,13},{... | collective-permute-start | bytes 196616 | tf_op jit(solution)/shard_map/ppermute | solution.py:336
  40.0 4.6 %collective-permute-start.8 = (f32[1,2,4,16,128]{4,3,2,1,0:T(8,128)S(1)}, f32[1,2,4,16,128]{4,3,2,1,0:T(8,128)S(1)}, u32[]{:S(2)}, u32[]{:S(2)}) collective-permute-start(f32[1,2,4,16,128]{4,3,2,1,0:T(8,128)S(1)} %pad_maximum_fusion.2.refs_0_), channel_id=1, source_target_pairs={{0,8},{4,12},{8,0},{12,4},{16,24},{20,28},{24,16},{28,20},{1,9},{5... | collective-permute-start | bytes 196616 | tf_op jit(solution)/shard_map/ppermute | solution.py:336
  41.6 4.3 %collective-permute-start.7 = (f32[1,2,4,16,128]{4,3,2,1,0:T(8,128)S(1)}, f32[1,2,4,16,128]{4,3,2,1,0:T(8,128)S(1)}, u32[]{:S(2)}, u32[]{:S(2)}) collective-permute-start(f32[1,2,4,16,128]{4,3,2,1,0:T(8,128)S(1)} %pad_maximum_fusion.2.refs_0_), channel_id=1, source_target_pairs={{0,4},{4,0},{8,12},{12,8},{16,20},{20,16},{24,28},{28,24},{1,5},{5... | collective-permute-start | bytes 196616 | tf_op jit(solution)/shard_map/ppermute | solution.py:336
  46.6 4.3 %collective-permute-start.10 = (f32[8,16,128]{2,1,0:T(8,128)S(1)}, f32[8,16,128]{2,1,0:T(8,128)S(1)}, u32[]{:S(2)}, u32[]{:S(2)}) collective-permute-start(f32[8,16,128]{2,1,0:T(8,128)S(1)} %get-tuple-element.18), channel_id=1, source_target_pairs={{0,3},{1,2},{2,1},{3,0},{4,7},{5,6},{6,5},{7,4},{8,11},{9,10},{10,... | collective-permute-start | bytes 196616 | tf_op jit(solution)/shard_map/ppermute | solution.py:424
  46.6 4.3 %collective-permute-start.11 = (f32[8,16,128]{2,1,0:T(8,128)S(1)}, f32[8,16,128]{2,1,0:T(8,128)S(1)}, u32[]{:S(2)}, u32[]{:S(2)}) collective-permute-start(f32[8,16,128]{2,1,0:T(8,128)S(1)} %get-tuple-element.19), channel_id=1, source_target_pairs={{0,1},{1,0},{2,3},{3,2},{4,5},{5,4},{6,7},{7,6},{8,9},{9,8},{10,11... | collective-permute-start | bytes 196616 | tf_op jit(solution)/shard_map/ppermute | solution.py:336
where the time goes:
time: 51.9 us; the launch traced here: 51.8 us
  waiting for transfers between devices  24.5 us (47%)
  starting transfers between devices  15.4 us (30%)
  Pallas kernels  9.82 us (19%)
  other arithmetic  1.29 us (2%)
  between operations  0.71 us (1%)
    ppermute x10, starting transfers between devices, exchange_xor(): return lax.ppermute(x, axis, [(i, i ^ bits) for i in range(count)])  13 us
    ppermute x10, waiting for transfers between devices, exchange_xor(): return lax.ppermute(x, axis, [(i, i ^ bits) for i in range(count)])  12.3 us
    ppermute x1, waiting for transfers between devices, local(): far_slab = lax.ppermute(own, 'grid', cross)  10.2 us
    pallas_call x4, Pallas kernels, call(): pl.pallas_call(kernel, out_shape=tuple((jax.ShapeDtypeStruct(s, jnp.float...  9.82 us
    ppermute x1, starting transfers between devices, local(): far_slab = lax.ppermute(own, 'grid', cross)  2.47 us
    ppermute x1, waiting for transfers between devices, local(): first = lax.ppermute(first, 'grid', cross)  1.93 us
    concatenate x1, other arithmetic, local(): jnp.concatenate([u_modes[0], v_modes[0], potential[None], pairing], axis=0)  1.17 us
  transfers between devices with their start and end apart: 12, of which 10 were waited for; matrix products, arithmetic and copies ran while one was open for 0% of the time, Pallas kernels for 1%

commit v1 on v0

--- a/solution.py
+++ b/solution.py
@@ -22,6 +22,11 @@
 LANES = 128
 BLOCK = 256
 WINDOW = BLOCK + 2 * LANES
+kinetic_coef = -0.5 * alpha_coef
+unit = stencil_coef[1]
+near_coef = tuple(c / unit for c in stencil_coef)
+unit_coef = kinetic_coef * unit
+centre_coef = 3.0 * kinetic_coef * stencil_coef[0]
 
 
 def in_plane_matrix():
@@ -32,58 +37,72 @@
             out = y * NX + x
             for k in range(1, REACH + 1):
                 for sign in (-1, 1):
-                    mat[(y + REACH) * NX + (x + sign * k) % NX, out] += stencil_coef[k]
-                    mat[(y + REACH + sign * k) * NX + x, out] += stencil_coef[k]
-    mat = mat.astype(np.float32)
-    high = mat.astype(jnp.bfloat16)
-    low = (mat - high.astype(np.float32)).astype(jnp.bfloat16)
-    return np.concatenate([high, high, low], axis=0)
+                    mat[(y + REACH) * NX + (x + sign * k) % NX, out] += near_coef[k]
+                    mat[(y + REACH + sign * k) * NX + x, out] += near_coef[k]
+    mat = mat.astype(jnp.bfloat16)
+    return np.concatenate([mat, mat], axis=0)
 
 
 def up16(n):
     return -(-n // 16) * 16
 
 
-def laplace_in_plane(read, rows, w_ref, hi_ref, lo_ref, xy_ref):
-    for c in range(4):
-        for j in range(8):
-            value = read(c, j)
-            high = value.astype(jnp.bfloat16)
-            low = (value - high.astype(jnp.float32)).astype(jnp.bfloat16)
-            if j % 2 == 0:
-                places = ((j // 2, 1), ((j // 2 + 3) % 4, 3))
-            else:
-                places = ((j // 2, 2), ((j // 2 + 1) % 4, 0))
-            for big, part in places:
-                hi_ref[big, c, :rows, part * LANES : (part + 1) * LANES] = high
-                lo_ref[big, c, :rows, part * LANES : (part + 1) * LANES] = low
-    high = hi_ref[:, :, :rows, :].reshape(16 * rows, WINDOW)
-    low = lo_ref[:, :, :rows, :].reshape(16 * rows, WINDOW)
+def put_split(value, c, j, row, hi_ref, lo_ref):
+    count = value.shape[0]
+    high = value.astype(jnp.bfloat16)
+    low = (value - high.astype(jnp.float32)).astype(jnp.bfloat16)
+    if j % 2 == 0:
+        places = ((j // 2, 1), ((j // 2 + 3) % 4, 3))
+    else:
+        places = ((j // 2, 2), ((j // 2 + 1) % 4, 0))
+    for big, part in places:
+        hi_ref[big, c, pl.ds(row, count), part * LANES : (part + 1) * LANES] = high
+        lo_ref[big, c, pl.ds(row, count), part * LANES : (part + 1) * LANES] = low
+
+
+GROUP = 2
+
+
+def in_plane(group, rows, w_ref, hi_ref, lo_ref, xy_ref):
+    span = slice(group * GROUP, (group + 1) * GROUP)
+    high = hi_ref[span, :, :rows, :].reshape(GROUP * 4 * rows, WINDOW)
+    low = lo_ref[span, :, :rows, :].reshape(GROUP * 4 * rows, WINDOW)
     total = jnp.dot(
-        jnp.concatenate([high, low, high], axis=1),
-        w_ref[...],
-        preferred_element_type=jnp.float32,
-    )
-    xy_ref[:, :, :rows, :] = total.reshape(4, 4, rows, BLOCK)
-
-
-def z_part(ref, c, j, start, count):
-    centre = ref[c, j, pl.ds(start, count), :]
-    total = (3.0 * stencil_coef[0]) * centre
+        jnp.concatenate([high, low], axis=1), w_ref[...], preferred_element_type=jnp.float32
+    )
+    for half in range(2):
+        xy_ref[span, :, half, :rows, :] = total[:, half * LANES : (half + 1) * LANES].reshape(
+            GROUP, 4, rows, LANES
+        )
+
+
+def in_plane_steps(rows, w_ref, hi_ref, lo_ref, xy_ref):
+    groups = 4 // GROUP
+    in_plane(0, rows, w_ref, hi_ref, lo_ref, xy_ref)
+    for group in range(groups):
+        if group + 1 < groups:
+            in_plane(group + 1, rows, w_ref, hi_ref, lo_ref, xy_ref)
+        for j in range(group * GROUP * 2, (group + 1) * GROUP * 2):
+            yield j
+
+
+def neighbours(ref, xy, c, j, start, xy_start, count):
+    total = xy[j // 2, c, j % 2, pl.ds(xy_start, count), :]
     for k in range(1, REACH + 1):
-        total = total + stencil_coef[k] * (
-            ref[c, j, pl.ds(start + k, count), :] + ref[c, j, pl.ds(start - k, count), :]
-        )
-    return centre, total
-
-
-def slope(f, lap, pot, pr, pi):
-    kin = [-0.5 * alpha_coef * lap[c] + pot * f[c] for c in range(4)]
+        pair = ref[c, j, pl.ds(start + k, count), :] + ref[c, j, pl.ds(start - k, count), :]
+        total = total + (pair if k == 1 else near_coef[k] * pair)
+    return total
+
+
+def slope(f, kin, pr, pi):
     upper_re = kin[0] + pr * f[2] - pi * f[3]
     upper_im = kin[1] + pr * f[3] + pi * f[2]
     lower_re = pr * f[0] + pi * f[1] - kin[2]
     lower_im = pr * f[1] - pi * f[0] - kin[3]
-    return upper_im, -upper_re, lower_im, -lower_re
+    return upper_im, upper_re, lower_im, lower_re
+
+
+signs = (1.0, -1.0, 1.0, -1.0)
 
 
 def chunks(rows, size=16):
@@ -94,8 +113,8 @@
     n = len(pieces)
     parts = refs[:n]
     w_ref = refs[n]
-    psi1_ref, lap1_ref, sums_ref = refs[n + 1 : n + 4]
-    b0, b1, b2, b3, b4, pd, hi, lo, xy = refs[n + 4 :]
+    psi1_ref, kin1_ref, sums_ref = refs[n + 1 : n + 4]
+    b0, b1, b2, b3, b4, pd, hi_a, lo_a, hi_b, lo_b, xy = refs[n + 4 :]
     odd = lax.rem(lax.axis_index("grid"), 2)
     quarter = lax.rem(lax.axis_index("modes"), low_bits)
 
@@ -105,97 +124,86 @@
                 dst = dst_even
                 dst_pd = dst_even - 8
             else:
-                dst = pl.multiple_of(dst_even + odd * (dst_odd - dst_even), 8)
-                dst_pd = pl.multiple_of(dst - 8, 8)
+                step = pl.multiple_of(odd * (dst_odd - dst_even), 16)
+                dst = pl.multiple_of(dst_even + step, 8)
+                dst_pd = pl.multiple_of(dst_even - 8 + step, 16 if (dst_even - 8) % 16 == 0 else 8)
             for c in range(channels):
                 for j in range(8):
                     value = ref[c, src : src + count, j * LANES : (j + 1) * LANES]
                     if c < 4:
                         b0[c, j, pl.ds(dst, count), :] = value
+                        if channels > 4:
+                            put_split(value, c, j, dst_pd, hi_a, lo_a)
                     else:
+                        if c == 4:
+                            value = value + centre_coef
                         pd[c - 4, j, pl.ds(dst_pd, count), :] = value
 
-    def run(src, start, rows, store):
-        tall = up16(rows)
-        laplace_in_plane(
-            lambda c, j: src[c, j, pl.ds(start, tall), :], tall, w_ref, hi, lo, xy
-        )
+    def run(src, start, xy_start, rows, hi, lo, store):
+        tall = up16(rows + 2 * xy_start)
         margin = (planes + 32 - rows) // 2
-
-        def body(big, carry):
-            for half in range(2):
-                j = big * 2 + half
-                for r, count in chunks(rows):
-                    centre, lap = [], []
-                    for c in range(4):
-                        f, z = z_part(src, c, j, start + r, count)
-                        centre.append(f)
-                        lap.append(
-                            z + xy[big, c, pl.ds(r, count), half * LANES : (half + 1) * LANES]
-                        )
-                    store(big, half, j, r, count, margin + r, centre, lap)
-            return carry
-
-        lax.fori_loop(0, 4, body, 0)
-
-    def fields_at(j, row, count):
-        return [pd[i, j, pl.ds(row, count), :] for i in range(3)]
-
-    def stage(dst, factor):
-        def store(big, half, j, r, count, row, centre, lap):
-            k = slope(centre, lap, *fields_at(j, row, count))
+        for j in in_plane_steps(tall, w_ref, hi, lo, xy):
+            for r, count in chunks(rows):
+                f = [src[c, j, pl.ds(start + r, count), :] for c in range(4)]
+                near = [
+                    neighbours(src, xy, c, j, start + r, xy_start + r, count) for c in range(4)
+                ]
+                store(j, r, count, margin + r, f, near)
+
+    def derivative(j, row, count, f, near):
+        pot, pr, pi = [pd[i, j, pl.ds(row, count), :] for i in range(3)]
+        return slope(f, [unit_coef * near[c] + pot * f[c] for c in range(4)], pr, pi)
+
+    def stage(dst, factor, hi, lo):
+        def store(j, r, count, row, f, near):
+            k = derivative(j, row, count, f, near)
             for c in range(4):
-                dst[c, j, pl.ds(r, count), :] = b0[c, j, pl.ds(row + 8, count), :] + factor * k[c]
+                value = b0[c, j, pl.ds(row + 8, count), :] + (signs[c] * factor) * k[c]
+                dst[c, j, pl.ds(r, count), :] = value
+                put_split(value, c, j, r, hi, lo)
 
         return store
 
-    run(b0, 8, planes + 32, stage(b1, 0.5 * time_step))
-    run(b1, 4, planes + 24, stage(b2, 0.5 * time_step))
-    run(b2, 4, planes + 16, stage(b3, time_step))
-
-    def last(big, half, j, r, count, row, centre, lap):
-        k = slope(centre, lap, *fields_at(j, row, count))
+    run(b0, 8, 0, planes + 32, hi_a, lo_a, stage(b1, 0.5 * time_step, hi_b, lo_b))
+    run(b1, 4, 4, planes + 24, hi_b, lo_b, stage(b2, 0.5 * time_step, hi_a, lo_a))
+    run(b2, 4, 4, planes + 16, hi_a, lo_a, stage(b3, time_step, hi_b, lo_b))
+
+    def last(j, r, count, row, f, near):
+        k = derivative(j, row, count, f, near)
         for c in range(4):
             early = (
                 b1[c, j, pl.ds(r + 12, count), :]
                 - b0[c, j, pl.ds(r + 20, count), :]
                 + 2.0 * b2[c, j, pl.ds(r + 8, count), :]
-                + centre[c]
+                + f[c]
             )
-            b4[c, j, pl.ds(r, count), :] = early * (1.0 / 3.0) + (time_step / 6.0) * k[c]
-
-    run(b3, 4, planes + 8, last)
-
-    def finish(big, half, j, r, count, row, f, lap):
+            value = early * (1.0 / 3.0) + (signs[c] * time_step / 6.0) * k[c]
+            b4[c, j, pl.ds(r, count), :] = value
+            put_split(value, c, j, r, hi_a, lo_a)
+
+    run(b3, 4, 4, planes + 8, hi_b, lo_b, last)
+
+    def finish(j, r, count, row, f, near):
+        full = [unit_coef * near[c] + centre_coef * f[c] for c in range(4)]
         for c in range(4):
             psi1_ref[c, j, pl.ds(r, count), :] = f[c]
-            lap1_ref[c, j, pl.ds(r, count), :] = lap[c]
+            kin1_ref[c, j, pl.ds(r, count), :] = full[c]
         sums = (
             f[2] * f[2] + f[3] * f[3],
-            f[2] * lap[2] + f[3] * lap[3],
+            f[2] * full[2] + f[3] * full[3],
             f[0] * f[2] + f[1] * f[3],
             f[1] * f[2] - f[0] * f[3],
         )
-        place = lax.bitwise_xor(big, quarter) if low_bits == 4 else big
+        place = lax.bitwise_xor(jnp.int32(j // 2), quarter) if low_bits == 4 else j // 2
         for s in range(4):
-            sums_ref[place, half, s, pl.ds(r, count), :] = sums[s]
-
-    run(b4, 4, planes, finish)
-
-
-def field_reader(parts, low_bits):
-    stack, = parts
-
-    def read(big, half, i):
-        return stack[big, half, i]
-
-    return read
+            sums_ref[place, j % 2, s, pl.ds(r, count), :] = sums[s]
+
+    run(b4, 4, 4, planes, hi_a, lo_a, finish)
 
 
 def middle_kernel(paired, planes, low_bits, *refs):
-    count = len(refs) - 6 - 2
     pieces = refs[:low_bits]
-    psi1, lap1 = refs[low_bits : low_bits + 2]
+    psi1, kin1 = refs[low_bits : low_bits + 2]
     mid, first_send, second_send, fields_out, fields_flat = refs[low_bits + 2 :]
     even = lax.rem(lax.axis_index("grid"), 2) == 0
     quarter = lax.rem(lax.axis_index("modes"), low_bits)
@@ -213,9 +221,9 @@
         for i in range(4):
             fields_out[i, :, j * LANES : (j + 1) * LANES] = now[i]
         f = [psi1[c, j] for c in range(4)]
-        q = slope(f, [lap1[c, j] for c in range(4)], now[0], now[1], now[2])
+        q = slope(f, [kin1[c, j] + now[0] * f[c] for c in range(4)], now[1], now[2])
         for c in range(4):
-            m = f[c] + (0.5 * time_step) * q[c]
+            m = f[c] + (signs[c] * 0.5 * time_step) * q[c]
             mid[c, j] = m
             top, bottom = m[:REACH], m[planes - REACH :]
             if paired:
@@ -227,37 +235,30 @@
 
 
 def inner_kernel(planes, *refs):
-    psi1, lap1, mid, fields_flat, w_ref, part_ref, pad, hi, lo, xy = refs
+    psi1, kin1, mid, fields_flat, w_ref, part_ref, pad, hi, lo, xy = refs
     tall = up16(planes)
     zero = jnp.zeros((8, LANES), jnp.float32)
     for c in range(4):
         for j in range(8):
+            value = mid[c, j]
             pad[c, j, 0:8, :] = zero
-            pad[c, j, 8 : 8 + planes, :] = mid[c, j]
-            for r in range(8 + planes, pad.shape[2], 8):
-                pad[c, j, r : r + 8, :] = zero
-    laplace_in_plane(lambda c, j: pad[c, j, 8 : 8 + tall, :], tall, w_ref, hi, lo, xy)
-
-    def body(big, carry):
-        for half in range(2):
-            j = big * 2 + half
-            for r, count in chunks(planes):
-                field = [fields_flat[big, half, i, pl.ds(r, count), :] for i in range(3)]
-                f = [psi1[c, j, pl.ds(r, count), :] for c in range(4)]
-                q1 = slope(f, [lap1[c, j, pl.ds(r, count), :] for c in range(4)], *field)
-                m, lap = [], []
-                for c in range(4):
-                    centre, z = z_part(pad, c, j, 8 + r, count)
-                    m.append(centre)
-                    lap.append(z + xy[big, c, pl.ds(r, count), half * LANES : (half + 1) * LANES])
-                q2 = slope(m, lap, *field)
-                for c in range(4):
-                    part_ref[c, j, pl.ds(r, count), :] = f[c] + (time_step / 6.0) * (
-                        q1[c] + 2.0 * q2[c]
-                    )
-        return carry
-
-    lax.fori_loop(0, 4, body, 0)
+            pad[c, j, 8 : 8 + planes, :] = value
+            pad[c, j, 8 + planes : 16 + planes, :] = zero
+            put_split(value, c, j, 0, hi, lo)
+
+    for j in in_plane_steps(tall, w_ref, hi, lo, xy):
+        for r, count in chunks(planes):
+            pot, pr, pi = [fields_flat[j // 2, j % 2, i, pl.ds(r, count), :] for i in range(3)]
+            f = [psi1[c, j, pl.ds(r, count), :] for c in range(4)]
+            q1 = slope(f, [kin1[c, j, pl.ds(r, count), :] + pot * f[c] for c in range(4)], pr, pi)
+            m = [pad[c, j, pl.ds(8 + r, count), :] for c in range(4)]
+            pot = pot + centre_coef
+            near = [neighbours(pad, xy, c, j, 8 + r, r, count) for c in range(4)]
+            q2 = slope(m, [unit_coef * near[c] + pot * m[c] for c in range(4)], pr, pi)
+            for c in range(4):
+                part_ref[c, j, pl.ds(r, count), :] = f[c] + (signs[c] * time_step / 6.0) * (
+                    q1[c] + 2.0 * q2[c]
+                )
 
 
 def edge_kernel(paired, planes, *refs):
@@ -299,7 +300,7 @@
 
 def potentials(raw, modes_total):
     density = 2.0 * raw[:, :, 0] / modes_total
-    kinetic = -2.0 * raw[:, :, 1] / modes_total
+    kinetic = (-2.0 / kinetic_coef) * raw[:, :, 1] / modes_total
     anomal_re = raw[:, :, 2] / modes_total
     anomal_im = raw[:, :, 3] / modes_total
     dense_safe = density + epsilon
@@ -381,7 +382,7 @@
     low_bits = 4 if modes % 4 == 0 else 1
     tall = up16(planes + 32)
     state = (4, 8, planes, LANES)
-    psi1, lap1, sums = call(
+    psi1, kin1, sums = call(
         functools.partial(stages_kernel, pieces, planes, low_bits),
         [state, state, (4, 2, 4, planes, LANES)],
         [
@@ -393,7 +394,9 @@
             ((3, 8, tall + 8, LANES), f32),
             ((4, 4, tall, WINDOW), bf16),
             ((4, 4, tall, WINDOW), bf16),
-            ((4, 4, tall, BLOCK), f32),
+            ((4, 4, tall, WINDOW), bf16),
+            ((4, 4, tall, WINDOW), bf16),
+            ((4, 4, 2, tall, LANES), f32),
         ],
         arrays + [weights],
         "stages",
@@ -417,7 +420,7 @@
         functools.partial(middle_kernel, paired, planes, low_bits),
         [state, edge, edge, (4, planes, NX * NY), (4, 2, 4, planes, LANES)],
         [],
-        got + [psi1, lap1],
+        got + [psi1, kin1],
         "middle",
     )
     if paired:
@@ -434,9 +437,9 @@
             ((4, 8, flat + 16, LANES), f32),
             ((4, 4, flat, WINDOW), bf16),
             ((4, 4, flat, WINDOW), bf16),
-            ((4, 4, flat, BLOCK), f32),
+            ((4, 4, 2, flat, LANES), f32),
         ],
-        [psi1, lap1, mid, fields_flat, weights],
+        [psi1, kin1, mid, fields_flat, weights],
         "inner",
     )
     u_next, v_next = call(

time: 51.9 us -> 49 us (0.944)
  Pallas kernels: 9.82 us -> 6.73 us
    pallas_call x4, Pallas kernels: 9.82 us -> 6.73 us  [call(): pl.pallas_call(kernel, out_shape=tuple((jax.ShapeDtypeStruct(s, jnp.float...]
where the time goes in v1:
time: 49 us; the launch traced here: 48.8 us
  waiting for transfers between devices  24.6 us (50%)
  starting transfers between devices  15.5 us (32%)
  Pallas kernels  6.73 us (14%)
  other arithmetic  1.28 us (3%)
  between operations  0.71 us (1%)
    ppermute x10, starting transfers between devices, exchange_xor(): return lax.ppermute(x, axis, [(i, i ^ bits) for i in range(count)])  13 us
    ppermute x10, waiting for transfers between devices, exchange_xor(): return lax.ppermute(x, axis, [(i, i ^ bits) for i in range(count)])  12.3 us
    ppermute x1, waiting for transfers between devices, local(): far_slab = lax.ppermute(own, 'grid', cross)  10.2 us
    pallas_call x4, Pallas kernels, call(): pl.pallas_call(kernel, out_shape=tuple((jax.ShapeDtypeStruct(s, jnp.float...  6.73 us
    ppermute x1, starting transfers between devices, local(): far_slab = lax.ppermute(own, 'grid', cross)  2.47 us
    ppermute x1, waiting for transfers between devices, local(): first = lax.ppermute(first, 'grid', cross)  2.1 us
    concatenate x1, other arithmetic, local(): jnp.concatenate([u_modes[0], v_modes[0], potential[None], pairing], axis=0)  1.15 us
  transfers between devices with their start and end apart: 12, of which 10 were waited for; matrix products, arithmetic and copies ran while one was open for 0% of the time, Pallas kernels for 1%

profile of v1, /device:TPU:0, one launch (start us, length us, event | category | flops | bytes accessed | tf_op | source)
XLA Modules:
  0.0 48.8 jit_solution(3536593391253460820)
XLA Ops:
  0.6 0.0 copy-start
  0.6 1.2 %pad_maximum_fusion.refs_0_ = f32[7,16,1024]{2,1,0:T(8,128)S(1)} fusion(f32[2,16,1024]{2,1,0:T(8,128)} %param.8, f32[1,16,1024]{2,1,0:T(8,128)} %bitcast.5, f32[2,16,1024]{2,1,0:T(8,128)} %bitcast.3, f32[2,16,1024]{2,1,0:T(8,128)} %bitcast.4), kind=kLoop, calls=%fused_computation | loop fusion | flops 344064 | bytes 917504 | tf_op jit(solution)/shard_map/concatenate | solution.py:347
  1.8 2.5 %collective-permute-start = (f32[7,16,1024]{2,1,0:T(8,128)S(1)}, f32[7,16,1024]{2,1,0:T(8,128)S(1)}, u32[]{:S(2)}, u32[]{:S(2)}) collective-permute-start(f32[7,16,1024]{2,1,0:T(8,128)S(1)} %pad_maximum_fusion.refs_0_), channel_id=1, source_target_pairs={{0,3},{1,2},{2,1},{3,0},{4,7},{5,6},{6,5},{7,4},{8,11},{9,10},{10,... | collective-permute-start | bytes 1376264 | tf_op jit(solution)/shard_map/ppermute | solution.py:355
  4.3 0.7 %collective-permute-start.1 = (f32[7,16,1024]{2,1,0:T(8,128)S(1)}, f32[7,16,1024]{2,1,0:T(8,128)S(1)}, u32[]{:S(2)}, u32[]{:S(2)}) collective-permute-start(f32[7,16,1024]{2,1,0:T(8,128)S(1)} %pad_maximum_fusion.refs_0_), channel_id=1, source_target_pairs={{0,1},{1,0},{2,3},{3,2},{4,5},{5,4},{6,7},{7,6},{8,9},{9,8},{10,11... | collective-permute-start | bytes 1376264 | tf_op jit(solution)/shard_map/ppermute | solution.py:337
  5.0 10.2 %collective-permute-done.refs_1_ = f32[7,16,1024]{2,1,0:T(8,128)S(1)} collective-permute-done((f32[7,16,1024]{2,1,0:T(8,128)S(1)}, f32[7,16,1024]{2,1,0:T(8,128)S(1)}, u32[]{:S(2)}, u32[]{:S(2)}) %collective-permute-start) | collective-permute-done | bytes 458784 | tf_op jit(solution)/shard_map/ppermute | solution.py:355
  15.3 0.2 collective-permute-start.2
  15.4 0.0 collective-permute-done.1.refs_2_
  15.4 1.3 %collective-permute-done.2.refs_3_ = f32[4,8,1024]{2,1,0:T(8,128)S(1)} collective-permute-done((f32[4,8,1024]{2,1,0:T(8,128)S(1)}, f32[4,8,1024]{2,1,0:T(8,128)S(1)}, u32[]{:S(2)}, u32[]{:S(2)}) %collective-permute-start.2) | collective-permute-done | bytes 131104 | tf_op jit(solution)/shard_map/ppermute | solution.py:337
  16.7 0.0 copy-done
  16.7 4.5 %stages.1 = (f32[4,8,16,128]{3,2,1,0:T(8,128)S(1)}, f32[4,8,16,128]{3,2,1,0:T(8,128)S(1)}, f32[4,2,4,16,128]{4,3,2,1,0:T(8,128)S(1)}) custom-call(f32[7,16,1024]{2,1,0:T(8,128)S(1)} %pad_maximum_fusion.refs_0_, f32[7,16,1024]{2,1,0:T(8,128)S(1)} %collective-permute-done.refs_1_, f32[7,16,1024]{2,1,0:T(8,128)S(1)} %collective-permute-done.1.refs_2_, ...), custom_call_target="tpu_custom_call" | custom-call | flops 393216000 | bytes 1572864 | tf_op jit(solution)/shard_map/stages/pallas_call | solution.py:324
  21.2 2.5 %collective-permute-start.3 = (f32[1,2,4,16,128]{4,3,2,1,0:T(8,128)S(1)}, f32[1,2,4,16,128]{4,3,2,1,0:T(8,128)S(1)}, u32[]{:S(2)}, u32[]{:S(2)}) collective-permute-start(f32[1,2,4,16,128]{4,3,2,1,0:T(8,128)S(1)} %get-tuple-element.25), channel_id=1, source_target_pairs={{0,4},{4,0},{8,12},{12,8},{16,20},{20,16},{24,28},{28,24},{1,5},{5... | collective-permute-start | bytes 196616 | tf_op jit(solution)/shard_map/ppermute | solution.py:337
  23.8 1.5 %collective-permute-start.5 = (f32[1,2,4,16,128]{4,3,2,1,0:T(8,128)S(1)}, f32[1,2,4,16,128]{4,3,2,1,0:T(8,128)S(1)}, u32[]{:S(2)}, u32[]{:S(2)}) collective-permute-start(f32[1,2,4,16,128]{4,3,2,1,0:T(8,128)S(1)} %get-tuple-element.26), channel_id=1, source_target_pairs={{0,12},{4,8},{8,4},{12,0},{16,28},{20,24},{24,20},{28,16},{1,13},{... | collective-permute-start | bytes 196616 | tf_op jit(solution)/shard_map/ppermute | solution.py:337
  25.3 0.1 collective-permute-start.4
  25.3 1.6 %collective-permute-done.3 = f32[1,2,4,16,128]{4,3,2,1,0:T(8,128)S(1)} collective-permute-done((f32[1,2,4,16,128]{4,3,2,1,0:T(8,128)S(1)}, f32[1,2,4,16,128]{4,3,2,1,0:T(8,128)S(1)}, u32[]{:S(2)}, u32[]{:S(2)}) %collective-permute-start.3) | collective-permute-done | bytes 65568 | tf_op jit(solution)/shard_map/ppermute | solution.py:337
  27.0 2.4 %collective-permute-done.5 = f32[1,2,4,16,128]{4,3,2,1,0:T(8,128)S(1)} collective-permute-done((f32[1,2,4,16,128]{4,3,2,1,0:T(8,128)S(1)}, f32[1,2,4,16,128]{4,3,2,1,0:T(8,128)S(1)}, u32[]{:S(2)}, u32[]{:S(2)}) %collective-permute-start.5) | collective-permute-done | bytes 65568 | tf_op jit(solution)/shard_map/ppermute | solution.py:337
  29.4 0.1 collective-permute-done.4
  29.6 2.7 %collective-permute-start.6 = (f32[1,2,4,16,128]{4,3,2,1,0:T(8,128)S(1)}, f32[1,2,4,16,128]{4,3,2,1,0:T(8,128)S(1)}, u32[]{:S(2)}, u32[]{:S(2)}) collective-permute-start(f32[1,2,4,16,128]{4,3,2,1,0:T(8,128)S(1)} %add_add_fusion), channel_id=1, source_target_pairs={{0,16},{4,20},{8,24},{12,28},{16,0},{20,4},{24,8},{28,12},{1,17},{... | collective-permute-start | bytes 196616 | tf_op jit(solution)/shard_map/ppermute | solution.py:337
  32.2 2.6 %collective-permute-done.6 = f32[1,2,4,16,128]{4,3,2,1,0:T(8,128)S(1)} collective-permute-done((f32[1,2,4,16,128]{4,3,2,1,0:T(8,128)S(1)}, f32[1,2,4,16,128]{4,3,2,1,0:T(8,128)S(1)}, u32[]{:S(2)}, u32[]{:S(2)}) %collective-permute-start.6) | collective-permute-done | bytes 65568 | tf_op jit(solution)/shard_map/ppermute | solution.py:337
  34.8 0.1 divide_subtract_fusion
  34.9 2.1 %collective-permute-start.9 = (f32[1,2,4,16,128]{4,3,2,1,0:T(8,128)S(1)}, f32[1,2,4,16,128]{4,3,2,1,0:T(8,128)S(1)}, u32[]{:S(2)}, u32[]{:S(2)}) collective-permute-start(f32[1,2,4,16,128]{4,3,2,1,0:T(8,128)S(1)} %pad_maximum_fusion.2.refs_0_), channel_id=1, source_target_pairs={{0,12},{4,8},{8,4},{12,0},{16,28},{20,24},{24,20},{28,16},{1,13},{... | collective-permute-start | bytes 196616 | tf_op jit(solution)/shard_map/ppermute | solution.py:337
  37.0 1.6 %collective-permute-start.8 = (f32[1,2,4,16,128]{4,3,2,1,0:T(8,128)S(1)}, f32[1,2,4,16,128]{4,3,2,1,0:T(8,128)S(1)}, u32[]{:S(2)}, u32[]{:S(2)}) collective-permute-start(f32[1,2,4,16,128]{4,3,2,1,0:T(8,128)S(1)} %pad_maximum_fusion.2.refs_0_), channel_id=1, source_target_pairs={{0,8},{4,12},{8,0},{12,4},{16,24},{20,28},{24,16},{28,20},{1,9},{5... | collective-permute-start | bytes 196616 | tf_op jit(solution)/shard_map/ppermute | solution.py:337
  38.6 0.0 collective-permute-start.7
  38.6 1.5 %collective-permute-done.9.refs_3_ = f32[1,2,4,16,128]{4,3,2,1,0:T(8,128)S(1)} collective-permute-done((f32[1,2,4,16,128]{4,3,2,1,0:T(8,128)S(1)}, f32[1,2,4,16,128]{4,3,2,1,0:T(8,128)S(1)}, u32[]{:S(2)}, u32[]{:S(2)}) %collective-permute-start.9) | collective-permute-done | bytes 65568 | tf_op jit(solution)/shard_map/ppermute | solution.py:337
  40.1 1.5 %collective-permute-done.8.refs_2_ = f32[1,2,4,16,128]{4,3,2,1,0:T(8,128)S(1)} collective-permute-done((f32[1,2,4,16,128]{4,3,2,1,0:T(8,128)S(1)}, f32[1,2,4,16,128]{4,3,2,1,0:T(8,128)S(1)}, u32[]{:S(2)}, u32[]{:S(2)}) %collective-permute-start.8) | collective-permute-done | bytes 65568 | tf_op jit(solution)/shard_map/ppermute | solution.py:337
  41.6 1.3 %collective-permute-done.7.refs_1_ = f32[1,2,4,16,128]{4,3,2,1,0:T(8,128)S(1)} collective-permute-done((f32[1,2,4,16,128]{4,3,2,1,0:T(8,128)S(1)}, f32[1,2,4,16,128]{4,3,2,1,0:T(8,128)S(1)}, u32[]{:S(2)}, u32[]{:S(2)}) %collective-permute-start.7) | collective-permute-done | bytes 65568 | tf_op jit(solution)/shard_map/ppermute | solution.py:337
  42.9 0.8 %middle.1 = (f32[4,8,16,128]{3,2,1,0:T(8,128)S(1)}, f32[8,16,128]{2,1,0:T(8,128)S(1)}, f32[8,16,128]{2,1,0:T(8,128)S(1)}, f32[4,16,1024]{2,1,0:T(8,128)}, f32[4,2,4,16,128]{4,3,2,1,0:T(8,128)S(1)}) custom-call(f32[1,2,4,16,128]{4,3,2,1,0:T(8,128)S(1)} %pad_maximum_fusion.2.refs_0_, f32[1,2,4,16,128]{4,3,2,1,0:T(8,128)S(1)} %collective-permute-done.7.refs_1_, ...), custom_call_target="tpu_custom_call" | custom-call | flops 458752000 | bytes 1835008 | tf_op jit(solution)/shard_map/middle/pallas_call | solution.py:324
  43.7 0.0 collective-permute-start.10
  43.7 1.6 %collective-permute-start.11 = (f32[8,16,128]{2,1,0:T(8,128)S(1)}, f32[8,16,128]{2,1,0:T(8,128)S(1)}, u32[]{:S(2)}, u32[]{:S(2)}) collective-permute-start(f32[8,16,128]{2,1,0:T(8,128)S(1)} %get-tuple-element.19), channel_id=1, source_target_pairs={{0,1},{1,0},{2,3},{3,2},{4,5},{5,4},{6,7},{7,6},{8,9},{9,8},{10,11... | collective-permute-start | bytes 196616 | tf_op jit(solution)/shard_map/ppermute | solution.py:337
  45.3 0.6 %inner.1.refs_0_ = f32[4,8,16,128]{3,2,1,0:T(8,128)S(1)} custom-call(f32[4,8,16,128]{3,2,1,0:T(8,128)S(1)} %get-tuple-element.13.refs_4_.refs_0_, f32[4,8,16,128]{3,2,1,0:T(8,128)S(1)} %get-tuple-element.14.refs_5_.refs_1_, f32[4,8,16,128]{3,2,1,0:T(8,128)S(1)} %get-tuple-element.16.refs_2_, f32[4,2,4,16,128]{4,3,2,1,0:T(8,128)S(1)} %get-tuple-element.17.refs_3_, ...), custom_call_target="tpu_custom_call" | custom-call | flops 131072000 | bytes 524288 | tf_op jit(solution)/shard_map/inner/pallas_call | solution.py:324
  45.9 2.1 %collective-permute-done.10.refs_1_ = f32[8,16,128]{2,1,0:T(8,128)S(1)} collective-permute-done((f32[8,16,128]{2,1,0:T(8,128)S(1)}, f32[8,16,128]{2,1,0:T(8,128)S(1)}, u32[]{:S(2)}, u32[]{:S(2)}) %collective-permute-start.10) | collective-permute-done | bytes 65568 | tf_op jit(solution)/shard_map/ppermute | solution.py:427
  48.0 0.0 collective-permute-done.11.refs_2_
  48.0 0.9 %edges.1 = (f32[1,2,16,1024]{3,2,1,0:T(8,128)}, f32[1,2,16,1024]{3,2,1,0:T(8,128)}) custom-call(f32[4,8,16,128]{3,2,1,0:T(8,128)S(1)} %inner.1.refs_0_, f32[8,16,128]{2,1,0:T(8,128)S(1)} %collective-permute-done.10.refs_1_, f32[8,16,128]{2,1,0:T(8,128)S(1)} %collective-permute-done.11.refs_2_), custom_call_target="tpu_custom_call" | custom-call | flops 131072000 | bytes 524288 | tf_op jit(solution)/shard_map/edges/pallas_call | solution.py:324
  (6 shorter events, 0.1 us)
Async XLA Ops:
  0.6 16.0 %copy-start = (bf16[1024,256]{1,0:T(8,128)(2,1)S(1)}, bf16[1024,256]{1,0:T(8,128)(2,1)}, u32[]{:S(2)}) copy-start(bf16[1024,256]{1,0:T(8,128)(2,1)} %constant.43.clone.refs_4_) | copy-start | bytes 1572868
  1.8 13.4 %collective-permute-start = (f32[7,16,1024]{2,1,0:T(8,128)S(1)}, f32[7,16,1024]{2,1,0:T(8,128)S(1)}, u32[]{:S(2)}, u32[]{:S(2)}) collective-permute-start(f32[7,16,1024]{2,1,0:T(8,128)S(1)} %pad_maximum_fusion.refs_0_), channel_id=1, source_target_pairs={{0,3},{1,2},{2,1},{3,0},{4,7},{5,6},{6,5},{7,4},{8,11},{9,10},{10,... | collective-permute-start | bytes 1376264 | tf_op jit(solution)/shard_map/ppermute | solution.py:355
  4.3 11.1 %collective-permute-start.1 = (f32[7,16,1024]{2,1,0:T(8,128)S(1)}, f32[7,16,1024]{2,1,0:T(8,128)S(1)}, u32[]{:S(2)}, u32[]{:S(2)}) collective-permute-start(f32[7,16,1024]{2,1,0:T(8,128)S(1)} %pad_maximum_fusion.refs_0_), channel_id=1, source_target_pairs={{0,1},{1,0},{2,3},{3,2},{4,5},{5,4},{6,7},{7,6},{8,9},{9,8},{10,11... | collective-permute-start | bytes 1376264 | tf_op jit(solution)/shard_map/ppermute | solution.py:337
  15.3 1.4 %collective-permute-start.2 = (f32[4,8,1024]{2,1,0:T(8,128)S(1)}, f32[4,8,1024]{2,1,0:T(8,128)S(1)}, u32[]{:S(2)}, u32[]{:S(2)}) collective-permute-start(f32[4,8,1024]{2,1,0:T(8,128)S(1)} %pad_maximum_fusion.1), channel_id=1, source_target_pairs={{0,1},{1,0},{2,3},{3,2},{4,5},{5,4},{6,7},{7,6},{8,9},{9,8},{10,11... | collective-permute-start | bytes 393224 | tf_op jit(solution)/shard_map/ppermute | solution.py:337
  21.2 5.7 %collective-permute-start.3 = (f32[1,2,4,16,128]{4,3,2,1,0:T(8,128)S(1)}, f32[1,2,4,16,128]{4,3,2,1,0:T(8,128)S(1)}, u32[]{:S(2)}, u32[]{:S(2)}) collective-permute-start(f32[1,2,4,16,128]{4,3,2,1,0:T(8,128)S(1)} %get-tuple-element.25), channel_id=1, source_target_pairs={{0,4},{4,0},{8,12},{12,8},{16,20},{20,16},{24,28},{28,24},{1,5},{5... | collective-permute-start | bytes 196616 | tf_op jit(solution)/shard_map/ppermute | solution.py:337
  23.8 5.7 %collective-permute-start.5 = (f32[1,2,4,16,128]{4,3,2,1,0:T(8,128)S(1)}, f32[1,2,4,16,128]{4,3,2,1,0:T(8,128)S(1)}, u32[]{:S(2)}, u32[]{:S(2)}) collective-permute-start(f32[1,2,4,16,128]{4,3,2,1,0:T(8,128)S(1)} %get-tuple-element.26), channel_id=1, source_target_pairs={{0,12},{4,8},{8,4},{12,0},{16,28},{20,24},{24,20},{28,16},{1,13},{... | collective-permute-start | bytes 196616 | tf_op jit(solution)/shard_map/ppermute | solution.py:337
  25.3 4.3 %collective-permute-start.4 = (f32[1,2,4,16,128]{4,3,2,1,0:T(8,128)S(1)}, f32[1,2,4,16,128]{4,3,2,1,0:T(8,128)S(1)}, u32[]{:S(2)}, u32[]{:S(2)}) collective-permute-start(f32[1,2,4,16,128]{4,3,2,1,0:T(8,128)S(1)} %get-tuple-element.27), channel_id=1, source_target_pairs={{0,8},{4,12},{8,0},{12,4},{16,24},{20,28},{24,16},{28,20},{1,9},{5... | collective-permute-start | bytes 196616 | tf_op jit(solution)/shard_map/ppermute | solution.py:337
  29.6 5.2 %collective-permute-start.6 = (f32[1,2,4,16,128]{4,3,2,1,0:T(8,128)S(1)}, f32[1,2,4,16,128]{4,3,2,1,0:T(8,128)S(1)}, u32[]{:S(2)}, u32[]{:S(2)}) collective-permute-start(f32[1,2,4,16,128]{4,3,2,1,0:T(8,128)S(1)} %add_add_fusion), channel_id=1, source_target_pairs={{0,16},{4,20},{8,24},{12,28},{16,0},{20,4},{24,8},{28,12},{1,17},{... | collective-permute-start | bytes 196616 | tf_op jit(solution)/shard_map/ppermute | solution.py:337
  34.9 5.2 %collective-permute-start.9 = (f32[1,2,4,16,128]{4,3,2,1,0:T(8,128)S(1)}, f32[1,2,4,16,128]{4,3,2,1,0:T(8,128)S(1)}, u32[]{:S(2)}, u32[]{:S(2)}) collective-permute-start(f32[1,2,4,16,128]{4,3,2,1,0:T(8,128)S(1)} %pad_maximum_fusion.2.refs_0_), channel_id=1, source_target_pairs={{0,12},{4,8},{8,4},{12,0},{16,28},{20,24},{24,20},{28,16},{1,13},{... | collective-permute-start | bytes 196616 | tf_op jit(solution)/shard_map/ppermute | solution.py:337
  37.0 4.6 %collective-permute-start.8 = (f32[1,2,4,16,128]{4,3,2,1,0:T(8,128)S(1)}, f32[1,2,4,16,128]{4,3,2,1,0:T(8,128)S(1)}, u32[]{:S(2)}, u32[]{:S(2)}) collective-permute-start(f32[1,2,4,16,128]{4,3,2,1,0:T(8,128)S(1)} %pad_maximum_fusion.2.refs_0_), channel_id=1, source_target_pairs={{0,8},{4,12},{8,0},{12,4},{16,24},{20,28},{24,16},{28,20},{1,9},{5... | collective-permute-start | bytes 196616 | tf_op jit(solution)/shard_map/ppermute | solution.py:337
  38.6 4.3 %collective-permute-start.7 = (f32[1,2,4,16,128]{4,3,2,1,0:T(8,128)S(1)}, f32[1,2,4,16,128]{4,3,2,1,0:T(8,128)S(1)}, u32[]{:S(2)}, u32[]{:S(2)}) collective-permute-start(f32[1,2,4,16,128]{4,3,2,1,0:T(8,128)S(1)} %pad_maximum_fusion.2.refs_0_), channel_id=1, source_target_pairs={{0,4},{4,0},{8,12},{12,8},{16,20},{20,16},{24,28},{28,24},{1,5},{5... | collective-permute-start | bytes 196616 | tf_op jit(solution)/shard_map/ppermute | solution.py:337
  43.7 4.3 %collective-permute-start.10 = (f32[8,16,128]{2,1,0:T(8,128)S(1)}, f32[8,16,128]{2,1,0:T(8,128)S(1)}, u32[]{:S(2)}, u32[]{:S(2)}) collective-permute-start(f32[8,16,128]{2,1,0:T(8,128)S(1)} %get-tuple-element.18), channel_id=1, source_target_pairs={{0,3},{1,2},{2,1},{3,0},{4,7},{5,6},{6,5},{7,4},{8,11},{9,10},{10,... | collective-permute-start | bytes 196616 | tf_op jit(solution)/shard_map/ppermute | solution.py:427
  43.7 4.3 %collective-permute-start.11 = (f32[8,16,128]{2,1,0:T(8,128)S(1)}, f32[8,16,128]{2,1,0:T(8,128)S(1)}, u32[]{:S(2)}, u32[]{:S(2)}) collective-permute-start(f32[8,16,128]{2,1,0:T(8,128)S(1)} %get-tuple-element.19), channel_id=1, source_target_pairs={{0,1},{1,0},{2,3},{3,2},{4,5},{5,4},{6,7},{7,6},{8,9},{9,8},{10,11... | collective-permute-start | bytes 196616 | tf_op jit(solution)/shard_map/ppermute | solution.py:337

commit v2 on v1

--- a/solution.py
+++ b/solution.py
@@ -109,67 +109,104 @@
     return [(r, min(size, rows - r)) for r in range(0, rows, size)]
 
 
-def stages_kernel(pieces, planes, low_bits, *refs):
+def laplace_rows(src, start, xy_start, rows, planes, refs, store):
+    w_ref, hi, lo, xy = refs
+    tall = up16(rows + 2 * xy_start)
+    margin = (planes + 32 - rows) // 2
+    for j in in_plane_steps(tall, w_ref, hi, lo, xy):
+        for r, count in chunks(rows):
+            f = [src[c, j, pl.ds(start + r, count), :] for c in range(4)]
+            near = [neighbours(src, xy, c, j, start + r, xy_start + r, count) for c in range(4)]
+            store(j, r, count, margin + r, f, near)
+
+
+def derivative(pd, j, row, count, f, near):
+    pot, pr, pi = [pd[i, j, pl.ds(row, count), :] for i in range(3)]
+    return slope(f, [unit_coef * near[c] + pot * f[c] for c in range(4)], pr, pi)
+
+
+def stage_store(b0, pd, dst, factor, hi, lo):
+    def store(j, r, count, row, f, near):
+        k = derivative(pd, j, row, count, f, near)
+        for c in range(4):
+            value = b0[c, j, pl.ds(row + 8, count), :] + (signs[c] * factor) * k[c]
+            dst[c, j, pl.ds(r, count), :] = value
+            put_split(value, c, j, r, hi, lo)
+
+    return store
+
+
+def first_kernel(pieces, planes, *refs):
     n = len(pieces)
-    parts = refs[:n]
-    w_ref = refs[n]
-    psi1_ref, kin1_ref, sums_ref = refs[n + 1 : n + 4]
-    b0, b1, b2, b3, b4, pd, hi_a, lo_a, hi_b, lo_b, xy = refs[n + 4 :]
+    parts, w_ref = refs[:n], refs[n]
+    b0, pd, b1, hi_b, lo_b, hi_a, lo_a, xy = refs[n + 1 :]
     odd = lax.rem(lax.axis_index("grid"), 2)
+    half = lax.rem(lax.axis_index("modes"), 2)
+    zero = jnp.zeros((8, LANES), jnp.float32)
+    for c in range(4):
+        for j in range(8):
+            b0[c, j, 0:8, :] = zero
+            b0[c, j, planes + 40 : planes + 48, :] = zero
+
+    for ref, (first, channels, count, row_even, row_odd, flip) in zip(parts, pieces):
+        row = row_even
+        if row_odd != row_even:
+            row = pl.multiple_of(row_even + odd * (row_odd - row_even), 16)
+        if flip is not None:
+            row = pl.multiple_of(row + (half if flip == 0 else 1 - half) * count, 8)
+        for i in range(channels):
+            c = first + i
+            for j in range(8):
+                value = ref[i, :, j * LANES : (j + 1) * LANES]
+                if c < 4:
+                    b0[c, j, pl.ds(row + 8, count), :] = value
+                    put_split(value, c, j, row, hi_a, lo_a)
+                else:
+                    pd[c - 4, j, pl.ds(row, count), :] = value + centre_coef if c == 4 else value
+
+    store = stage_store(b0, pd, b1, 0.5 * time_step, hi_b, lo_b)
+    laplace_rows(b0, 8, 0, planes + 32, planes, (w_ref, hi_a, lo_a, xy), store)
+
+
+def stages_kernel(far, planes, low_bits, *refs):
+    lead_ref, tail_ref, b0, pd = refs[:4]
+    w_ref = refs[7]
+    psi1_ref, kin1_ref, sums_ref, b1, hi_b, lo_b = refs[8:14]
+    b2, b3, b4, hi_a, lo_a, xy, past = refs[14:]
     quarter = lax.rem(lax.axis_index("modes"), low_bits)
 
-    for ref, (channels, moves) in zip(parts, pieces):
-        for src, count, dst_even, dst_odd in moves:
-            if dst_even == dst_odd:
-                dst = dst_even
-                dst_pd = dst_even - 8
-            else:
-                step = pl.multiple_of(odd * (dst_odd - dst_even), 16)
-                dst = pl.multiple_of(dst_even + step, 8)
-                dst_pd = pl.multiple_of(dst_even - 8 + step, 16 if (dst_even - 8) % 16 == 0 else 8)
-            for c in range(channels):
-                for j in range(8):
-                    value = ref[c, src : src + count, j * LANES : (j + 1) * LANES]
-                    if c < 4:
-                        b0[c, j, pl.ds(dst, count), :] = value
-                        if channels > 4:
-                            put_split(value, c, j, dst_pd, hi_a, lo_a)
-                    else:
-                        if c == 4:
-                            value = value + centre_coef
-                        pd[c - 4, j, pl.ds(dst_pd, count), :] = value
+    zero = jnp.zeros((8, LANES), jnp.float32)
+    for c in range(4):
+        for j in range(8):
+            lanes = slice(j * LANES, (j + 1) * LANES)
+            past[c, j, 4:12, :] = zero
+            past[c, j, 16:24, :] = zero
+            past[c, j, 0:REACH, :] = lead_ref[c, far[0] : far[0] + REACH, lanes]
+            past[c, j, 24 : 24 + REACH, :] = tail_ref[c, far[1] : far[1] + REACH, lanes]
+    scale = 0.5 * time_step * unit_coef
+    for j in range(8):
+        for row, begin, sign in ((0, 4, -1), (planes + 24, 16, 1)):
+            change = []
+            for c in range(4):
+                total = past[c, j, pl.ds(begin + sign, 8), :]
+                for k in range(2, REACH + 1):
+                    total = total + near_coef[k] * past[c, j, pl.ds(begin + sign * k, 8), :]
+                change.append(scale * total)
+            for c, delta in enumerate((change[1], -change[0], -change[3], change[2])):
+                value = b1[c, j, row : row + 8, :] + delta
+                b1[c, j, row : row + 8, :] = value
+                put_split(value, c, j, row, hi_b, lo_b)
 
     def run(src, start, xy_start, rows, hi, lo, store):
-        tall = up16(rows + 2 * xy_start)
-        margin = (planes + 32 - rows) // 2
-        for j in in_plane_steps(tall, w_ref, hi, lo, xy):
-            for r, count in chunks(rows):
-                f = [src[c, j, pl.ds(start + r, count), :] for c in range(4)]
-                near = [
-                    neighbours(src, xy, c, j, start + r, xy_start + r, count) for c in range(4)
-                ]
-                store(j, r, count, margin + r, f, near)
-
-    def derivative(j, row, count, f, near):
-        pot, pr, pi = [pd[i, j, pl.ds(row, count), :] for i in range(3)]
-        return slope(f, [unit_coef * near[c] + pot * f[c] for c in range(4)], pr, pi)
-
-    def stage(dst, factor, hi, lo):
-        def store(j, r, count, row, f, near):
-            k = derivative(j, row, count, f, near)
-            for c in range(4):
-                value = b0[c, j, pl.ds(row + 8, count), :] + (signs[c] * factor) * k[c]
-                dst[c, j, pl.ds(r, count), :] = value
-                put_split(value, c, j, r, hi, lo)
-
-        return store
-
-    run(b0, 8, 0, planes + 32, hi_a, lo_a, stage(b1, 0.5 * time_step, hi_b, lo_b))
-    run(b1, 4, 4, planes + 24, hi_b, lo_b, stage(b2, 0.5 * time_step, hi_a, lo_a))
-    run(b2, 4, 4, planes + 16, hi_a, lo_a, stage(b3, time_step, hi_b, lo_b))
+        laplace_rows(src, start, xy_start, rows, planes, (w_ref, hi, lo, xy), store)
+
+    store = stage_store(b0, pd, b2, 0.5 * time_step, hi_a, lo_a)
+    run(b1, 4, 4, planes + 24, hi_b, lo_b, store)
+    store = stage_store(b0, pd, b3, time_step, hi_b, lo_b)
+    run(b2, 4, 4, planes + 16, hi_a, lo_a, store)
 
     def last(j, r, count, row, f, near):
-        k = derivative(j, row, count, f, near)
+        k = derivative(pd, j, row, count, f, near)
         for c in range(4):
             early = (
                 b1[c, j, pl.ds(r + 12, count), :]
@@ -318,16 +355,18 @@
     return jnp.stack([field_pot, pair_re, pair_im, energy], axis=2)
 
 
-def call(kernel, outs, scratch, args, name):
+def call(kernel, outs, scratch, args, name, aliases=None):
     vmem = pl.BlockSpec(memory_space=pltpu.VMEM)
-    flops = 2 * sum(int(np.prod(s)) for s in outs)
+    shapes = [o if isinstance(o[0], tuple) else (o, jnp.float32) for o in outs]
+    flops = 2 * sum(int(np.prod(s)) for s, d in shapes)
     return pl.pallas_call(
         kernel,
-        out_shape=tuple(jax.ShapeDtypeStruct(s, jnp.float32) for s in outs),
+        out_shape=tuple(jax.ShapeDtypeStruct(s, d) for s, d in shapes),
         in_specs=[vmem] * len(args),
         out_specs=tuple([vmem] * len(outs)),
         scratch_shapes=[pltpu.VMEM(s, d) for s, d in scratch],
-        compiler_params=pltpu.CompilerParams(vmem_limit_bytes=48 << 20),
+        input_output_aliases=aliases or {},
+        compiler_params=pltpu.CompilerParams(vmem_limit_bytes=32 << 20),
         cost_estimate=pl.CostEstimate(flops=1000 * flops, bytes_accessed=4 * flops, transcendentals=0),
         name=name,
     )(*args)
@@ -341,28 +380,49 @@
     planes = u_modes.shape[2]
     slabs = lax.axis_size("grid")
     modes = lax.axis_size("modes")
-    paired = slabs == 4 and planes == 16
+    low_bits = 4 if modes % 4 == 0 else 1
+    paired = slabs == 4 and planes == 16 and low_bits == 4
     f32, bf16 = jnp.float32, jnp.bfloat16
     weights = jnp.asarray(in_plane_matrix())
-    own = jnp.concatenate([u_modes[0], v_modes[0], potential[None], pairing], axis=0)
+    frozen = jnp.concatenate([potential[None], pairing], axis=0)
+    psi = (u_modes[0], v_modes[0])
 
     cross = [(i, (i - 1 if i % 2 == 0 else i + 1) % slabs) for i in range(slabs)]
     up = [(i, (i + 1) % slabs) for i in range(slabs)]
     down = [(j, i) for i, j in up]
-    base = 24
-    pieces, arrays = [(7, [(0, planes, base, base)])], [own]
+    pieces = [(0, 2, planes, 16, 16, None), (2, 2, planes, 16, 16, None), (4, 3, planes, 16, 16, None)]
+    arrays = [*psi, frozen]
     if paired:
-        far_slab = lax.ppermute(own, "grid", cross)
-        near_slab = exchange_xor(own, "grid", 1, slabs)
-        both = jnp.concatenate([far_slab[:4, :REACH], far_slab[:4, planes - REACH :]], axis=1)
-        relayed = exchange_xor(both, "grid", 1, slabs)
+        part = planes // 2
+        upper = lax.rem(lax.axis_index("modes"), 2) == 1
+        mine = lax.ppermute(
+            jnp.where(upper, frozen[:, part:], frozen[:, :part]), "grid", cross
+        )
+        far_u, far_v = [lax.ppermute(x, "grid", cross) for x in psi]
+        near_u, near_v, near_f = [exchange_xor(x, "grid", 1, slabs) for x in (*psi, frozen)]
+        other = exchange_xor(mine, "modes", 1, modes)
+        lead, tail = 16 - planes, 16 + planes
         pieces += [
-            (7, [(0, planes, base - planes, base + planes)]),
-            (7, [(0, planes, base + planes, base - planes)]),
-            (4, [(0, REACH, base + 2 * planes, base + 2 * planes), (REACH, REACH, base - planes - REACH, base - planes - REACH)]),
+            (0, 2, planes, tail, lead, None),
+            (2, 2, planes, tail, lead, None),
+            (4, 3, planes, tail, lead, None),
+            (4, 3, part, lead, tail, 0),
+            (4, 3, part, lead, tail, 1),
+            (0, 2, planes, lead, tail, None),
+            (2, 2, planes, lead, tail, None),
         ]
-        arrays += [far_slab, near_slab, relayed]
+        arrays += [near_u, near_v, near_f, mine, other, far_u, far_v]
+        both = jnp.concatenate(
+            [
+                jnp.concatenate([x[:, :REACH], x[:, planes - REACH :]], axis=1)
+                for x in (far_u, far_v)
+            ],
+            axis=0,
+        )
+        lead_far = tail_far = exchange_xor(both, "grid", 1, slabs)
+        far = (REACH, 0)
     else:
+        own = jnp.concatenate([*psi, frozen], axis=0)
         reach, step = 0, 0
         while reach < 5 * REACH:
             step += 1
@@ -374,32 +434,46 @@
             after = lax.ppermute(
                 own[:wide, :count], "grid", [((i + step) % slabs, i) for i in range(slabs)]
             )
-            lead, tail = base - reach - count, base + planes + reach
-            pieces += [(wide, [(0, count, lead, lead)]), (wide, [(0, count, tail, tail)])]
-            arrays += [before, after]
+            lead, tail = 16 - reach - count, 16 + planes + reach
+            if wide == 7:
+                pieces += [(0, 7, count, lead, lead, None), (0, 7, count, tail, tail, None)]
+                arrays += [before, after]
+            else:
+                lead_far, tail_far, far = before, after, (0, 0)
             reach += count
 
-    low_bits = 4 if modes % 4 == 0 else 1
     tall = up16(planes + 32)
     state = (4, 8, planes, LANES)
-    psi1, kin1, sums = call(
-        functools.partial(stages_kernel, pieces, planes, low_bits),
-        [state, state, (4, 2, 4, planes, LANES)],
+    split = ((4, 4, tall, WINDOW), bf16)
+    b0, pd, b1, hi, lo = call(
+        functools.partial(first_kernel, pieces, planes),
         [
-            ((4, 8, tall + 24, LANES), f32),
+            (4, 8, tall + 16, LANES),
+            (3, 8, tall, LANES),
+            (4, 8, tall + 8, LANES),
+            split,
+            split,
+        ],
+        [split, split, ((4, 4, 2, tall, LANES), f32)],
+        arrays + [weights],
+        "first",
+    )
+    inputs = [lead_far, tail_far, b0, pd, b1, hi, lo, weights]
+    psi1, kin1, sums, *rest = call(
+        functools.partial(stages_kernel, far, planes, low_bits),
+        [state, state, (4, 2, 4, planes, LANES), b1.shape, split, split],
+        [
             ((4, 8, tall + 8, LANES), f32),
             ((4, 8, tall + 8, LANES), f32),
             ((4, 8, tall + 8, LANES), f32),
-            ((4, 8, tall + 8, LANES), f32),
-            ((3, 8, tall + 8, LANES), f32),
-            ((4, 4, tall, WINDOW), bf16),
-            ((4, 4, tall, WINDOW), bf16),
-            ((4, 4, tall, WINDOW), bf16),
-            ((4, 4, tall, WINDOW), bf16),
+            split,
+            split,
             ((4, 4, 2, tall, LANES), f32),
+            ((4, 8, 32, LANES), f32),
         ],
-        arrays + [weights],
+        inputs,
         "stages",
+        {4: 3, 5: 4, 6: 5},
     )
 
     if low_bits == 4:

time: 49 us -> 49.5 us (1.010)
  starting transfers between devices: 15.5 us -> 18.5 us
  waiting for transfers between devices: 24.6 us -> 22 us
    ppermute x1 -> x3, waiting for transfers between devices: 10.2 us -> 6.05 us  [the longest x1 6.05 us: local(): lax.ppermute(jnp.where(upper, frozen[:, part:], frozen[:, :part]), 'grid'...]
    ppermute x1 -> x3, starting transfers between devices: 2.47 us -> 4.4 us  [the longest x2 2.67 us: local(): far_u, far_v = [lax.ppermute(x, 'grid', cross) for x in psi]]
    ppermute x10 -> x13, waiting for transfers between devices: 12.3 us -> 13.8 us  [exchange_xor(): return lax.ppermute(x, axis, [(i, i ^ bits) for i in range(count)])]
    concatenate x2, other arithmetic: 1.18 us -> 0.05 us  [the longest x1 0.03 us: local(): jnp.concatenate([jnp.concatenate([x[:, :REACH], x[:, planes - REACH:]], a...]
    ppermute x10 -> x13, starting transfers between devices: 13 us -> 14.1 us  [exchange_xor(): return lax.ppermute(x, axis, [(i, i ^ bits) for i in range(count)])]
    select_n x0 -> x1, other arithmetic: none -> 0.93 us  [local(): jnp.where(upper, frozen[:, part:], frozen[:, :part])]
    pallas_call x4 -> x5, Pallas kernels: 6.73 us -> 6.94 us  [call(): pl.pallas_call(kernel, out_shape=tuple((jax.ShapeDtypeStruct(s, d) for s,...]
  transfers between devices with their start and end apart: 12 -> 17, of which waited for: 10 -> 10; matrix products, arithmetic and copies ran while one was open for 0% -> 2% of each run, Pallas kernels for 1% -> 4%
where the time goes in v2:
time: 49.5 us; the launch traced here: 49.4 us
  waiting for transfers between devices  22 us (44%)
  starting transfers between devices  18.5 us (37%)
  Pallas kernels  6.94 us (14%)
  other arithmetic  1.07 us (2%)
  between operations  0.79 us (2%)
    ppermute x13, starting transfers between devices, exchange_xor(): return lax.ppermute(x, axis, [(i, i ^ bits) for i in range(count)])  14.1 us
    ppermute x13, waiting for transfers between devices, exchange_xor(): return lax.ppermute(x, axis, [(i, i ^ bits) for i in range(count)])  13.8 us
    pallas_call x5, Pallas kernels, call(): pl.pallas_call(kernel, out_shape=tuple((jax.ShapeDtypeStruct(s, d) for s,...  6.94 us
    ppermute x1, waiting for transfers between devices, local(): lax.ppermute(jnp.where(upper, frozen[:, part:], frozen[:, :part]), 'grid'...  6.05 us
    ppermute x2, starting transfers between devices, local(): far_u, far_v = [lax.ppermute(x, 'grid', cross) for x in psi]  2.67 us
    ppermute x1, waiting for transfers between devices, local(): first = lax.ppermute(first, 'grid', cross)  2.16 us
    ppermute x1, starting transfers between devices, local(): lax.ppermute(jnp.where(upper, frozen[:, part:], frozen[:, :part]), 'grid'...  1.73 us
  transfers between devices with their start and end apart: 17, of which 10 were waited for; matrix products, arithmetic and copies ran while one was open for 2% of the time, Pallas kernels for 4%

profile of v2, /device:TPU:0, one launch (start us, length us, event | category | flops | bytes accessed | tf_op | source)
XLA Modules:
  0.0 49.4 jit_solution(7328129097919721506)
XLA Ops:
  0.6 0.6 %collective-permute-start.3 = (f32[2,16,1024]{2,1,0:T(8,128)}, f32[2,16,1024]{2,1,0:T(8,128)S(1)}, u32[]{:S(2)}, u32[]{:S(2)}) collective-permute-start(f32[2,16,1024]{2,1,0:T(8,128)} %bitcast.6), channel_id=1, source_target_pairs={{0,1},{1,0},{2,3},{3,2},{4,5},{5,4},{6,7},{7,6},{8,9},{9,8},{10,11... | collective-permute-start | bytes 393224 | tf_op jit(solution)/shard_map/ppermute | solution.py:376
  1.2 2.6 %collective-permute-start = (f32[2,16,1024]{2,1,0:T(8,128)}, f32[2,16,1024]{2,1,0:T(8,128)S(1)}, u32[]{:S(2)}, u32[]{:S(2)}) collective-permute-start(f32[2,16,1024]{2,1,0:T(8,128)} %bitcast.7), channel_id=1, source_target_pairs={{0,3},{1,2},{2,1},{3,0},{4,7},{5,6},{6,5},{7,4},{8,11},{9,10},{10,... | collective-permute-start | bytes 393224 | tf_op jit(solution)/shard_map/ppermute | solution.py:401
  3.8 0.1 collective-permute-start.4
  3.9 0.1 collective-permute-start.1
  3.9 0.0 copy-start.3
  3.9 0.0 copy-start.4
  3.9 0.9 %fusion.1 = f32[3,8,1024]{2,1,0:T(8,128)S(1)} fusion(f32[2,16,1024]{2,1,0:T(8,128)} %param.8, f32[1,16,1024]{2,1,0:T(8,128)} %bitcast.9, pred[]{:T(512)S(6)} %eq.3), kind=kLoop, calls=%fused_computation.7 | loop fusion | flops 73728 | bytes 294913 | tf_op jit(solution)/shard_map/jit(_where)/select_n | solution.py:399
  4.9 0.0 copy-start
  4.9 1.7 %collective-permute-start.6 = (f32[3,8,1024]{2,1,0:T(8,128)S(1)}, f32[3,8,1024]{2,1,0:T(8,128)S(1)}, u32[]{:S(2)}, u32[]{:S(2)}) collective-permute-start(f32[3,8,1024]{2,1,0:T(8,128)S(1)} %fusion.1), channel_id=1, source_target_pairs={{0,3},{1,2},{2,1},{3,0},{4,7},{5,6},{6,5},{7,4},{8,11},{9,10},{10,... | collective-permute-start | bytes 294920 | tf_op jit(solution)/shard_map/ppermute | solution.py:398
  6.6 0.0 copy-done.3
  6.6 0.0 copy-done.4
  6.6 6.0 %collective-permute-done.6.refs_6_ = f32[3,8,1024]{2,1,0:T(8,128)S(1)} collective-permute-done((f32[3,8,1024]{2,1,0:T(8,128)S(1)}, f32[3,8,1024]{2,1,0:T(8,128)S(1)}, u32[]{:S(2)}, u32[]{:S(2)}) %collective-permute-start.6) | collective-permute-done | bytes 98336 | tf_op jit(solution)/shard_map/ppermute | solution.py:398
  12.7 0.1 collective-permute-start.5
  12.8 0.0 collective-permute-done.refs_8_
  12.8 1.7 %collective-permute-start.7 = (f32[3,8,1024]{2,1,0:T(8,128)S(1)}, f32[3,8,1024]{2,1,0:T(8,128)S(1)}, u32[]{:S(2)}, u32[]{:S(2)}) collective-permute-start(f32[3,8,1024]{2,1,0:T(8,128)S(1)} %collective-permute-done.6.refs_6_), channel_id=1, source_target_pairs={{0,4},{4,0},{8,12},{12,8},{16,20},{20,16},{24,28},{28,24},{1,5},{5... | collective-permute-start | bytes 294920 | tf_op jit(solution)/shard_map/ppermute | solution.py:376
  14.5 0.0 collective-permute-done.1.refs_9_
  14.6 0.0 copy-start.1
  14.6 0.0 copy-start.2
  14.6 0.1 collective-permute-start.2
  14.7 0.0 collective-permute-done.3.refs_3_
  14.7 0.0 collective-permute-done.4.refs_4_
  14.7 3.2 %collective-permute-done.7.refs_7_ = f32[3,8,1024]{2,1,0:T(8,128)S(1)} collective-permute-done((f32[3,8,1024]{2,1,0:T(8,128)S(1)}, f32[3,8,1024]{2,1,0:T(8,128)S(1)}, u32[]{:S(2)}, u32[]{:S(2)}) %collective-permute-start.7) | collective-permute-done | bytes 98336 | tf_op jit(solution)/shard_map/ppermute | solution.py:376
  17.9 0.0 collective-permute-done.5.refs_5_
  17.9 0.0 copy-done
  17.9 0.0 copy-done.1
  17.9 0.0 copy-done.2
  17.9 1.5 %first.1 = (f32[4,8,64,128]{3,2,1,0:T(8,128)S(1)}, f32[3,8,48,128]{3,2,1,0:T(8,128)S(1)}, f32[4,8,56,128]{3,2,1,0:T(8,128)S(1)}, bf16[4,4,48,512]{3,2,1,0:T(8,128)(2,1)S(1)}, bf16[4,4,48,512]{3,2,1,0:T(8,128)(2,1)S(1)}) custom-call(f32[2,16,1024]{2,1,0:T(8,128)S(1)} %bitcast.8, f32[2,16,1024]{2,1,0:T(8,128)S(1)} %bitcast.5, ...), custom_call_target="tpu_custom_call" | custom-call | flops 2850816000 | bytes 11403264 | tf_op jit(solution)/shard_map/first/pallas_call | solution.py:362
  19.4 0.0 collective-permute-done.2.refs_0_.refs_1_
  19.4 3.2 %stages.1 = (f32[4,8,16,128]{3,2,1,0:T(8,128)S(1)}, f32[4,8,16,128]{3,2,1,0:T(8,128)S(1)}, f32[4,2,4,16,128]{4,3,2,1,0:T(8,128)S(1)}, f32[4,8,56,128]{3,2,1,0:T(...) custom-call(f32[4,8,1024]{2,1,0:T(8,128)S(1)} %collective-permute-do, ...), custom_call_target="tpu_custom_call", output_to_operand_aliasing={{3}: (4, {}), {4}: (5, {}), {5}: (6, {})} | custom-call | flops 2424832000 | bytes 9699328 | tf_op jit(solution)/shard_map/stages/pallas_call | solution.py:362
  22.7 1.5 %collective-permute-start.8 = (f32[1,2,4,16,128]{4,3,2,1,0:T(8,128)S(1)}, f32[1,2,4,16,128]{4,3,2,1,0:T(8,128)S(1)}, u32[]{:S(2)}, u32[]{:S(2)}) collective-permute-start(f32[1,2,4,16,128]{4,3,2,1,0:T(8,128)S(1)} %get-tuple-element.33), channel_id=1, source_target_pairs={{0,4},{4,0},{8,12},{12,8},{16,20},{20,16},{24,28},{28,24},{1,5},{5... | collective-permute-start | bytes 196616 | tf_op jit(solution)/shard_map/ppermute | solution.py:376
  24.2 1.5 %collective-permute-start.10 = (f32[1,2,4,16,128]{4,3,2,1,0:T(8,128)S(1)}, f32[1,2,4,16,128]{4,3,2,1,0:T(8,128)S(1)}, u32[]{:S(2)}, u32[]{:S(2)}) collective-permute-start(f32[1,2,4,16,128]{4,3,2,1,0:T(8,128)S(1)} %get-tuple-element.34), channel_id=1, source_target_pairs={{0,12},{4,8},{8,4},{12,0},{16,28},{20,24},{24,20},{28,16},{1,13},{... | collective-permute-start | bytes 196616 | tf_op jit(solution)/shard_map/ppermute | solution.py:376
  25.7 0.6 %collective-permute-start.9 = (f32[1,2,4,16,128]{4,3,2,1,0:T(8,128)S(1)}, f32[1,2,4,16,128]{4,3,2,1,0:T(8,128)S(1)}, u32[]{:S(2)}, u32[]{:S(2)}) collective-permute-start(f32[1,2,4,16,128]{4,3,2,1,0:T(8,128)S(1)} %get-tuple-element.35), channel_id=1, source_target_pairs={{0,8},{4,12},{8,0},{12,4},{16,24},{20,28},{24,16},{28,20},{1,9},{5... | collective-permute-start | bytes 196616 | tf_op jit(solution)/shard_map/ppermute | solution.py:376
  26.3 1.5 %collective-permute-done.8 = f32[1,2,4,16,128]{4,3,2,1,0:T(8,128)S(1)} collective-permute-done((f32[1,2,4,16,128]{4,3,2,1,0:T(8,128)S(1)}, f32[1,2,4,16,128]{4,3,2,1,0:T(8,128)S(1)}, u32[]{:S(2)}, u32[]{:S(2)}) %collective-permute-start.8) | collective-permute-done | bytes 65568 | tf_op jit(solution)/shard_map/ppermute | solution.py:376
  27.8 1.6 %collective-permute-done.10 = f32[1,2,4,16,128]{4,3,2,1,0:T(8,128)S(1)} collective-permute-done((f32[1,2,4,16,128]{4,3,2,1,0:T(8,128)S(1)}, f32[1,2,4,16,128]{4,3,2,1,0:T(8,128)S(1)}, u32[]{:S(2)}, u32[]{:S(2)}) %collective-permute-start.10) | collective-permute-done | bytes 65568 | tf_op jit(solution)/shard_map/ppermute | solution.py:376
  29.4 0.6 %collective-permute-done.9 = f32[1,2,4,16,128]{4,3,2,1,0:T(8,128)S(1)} collective-permute-done((f32[1,2,4,16,128]{4,3,2,1,0:T(8,128)S(1)}, f32[1,2,4,16,128]{4,3,2,1,0:T(8,128)S(1)}, u32[]{:S(2)}, u32[]{:S(2)}) %collective-permute-start.9) | collective-permute-done | bytes 65568 | tf_op jit(solution)/shard_map/ppermute | solution.py:376
  30.0 2.8 %collective-permute-start.11 = (f32[1,2,4,16,128]{4,3,2,1,0:T(8,128)S(1)}, f32[1,2,4,16,128]{4,3,2,1,0:T(8,128)S(1)}, u32[]{:S(2)}, u32[]{:S(2)}) collective-permute-start(f32[1,2,4,16,128]{4,3,2,1,0:T(8,128)S(1)} %add_add_fusion), channel_id=1, source_target_pairs={{0,16},{4,20},{8,24},{12,28},{16,0},{20,4},{24,8},{28,12},{1,17},{... | collective-permute-start | bytes 196616 | tf_op jit(solution)/shard_map/ppermute | solution.py:376
  32.8 3.1 %collective-permute-done.11 = f32[1,2,4,16,128]{4,3,2,1,0:T(8,128)S(1)} collective-permute-done((f32[1,2,4,16,128]{4,3,2,1,0:T(8,128)S(1)}, f32[1,2,4,16,128]{4,3,2,1,0:T(8,128)S(1)}, u32[]{:S(2)}, u32[]{:S(2)}) %collective-permute-start.11) | collective-permute-done | bytes 65568 | tf_op jit(solution)/shard_map/ppermute | solution.py:376
  35.9 0.1 divide_subtract_fusion
  36.0 1.1 %collective-permute-start.14 = (f32[1,2,4,16,128]{4,3,2,1,0:T(8,128)S(1)}, f32[1,2,4,16,128]{4,3,2,1,0:T(8,128)S(1)}, u32[]{:S(2)}, u32[]{:S(2)}) collective-permute-start(f32[1,2,4,16,128]{4,3,2,1,0:T(8,128)S(1)} %pad_maximum_fusion.1.refs_0_), channel_id=1, source_target_pairs={{0,12},{4,8},{8,4},{12,0},{16,28},{20,24},{24,20},{28,16},{1,13},{... | collective-permute-start | bytes 196616 | tf_op jit(solution)/shard_map/ppermute | solution.py:376
  37.1 2.0 %collective-permute-start.13 = (f32[1,2,4,16,128]{4,3,2,1,0:T(8,128)S(1)}, f32[1,2,4,16,128]{4,3,2,1,0:T(8,128)S(1)}, u32[]{:S(2)}, u32[]{:S(2)}) collective-permute-start(f32[1,2,4,16,128]{4,3,2,1,0:T(8,128)S(1)} %pad_maximum_fusion.1.refs_0_), channel_id=1, source_target_pairs={{0,8},{4,12},{8,0},{12,4},{16,24},{20,28},{24,16},{28,20},{1,9},{5... | collective-permute-start | bytes 196616 | tf_op jit(solution)/shard_map/ppermute | solution.py:376
  39.1 0.5 collective-permute-start.12
  39.6 1.7 %collective-permute-done.14.refs_3_ = f32[1,2,4,16,128]{4,3,2,1,0:T(8,128)S(1)} collective-permute-done((f32[1,2,4,16,128]{4,3,2,1,0:T(8,128)S(1)}, f32[1,2,4,16,128]{4,3,2,1,0:T(8,128)S(1)}, u32[]{:S(2)}, u32[]{:S(2)}) %collective-permute-start.14) | collective-permute-done | bytes 65568 | tf_op jit(solution)/shard_map/ppermute | solution.py:376
  41.3 0.8 %collective-permute-done.13.refs_2_ = f32[1,2,4,16,128]{4,3,2,1,0:T(8,128)S(1)} collective-permute-done((f32[1,2,4,16,128]{4,3,2,1,0:T(8,128)S(1)}, f32[1,2,4,16,128]{4,3,2,1,0:T(8,128)S(1)}, u32[]{:S(2)}, u32[]{:S(2)}) %collective-permute-start.13) | collective-permute-done | bytes 65568 | tf_op jit(solution)/shard_map/ppermute | solution.py:376
  42.1 1.3 %collective-permute-done.12.refs_1_ = f32[1,2,4,16,128]{4,3,2,1,0:T(8,128)S(1)} collective-permute-done((f32[1,2,4,16,128]{4,3,2,1,0:T(8,128)S(1)}, f32[1,2,4,16,128]{4,3,2,1,0:T(8,128)S(1)}, u32[]{:S(2)}, u32[]{:S(2)}) %collective-permute-start.12) | collective-permute-done | bytes 65568 | tf_op jit(solution)/shard_map/ppermute | solution.py:376
  43.4 0.8 %middle.1 = (f32[4,8,16,128]{3,2,1,0:T(8,128)S(1)}, f32[8,16,128]{2,1,0:T(8,128)S(1)}, f32[8,16,128]{2,1,0:T(8,128)S(1)}, f32[4,16,1024]{2,1,0:T(8,128)}, f32[4,2,4,16,128]{4,3,2,1,0:T(8,128)S(1)}) custom-call(f32[1,2,4,16,128]{4,3,2,1,0:T(8,128)S(1)} %pad_maximum_fusion.1.refs_0_, f32[1,2,4,16,128]{4,3,2,1,0:T(8,128)S(1)} %collective-permute-done.12.refs_1_, ...), custom_call_target="tpu_custom_call" | custom-call | flops 458752000 | bytes 1835008 | tf_op jit(solution)/shard_map/middle/pallas_call | solution.py:362
  44.2 0.0 collective-permute-start.15
  44.2 1.6 %collective-permute-start.16 = (f32[8,16,128]{2,1,0:T(8,128)S(1)}, f32[8,16,128]{2,1,0:T(8,128)S(1)}, u32[]{:S(2)}, u32[]{:S(2)}) collective-permute-start(f32[8,16,128]{2,1,0:T(8,128)S(1)} %get-tuple-element.29), channel_id=1, source_target_pairs={{0,1},{1,0},{2,3},{3,2},{4,5},{5,4},{6,7},{7,6},{8,9},{9,8},{10,11... | collective-permute-start | bytes 196616 | tf_op jit(solution)/shard_map/ppermute | solution.py:376
  45.8 0.6 %inner.1.refs_0_ = f32[4,8,16,128]{3,2,1,0:T(8,128)S(1)} custom-call(f32[4,8,16,128]{3,2,1,0:T(8,128)S(1)} %get-tuple-element.23.refs_4_.refs_0_, f32[4,8,16,128]{3,2,1,0:T(8,128)S(1)} %get-tuple-element.24.refs_5_.refs_1_, f32[4,8,16,128]{3,2,1,0:T(8,128)S(1)} %get-tuple-element.26.refs_2_, f32[4,2,4,16,128]{4,3,2,1,0:T(8,128)S(1)} %get-tuple-element.27.refs_3_, ...), custom_call_target="tpu_custom_call" | custom-call | flops 131072000 | bytes 524288 | tf_op jit(solution)/shard_map/inner/pallas_call | solution.py:362
  46.3 2.2 %collective-permute-done.15.refs_1_ = f32[8,16,128]{2,1,0:T(8,128)S(1)} collective-permute-done((f32[8,16,128]{2,1,0:T(8,128)S(1)}, f32[8,16,128]{2,1,0:T(8,128)S(1)}, u32[]{:S(2)}, u32[]{:S(2)}) %collective-permute-start.15) | collective-permute-done | bytes 65568 | tf_op jit(solution)/shard_map/ppermute | solution.py:501
  48.5 0.0 collective-permute-done.16.refs_2_
  48.5 0.9 %edges.1 = (f32[1,2,16,1024]{3,2,1,0:T(8,128)}, f32[1,2,16,1024]{3,2,1,0:T(8,128)}) custom-call(f32[4,8,16,128]{3,2,1,0:T(8,128)S(1)} %inner.1.refs_0_, f32[8,16,128]{2,1,0:T(8,128)S(1)} %collective-permute-done.15.refs_1_, f32[8,16,128]{2,1,0:T(8,128)S(1)} %collective-permute-done.16.refs_2_), custom_call_target="tpu_custom_call" | custom-call | flops 131072000 | bytes 524288 | tf_op jit(solution)/shard_map/edges/pallas_call | solution.py:362
  (8 shorter events, 0.1 us)
Async XLA Ops:
  0.6 14.1 %collective-permute-start.3 = (f32[2,16,1024]{2,1,0:T(8,128)}, f32[2,16,1024]{2,1,0:T(8,128)S(1)}, u32[]{:S(2)}, u32[]{:S(2)}) collective-permute-start(f32[2,16,1024]{2,1,0:T(8,128)} %bitcast.6), channel_id=1, source_target_pairs={{0,1},{1,0},{2,3},{3,2},{4,5},{5,4},{6,7},{7,6},{8,9},{9,8},{10,11... | collective-permute-start | bytes 393224 | tf_op jit(solution)/shard_map/ppermute | solution.py:376
  1.2 11.6 %collective-permute-start = (f32[2,16,1024]{2,1,0:T(8,128)}, f32[2,16,1024]{2,1,0:T(8,128)S(1)}, u32[]{:S(2)}, u32[]{:S(2)}) collective-permute-start(f32[2,16,1024]{2,1,0:T(8,128)} %bitcast.7), channel_id=1, source_target_pairs={{0,3},{1,2},{2,1},{3,0},{4,7},{5,6},{6,5},{7,4},{8,11},{9,10},{10,... | collective-permute-start | bytes 393224 | tf_op jit(solution)/shard_map/ppermute | solution.py:401
  3.8 10.9 %collective-permute-start.4 = (f32[2,16,1024]{2,1,0:T(8,128)}, f32[2,16,1024]{2,1,0:T(8,128)S(1)}, u32[]{:S(2)}, u32[]{:S(2)}) collective-permute-start(f32[2,16,1024]{2,1,0:T(8,128)} %bitcast.3), channel_id=1, source_target_pairs={{0,1},{1,0},{2,3},{3,2},{4,5},{5,4},{6,7},{7,6},{8,9},{9,8},{10,11... | collective-permute-start | bytes 393224 | tf_op jit(solution)/shard_map/ppermute | solution.py:376
  3.9 10.7 %collective-permute-start.1 = (f32[2,16,1024]{2,1,0:T(8,128)}, f32[2,16,1024]{2,1,0:T(8,128)S(1)}, u32[]{:S(2)}, u32[]{:S(2)}) collective-permute-start(f32[2,16,1024]{2,1,0:T(8,128)} %bitcast.4), channel_id=1, source_target_pairs={{0,3},{1,2},{2,1},{3,0},{4,7},{5,6},{6,5},{7,4},{8,11},{9,10},{10,... | collective-permute-start | bytes 393224 | tf_op jit(solution)/shard_map/ppermute | solution.py:401
  3.9 2.7 %copy-start.3 = (f32[2,16,1024]{2,1,0:T(8,128)S(1)}, f32[2,16,1024]{2,1,0:T(8,128)}, u32[]{:S(2)}) copy-start(f32[2,16,1024]{2,1,0:T(8,128)} %param.8) | copy-start | bytes 393220
  3.9 2.7 %copy-start.4 = (f32[16,1024]{1,0:T(8,128)S(1)}, f32[16,1024]{1,0:T(8,128)}, u32[]{:S(2)}) copy-start(f32[16,1024]{1,0:T(8,128)} %param.7) | copy-start | bytes 196612
  4.9 13.0 %copy-start = (bf16[1024,256]{1,0:T(8,128)(2,1)S(1)}, bf16[1024,256]{1,0:T(8,128)(2,1)}, u32[]{:S(2)}) copy-start(bf16[1024,256]{1,0:T(8,128)(2,1)} %constant.55.clone.refs_10_.refs_7_.refs_4_) | copy-start | bytes 1572868
  4.9 7.8 %collective-permute-start.6 = (f32[3,8,1024]{2,1,0:T(8,128)S(1)}, f32[3,8,1024]{2,1,0:T(8,128)S(1)}, u32[]{:S(2)}, u32[]{:S(2)}) collective-permute-start(f32[3,8,1024]{2,1,0:T(8,128)S(1)} %fusion.1), channel_id=1, source_target_pairs={{0,3},{1,2},{2,1},{3,0},{4,7},{5,6},{6,5},{7,4},{8,11},{9,10},{10,... | collective-permute-start | bytes 294920 | tf_op jit(solution)/shard_map/ppermute | solution.py:398
  12.7 5.2 %collective-permute-start.5 = (f32[3,16,1024]{2,1,0:T(8,128)S(1)}, f32[3,16,1024]{2,1,0:T(8,128)S(1)}, u32[]{:S(2)}, u32[]{:S(2)}) collective-permute-start(f32[3,16,1024]{2,1,0:T(8,128)S(1)} %pad_maximum_fusion.refs_2_), channel_id=1, source_target_pairs={{0,1},{1,0},{2,3},{3,2},{4,5},{5,4},{6,7},{7,6},{8,9},{9,8},{10,11... | collective-permute-start | bytes 589832 | tf_op jit(solution)/shard_map/ppermute | solution.py:376
  12.8 5.1 %collective-permute-start.7 = (f32[3,8,1024]{2,1,0:T(8,128)S(1)}, f32[3,8,1024]{2,1,0:T(8,128)S(1)}, u32[]{:S(2)}, u32[]{:S(2)}) collective-permute-start(f32[3,8,1024]{2,1,0:T(8,128)S(1)} %collective-permute-done.6.refs_6_), channel_id=1, source_target_pairs={{0,4},{4,0},{8,12},{12,8},{16,20},{20,16},{24,28},{28,24},{1,5},{5... | collective-permute-start | bytes 294920 | tf_op jit(solution)/shard_map/ppermute | solution.py:376
  14.6 3.3 %copy-start.1 = (f32[1,2,16,1024]{3,2,1,0:T(8,128)S(1)}, f32[1,2,16,1024]{3,2,1,0:T(8,128)}, u32[]{:S(2)}) copy-start(f32[1,2,16,1024]{3,2,1,0:T(8,128)} %param.6) | copy-start | bytes 393220
  14.6 3.3 %copy-start.2 = (f32[1,2,16,1024]{3,2,1,0:T(8,128)S(1)}, f32[1,2,16,1024]{3,2,1,0:T(8,128)}, u32[]{:S(2)}) copy-start(f32[1,2,16,1024]{3,2,1,0:T(8,128)} %param.5) | copy-start | bytes 393220
  14.6 4.8 %collective-permute-start.2 = (f32[4,8,1024]{2,1,0:T(8,128)S(1)}, f32[4,8,1024]{2,1,0:T(8,128)S(1)}, u32[]{:S(2)}, u32[]{:S(2)}) collective-permute-start(f32[4,8,1024]{2,1,0:T(8,128)S(1)} %maximum_maximum_fusion), channel_id=1, source_target_pairs={{0,1},{1,0},{2,3},{3,2},{4,5},{5,4},{6,7},{7,6},{8,9},{9,8},{10,11... | collective-permute-start | bytes 393224 | tf_op jit(solution)/shard_map/ppermute | solution.py:376
  22.7 5.0 %collective-permute-start.8 = (f32[1,2,4,16,128]{4,3,2,1,0:T(8,128)S(1)}, f32[1,2,4,16,128]{4,3,2,1,0:T(8,128)S(1)}, u32[]{:S(2)}, u32[]{:S(2)}) collective-permute-start(f32[1,2,4,16,128]{4,3,2,1,0:T(8,128)S(1)} %get-tuple-element.33), channel_id=1, source_target_pairs={{0,4},{4,0},{8,12},{12,8},{16,20},{20,16},{24,28},{28,24},{1,5},{5... | collective-permute-start | bytes 196616 | tf_op jit(solution)/shard_map/ppermute | solution.py:376
  24.2 5.2 %collective-permute-start.10 = (f32[1,2,4,16,128]{4,3,2,1,0:T(8,128)S(1)}, f32[1,2,4,16,128]{4,3,2,1,0:T(8,128)S(1)}, u32[]{:S(2)}, u32[]{:S(2)}) collective-permute-start(f32[1,2,4,16,128]{4,3,2,1,0:T(8,128)S(1)} %get-tuple-element.34), channel_id=1, source_target_pairs={{0,12},{4,8},{8,4},{12,0},{16,28},{20,24},{24,20},{28,16},{1,13},{... | collective-permute-start | bytes 196616 | tf_op jit(solution)/shard_map/ppermute | solution.py:376
  25.7 4.3 %collective-permute-start.9 = (f32[1,2,4,16,128]{4,3,2,1,0:T(8,128)S(1)}, f32[1,2,4,16,128]{4,3,2,1,0:T(8,128)S(1)}, u32[]{:S(2)}, u32[]{:S(2)}) collective-permute-start(f32[1,2,4,16,128]{4,3,2,1,0:T(8,128)S(1)} %get-tuple-element.35), channel_id=1, source_target_pairs={{0,8},{4,12},{8,0},{12,4},{16,24},{20,28},{24,16},{28,20},{1,9},{5... | collective-permute-start | bytes 196616 | tf_op jit(solution)/shard_map/ppermute | solution.py:376
  30.0 5.9 %collective-permute-start.11 = (f32[1,2,4,16,128]{4,3,2,1,0:T(8,128)S(1)}, f32[1,2,4,16,128]{4,3,2,1,0:T(8,128)S(1)}, u32[]{:S(2)}, u32[]{:S(2)}) collective-permute-start(f32[1,2,4,16,128]{4,3,2,1,0:T(8,128)S(1)} %add_add_fusion), channel_id=1, source_target_pairs={{0,16},{4,20},{8,24},{12,28},{16,0},{20,4},{24,8},{28,12},{1,17},{... | collective-permute-start | bytes 196616 | tf_op jit(solution)/shard_map/ppermute | solution.py:376
  36.0 5.2 %collective-permute-start.14 = (f32[1,2,4,16,128]{4,3,2,1,0:T(8,128)S(1)}, f32[1,2,4,16,128]{4,3,2,1,0:T(8,128)S(1)}, u32[]{:S(2)}, u32[]{:S(2)}) collective-permute-start(f32[1,2,4,16,128]{4,3,2,1,0:T(8,128)S(1)} %pad_maximum_fusion.1.refs_0_), channel_id=1, source_target_pairs={{0,12},{4,8},{8,4},{12,0},{16,28},{20,24},{24,20},{28,16},{1,13},{... | collective-permute-start | bytes 196616 | tf_op jit(solution)/shard_map/ppermute | solution.py:376
  37.1 4.9 %collective-permute-start.13 = (f32[1,2,4,16,128]{4,3,2,1,0:T(8,128)S(1)}, f32[1,2,4,16,128]{4,3,2,1,0:T(8,128)S(1)}, u32[]{:S(2)}, u32[]{:S(2)}) collective-permute-start(f32[1,2,4,16,128]{4,3,2,1,0:T(8,128)S(1)} %pad_maximum_fusion.1.refs_0_), channel_id=1, source_target_pairs={{0,8},{4,12},{8,0},{12,4},{16,24},{20,28},{24,16},{28,20},{1,9},{5... | collective-permute-start | bytes 196616 | tf_op jit(solution)/shard_map/ppermute | solution.py:376
  39.1 4.3 %collective-permute-start.12 = (f32[1,2,4,16,128]{4,3,2,1,0:T(8,128)S(1)}, f32[1,2,4,16,128]{4,3,2,1,0:T(8,128)S(1)}, u32[]{:S(2)}, u32[]{:S(2)}) collective-permute-start(f32[1,2,4,16,128]{4,3,2,1,0:T(8,128)S(1)} %pad_maximum_fusion.1.refs_0_), channel_id=1, source_target_pairs={{0,4},{4,0},{8,12},{12,8},{16,20},{20,16},{24,28},{28,24},{1,5},{5... | collective-permute-start | bytes 196616 | tf_op jit(solution)/shard_map/ppermute | solution.py:376
  44.2 4.3 %collective-permute-start.15 = (f32[8,16,128]{2,1,0:T(8,128)S(1)}, f32[8,16,128]{2,1,0:T(8,128)S(1)}, u32[]{:S(2)}, u32[]{:S(2)}) collective-permute-start(f32[8,16,128]{2,1,0:T(8,128)S(1)} %get-tuple-element.28), channel_id=1, source_target_pairs={{0,3},{1,2},{2,1},{3,0},{4,7},{5,6},{6,5},{7,4},{8,11},{9,10},{10,... | collective-permute-start | bytes 196616 | tf_op jit(solution)/shard_map/ppermute | solution.py:501
  44.2 4.3 %collective-permute-start.16 = (f32[8,16,128]{2,1,0:T(8,128)S(1)}, f32[8,16,128]{2,1,0:T(8,128)S(1)}, u32[]{:S(2)}, u32[]{:S(2)}) collective-permute-start(f32[8,16,128]{2,1,0:T(8,128)S(1)} %get-tuple-element.29), channel_id=1, source_target_pairs={{0,1},{1,0},{2,3},{3,2},{4,5},{5,4},{6,7},{7,6},{8,9},{9,8},{10,11... | collective-permute-start | bytes 196616 | tf_op jit(solution)/shard_map/ppermute | solution.py:376

commit v3 on v2

--- a/solution.py
+++ b/solution.py
@@ -7,6 +7,7 @@
 from jax.experimental import pallas as pl
 from jax.experimental.pallas import tpu as pltpu
 from jax.sharding import PartitionSpec as P
+
 
 NX = 32
 NY = 32
@@ -355,7 +356,7 @@
     return jnp.stack([field_pot, pair_re, pair_im, energy], axis=2)
 
 
-def call(kernel, outs, scratch, args, name, aliases=None):
+def call(kernel, outs, scratch, args, aliases=None):
     vmem = pl.BlockSpec(memory_space=pltpu.VMEM)
     shapes = [o if isinstance(o[0], tuple) else (o, jnp.float32) for o in outs]
     flops = 2 * sum(int(np.prod(s)) for s, d in shapes)
@@ -368,7 +369,6 @@
         input_output_aliases=aliases or {},
         compiler_params=pltpu.CompilerParams(vmem_limit_bytes=32 << 20),
         cost_estimate=pl.CostEstimate(flops=1000 * flops, bytes_accessed=4 * flops, transcendentals=0),
-        name=name,
     )(*args)
 
 
@@ -395,12 +395,13 @@
     if paired:
         part = planes // 2
         upper = lax.rem(lax.axis_index("modes"), 2) == 1
-        mine = lax.ppermute(
-            jnp.where(upper, frozen[:, part:], frozen[:, :part]), "grid", cross
-        )
+        mine = lax.ppermute(jnp.where(upper, frozen[:, part:], frozen[:, :part]), "grid", cross)
         far_u, far_v = [lax.ppermute(x, "grid", cross) for x in psi]
-        near_u, near_v, near_f = [exchange_xor(x, "grid", 1, slabs) for x in (*psi, frozen)]
+        near_u, near_v, near_f = [
+            exchange_xor(x, "grid", 1, slabs) for x in (*psi, frozen)
+        ]
         other = exchange_xor(mine, "modes", 1, modes)
+        far_u, far_v, other = lax.optimization_barrier((far_u, far_v, other))
         lead, tail = 16 - planes, 16 + planes
         pieces += [
             (0, 2, planes, tail, lead, None),
@@ -456,7 +457,6 @@
         ],
         [split, split, ((4, 4, 2, tall, LANES), f32)],
         arrays + [weights],
-        "first",
     )
     inputs = [lead_far, tail_far, b0, pd, b1, hi, lo, weights]
     psi1, kin1, sums, *rest = call(
@@ -472,7 +472,6 @@
             ((4, 8, 32, LANES), f32),
         ],
         inputs,
-        "stages",
         {4: 3, 5: 4, 6: 5},
     )
 
@@ -495,7 +494,6 @@
         [state, edge, edge, (4, planes, NX * NY), (4, 2, 4, planes, LANES)],
         [],
         got + [psi1, kin1],
-        "middle",
     )
     if paired:
         first = lax.ppermute(first, "grid", cross)
@@ -514,14 +512,12 @@
             ((4, 4, 2, flat, LANES), f32),
         ],
         [psi1, kin1, mid, fields_flat, weights],
-        "inner",
     )
     u_next, v_next = call(
         functools.partial(edge_kernel, paired, planes),
         [u_modes.shape, v_modes.shape],
         [],
         [part, first, second],
-        "edges",
     )
     return u_next, v_next, fields
 

time: 49.5 us -> 45 us (0.909)
  waiting for transfers between devices: 22 us -> 15.5 us
  starting transfers between devices: 18.5 us -> 19.6 us
  other arithmetic: 1.07 us -> 2.01 us
    ppermute x1, waiting for transfers between devices: 6.05 us -> 0.75 us  [local(): lax.ppermute(jnp.where(upper, frozen[:, part:], frozen[:, :part]), 'grid'...]
    ppermute x13, waiting for transfers between devices: 13.8 us -> 10.6 us  [exchange_xor(): return lax.ppermute(x, axis, [(i, i ^ bits) for i in range(count)])]
    ppermute x2, waiting for transfers between devices: 0.01 us -> 2.04 us  [local(): far_u, far_v = [lax.ppermute(x, 'grid', cross) for x in psi]]
    ppermute x13, starting transfers between devices: 14.1 us -> 15.4 us  [exchange_xor(): return lax.ppermute(x, axis, [(i, i ^ bits) for i in range(count)])]
    concatenate x1, other arithmetic: 0.01 us -> 0.96 us  [local(): frozen = jnp.concatenate([potential[None], pairing], axis=0)]
    ppermute x2, starting transfers between devices: 2.67 us -> 1.75 us  [local(): far_u, far_v = [lax.ppermute(x, 'grid', cross) for x in psi]]
    ppermute x1, starting transfers between devices: 1.73 us -> 2.47 us  [local(): lax.ppermute(jnp.where(upper, frozen[:, part:], frozen[:, :part]), 'grid'...]
  transfers between devices with their start and end apart: 17 -> 17, of which waited for: 10 -> 10; matrix products, arithmetic and copies ran while one was open for 2% -> 2% of each run, Pallas kernels for 4% -> 5%
where the time goes in v3:
time: 45 us; the launch traced here: 44.9 us
  starting transfers between devices  19.6 us (44%)
  waiting for transfers between devices  15.5 us (34%)
  Pallas kernels  6.94 us (15%)
  other arithmetic  2.01 us (4%)
  between operations  0.77 us (2%)
    ppermute x13, starting transfers between devices, exchange_xor(): return lax.ppermute(x, axis, [(i, i ^ bits) for i in range(count)])  15.4 us
    ppermute x13, waiting for transfers between devices, exchange_xor(): return lax.ppermute(x, axis, [(i, i ^ bits) for i in range(count)])  10.6 us
    pallas_call x5, Pallas kernels, call(): pl.pallas_call(kernel, out_shape=tuple((jax.ShapeDtypeStruct(s, d) for s,...  6.94 us
    ppermute x1, starting transfers between devices, local(): lax.ppermute(jnp.where(upper, frozen[:, part:], frozen[:, :part]), 'grid'...  2.47 us
    ppermute x1, waiting for transfers between devices, local(): first = lax.ppermute(first, 'grid', cross)  2.1 us
    ppermute x2, waiting for transfers between devices, local(): far_u, far_v = [lax.ppermute(x, 'grid', cross) for x in psi]  2.04 us
    ppermute x2, starting transfers between devices, local(): far_u, far_v = [lax.ppermute(x, 'grid', cross) for x in psi]  1.75 us
    concatenate x1, other arithmetic, local(): frozen = jnp.concatenate([potential[None], pairing], axis=0)  0.96 us
  transfers between devices with their start and end apart: 17, of which 10 were waited for; matrix products, arithmetic and copies ran while one was open for 2% of the time, Pallas kernels for 5%

profile of v3, /device:TPU:0, one launch (start us, length us, event | category | flops | bytes accessed | tf_op | source)
XLA Modules:
  0.0 44.9 jit_solution(16903339718049987486)
XLA Ops:
  0.6 0.0 copy-start.1
  0.6 0.0 copy-start.2
  0.7 0.9 %fusion.1 = f32[3,8,1024]{2,1,0:T(8,128)S(1)} fusion(f32[2,16,1024]{2,1,0:T(8,128)} %param.8, f32[1,16,1024]{2,1,0:T(8,128)} %bitcast.9, pred[]{:T(512)S(6)} %eq.3), kind=kLoop, calls=%fused_computation.7 | loop fusion | flops 73728 | bytes 294913 | tf_op jit(solution)/shard_map/jit(_where)/select_n | solution.py:398
  1.6 0.0 copy-start
  1.6 2.5 %collective-permute-start.2 = (f32[3,8,1024]{2,1,0:T(8,128)S(1)}, f32[3,8,1024]{2,1,0:T(8,128)S(1)}, u32[]{:S(2)}, u32[]{:S(2)}) collective-permute-start(f32[3,8,1024]{2,1,0:T(8,128)S(1)} %fusion.1), channel_id=1, source_target_pairs={{0,3},{1,2},{2,1},{3,0},{4,7},{5,6},{6,5},{7,4},{8,11},{9,10},{10,... | collective-permute-start | bytes 294920 | tf_op jit(solution)/shard_map/ppermute | solution.py:398
  4.1 0.0 copy-done.1
  4.1 0.1 collective-permute-start
  4.2 0.0 copy-done.2
  4.2 1.7 %collective-permute-start.1 = (f32[2,16,1024]{2,1,0:T(8,128)S(1)}, f32[2,16,1024]{2,1,0:T(8,128)S(1)}, u32[]{:S(2)}, u32[]{:S(2)}) collective-permute-start(f32[2,16,1024]{2,1,0:T(8,128)S(1)} %bitcast.6), channel_id=1, source_target_pairs={{0,3},{1,2},{2,1},{3,0},{4,7},{5,6},{6,5},{7,4},{8,11},{9,10},{10,... | collective-permute-start | bytes 393224 | tf_op jit(solution)/shard_map/ppermute | solution.py:399
  5.8 0.7 %collective-permute-start.5 = (f32[2,16,1024]{2,1,0:T(8,128)S(1)}, f32[2,16,1024]{2,1,0:T(8,128)S(1)}, u32[]{:S(2)}, u32[]{:S(2)}) collective-permute-start(f32[2,16,1024]{2,1,0:T(8,128)S(1)} %bitcast.4), channel_id=1, source_target_pairs={{0,1},{1,0},{2,3},{3,2},{4,5},{5,4},{6,7},{7,6},{8,9},{9,8},{10,11... | collective-permute-start | bytes 393224 | tf_op jit(solution)/shard_map/ppermute | solution.py:376
  6.5 0.0 collective-permute-start.6
  6.5 0.8 %collective-permute-done.2.refs_6_ = f32[3,8,1024]{2,1,0:T(8,128)S(1)} collective-permute-done((f32[3,8,1024]{2,1,0:T(8,128)S(1)}, f32[3,8,1024]{2,1,0:T(8,128)S(1)}, u32[]{:S(2)}, u32[]{:S(2)}) %collective-permute-start.2) | collective-permute-done | bytes 98336 | tf_op jit(solution)/shard_map/ppermute | solution.py:398
  7.3 2.4 %collective-permute-start.3 = (f32[3,8,1024]{2,1,0:T(8,128)S(1)}, f32[3,8,1024]{2,1,0:T(8,128)S(1)}, u32[]{:S(2)}, u32[]{:S(2)}) collective-permute-start(f32[3,8,1024]{2,1,0:T(8,128)S(1)} %collective-permute-done.2.refs_6_), channel_id=1, source_target_pairs={{0,4},{4,0},{8,12},{12,8},{16,20},{20,16},{24,28},{28,24},{1,5},{5... | collective-permute-start | bytes 294920 | tf_op jit(solution)/shard_map/ppermute | solution.py:376
  9.7 1.0 %pad_maximum_fusion.refs_2_ = f32[3,16,1024]{2,1,0:T(8,128)S(1)} fusion(f32[1,16,1024]{2,1,0:T(8,128)} %bitcast.10, f32[2,16,1024]{2,1,0:T(8,128)} %param.8), kind=kLoop, calls=%fused_computation.2 | loop fusion | flops 49152 | bytes 393216 | tf_op jit(solution)/shard_map/concatenate | solution.py:387
  10.7 0.0 collective-permute-done.refs_8_
  10.7 0.2 collective-permute-start.7
  10.8 2.0 %collective-permute-done.1.refs_9_ = f32[2,16,1024]{2,1,0:T(8,128)S(1)} collective-permute-done((f32[2,16,1024]{2,1,0:T(8,128)S(1)}, f32[2,16,1024]{2,1,0:T(8,128)S(1)}, u32[]{:S(2)}, u32[]{:S(2)}) %collective-permute-start.1) | collective-permute-done | bytes 131104 | tf_op jit(solution)/shard_map/ppermute | solution.py:399
  12.9 0.0 collective-permute-done.3.refs_7_
  12.9 0.2 collective-permute-start.4
  13.1 0.0 collective-permute-done.5.refs_3_
  13.1 0.0 collective-permute-done.6.refs_4_
  13.1 0.0 collective-permute-done.7.refs_5_
  13.1 0.0 copy-done
  13.2 1.5 %shard_map.76 = (f32[4,8,64,128]{3,2,1,0:T(8,128)S(1)}, f32[3,8,48,128]{3,2,1,0:T(8,128)S(1)}, f32[4,8,56,128]{3,2,1,0:T(8,128)S(1)}, bf16[4,4,48,512]{3,2,1,0:T(8,128)(2,1)S(1)}, bf16[4,4,48,512]{3,2,1,0:T(8,128)(2,1)S(1)}) custom-call(f32[2,16,1024]{2,1,0:T(8,128)S(1)} %bitcast.5, f32[2,16,1024]{2,1,0:T(8,128)S(1)} %bitcast.8, ...), custom_call_target="tpu_custom_call" | custom-call | flops 2850816000 | bytes 11403264 | tf_op jit(solution)/shard_map/pallas_call | solution.py:363
  14.7 0.0 collective-permute-done.4.refs_0_.refs_1_
  14.7 3.2 %shard_map.77 = (f32[4,8,16,128]{3,2,1,0:T(8,128)S(1)}, f32[4,8,16,128]{3,2,1,0:T(8,128)S(1)}, f32[4,2,4,16,128]{4,3,2,1,0:T(8,128)S(1)}, f32[4,8,56,128]{3,2,1,...) custom-call(f32[4,8,1024]{2,1,0:T(8,128)S(1)} %collective-permute-do, ...), custom_call_target="tpu_custom_call", output_to_operand_aliasing={{3}: (4, {}), {4}: (5, {}), {5}: (6, {})} | custom-call | flops 2424832000 | bytes 9699328 | tf_op jit(solution)/shard_map/pallas_call | solution.py:363
  17.9 2.5 %collective-permute-start.8 = (f32[1,2,4,16,128]{4,3,2,1,0:T(8,128)S(1)}, f32[1,2,4,16,128]{4,3,2,1,0:T(8,128)S(1)}, u32[]{:S(2)}, u32[]{:S(2)}) collective-permute-start(f32[1,2,4,16,128]{4,3,2,1,0:T(8,128)S(1)} %get-tuple-element.39), channel_id=1, source_target_pairs={{0,4},{4,0},{8,12},{12,8},{16,20},{20,16},{24,28},{28,24},{1,5},{5... | collective-permute-start | bytes 196616 | tf_op jit(solution)/shard_map/ppermute | solution.py:376
  20.5 1.5 %collective-permute-start.10 = (f32[1,2,4,16,128]{4,3,2,1,0:T(8,128)S(1)}, f32[1,2,4,16,128]{4,3,2,1,0:T(8,128)S(1)}, u32[]{:S(2)}, u32[]{:S(2)}) collective-permute-start(f32[1,2,4,16,128]{4,3,2,1,0:T(8,128)S(1)} %get-tuple-element.40), channel_id=1, source_target_pairs={{0,12},{4,8},{8,4},{12,0},{16,28},{20,24},{24,20},{28,16},{1,13},{... | collective-permute-start | bytes 196616 | tf_op jit(solution)/shard_map/ppermute | solution.py:376
  22.0 0.1 collective-permute-start.9
  22.0 1.8 %collective-permute-done.8 = f32[1,2,4,16,128]{4,3,2,1,0:T(8,128)S(1)} collective-permute-done((f32[1,2,4,16,128]{4,3,2,1,0:T(8,128)S(1)}, f32[1,2,4,16,128]{4,3,2,1,0:T(8,128)S(1)}, u32[]{:S(2)}, u32[]{:S(2)}) %collective-permute-start.8) | collective-permute-done | bytes 65568 | tf_op jit(solution)/shard_map/ppermute | solution.py:376
  23.8 2.1 %collective-permute-done.10 = f32[1,2,4,16,128]{4,3,2,1,0:T(8,128)S(1)} collective-permute-done((f32[1,2,4,16,128]{4,3,2,1,0:T(8,128)S(1)}, f32[1,2,4,16,128]{4,3,2,1,0:T(8,128)S(1)}, u32[]{:S(2)}, u32[]{:S(2)}) %collective-permute-start.10) | collective-permute-done | bytes 65568 | tf_op jit(solution)/shard_map/ppermute | solution.py:376
  25.9 0.4 collective-permute-done.9
  26.3 2.7 %collective-permute-start.11 = (f32[1,2,4,16,128]{4,3,2,1,0:T(8,128)S(1)}, f32[1,2,4,16,128]{4,3,2,1,0:T(8,128)S(1)}, u32[]{:S(2)}, u32[]{:S(2)}) collective-permute-start(f32[1,2,4,16,128]{4,3,2,1,0:T(8,128)S(1)} %add_add_fusion), channel_id=1, source_target_pairs={{0,16},{4,20},{8,24},{12,28},{16,0},{20,4},{24,8},{28,12},{1,17},{... | collective-permute-start | bytes 196616 | tf_op jit(solution)/shard_map/ppermute | solution.py:376
  28.9 2.6 %collective-permute-done.11 = f32[1,2,4,16,128]{4,3,2,1,0:T(8,128)S(1)} collective-permute-done((f32[1,2,4,16,128]{4,3,2,1,0:T(8,128)S(1)}, f32[1,2,4,16,128]{4,3,2,1,0:T(8,128)S(1)}, u32[]{:S(2)}, u32[]{:S(2)}) %collective-permute-start.11) | collective-permute-done | bytes 65568 | tf_op jit(solution)/shard_map/ppermute | solution.py:376
  31.5 0.1 divide_subtract_fusion
  31.6 2.3 %collective-permute-start.14 = (f32[1,2,4,16,128]{4,3,2,1,0:T(8,128)S(1)}, f32[1,2,4,16,128]{4,3,2,1,0:T(8,128)S(1)}, u32[]{:S(2)}, u32[]{:S(2)}) collective-permute-start(f32[1,2,4,16,128]{4,3,2,1,0:T(8,128)S(1)} %pad_maximum_fusion.1.refs_0_), channel_id=1, source_target_pairs={{0,12},{4,8},{8,4},{12,0},{16,28},{20,24},{24,20},{28,16},{1,13},{... | collective-permute-start | bytes 196616 | tf_op jit(solution)/shard_map/ppermute | solution.py:376
  33.9 0.8 %collective-permute-start.13 = (f32[1,2,4,16,128]{4,3,2,1,0:T(8,128)S(1)}, f32[1,2,4,16,128]{4,3,2,1,0:T(8,128)S(1)}, u32[]{:S(2)}, u32[]{:S(2)}) collective-permute-start(f32[1,2,4,16,128]{4,3,2,1,0:T(8,128)S(1)} %pad_maximum_fusion.1.refs_0_), channel_id=1, source_target_pairs={{0,8},{4,12},{8,0},{12,4},{16,24},{20,28},{24,16},{28,20},{1,9},{5... | collective-permute-start | bytes 196616 | tf_op jit(solution)/shard_map/ppermute | solution.py:376
  34.7 0.5 %collective-permute-start.12 = (f32[1,2,4,16,128]{4,3,2,1,0:T(8,128)S(1)}, f32[1,2,4,16,128]{4,3,2,1,0:T(8,128)S(1)}, u32[]{:S(2)}, u32[]{:S(2)}) collective-permute-start(f32[1,2,4,16,128]{4,3,2,1,0:T(8,128)S(1)} %pad_maximum_fusion.1.refs_0_), channel_id=1, source_target_pairs={{0,4},{4,0},{8,12},{12,8},{16,20},{20,16},{24,28},{28,24},{1,5},{5... | collective-permute-start | bytes 196616 | tf_op jit(solution)/shard_map/ppermute | solution.py:376
  35.2 1.7 %collective-permute-done.14.refs_3_ = f32[1,2,4,16,128]{4,3,2,1,0:T(8,128)S(1)} collective-permute-done((f32[1,2,4,16,128]{4,3,2,1,0:T(8,128)S(1)}, f32[1,2,4,16,128]{4,3,2,1,0:T(8,128)S(1)}, u32[]{:S(2)}, u32[]{:S(2)}) %collective-permute-start.14) | collective-permute-done | bytes 65568 | tf_op jit(solution)/shard_map/ppermute | solution.py:376
  36.8 1.3 %collective-permute-done.13.refs_2_ = f32[1,2,4,16,128]{4,3,2,1,0:T(8,128)S(1)} collective-permute-done((f32[1,2,4,16,128]{4,3,2,1,0:T(8,128)S(1)}, f32[1,2,4,16,128]{4,3,2,1,0:T(8,128)S(1)}, u32[]{:S(2)}, u32[]{:S(2)}) %collective-permute-start.13) | collective-permute-done | bytes 65568 | tf_op jit(solution)/shard_map/ppermute | solution.py:376
  38.1 0.8 %collective-permute-done.12.refs_1_ = f32[1,2,4,16,128]{4,3,2,1,0:T(8,128)S(1)} collective-permute-done((f32[1,2,4,16,128]{4,3,2,1,0:T(8,128)S(1)}, f32[1,2,4,16,128]{4,3,2,1,0:T(8,128)S(1)}, u32[]{:S(2)}, u32[]{:S(2)}) %collective-permute-start.12) | collective-permute-done | bytes 65568 | tf_op jit(solution)/shard_map/ppermute | solution.py:376
  38.9 0.8 %shard_map.78 = (f32[4,8,16,128]{3,2,1,0:T(8,128)S(1)}, f32[8,16,128]{2,1,0:T(8,128)S(1)}, f32[8,16,128]{2,1,0:T(8,128)S(1)}, f32[4,16,1024]{2,1,0:T(8,128)}, f32[4,2,4,16,128]{4,3,2,1,0:T(8,128)S(1)}) custom-call(f32[1,2,4,16,128]{4,3,2,1,0:T(8,128)S(1)} %pad_maximum_fusion.1.refs_0_, f32[1,2,4,16,128]{4,3,2,1,0:T(8,128)S(1)} %collective-permute-done.12.refs_1_, ...), custom_call_target="tpu_custom_call" | custom-call | flops 458752000 | bytes 1835008 | tf_op jit(solution)/shard_map/pallas_call | solution.py:363
  39.7 0.0 collective-permute-start.15
  39.7 1.6 %collective-permute-start.16 = (f32[8,16,128]{2,1,0:T(8,128)S(1)}, f32[8,16,128]{2,1,0:T(8,128)S(1)}, u32[]{:S(2)}, u32[]{:S(2)}) collective-permute-start(f32[8,16,128]{2,1,0:T(8,128)S(1)} %get-tuple-element.35), channel_id=1, source_target_pairs={{0,1},{1,0},{2,3},{3,2},{4,5},{5,4},{6,7},{7,6},{8,9},{9,8},{10,11... | collective-permute-start | bytes 196616 | tf_op jit(solution)/shard_map/ppermute | solution.py:376
  41.3 0.6 %shard_map.79.refs_0_ = f32[4,8,16,128]{3,2,1,0:T(8,128)S(1)} custom-call(f32[4,8,16,128]{3,2,1,0:T(8,128)S(1)} %get-tuple-element.29.refs_4_.refs_0_, f32[4,8,16,128]{3,2,1,0:T(8,128)S(1)} %get-tuple-element.30.refs_5_.refs_1_, f32[4,8,16,128]{3,2,1,0:T(8,128)S(1)} %get-tuple-element.32.refs_2_, f32[4,2,4,16,128]{4,3,2,1,0:T(8,128)S(1)} %get-tuple-element.33.refs_3_, ...), custom_call_target="tpu_custom_call" | custom-call | flops 131072000 | bytes 524288 | tf_op jit(solution)/shard_map/pallas_call | solution.py:363
  41.9 2.1 %collective-permute-done.15.refs_1_ = f32[8,16,128]{2,1,0:T(8,128)S(1)} collective-permute-done((f32[8,16,128]{2,1,0:T(8,128)S(1)}, f32[8,16,128]{2,1,0:T(8,128)S(1)}, u32[]{:S(2)}, u32[]{:S(2)}) %collective-permute-start.15) | collective-permute-done | bytes 65568 | tf_op jit(solution)/shard_map/ppermute | solution.py:499
  44.0 0.0 collective-permute-done.16.refs_2_
  44.0 0.9 %shard_map.80 = (f32[1,2,16,1024]{3,2,1,0:T(8,128)}, f32[1,2,16,1024]{3,2,1,0:T(8,128)}) custom-call(f32[4,8,16,128]{3,2,1,0:T(8,128)S(1)} %shard_map.79.refs_0_, f32[8,16,128]{2,1,0:T(8,128)S(1)} %collective-permute-done.15.refs_1_, f32[8,16,128]{2,1,0:T(8,128)S(1)} %collective-permute-done.16.refs_2_), custom_call_target="tpu_custom_call" | custom-call | flops 131072000 | bytes 524288 | tf_op jit(solution)/shard_map/pallas_call | solution.py:363
  (6 shorter events, 0.1 us)
Async XLA Ops:
  0.6 3.4 %copy-start.1 = (f32[1,2,16,1024]{3,2,1,0:T(8,128)S(1)}, f32[1,2,16,1024]{3,2,1,0:T(8,128)}, u32[]{:S(2)}) copy-start(f32[1,2,16,1024]{3,2,1,0:T(8,128)} %param.5) | copy-start | bytes 393220
  0.6 3.5 %copy-start.2 = (f32[1,2,16,1024]{3,2,1,0:T(8,128)S(1)}, f32[1,2,16,1024]{3,2,1,0:T(8,128)}, u32[]{:S(2)}) copy-start(f32[1,2,16,1024]{3,2,1,0:T(8,128)} %param.6) | copy-start | bytes 393220
  1.6 11.6 %copy-start = (bf16[1024,256]{1,0:T(8,128)(2,1)S(1)}, bf16[1024,256]{1,0:T(8,128)(2,1)}, u32[]{:S(2)}) copy-start(bf16[1024,256]{1,0:T(8,128)(2,1)} %constant.55.clone.refs_10_.refs_7_.refs_4_) | copy-start | bytes 1572868
  1.6 5.7 %collective-permute-start.2 = (f32[3,8,1024]{2,1,0:T(8,128)S(1)}, f32[3,8,1024]{2,1,0:T(8,128)S(1)}, u32[]{:S(2)}, u32[]{:S(2)}) collective-permute-start(f32[3,8,1024]{2,1,0:T(8,128)S(1)} %fusion.1), channel_id=1, source_target_pairs={{0,3},{1,2},{2,1},{3,0},{4,7},{5,6},{6,5},{7,4},{8,11},{9,10},{10,... | collective-permute-start | bytes 294920 | tf_op jit(solution)/shard_map/ppermute | solution.py:398
  4.1 6.6 %collective-permute-start = (f32[2,16,1024]{2,1,0:T(8,128)S(1)}, f32[2,16,1024]{2,1,0:T(8,128)S(1)}, u32[]{:S(2)}, u32[]{:S(2)}) collective-permute-start(f32[2,16,1024]{2,1,0:T(8,128)S(1)} %bitcast.3), channel_id=1, source_target_pairs={{0,3},{1,2},{2,1},{3,0},{4,7},{5,6},{6,5},{7,4},{8,11},{9,10},{10,... | collective-permute-start | bytes 393224 | tf_op jit(solution)/shard_map/ppermute | solution.py:399
  4.2 8.7 %collective-permute-start.1 = (f32[2,16,1024]{2,1,0:T(8,128)S(1)}, f32[2,16,1024]{2,1,0:T(8,128)S(1)}, u32[]{:S(2)}, u32[]{:S(2)}) collective-permute-start(f32[2,16,1024]{2,1,0:T(8,128)S(1)} %bitcast.6), channel_id=1, source_target_pairs={{0,3},{1,2},{2,1},{3,0},{4,7},{5,6},{6,5},{7,4},{8,11},{9,10},{10,... | collective-permute-start | bytes 393224 | tf_op jit(solution)/shard_map/ppermute | solution.py:399
  5.8 7.3 %collective-permute-start.5 = (f32[2,16,1024]{2,1,0:T(8,128)S(1)}, f32[2,16,1024]{2,1,0:T(8,128)S(1)}, u32[]{:S(2)}, u32[]{:S(2)}) collective-permute-start(f32[2,16,1024]{2,1,0:T(8,128)S(1)} %bitcast.4), channel_id=1, source_target_pairs={{0,1},{1,0},{2,3},{3,2},{4,5},{5,4},{6,7},{7,6},{8,9},{9,8},{10,11... | collective-permute-start | bytes 393224 | tf_op jit(solution)/shard_map/ppermute | solution.py:376
  6.5 6.6 %collective-permute-start.6 = (f32[2,16,1024]{2,1,0:T(8,128)S(1)}, f32[2,16,1024]{2,1,0:T(8,128)S(1)}, u32[]{:S(2)}, u32[]{:S(2)}) collective-permute-start(f32[2,16,1024]{2,1,0:T(8,128)S(1)} %bitcast.7), channel_id=1, source_target_pairs={{0,1},{1,0},{2,3},{3,2},{4,5},{5,4},{6,7},{7,6},{8,9},{9,8},{10,11... | collective-permute-start | bytes 393224 | tf_op jit(solution)/shard_map/ppermute | solution.py:376
  7.3 5.6 %collective-permute-start.3 = (f32[3,8,1024]{2,1,0:T(8,128)S(1)}, f32[3,8,1024]{2,1,0:T(8,128)S(1)}, u32[]{:S(2)}, u32[]{:S(2)}) collective-permute-start(f32[3,8,1024]{2,1,0:T(8,128)S(1)} %collective-permute-done.2.refs_6_), channel_id=1, source_target_pairs={{0,4},{4,0},{8,12},{12,8},{16,20},{20,16},{24,28},{28,24},{1,5},{5... | collective-permute-start | bytes 294920 | tf_op jit(solution)/shard_map/ppermute | solution.py:376
  10.7 2.5 %collective-permute-start.7 = (f32[3,16,1024]{2,1,0:T(8,128)S(1)}, f32[3,16,1024]{2,1,0:T(8,128)S(1)}, u32[]{:S(2)}, u32[]{:S(2)}) collective-permute-start(f32[3,16,1024]{2,1,0:T(8,128)S(1)} %pad_maximum_fusion.refs_2_), channel_id=1, source_target_pairs={{0,1},{1,0},{2,3},{3,2},{4,5},{5,4},{6,7},{7,6},{8,9},{9,8},{10,11... | collective-permute-start | bytes 589832 | tf_op jit(solution)/shard_map/ppermute | solution.py:376
  12.9 1.7 %collective-permute-start.4 = (f32[4,8,1024]{2,1,0:T(8,128)S(1)}, f32[4,8,1024]{2,1,0:T(8,128)S(1)}, u32[]{:S(2)}, u32[]{:S(2)}) collective-permute-start(f32[4,8,1024]{2,1,0:T(8,128)S(1)} %maximum_maximum_fusion), channel_id=1, source_target_pairs={{0,1},{1,0},{2,3},{3,2},{4,5},{5,4},{6,7},{7,6},{8,9},{9,8},{10,11... | collective-permute-start | bytes 393224 | tf_op jit(solution)/shard_map/ppermute | solution.py:376
  17.9 5.9 %collective-permute-start.8 = (f32[1,2,4,16,128]{4,3,2,1,0:T(8,128)S(1)}, f32[1,2,4,16,128]{4,3,2,1,0:T(8,128)S(1)}, u32[]{:S(2)}, u32[]{:S(2)}) collective-permute-start(f32[1,2,4,16,128]{4,3,2,1,0:T(8,128)S(1)} %get-tuple-element.39), channel_id=1, source_target_pairs={{0,4},{4,0},{8,12},{12,8},{16,20},{20,16},{24,28},{28,24},{1,5},{5... | collective-permute-start | bytes 196616 | tf_op jit(solution)/shard_map/ppermute | solution.py:376
  20.5 5.4 %collective-permute-start.10 = (f32[1,2,4,16,128]{4,3,2,1,0:T(8,128)S(1)}, f32[1,2,4,16,128]{4,3,2,1,0:T(8,128)S(1)}, u32[]{:S(2)}, u32[]{:S(2)}) collective-permute-start(f32[1,2,4,16,128]{4,3,2,1,0:T(8,128)S(1)} %get-tuple-element.40), channel_id=1, source_target_pairs={{0,12},{4,8},{8,4},{12,0},{16,28},{20,24},{24,20},{28,16},{1,13},{... | collective-permute-start | bytes 196616 | tf_op jit(solution)/shard_map/ppermute | solution.py:376
  22.0 4.3 %collective-permute-start.9 = (f32[1,2,4,16,128]{4,3,2,1,0:T(8,128)S(1)}, f32[1,2,4,16,128]{4,3,2,1,0:T(8,128)S(1)}, u32[]{:S(2)}, u32[]{:S(2)}) collective-permute-start(f32[1,2,4,16,128]{4,3,2,1,0:T(8,128)S(1)} %get-tuple-element.41), channel_id=1, source_target_pairs={{0,8},{4,12},{8,0},{12,4},{16,24},{20,28},{24,16},{28,20},{1,9},{5... | collective-permute-start | bytes 196616 | tf_op jit(solution)/shard_map/ppermute | solution.py:376
  26.3 5.2 %collective-permute-start.11 = (f32[1,2,4,16,128]{4,3,2,1,0:T(8,128)S(1)}, f32[1,2,4,16,128]{4,3,2,1,0:T(8,128)S(1)}, u32[]{:S(2)}, u32[]{:S(2)}) collective-permute-start(f32[1,2,4,16,128]{4,3,2,1,0:T(8,128)S(1)} %add_add_fusion), channel_id=1, source_target_pairs={{0,16},{4,20},{8,24},{12,28},{16,0},{20,4},{24,8},{28,12},{1,17},{... | collective-permute-start | bytes 196616 | tf_op jit(solution)/shard_map/ppermute | solution.py:376
  31.6 5.2 %collective-permute-start.14 = (f32[1,2,4,16,128]{4,3,2,1,0:T(8,128)S(1)}, f32[1,2,4,16,128]{4,3,2,1,0:T(8,128)S(1)}, u32[]{:S(2)}, u32[]{:S(2)}) collective-permute-start(f32[1,2,4,16,128]{4,3,2,1,0:T(8,128)S(1)} %pad_maximum_fusion.1.refs_0_), channel_id=1, source_target_pairs={{0,12},{4,8},{8,4},{12,0},{16,28},{20,24},{24,20},{28,16},{1,13},{... | collective-permute-start | bytes 196616 | tf_op jit(solution)/shard_map/ppermute | solution.py:376
  33.9 4.3 %collective-permute-start.13 = (f32[1,2,4,16,128]{4,3,2,1,0:T(8,128)S(1)}, f32[1,2,4,16,128]{4,3,2,1,0:T(8,128)S(1)}, u32[]{:S(2)}, u32[]{:S(2)}) collective-permute-start(f32[1,2,4,16,128]{4,3,2,1,0:T(8,128)S(1)} %pad_maximum_fusion.1.refs_0_), channel_id=1, source_target_pairs={{0,8},{4,12},{8,0},{12,4},{16,24},{20,28},{24,16},{28,20},{1,9},{5... | collective-permute-start | bytes 196616 | tf_op jit(solution)/shard_map/ppermute | solution.py:376
  34.7 4.3 %collective-permute-start.12 = (f32[1,2,4,16,128]{4,3,2,1,0:T(8,128)S(1)}, f32[1,2,4,16,128]{4,3,2,1,0:T(8,128)S(1)}, u32[]{:S(2)}, u32[]{:S(2)}) collective-permute-start(f32[1,2,4,16,128]{4,3,2,1,0:T(8,128)S(1)} %pad_maximum_fusion.1.refs_0_), channel_id=1, source_target_pairs={{0,4},{4,0},{8,12},{12,8},{16,20},{20,16},{24,28},{28,24},{1,5},{5... | collective-permute-start | bytes 196616 | tf_op jit(solution)/shard_map/ppermute | solution.py:376
  39.7 4.3 %collective-permute-start.15 = (f32[8,16,128]{2,1,0:T(8,128)S(1)}, f32[8,16,128]{2,1,0:T(8,128)S(1)}, u32[]{:S(2)}, u32[]{:S(2)}) collective-permute-start(f32[8,16,128]{2,1,0:T(8,128)S(1)} %get-tuple-element.34), channel_id=1, source_target_pairs={{0,3},{1,2},{2,1},{3,0},{4,7},{5,6},{6,5},{7,4},{8,11},{9,10},{10,... | collective-permute-start | bytes 196616 | tf_op jit(solution)/shard_map/ppermute | solution.py:499
  39.7 4.3 %collective-permute-start.16 = (f32[8,16,128]{2,1,0:T(8,128)S(1)}, f32[8,16,128]{2,1,0:T(8,128)S(1)}, u32[]{:S(2)}, u32[]{:S(2)}) collective-permute-start(f32[8,16,128]{2,1,0:T(8,128)S(1)} %get-tuple-element.35), channel_id=1, source_target_pairs={{0,1},{1,0},{2,3},{3,2},{4,5},{5,4},{6,7},{7,6},{8,9},{9,8},{10,11... | collective-permute-start | bytes 196616 | tf_op jit(solution)/shard_map/ppermute | solution.py:376

commit v4 on v3

--- a/solution.py
+++ b/solution.py
@@ -242,7 +242,7 @@
 def middle_kernel(paired, planes, low_bits, *refs):
     pieces = refs[:low_bits]
     psi1, kin1 = refs[low_bits : low_bits + 2]
-    mid, first_send, second_send, fields_out, fields_flat = refs[low_bits + 2 :]
+    mid, first_send, second_send, fields_flat = refs[low_bits + 2 :]
     even = lax.rem(lax.axis_index("grid"), 2) == 0
     quarter = lax.rem(lax.axis_index("modes"), low_bits)
     per = 4 // low_bits
@@ -255,9 +255,7 @@
 
     for j in range(8):
         big, half = j // 2, j % 2
-        now = [fields_flat[big, half, i] for i in range(4)]
-        for i in range(4):
-            fields_out[i, :, j * LANES : (j + 1) * LANES] = now[i]
+        now = [fields_flat[big, half, i] for i in range(3)]
         f = [psi1[c, j] for c in range(4)]
         q = slope(f, [kin1[c, j] + now[0] * f[c] for c in range(4)], now[1], now[2])
         for c in range(4):
@@ -273,9 +271,12 @@
 
 
 def inner_kernel(planes, *refs):
-    psi1, kin1, mid, fields_flat, w_ref, part_ref, pad, hi, lo, xy = refs
+    psi1, kin1, mid, fields_flat, w_ref, part_ref, fields_out, pad, hi, lo, xy = refs
     tall = up16(planes)
     zero = jnp.zeros((8, LANES), jnp.float32)
+    for j in range(8):
+        for i in range(4):
+            fields_out[i, :, j * LANES : (j + 1) * LANES] = fields_flat[j // 2, j % 2, i]
     for c in range(4):
         for j in range(8):
             value = mid[c, j]
@@ -489,9 +490,9 @@
     got = [quarter] + [exchange_xor(quarter, "modes", k, modes) for k in range(1, low_bits)]
 
     edge = (8, 4 * REACH, LANES)
-    mid, first, second, fields, fields_flat = call(
+    mid, first, second, fields_flat = call(
         functools.partial(middle_kernel, paired, planes, low_bits),
-        [state, edge, edge, (4, planes, NX * NY), (4, 2, 4, planes, LANES)],
+        [state, edge, edge, (4, 2, 4, planes, LANES)],
         [],
         got + [psi1, kin1],
     )
@@ -502,9 +503,9 @@
         first = lax.ppermute(first, "grid", down)
         second = lax.ppermute(second, "grid", up)
     flat = up16(planes)
-    (part,) = call(
+    part, fields = call(
         functools.partial(inner_kernel, planes),
-        [state],
+        [state, (4, planes, NX * NY)],
         [
             ((4, 8, flat + 16, LANES), f32),
             ((4, 4, flat, WINDOW), bf16),

time: 45 us -> 44.4 us (0.987)
  waiting for transfers between devices: 15.5 us -> 14.8 us
    ppermute x1, waiting for transfers between devices: 2.1 us -> 1.45 us  [local(): first = lax.ppermute(first, 'grid', cross)]
  transfers between devices with their start and end apart: 17 -> 17, of which waited for: 10 -> 10; matrix products, arithmetic and copies ran while one was open for 2% -> 2% of each run, Pallas kernels for 5% -> 6%
where the time goes in v4:
time: 44.4 us; the launch traced here: 44.3 us
  starting transfers between devices  19.7 us (44%)
  waiting for transfers between devices  14.8 us (33%)
  Pallas kernels  6.94 us (16%)
  other arithmetic  2.01 us (5%)
  between operations  0.78 us (2%)
    ppermute x13, starting transfers between devices, exchange_xor(): return lax.ppermute(x, axis, [(i, i ^ bits) for i in range(count)])  15.4 us
    ppermute x13, waiting for transfers between devices, exchange_xor(): return lax.ppermute(x, axis, [(i, i ^ bits) for i in range(count)])  10.6 us
    pallas_call x5, Pallas kernels, call(): pl.pallas_call(kernel, out_shape=tuple((jax.ShapeDtypeStruct(s, d) for s,...  6.94 us
    ppermute x1, starting transfers between devices, local(): lax.ppermute(jnp.where(upper, frozen[:, part:], frozen[:, :part]), 'grid'...  2.47 us
    ppermute x2, waiting for transfers between devices, local(): far_u, far_v = [lax.ppermute(x, 'grid', cross) for x in psi]  2.04 us
    ppermute x2, starting transfers between devices, local(): far_u, far_v = [lax.ppermute(x, 'grid', cross) for x in psi]  1.75 us
    ppermute x1, waiting for transfers between devices, local(): first = lax.ppermute(first, 'grid', cross)  1.45 us
    concatenate x1, other arithmetic, local(): frozen = jnp.concatenate([potential[None], pairing], axis=0)  0.96 us
  transfers between devices with their start and end apart: 17, of which 10 were waited for; matrix products, arithmetic and copies ran while one was open for 2% of the time, Pallas kernels for 6%

profile of v4, /device:TPU:0, one launch (start us, length us, event | category | flops | bytes accessed | tf_op | source)
XLA Modules:
  0.0 44.3 jit_solution(7871731532616658215)
XLA Ops:
  0.6 0.0 copy-start.1
  0.6 0.0 copy-start.2
  0.7 0.9 %fusion.1 = f32[3,8,1024]{2,1,0:T(8,128)S(1)} fusion(f32[2,16,1024]{2,1,0:T(8,128)} %param.8, f32[1,16,1024]{2,1,0:T(8,128)} %bitcast.9, pred[]{:T(512)S(6)} %eq.3), kind=kLoop, calls=%fused_computation.7 | loop fusion | flops 73728 | bytes 294913 | tf_op jit(solution)/shard_map/jit(_where)/select_n | solution.py:399
  1.6 0.0 copy-start
  1.6 2.5 %collective-permute-start.2 = (f32[3,8,1024]{2,1,0:T(8,128)S(1)}, f32[3,8,1024]{2,1,0:T(8,128)S(1)}, u32[]{:S(2)}, u32[]{:S(2)}) collective-permute-start(f32[3,8,1024]{2,1,0:T(8,128)S(1)} %fusion.1), channel_id=1, source_target_pairs={{0,3},{1,2},{2,1},{3,0},{4,7},{5,6},{6,5},{7,4},{8,11},{9,10},{10,... | collective-permute-start | bytes 294920 | tf_op jit(solution)/shard_map/ppermute | solution.py:399
  4.1 0.0 copy-done.1
  4.1 0.1 collective-permute-start
  4.2 0.0 copy-done.2
  4.2 1.7 %collective-permute-start.1 = (f32[2,16,1024]{2,1,0:T(8,128)S(1)}, f32[2,16,1024]{2,1,0:T(8,128)S(1)}, u32[]{:S(2)}, u32[]{:S(2)}) collective-permute-start(f32[2,16,1024]{2,1,0:T(8,128)S(1)} %bitcast.6), channel_id=1, source_target_pairs={{0,3},{1,2},{2,1},{3,0},{4,7},{5,6},{6,5},{7,4},{8,11},{9,10},{10,... | collective-permute-start | bytes 393224 | tf_op jit(solution)/shard_map/ppermute | solution.py:400
  5.8 0.7 %collective-permute-start.5 = (f32[2,16,1024]{2,1,0:T(8,128)S(1)}, f32[2,16,1024]{2,1,0:T(8,128)S(1)}, u32[]{:S(2)}, u32[]{:S(2)}) collective-permute-start(f32[2,16,1024]{2,1,0:T(8,128)S(1)} %bitcast.4), channel_id=1, source_target_pairs={{0,1},{1,0},{2,3},{3,2},{4,5},{5,4},{6,7},{7,6},{8,9},{9,8},{10,11... | collective-permute-start | bytes 393224 | tf_op jit(solution)/shard_map/ppermute | solution.py:377
  6.5 0.0 collective-permute-start.6
  6.5 0.8 %collective-permute-done.2.refs_6_ = f32[3,8,1024]{2,1,0:T(8,128)S(1)} collective-permute-done((f32[3,8,1024]{2,1,0:T(8,128)S(1)}, f32[3,8,1024]{2,1,0:T(8,128)S(1)}, u32[]{:S(2)}, u32[]{:S(2)}) %collective-permute-start.2) | collective-permute-done | bytes 98336 | tf_op jit(solution)/shard_map/ppermute | solution.py:399
  7.3 2.4 %collective-permute-start.3 = (f32[3,8,1024]{2,1,0:T(8,128)S(1)}, f32[3,8,1024]{2,1,0:T(8,128)S(1)}, u32[]{:S(2)}, u32[]{:S(2)}) collective-permute-start(f32[3,8,1024]{2,1,0:T(8,128)S(1)} %collective-permute-done.2.refs_6_), channel_id=1, source_target_pairs={{0,4},{4,0},{8,12},{12,8},{16,20},{20,16},{24,28},{28,24},{1,5},{5... | collective-permute-start | bytes 294920 | tf_op jit(solution)/shard_map/ppermute | solution.py:377
  9.7 1.0 %pad_maximum_fusion.refs_2_ = f32[3,16,1024]{2,1,0:T(8,128)S(1)} fusion(f32[1,16,1024]{2,1,0:T(8,128)} %bitcast.10, f32[2,16,1024]{2,1,0:T(8,128)} %param.8), kind=kLoop, calls=%fused_computation.2 | loop fusion | flops 49152 | bytes 393216 | tf_op jit(solution)/shard_map/concatenate | solution.py:388
  10.7 0.0 collective-permute-done.refs_8_
  10.7 0.2 collective-permute-start.7
  10.8 2.0 %collective-permute-done.1.refs_9_ = f32[2,16,1024]{2,1,0:T(8,128)S(1)} collective-permute-done((f32[2,16,1024]{2,1,0:T(8,128)S(1)}, f32[2,16,1024]{2,1,0:T(8,128)S(1)}, u32[]{:S(2)}, u32[]{:S(2)}) %collective-permute-start.1) | collective-permute-done | bytes 131104 | tf_op jit(solution)/shard_map/ppermute | solution.py:400
  12.9 0.0 collective-permute-done.3.refs_7_
  12.9 0.2 collective-permute-start.4
  13.1 0.0 collective-permute-done.5.refs_3_
  13.1 0.0 collective-permute-done.6.refs_4_
  13.1 0.0 collective-permute-done.7.refs_5_
  13.1 0.0 copy-done
  13.2 1.5 %shard_map.76 = (f32[4,8,64,128]{3,2,1,0:T(8,128)S(1)}, f32[3,8,48,128]{3,2,1,0:T(8,128)S(1)}, f32[4,8,56,128]{3,2,1,0:T(8,128)S(1)}, bf16[4,4,48,512]{3,2,1,0:T(8,128)(2,1)S(1)}, bf16[4,4,48,512]{3,2,1,0:T(8,128)(2,1)S(1)}) custom-call(f32[2,16,1024]{2,1,0:T(8,128)S(1)} %bitcast.5, f32[2,16,1024]{2,1,0:T(8,128)S(1)} %bitcast.8, ...), custom_call_target="tpu_custom_call" | custom-call | flops 2850816000 | bytes 11403264 | tf_op jit(solution)/shard_map/pallas_call | solution.py:364
  14.7 0.0 collective-permute-done.4.refs_0_.refs_1_
  14.7 3.2 %shard_map.77 = (f32[4,8,16,128]{3,2,1,0:T(8,128)S(1)}, f32[4,8,16,128]{3,2,1,0:T(8,128)S(1)}, f32[4,2,4,16,128]{4,3,2,1,0:T(8,128)S(1)}, f32[4,8,56,128]{3,2,1,...) custom-call(f32[4,8,1024]{2,1,0:T(8,128)S(1)} %collective-permute-do, ...), custom_call_target="tpu_custom_call", output_to_operand_aliasing={{3}: (4, {}), {4}: (5, {}), {5}: (6, {})} | custom-call | flops 2424832000 | bytes 9699328 | tf_op jit(solution)/shard_map/pallas_call | solution.py:364
  17.9 2.5 %collective-permute-start.8 = (f32[1,2,4,16,128]{4,3,2,1,0:T(8,128)S(1)}, f32[1,2,4,16,128]{4,3,2,1,0:T(8,128)S(1)}, u32[]{:S(2)}, u32[]{:S(2)}) collective-permute-start(f32[1,2,4,16,128]{4,3,2,1,0:T(8,128)S(1)} %get-tuple-element.41), channel_id=1, source_target_pairs={{0,4},{4,0},{8,12},{12,8},{16,20},{20,16},{24,28},{28,24},{1,5},{5... | collective-permute-start | bytes 196616 | tf_op jit(solution)/shard_map/ppermute | solution.py:377
  20.5 1.5 %collective-permute-start.10 = (f32[1,2,4,16,128]{4,3,2,1,0:T(8,128)S(1)}, f32[1,2,4,16,128]{4,3,2,1,0:T(8,128)S(1)}, u32[]{:S(2)}, u32[]{:S(2)}) collective-permute-start(f32[1,2,4,16,128]{4,3,2,1,0:T(8,128)S(1)} %get-tuple-element.42), channel_id=1, source_target_pairs={{0,12},{4,8},{8,4},{12,0},{16,28},{20,24},{24,20},{28,16},{1,13},{... | collective-permute-start | bytes 196616 | tf_op jit(solution)/shard_map/ppermute | solution.py:377
  22.0 0.1 collective-permute-start.9
  22.0 1.8 %collective-permute-done.8 = f32[1,2,4,16,128]{4,3,2,1,0:T(8,128)S(1)} collective-permute-done((f32[1,2,4,16,128]{4,3,2,1,0:T(8,128)S(1)}, f32[1,2,4,16,128]{4,3,2,1,0:T(8,128)S(1)}, u32[]{:S(2)}, u32[]{:S(2)}) %collective-permute-start.8) | collective-permute-done | bytes 65568 | tf_op jit(solution)/shard_map/ppermute | solution.py:377
  23.8 2.1 %collective-permute-done.10 = f32[1,2,4,16,128]{4,3,2,1,0:T(8,128)S(1)} collective-permute-done((f32[1,2,4,16,128]{4,3,2,1,0:T(8,128)S(1)}, f32[1,2,4,16,128]{4,3,2,1,0:T(8,128)S(1)}, u32[]{:S(2)}, u32[]{:S(2)}) %collective-permute-start.10) | collective-permute-done | bytes 65568 | tf_op jit(solution)/shard_map/ppermute | solution.py:377
  25.9 0.4 collective-permute-done.9
  26.3 2.7 %collective-permute-start.11 = (f32[1,2,4,16,128]{4,3,2,1,0:T(8,128)S(1)}, f32[1,2,4,16,128]{4,3,2,1,0:T(8,128)S(1)}, u32[]{:S(2)}, u32[]{:S(2)}) collective-permute-start(f32[1,2,4,16,128]{4,3,2,1,0:T(8,128)S(1)} %add_add_fusion), channel_id=1, source_target_pairs={{0,16},{4,20},{8,24},{12,28},{16,0},{20,4},{24,8},{28,12},{1,17},{... | collective-permute-start | bytes 196616 | tf_op jit(solution)/shard_map/ppermute | solution.py:377
  28.9 2.6 %collective-permute-done.11 = f32[1,2,4,16,128]{4,3,2,1,0:T(8,128)S(1)} collective-permute-done((f32[1,2,4,16,128]{4,3,2,1,0:T(8,128)S(1)}, f32[1,2,4,16,128]{4,3,2,1,0:T(8,128)S(1)}, u32[]{:S(2)}, u32[]{:S(2)}) %collective-permute-start.11) | collective-permute-done | bytes 65568 | tf_op jit(solution)/shard_map/ppermute | solution.py:377
  31.5 0.1 divide_subtract_fusion
  31.6 2.3 %collective-permute-start.14 = (f32[1,2,4,16,128]{4,3,2,1,0:T(8,128)S(1)}, f32[1,2,4,16,128]{4,3,2,1,0:T(8,128)S(1)}, u32[]{:S(2)}, u32[]{:S(2)}) collective-permute-start(f32[1,2,4,16,128]{4,3,2,1,0:T(8,128)S(1)} %pad_maximum_fusion.1.refs_0_), channel_id=1, source_target_pairs={{0,12},{4,8},{8,4},{12,0},{16,28},{20,24},{24,20},{28,16},{1,13},{... | collective-permute-start | bytes 196616 | tf_op jit(solution)/shard_map/ppermute | solution.py:377
  33.9 0.8 %collective-permute-start.13 = (f32[1,2,4,16,128]{4,3,2,1,0:T(8,128)S(1)}, f32[1,2,4,16,128]{4,3,2,1,0:T(8,128)S(1)}, u32[]{:S(2)}, u32[]{:S(2)}) collective-permute-start(f32[1,2,4,16,128]{4,3,2,1,0:T(8,128)S(1)} %pad_maximum_fusion.1.refs_0_), channel_id=1, source_target_pairs={{0,8},{4,12},{8,0},{12,4},{16,24},{20,28},{24,16},{28,20},{1,9},{5... | collective-permute-start | bytes 196616 | tf_op jit(solution)/shard_map/ppermute | solution.py:377
  34.7 0.5 %collective-permute-start.12 = (f32[1,2,4,16,128]{4,3,2,1,0:T(8,128)S(1)}, f32[1,2,4,16,128]{4,3,2,1,0:T(8,128)S(1)}, u32[]{:S(2)}, u32[]{:S(2)}) collective-permute-start(f32[1,2,4,16,128]{4,3,2,1,0:T(8,128)S(1)} %pad_maximum_fusion.1.refs_0_), channel_id=1, source_target_pairs={{0,4},{4,0},{8,12},{12,8},{16,20},{20,16},{24,28},{28,24},{1,5},{5... | collective-permute-start | bytes 196616 | tf_op jit(solution)/shard_map/ppermute | solution.py:377
  35.2 1.7 %collective-permute-done.14.refs_3_ = f32[1,2,4,16,128]{4,3,2,1,0:T(8,128)S(1)} collective-permute-done((f32[1,2,4,16,128]{4,3,2,1,0:T(8,128)S(1)}, f32[1,2,4,16,128]{4,3,2,1,0:T(8,128)S(1)}, u32[]{:S(2)}, u32[]{:S(2)}) %collective-permute-start.14) | collective-permute-done | bytes 65568 | tf_op jit(solution)/shard_map/ppermute | solution.py:377
  36.8 1.3 %collective-permute-done.13.refs_2_ = f32[1,2,4,16,128]{4,3,2,1,0:T(8,128)S(1)} collective-permute-done((f32[1,2,4,16,128]{4,3,2,1,0:T(8,128)S(1)}, f32[1,2,4,16,128]{4,3,2,1,0:T(8,128)S(1)}, u32[]{:S(2)}, u32[]{:S(2)}) %collective-permute-start.13) | collective-permute-done | bytes 65568 | tf_op jit(solution)/shard_map/ppermute | solution.py:377
  38.1 0.8 %collective-permute-done.12.refs_1_ = f32[1,2,4,16,128]{4,3,2,1,0:T(8,128)S(1)} collective-permute-done((f32[1,2,4,16,128]{4,3,2,1,0:T(8,128)S(1)}, f32[1,2,4,16,128]{4,3,2,1,0:T(8,128)S(1)}, u32[]{:S(2)}, u32[]{:S(2)}) %collective-permute-start.12) | collective-permute-done | bytes 65568 | tf_op jit(solution)/shard_map/ppermute | solution.py:377
  38.9 0.1 shard_map.78
  39.0 0.1 collective-permute-start.15
  39.1 1.6 %collective-permute-start.16 = (f32[8,16,128]{2,1,0:T(8,128)S(1)}, f32[8,16,128]{2,1,0:T(8,128)S(1)}, u32[]{:S(2)}, u32[]{:S(2)}) collective-permute-start(f32[8,16,128]{2,1,0:T(8,128)S(1)} %get-tuple-element.37), channel_id=1, source_target_pairs={{0,1},{1,0},{2,3},{3,2},{4,5},{5,4},{6,7},{7,6},{8,9},{9,8},{10,11... | collective-permute-start | bytes 196616 | tf_op jit(solution)/shard_map/ppermute | solution.py:377
  40.7 1.2 %shard_map.79 = (f32[4,8,16,128]{3,2,1,0:T(8,128)S(1)}, f32[4,16,1024]{2,1,0:T(8,128)}) custom-call(f32[4,8,16,128]{3,2,1,0:T(8,128)S(1)} %get-tuple-element.30.refs_4_.refs_0_, f32[4,8,16,128]{3,2,1,0:T(8,128)S(1)} %get-tuple-element.31.refs_5_.refs_1_, f32[4,8,16,128]{3,2,1,0:T(8,128)S(1)} %get-tuple-element.33.refs_2_, ...), custom_call_target="tpu_custom_call" | custom-call | flops 262144000 | bytes 1048576 | tf_op jit(solution)/shard_map/pallas_call | solution.py:364
  42.0 1.5 %collective-permute-done.15.refs_1_ = f32[8,16,128]{2,1,0:T(8,128)S(1)} collective-permute-done((f32[8,16,128]{2,1,0:T(8,128)S(1)}, f32[8,16,128]{2,1,0:T(8,128)S(1)}, u32[]{:S(2)}, u32[]{:S(2)}) %collective-permute-start.15) | collective-permute-done | bytes 65568 | tf_op jit(solution)/shard_map/ppermute | solution.py:500
  43.4 0.0 collective-permute-done.16.refs_2_
  43.4 0.9 %shard_map.80 = (f32[1,2,16,1024]{3,2,1,0:T(8,128)}, f32[1,2,16,1024]{3,2,1,0:T(8,128)}) custom-call(f32[4,8,16,128]{3,2,1,0:T(8,128)S(1)} %get-tuple-element.35.refs_0_, f32[8,16,128]{2,1,0:T(8,128)S(1)} %collective-permute-done.15.refs_1_, f32[8,16,128]{2,1,0:T(8,128)S(1)} %collective-permute-done.16.refs_2_), custom_call_target="tpu_custom_call" | custom-call | flops 131072000 | bytes 524288 | tf_op jit(solution)/shard_map/pallas_call | solution.py:364
  (6 shorter events, 0.1 us)
Async XLA Ops:
  0.6 3.4 %copy-start.1 = (f32[1,2,16,1024]{3,2,1,0:T(8,128)S(1)}, f32[1,2,16,1024]{3,2,1,0:T(8,128)}, u32[]{:S(2)}) copy-start(f32[1,2,16,1024]{3,2,1,0:T(8,128)} %param.5) | copy-start | bytes 393220
  0.6 3.5 %copy-start.2 = (f32[1,2,16,1024]{3,2,1,0:T(8,128)S(1)}, f32[1,2,16,1024]{3,2,1,0:T(8,128)}, u32[]{:S(2)}) copy-start(f32[1,2,16,1024]{3,2,1,0:T(8,128)} %param.6) | copy-start | bytes 393220
  1.6 11.6 %copy-start = (bf16[1024,256]{1,0:T(8,128)(2,1)S(1)}, bf16[1024,256]{1,0:T(8,128)(2,1)}, u32[]{:S(2)}) copy-start(bf16[1024,256]{1,0:T(8,128)(2,1)} %constant.55.clone.refs_10_.refs_7_.refs_4_) | copy-start | bytes 1572868
  1.6 5.7 %collective-permute-start.2 = (f32[3,8,1024]{2,1,0:T(8,128)S(1)}, f32[3,8,1024]{2,1,0:T(8,128)S(1)}, u32[]{:S(2)}, u32[]{:S(2)}) collective-permute-start(f32[3,8,1024]{2,1,0:T(8,128)S(1)} %fusion.1), channel_id=1, source_target_pairs={{0,3},{1,2},{2,1},{3,0},{4,7},{5,6},{6,5},{7,4},{8,11},{9,10},{10,... | collective-permute-start | bytes 294920 | tf_op jit(solution)/shard_map/ppermute | solution.py:399
  4.1 6.6 %collective-permute-start = (f32[2,16,1024]{2,1,0:T(8,128)S(1)}, f32[2,16,1024]{2,1,0:T(8,128)S(1)}, u32[]{:S(2)}, u32[]{:S(2)}) collective-permute-start(f32[2,16,1024]{2,1,0:T(8,128)S(1)} %bitcast.3), channel_id=1, source_target_pairs={{0,3},{1,2},{2,1},{3,0},{4,7},{5,6},{6,5},{7,4},{8,11},{9,10},{10,... | collective-permute-start | bytes 393224 | tf_op jit(solution)/shard_map/ppermute | solution.py:400
  4.2 8.7 %collective-permute-start.1 = (f32[2,16,1024]{2,1,0:T(8,128)S(1)}, f32[2,16,1024]{2,1,0:T(8,128)S(1)}, u32[]{:S(2)}, u32[]{:S(2)}) collective-permute-start(f32[2,16,1024]{2,1,0:T(8,128)S(1)} %bitcast.6), channel_id=1, source_target_pairs={{0,3},{1,2},{2,1},{3,0},{4,7},{5,6},{6,5},{7,4},{8,11},{9,10},{10,... | collective-permute-start | bytes 393224 | tf_op jit(solution)/shard_map/ppermute | solution.py:400
  5.8 7.3 %collective-permute-start.5 = (f32[2,16,1024]{2,1,0:T(8,128)S(1)}, f32[2,16,1024]{2,1,0:T(8,128)S(1)}, u32[]{:S(2)}, u32[]{:S(2)}) collective-permute-start(f32[2,16,1024]{2,1,0:T(8,128)S(1)} %bitcast.4), channel_id=1, source_target_pairs={{0,1},{1,0},{2,3},{3,2},{4,5},{5,4},{6,7},{7,6},{8,9},{9,8},{10,11... | collective-permute-start | bytes 393224 | tf_op jit(solution)/shard_map/ppermute | solution.py:377
  6.5 6.6 %collective-permute-start.6 = (f32[2,16,1024]{2,1,0:T(8,128)S(1)}, f32[2,16,1024]{2,1,0:T(8,128)S(1)}, u32[]{:S(2)}, u32[]{:S(2)}) collective-permute-start(f32[2,16,1024]{2,1,0:T(8,128)S(1)} %bitcast.7), channel_id=1, source_target_pairs={{0,1},{1,0},{2,3},{3,2},{4,5},{5,4},{6,7},{7,6},{8,9},{9,8},{10,11... | collective-permute-start | bytes 393224 | tf_op jit(solution)/shard_map/ppermute | solution.py:377
  7.3 5.6 %collective-permute-start.3 = (f32[3,8,1024]{2,1,0:T(8,128)S(1)}, f32[3,8,1024]{2,1,0:T(8,128)S(1)}, u32[]{:S(2)}, u32[]{:S(2)}) collective-permute-start(f32[3,8,1024]{2,1,0:T(8,128)S(1)} %collective-permute-done.2.refs_6_), channel_id=1, source_target_pairs={{0,4},{4,0},{8,12},{12,8},{16,20},{20,16},{24,28},{28,24},{1,5},{5... | collective-permute-start | bytes 294920 | tf_op jit(solution)/shard_map/ppermute | solution.py:377
  10.7 2.5 %collective-permute-start.7 = (f32[3,16,1024]{2,1,0:T(8,128)S(1)}, f32[3,16,1024]{2,1,0:T(8,128)S(1)}, u32[]{:S(2)}, u32[]{:S(2)}) collective-permute-start(f32[3,16,1024]{2,1,0:T(8,128)S(1)} %pad_maximum_fusion.refs_2_), channel_id=1, source_target_pairs={{0,1},{1,0},{2,3},{3,2},{4,5},{5,4},{6,7},{7,6},{8,9},{9,8},{10,11... | collective-permute-start | bytes 589832 | tf_op jit(solution)/shard_map/ppermute | solution.py:377
  12.9 1.7 %collective-permute-start.4 = (f32[4,8,1024]{2,1,0:T(8,128)S(1)}, f32[4,8,1024]{2,1,0:T(8,128)S(1)}, u32[]{:S(2)}, u32[]{:S(2)}) collective-permute-start(f32[4,8,1024]{2,1,0:T(8,128)S(1)} %maximum_maximum_fusion), channel_id=1, source_target_pairs={{0,1},{1,0},{2,3},{3,2},{4,5},{5,4},{6,7},{7,6},{8,9},{9,8},{10,11... | collective-permute-start | bytes 393224 | tf_op jit(solution)/shard_map/ppermute | solution.py:377
  17.9 5.9 %collective-permute-start.8 = (f32[1,2,4,16,128]{4,3,2,1,0:T(8,128)S(1)}, f32[1,2,4,16,128]{4,3,2,1,0:T(8,128)S(1)}, u32[]{:S(2)}, u32[]{:S(2)}) collective-permute-start(f32[1,2,4,16,128]{4,3,2,1,0:T(8,128)S(1)} %get-tuple-element.41), channel_id=1, source_target_pairs={{0,4},{4,0},{8,12},{12,8},{16,20},{20,16},{24,28},{28,24},{1,5},{5... | collective-permute-start | bytes 196616 | tf_op jit(solution)/shard_map/ppermute | solution.py:377
  20.5 5.4 %collective-permute-start.10 = (f32[1,2,4,16,128]{4,3,2,1,0:T(8,128)S(1)}, f32[1,2,4,16,128]{4,3,2,1,0:T(8,128)S(1)}, u32[]{:S(2)}, u32[]{:S(2)}) collective-permute-start(f32[1,2,4,16,128]{4,3,2,1,0:T(8,128)S(1)} %get-tuple-element.42), channel_id=1, source_target_pairs={{0,12},{4,8},{8,4},{12,0},{16,28},{20,24},{24,20},{28,16},{1,13},{... | collective-permute-start | bytes 196616 | tf_op jit(solution)/shard_map/ppermute | solution.py:377
  22.0 4.3 %collective-permute-start.9 = (f32[1,2,4,16,128]{4,3,2,1,0:T(8,128)S(1)}, f32[1,2,4,16,128]{4,3,2,1,0:T(8,128)S(1)}, u32[]{:S(2)}, u32[]{:S(2)}) collective-permute-start(f32[1,2,4,16,128]{4,3,2,1,0:T(8,128)S(1)} %get-tuple-element.43), channel_id=1, source_target_pairs={{0,8},{4,12},{8,0},{12,4},{16,24},{20,28},{24,16},{28,20},{1,9},{5... | collective-permute-start | bytes 196616 | tf_op jit(solution)/shard_map/ppermute | solution.py:377
  26.3 5.2 %collective-permute-start.11 = (f32[1,2,4,16,128]{4,3,2,1,0:T(8,128)S(1)}, f32[1,2,4,16,128]{4,3,2,1,0:T(8,128)S(1)}, u32[]{:S(2)}, u32[]{:S(2)}) collective-permute-start(f32[1,2,4,16,128]{4,3,2,1,0:T(8,128)S(1)} %add_add_fusion), channel_id=1, source_target_pairs={{0,16},{4,20},{8,24},{12,28},{16,0},{20,4},{24,8},{28,12},{1,17},{... | collective-permute-start | bytes 196616 | tf_op jit(solution)/shard_map/ppermute | solution.py:377
  31.6 5.2 %collective-permute-start.14 = (f32[1,2,4,16,128]{4,3,2,1,0:T(8,128)S(1)}, f32[1,2,4,16,128]{4,3,2,1,0:T(8,128)S(1)}, u32[]{:S(2)}, u32[]{:S(2)}) collective-permute-start(f32[1,2,4,16,128]{4,3,2,1,0:T(8,128)S(1)} %pad_maximum_fusion.1.refs_0_), channel_id=1, source_target_pairs={{0,12},{4,8},{8,4},{12,0},{16,28},{20,24},{24,20},{28,16},{1,13},{... | collective-permute-start | bytes 196616 | tf_op jit(solution)/shard_map/ppermute | solution.py:377
  33.9 4.3 %collective-permute-start.13 = (f32[1,2,4,16,128]{4,3,2,1,0:T(8,128)S(1)}, f32[1,2,4,16,128]{4,3,2,1,0:T(8,128)S(1)}, u32[]{:S(2)}, u32[]{:S(2)}) collective-permute-start(f32[1,2,4,16,128]{4,3,2,1,0:T(8,128)S(1)} %pad_maximum_fusion.1.refs_0_), channel_id=1, source_target_pairs={{0,8},{4,12},{8,0},{12,4},{16,24},{20,28},{24,16},{28,20},{1,9},{5... | collective-permute-start | bytes 196616 | tf_op jit(solution)/shard_map/ppermute | solution.py:377
  34.7 4.3 %collective-permute-start.12 = (f32[1,2,4,16,128]{4,3,2,1,0:T(8,128)S(1)}, f32[1,2,4,16,128]{4,3,2,1,0:T(8,128)S(1)}, u32[]{:S(2)}, u32[]{:S(2)}) collective-permute-start(f32[1,2,4,16,128]{4,3,2,1,0:T(8,128)S(1)} %pad_maximum_fusion.1.refs_0_), channel_id=1, source_target_pairs={{0,4},{4,0},{8,12},{12,8},{16,20},{20,16},{24,28},{28,24},{1,5},{5... | collective-permute-start | bytes 196616 | tf_op jit(solution)/shard_map/ppermute | solution.py:377
  39.0 4.4 %collective-permute-start.15 = (f32[8,16,128]{2,1,0:T(8,128)S(1)}, f32[8,16,128]{2,1,0:T(8,128)S(1)}, u32[]{:S(2)}, u32[]{:S(2)}) collective-permute-start(f32[8,16,128]{2,1,0:T(8,128)S(1)} %get-tuple-element.36), channel_id=1, source_target_pairs={{0,3},{1,2},{2,1},{3,0},{4,7},{5,6},{6,5},{7,4},{8,11},{9,10},{10,... | collective-permute-start | bytes 196616 | tf_op jit(solution)/shard_map/ppermute | solution.py:500
  39.1 4.3 %collective-permute-start.16 = (f32[8,16,128]{2,1,0:T(8,128)S(1)}, f32[8,16,128]{2,1,0:T(8,128)S(1)}, u32[]{:S(2)}, u32[]{:S(2)}) collective-permute-start(f32[8,16,128]{2,1,0:T(8,128)S(1)} %get-tuple-element.37), channel_id=1, source_target_pairs={{0,1},{1,0},{2,3},{3,2},{4,5},{5,4},{6,7},{7,6},{8,9},{9,8},{10,11... | collective-permute-start | bytes 196616 | tf_op jit(solution)/shard_map/ppermute | solution.py:377

commit v5 on v4

--- a/solution.py
+++ b/solution.py
@@ -61,30 +61,17 @@
         lo_ref[big, c, pl.ds(row, count), part * LANES : (part + 1) * LANES] = low
 
 
-GROUP = 2
-
-
-def in_plane(group, rows, w_ref, hi_ref, lo_ref, xy_ref):
-    span = slice(group * GROUP, (group + 1) * GROUP)
-    high = hi_ref[span, :, :rows, :].reshape(GROUP * 4 * rows, WINDOW)
-    low = lo_ref[span, :, :rows, :].reshape(GROUP * 4 * rows, WINDOW)
+def in_plane(first, number, rows, w_ref, hi_ref, lo_ref, xy_ref):
+    span = slice(first, first + number)
+    high = hi_ref[span, :, :rows, :].reshape(number * 4 * rows, WINDOW)
+    low = lo_ref[span, :, :rows, :].reshape(number * 4 * rows, WINDOW)
     total = jnp.dot(
         jnp.concatenate([high, low], axis=1), w_ref[...], preferred_element_type=jnp.float32
     )
     for half in range(2):
         xy_ref[span, :, half, :rows, :] = total[:, half * LANES : (half + 1) * LANES].reshape(
-            GROUP, 4, rows, LANES
-        )
-
-
-def in_plane_steps(rows, w_ref, hi_ref, lo_ref, xy_ref):
-    groups = 4 // GROUP
-    in_plane(0, rows, w_ref, hi_ref, lo_ref, xy_ref)
-    for group in range(groups):
-        if group + 1 < groups:
-            in_plane(group + 1, rows, w_ref, hi_ref, lo_ref, xy_ref)
-        for j in range(group * GROUP * 2, (group + 1) * GROUP * 2):
-            yield j
+            number, 4, rows, LANES
+        )
 
 
 def neighbours(ref, xy, c, j, start, xy_start, count):
@@ -110,15 +97,28 @@
     return [(r, min(size, rows - r)) for r in range(0, rows, size)]
 
 
-def laplace_rows(src, start, xy_start, rows, planes, refs, store):
-    w_ref, hi, lo, xy = refs
-    tall = up16(rows + 2 * xy_start)
-    margin = (planes + 32 - rows) // 2
-    for j in in_plane_steps(tall, w_ref, hi, lo, xy):
-        for r, count in chunks(rows):
-            f = [src[c, j, pl.ds(start + r, count), :] for c in range(4)]
-            near = [neighbours(src, xy, c, j, start + r, xy_start + r, count) for c in range(4)]
-            store(j, r, count, margin + r, f, near)
+def pipeline(steps, planes, w_ref, xys):
+    def product(s, big):
+        _, _, xy_start, rows, hi, lo, _ = steps[s]
+        in_plane(big % 4, 1, up16(rows + 2 * xy_start), w_ref, hi, lo, xys[s % 2])
+
+    product(0, 0)
+    for s, (src, start, xy_start, rows, hi, lo, store) in enumerate(steps):
+        margin = (planes + 32 - rows) // 2
+        for i in range(8):
+            if s == 0 and i in (0, 2, 4):
+                product(0, i // 2 + 1)
+            j = (2 * s + i) % 8
+            for r, count in chunks(rows):
+                f = [src[c, j, pl.ds(start + r, count), :] for c in range(4)]
+                near = [
+                    neighbours(src, xys[s % 2], c, j, start + r, xy_start + r, count)
+                    for c in range(4)
+                ]
+                store(j, r, count, margin + r, f, near)
+            if s + 1 < len(steps):
+                for ahead in {4: (1,), 6: (2,), 7: (3, 4)}.get(i, ()):
+                    product(s + 1, s + ahead)
 
 
 def derivative(pd, j, row, count, f, near):
@@ -126,85 +126,139 @@
     return slope(f, [unit_coef * near[c] + pot * f[c] for c in range(4)], pr, pi)
 
 
-def stage_store(b0, pd, dst, factor, hi, lo):
+def stage_store(b0, pd, dst, factor, hi, lo, base=None):
     def store(j, r, count, row, f, near):
+        if base is not None:
+            row = pl.multiple_of(base + r, 8)
         k = derivative(pd, j, row, count, f, near)
         for c in range(4):
             value = b0[c, j, pl.ds(row + 8, count), :] + (signs[c] * factor) * k[c]
-            dst[c, j, pl.ds(r, count), :] = value
-            put_split(value, c, j, r, hi, lo)
+            place = r if base is None else row
+            dst[c, j, pl.ds(place, count), :] = value
+            put_split(value, c, j, place, hi, lo)
 
     return store
+
+
+def place_rows(ref, channel, row, b0, pd, hi, lo, split_row):
+    for i in range(ref.shape[0]):
+        c = channel + i
+        for j in range(8):
+            value = ref[i, :, j * LANES : (j + 1) * LANES]
+            if c < 4:
+                b0[c, j, pl.ds(pl.multiple_of(row + 8, 8), ref.shape[1]), :] = value
+                put_split(value, c, j, split_row, hi, lo)
+            else:
+                value = value + centre_coef if c == 4 else value
+                pd[c - 4, j, pl.ds(row, ref.shape[1]), :] = value
+
+
+def clear_rows(b0, row):
+    for c in range(4):
+        for j in range(8):
+            b0[c, j, pl.ds(row, 8), :] = jnp.zeros((8, LANES), jnp.float32)
+
+
+def add_share(past, b1, hi, lo, row, terms):
+    scale = 0.5 * time_step * unit_coef
+    for j in range(8):
+        change = []
+        for c in range(4):
+            total = None
+            for begin, sign in terms:
+                for k in range(1, REACH + 1):
+                    value = past[c, j, pl.ds(begin + sign * k, 8), :]
+                    value = value if k == 1 else near_coef[k] * value
+                    total = value if total is None else total + value
+            change.append(scale * total)
+        for c, delta in enumerate((change[1], -change[0], -change[3], change[2])):
+            value = b1[c, j, pl.ds(row, 8), :] + delta
+            b1[c, j, pl.ds(row, 8), :] = value
+            put_split(value, c, j, row, hi, lo)
+
+
+LEAD, TAIL = (4, -1), (16, 1)
+
+
+def clear_past(past):
+    zero = jnp.zeros((8, LANES), jnp.float32)
+    for c in range(4):
+        for j in range(8):
+            past[c, j, 4:12, :] = zero
+            past[c, j, 16:24, :] = zero
 
 
 def first_kernel(pieces, planes, *refs):
     n = len(pieces)
     parts, w_ref = refs[:n], refs[n]
-    b0, pd, b1, hi_b, lo_b, hi_a, lo_a, xy = refs[n + 1 :]
+    b0, pd, b1, hi_b, lo_b, hi_a, lo_a, *xys = refs[n + 1 :]
+    clear_rows(b0, 0)
+    clear_rows(b0, planes + 40)
+    for ref, row in zip(parts, pieces):
+        place_rows(ref, 0, row, b0, pd, hi_a, lo_a, row)
+    store = stage_store(b0, pd, b1, 0.5 * time_step, hi_b, lo_b)
+    pipeline([(b0, 8, 0, planes + 32, hi_a, lo_a, store)], planes, w_ref, xys)
+
+
+def early_kernel(planes, *refs):
+    parts, w_ref = refs[:8], refs[8]
+    b0, pd, b1, hi_b, lo_b, hi_a, lo_a, *xys = refs[9:]
+    odd = lax.rem(lax.axis_index("grid"), 2)
+    base = pl.multiple_of((1 - odd) * planes, 16)
+    clear_rows(b0, base)
+    clear_rows(b0, pl.multiple_of(base + 2 * planes + 8, 8))
+    for i, ref in enumerate(parts):
+        inner = pl.multiple_of((odd if i < 4 else 1 - odd) * planes, 16)
+        channel = (0, 2, 4, 5)[i % 4]
+        place_rows(ref, channel, pl.multiple_of(base + inner, 16), b0, pd, hi_a, lo_a, inner)
+    store = stage_store(b0, pd, b1, 0.5 * time_step, hi_b, lo_b, base)
+    pipeline([(b0, base + 8, 0, 2 * planes, hi_a, lo_a, store)], planes, w_ref, xys)
+
+
+def late_kernel(planes, *refs):
+    far_u, far_v, mine, other = refs[:4]
+    w_ref = refs[9]
+    b0, pd, b1, hi_b, lo_b, hi_a, lo_a, past, *xys = refs[10:]
     odd = lax.rem(lax.axis_index("grid"), 2)
     half = lax.rem(lax.axis_index("modes"), 2)
-    zero = jnp.zeros((8, LANES), jnp.float32)
+    base = pl.multiple_of(odd * (2 * planes), 16)
+    clear_rows(b0, pl.multiple_of(odd * (3 * planes + 8), 8))
+    for ref, channel in ((far_u, 0), (far_v, 2)):
+        place_rows(ref, channel, base, b0, pd, hi_a, lo_a, 0)
+    for ref, which in ((mine, half), (other, 1 - half)):
+        row = pl.multiple_of(base + which * (planes // 2), 8)
+        place_rows(ref, 4, row, b0, pd, hi_a, lo_a, 0)
+    store = stage_store(b0, pd, b1, 0.5 * time_step, hi_b, lo_b, base)
+    pipeline([(b0, base + 8, 0, planes, hi_a, lo_a, store)], planes, w_ref, xys)
+
+    clear_past(past)
+    none = jnp.zeros((REACH, LANES), jnp.float32)
     for c in range(4):
+        ref = far_u if c < 2 else far_v
         for j in range(8):
-            b0[c, j, 0:8, :] = zero
-            b0[c, j, planes + 40 : planes + 48, :] = zero
-
-    for ref, (first, channels, count, row_even, row_odd, flip) in zip(parts, pieces):
-        row = row_even
-        if row_odd != row_even:
-            row = pl.multiple_of(row_even + odd * (row_odd - row_even), 16)
-        if flip is not None:
-            row = pl.multiple_of(row + (half if flip == 0 else 1 - half) * count, 8)
-        for i in range(channels):
-            c = first + i
-            for j in range(8):
-                value = ref[i, :, j * LANES : (j + 1) * LANES]
-                if c < 4:
-                    b0[c, j, pl.ds(row + 8, count), :] = value
-                    put_split(value, c, j, row, hi_a, lo_a)
-                else:
-                    pd[c - 4, j, pl.ds(row, count), :] = value + centre_coef if c == 4 else value
-
-    store = stage_store(b0, pd, b1, 0.5 * time_step, hi_b, lo_b)
-    laplace_rows(b0, 8, 0, planes + 32, planes, (w_ref, hi_a, lo_a, xy), store)
+            lanes = slice(j * LANES, (j + 1) * LANES)
+            ahead, behind = ref[c % 2, planes - REACH :, lanes], ref[c % 2, :REACH, lanes]
+            past[c, j, 0:REACH, :] = jnp.where(odd == 0, ahead, none)
+            past[c, j, 24 : 24 + REACH, :] = jnp.where(odd == 0, none, behind)
+    row = pl.multiple_of(planes + odd * (planes - 8), 8)
+    add_share(past, b1, hi_b, lo_b, row, (LEAD, TAIL))
 
 
 def stages_kernel(far, planes, low_bits, *refs):
     lead_ref, tail_ref, b0, pd = refs[:4]
     w_ref = refs[7]
     psi1_ref, kin1_ref, sums_ref, b1, hi_b, lo_b = refs[8:14]
-    b2, b3, b4, hi_a, lo_a, xy, past = refs[14:]
+    b2, b3, b4, hi_a, lo_a, past, *xys = refs[14:]
     quarter = lax.rem(lax.axis_index("modes"), low_bits)
 
-    zero = jnp.zeros((8, LANES), jnp.float32)
+    clear_past(past)
     for c in range(4):
         for j in range(8):
             lanes = slice(j * LANES, (j + 1) * LANES)
-            past[c, j, 4:12, :] = zero
-            past[c, j, 16:24, :] = zero
             past[c, j, 0:REACH, :] = lead_ref[c, far[0] : far[0] + REACH, lanes]
             past[c, j, 24 : 24 + REACH, :] = tail_ref[c, far[1] : far[1] + REACH, lanes]
-    scale = 0.5 * time_step * unit_coef
-    for j in range(8):
-        for row, begin, sign in ((0, 4, -1), (planes + 24, 16, 1)):
-            change = []
-            for c in range(4):
-                total = past[c, j, pl.ds(begin + sign, 8), :]
-                for k in range(2, REACH + 1):
-                    total = total + near_coef[k] * past[c, j, pl.ds(begin + sign * k, 8), :]
-                change.append(scale * total)
-            for c, delta in enumerate((change[1], -change[0], -change[3], change[2])):
-                value = b1[c, j, row : row + 8, :] + delta
-                b1[c, j, row : row + 8, :] = value
-                put_split(value, c, j, row, hi_b, lo_b)
-
-    def run(src, start, xy_start, rows, hi, lo, store):
-        laplace_rows(src, start, xy_start, rows, planes, (w_ref, hi, lo, xy), store)
-
-    store = stage_store(b0, pd, b2, 0.5 * time_step, hi_a, lo_a)
-    run(b1, 4, 4, planes + 24, hi_b, lo_b, store)
-    store = stage_store(b0, pd, b3, time_step, hi_b, lo_b)
-    run(b2, 4, 4, planes + 16, hi_a, lo_a, store)
+    add_share(past, b1, hi_b, lo_b, 0, (LEAD,))
+    add_share(past, b1, hi_b, lo_b, planes + 24, (TAIL,))
 
     def last(j, r, count, row, f, near):
         k = derivative(pd, j, row, count, f, near)
@@ -219,8 +273,6 @@
             b4[c, j, pl.ds(r, count), :] = value
             put_split(value, c, j, r, hi_a, lo_a)
 
-    run(b3, 4, 4, planes + 8, hi_b, lo_b, last)
-
     def finish(j, r, count, row, f, near):
         full = [unit_coef * near[c] + centre_coef * f[c] for c in range(4)]
         for c in range(4):
@@ -236,7 +288,15 @@
         for s in range(4):
             sums_ref[place, j % 2, s, pl.ds(r, count), :] = sums[s]
 
-    run(b4, 4, 4, planes, hi_a, lo_a, finish)
+    second = stage_store(b0, pd, b2, 0.5 * time_step, hi_a, lo_a)
+    third = stage_store(b0, pd, b3, time_step, hi_b, lo_b)
+    steps = [
+        (b1, 4, 4, planes + 24, hi_b, lo_b, second),
+        (b2, 4, 4, planes + 16, hi_a, lo_a, third),
+        (b3, 4, 4, planes + 8, hi_b, lo_b, last),
+        (b4, 4, 4, planes, hi_a, lo_a, finish),
+    ]
+    pipeline(steps, planes, w_ref, xys)
 
 
 def middle_kernel(paired, planes, low_bits, *refs):
@@ -272,7 +332,6 @@
 
 def inner_kernel(planes, *refs):
     psi1, kin1, mid, fields_flat, w_ref, part_ref, fields_out, pad, hi, lo, xy = refs
-    tall = up16(planes)
     zero = jnp.zeros((8, LANES), jnp.float32)
     for j in range(8):
         for i in range(4):
@@ -285,19 +344,18 @@
             pad[c, j, 8 + planes : 16 + planes, :] = zero
             put_split(value, c, j, 0, hi, lo)
 
-    for j in in_plane_steps(tall, w_ref, hi, lo, xy):
-        for r, count in chunks(planes):
-            pot, pr, pi = [fields_flat[j // 2, j % 2, i, pl.ds(r, count), :] for i in range(3)]
-            f = [psi1[c, j, pl.ds(r, count), :] for c in range(4)]
-            q1 = slope(f, [kin1[c, j, pl.ds(r, count), :] + pot * f[c] for c in range(4)], pr, pi)
-            m = [pad[c, j, pl.ds(8 + r, count), :] for c in range(4)]
-            pot = pot + centre_coef
-            near = [neighbours(pad, xy, c, j, 8 + r, r, count) for c in range(4)]
-            q2 = slope(m, [unit_coef * near[c] + pot * m[c] for c in range(4)], pr, pi)
-            for c in range(4):
-                part_ref[c, j, pl.ds(r, count), :] = f[c] + (signs[c] * time_step / 6.0) * (
-                    q1[c] + 2.0 * q2[c]
-                )
+    def store(j, r, count, row, m, near):
+        pot, pr, pi = [fields_flat[j // 2, j % 2, i, pl.ds(r, count), :] for i in range(3)]
+        f = [psi1[c, j, pl.ds(r, count), :] for c in range(4)]
+        q1 = slope(f, [kin1[c, j, pl.ds(r, count), :] + pot * f[c] for c in range(4)], pr, pi)
+        pot = pot + centre_coef
+        q2 = slope(m, [unit_coef * near[c] + pot * m[c] for c in range(4)], pr, pi)
+        for c in range(4):
+            part_ref[c, j, pl.ds(r, count), :] = f[c] + (signs[c] * time_step / 6.0) * (
+                q1[c] + 2.0 * q2[c]
+            )
+
+    pipeline([(pad, 8, 0, planes, hi, lo, store)], planes, w_ref, [xy])
 
 
 def edge_kernel(paired, planes, *refs):
@@ -385,35 +443,38 @@
     paired = slabs == 4 and planes == 16 and low_bits == 4
     f32, bf16 = jnp.float32, jnp.bfloat16
     weights = jnp.asarray(in_plane_matrix())
-    frozen = jnp.concatenate([potential[None], pairing], axis=0)
     psi = (u_modes[0], v_modes[0])
+    tall = up16(planes + 32)
+    state = (4, 8, planes, LANES)
+    split = ((4, 4, tall, WINDOW), bf16)
+    product = ((4, 4, 2, tall, LANES), f32)
+    past = ((4, 8, 32, LANES), f32)
+    buffers = [
+        (4, 8, tall + 16, LANES),
+        (3, 8, tall, LANES),
+        (4, 8, tall + 8, LANES),
+        split,
+        split,
+    ]
 
     cross = [(i, (i - 1 if i % 2 == 0 else i + 1) % slabs) for i in range(slabs)]
     up = [(i, (i + 1) % slabs) for i in range(slabs)]
     down = [(j, i) for i, j in up]
-    pieces = [(0, 2, planes, 16, 16, None), (2, 2, planes, 16, 16, None), (4, 3, planes, 16, 16, None)]
-    arrays = [*psi, frozen]
     if paired:
         part = planes // 2
         upper = lax.rem(lax.axis_index("modes"), 2) == 1
-        mine = lax.ppermute(jnp.where(upper, frozen[:, part:], frozen[:, :part]), "grid", cross)
+        frozen = (potential[None], pairing)
+        both = jnp.concatenate(frozen, axis=0)
+        mine = lax.ppermute(
+            jnp.where(upper, both[:, part:], both[:, :part]), "grid", cross
+        )
         far_u, far_v = [lax.ppermute(x, "grid", cross) for x in psi]
-        near_u, near_v, near_f = [
-            exchange_xor(x, "grid", 1, slabs) for x in (*psi, frozen)
-        ]
+        near = [exchange_xor(x, "grid", 1, slabs) for x in (*psi, *frozen)]
         other = exchange_xor(mine, "modes", 1, modes)
+        ready = call(
+            functools.partial(early_kernel, planes), buffers, [split, split, product], [*psi, *frozen, *near, weights]
+        )
         far_u, far_v, other = lax.optimization_barrier((far_u, far_v, other))
-        lead, tail = 16 - planes, 16 + planes
-        pieces += [
-            (0, 2, planes, tail, lead, None),
-            (2, 2, planes, tail, lead, None),
-            (4, 3, planes, tail, lead, None),
-            (4, 3, part, lead, tail, 0),
-            (4, 3, part, lead, tail, 1),
-            (0, 2, planes, lead, tail, None),
-            (2, 2, planes, lead, tail, None),
-        ]
-        arrays += [near_u, near_v, near_f, mine, other, far_u, far_v]
         both = jnp.concatenate(
             [
                 jnp.concatenate([x[:, :REACH], x[:, planes - REACH :]], axis=1)
@@ -423,8 +484,16 @@
         )
         lead_far = tail_far = exchange_xor(both, "grid", 1, slabs)
         far = (REACH, 0)
+        b0, pd, b1, hi, lo = call(
+            functools.partial(late_kernel, planes),
+            buffers,
+            [split, split, past, product],
+            [far_u, far_v, mine, other, *ready, weights],
+            {4 + i: i for i in range(5)},
+        )
     else:
-        own = jnp.concatenate([*psi, frozen], axis=0)
+        own = jnp.concatenate([*psi, potential[None], pairing], axis=0)
+        pieces, arrays = [16], [own]
         reach, step = 0, 0
         while reach < 5 * REACH:
             step += 1
@@ -436,29 +505,16 @@
             after = lax.ppermute(
                 own[:wide, :count], "grid", [((i + step) % slabs, i) for i in range(slabs)]
             )
-            lead, tail = 16 - reach - count, 16 + planes + reach
             if wide == 7:
-                pieces += [(0, 7, count, lead, lead, None), (0, 7, count, tail, tail, None)]
+                pieces += [16 - reach - count, 16 + planes + reach]
                 arrays += [before, after]
             else:
                 lead_far, tail_far, far = before, after, (0, 0)
             reach += count
-
-    tall = up16(planes + 32)
-    state = (4, 8, planes, LANES)
-    split = ((4, 4, tall, WINDOW), bf16)
-    b0, pd, b1, hi, lo = call(
-        functools.partial(first_kernel, pieces, planes),
-        [
-            (4, 8, tall + 16, LANES),
-            (3, 8, tall, LANES),
-            (4, 8, tall + 8, LANES),
-            split,
-            split,
-        ],
-        [split, split, ((4, 4, 2, tall, LANES), f32)],
-        arrays + [weights],
-    )
+        b0, pd, b1, hi, lo = call(
+            functools.partial(first_kernel, pieces, planes), buffers, [split, split, product], arrays + [weights]
+        )
+
     inputs = [lead_far, tail_far, b0, pd, b1, hi, lo, weights]
     psi1, kin1, sums, *rest = call(
         functools.partial(stages_kernel, far, planes, low_bits),
@@ -469,8 +525,9 @@
             ((4, 8, tall + 8, LANES), f32),
             split,
             split,
-            ((4, 4, 2, tall, LANES), f32),
-            ((4, 8, 32, LANES), f32),
+            past,
+            product,
+            product,
         ],
         inputs,
         {4: 3, 5: 4, 6: 5},
@@ -515,10 +572,7 @@
         [psi1, kin1, mid, fields_flat, weights],
     )
     u_next, v_next = call(
-        functools.partial(edge_kernel, paired, planes),
-        [u_modes.shape, v_modes.shape],
-        [],
-        [part, first, second],
+        functools.partial(edge_kernel, paired, planes), [u_modes.shape, v_modes.shape], [], [part, first, second]
     )
     return u_next, v_next, fields
 

time: 44.4 us -> 45.6 us (1.027)
  local copies, waits for them, and re-layouts: 0.06 us -> 3.75 us
  starting transfers between devices: 19.7 us -> 17.3 us
  other arithmetic: 2.01 us -> 1.08 us
  waiting for transfers between devices: 14.8 us -> 15.3 us
    unnamed x6 -> x12, local copies, waits for them, and re-layouts: 0.02 us -> 3.71 us
    ppermute x13 -> x14, starting transfers between devices: 15.4 us -> 12.3 us  [exchange_xor(): return lax.ppermute(x, axis, [(i, i ^ bits) for i in range(count)])]
    ppermute x2, waiting for transfers between devices: 2.04 us -> 0.01 us  [local(): far_u, far_v = [lax.ppermute(x, 'grid', cross) for x in psi]]
    ppermute x13 -> x14, waiting for transfers between devices: 10.6 us -> 11.6 us  [exchange_xor(): return lax.ppermute(x, axis, [(i, i ^ bits) for i in range(count)])]
    ppermute x1, waiting for transfers between devices: 0.75 us -> 1.75 us  [local(): lax.ppermute(jnp.where(upper, both[:, part:], both[:, :part]), 'grid', cr...]
    concatenate x1 -> x0, other arithmetic: 0.96 us -> none  [local(): frozen = jnp.concatenate([potential[None], pairing], axis=0)]
    ppermute x2, starting transfers between devices: 1.75 us -> 2.25 us  [local(): far_u, far_v = [lax.ppermute(x, 'grid', cross) for x in psi]]
    pallas_call x5 -> x6, Pallas kernels: 6.94 us -> 7.14 us  [call(): pl.pallas_call(kernel, out_shape=tuple((jax.ShapeDtypeStruct(s, d) for s,...]
  transfers between devices with their start and end apart: 17 -> 18, of which waited for: 10 -> 10; matrix products, arithmetic and copies ran while one was open for 2% -> 2% of each run, Pallas kernels for 6% -> 7%
where the time goes in v5:
time: 45.6 us; the launch traced here: 45.3 us
  starting transfers between devices  17.3 us (38%)
  waiting for transfers between devices  15.3 us (34%)
  Pallas kernels  7.14 us (16%)
  local copies, waits for them, and re-layouts  3.75 us (8%)
  other arithmetic  1.08 us (2%)
  between operations  0.78 us (2%)
    ppermute x14, starting transfers between devices, exchange_xor(): return lax.ppermute(x, axis, [(i, i ^ bits) for i in range(count)])  12.3 us
    ppermute x14, waiting for transfers between devices, exchange_xor(): return lax.ppermute(x, axis, [(i, i ^ bits) for i in range(count)])  11.6 us
    pallas_call x6, Pallas kernels, call(): pl.pallas_call(kernel, out_shape=tuple((jax.ShapeDtypeStruct(s, d) for s,...  7.14 us
    unnamed x12, local copies, waits for them, and re-layouts  3.71 us
    ppermute x1, starting transfers between devices, local(): lax.ppermute(jnp.where(upper, both[:, part:], both[:, :part]), 'grid', cr...  2.65 us
    ppermute x2, starting transfers between devices, local(): far_u, far_v = [lax.ppermute(x, 'grid', cross) for x in psi]  2.25 us
    ppermute x1, waiting for transfers between devices, local(): first = lax.ppermute(first, 'grid', cross)  1.88 us
    ppermute x1, waiting for transfers between devices, local(): lax.ppermute(jnp.where(upper, both[:, part:], both[:, :part]), 'grid', cr...  1.75 us
  transfers between devices with their start and end apart: 18, of which 10 were waited for; matrix products, arithmetic and copies ran while one was open for 2% of the time, Pallas kernels for 7%

profile of v5, /device:TPU:0, one launch (start us, length us, event | category | flops | bytes accessed | tf_op | source)
XLA Modules:
  0.0 45.3 jit_solution(15085673710231152955)
XLA Ops:
  0.6 0.6 %collective-permute-start.5 = (f32[2,16,1024]{2,1,0:T(8,128)}, f32[2,16,1024]{2,1,0:T(8,128)S(1)}, u32[]{:S(2)}, u32[]{:S(2)}) collective-permute-start(f32[2,16,1024]{2,1,0:T(8,128)} %bitcast.6), channel_id=1, source_target_pairs={{0,1},{1,0},{2,3},{3,2},{4,5},{5,4},{6,7},{7,6},{8,9},{9,8},{10,11... | collective-permute-start | bytes 393224 | tf_op jit(solution)/shard_map/ppermute | solution.py:435
  1.2 0.1 collective-permute-start.6
  1.3 0.4 collective-permute-start.8
  1.7 0.0 copy-start.3
  1.7 0.0 copy-start.2
  1.7 1.0 %fusion.1 = f32[3,8,1024]{2,1,0:T(8,128)S(1)} fusion(f32[1,16,1024]{2,1,0:T(8,128)} %bitcast.3, f32[2,16,1024]{2,1,0:T(8,128)} %refs_3_.1, pred[]{:T(512)S(6)} %eq.3), kind=kLoop, calls=%fused_computation.4 | loop fusion | flops 73728 | bytes 294913 | tf_op jit(solution)/shard_map/jit(_where)/select_n | solution.py:469
  2.7 2.7 %collective-permute-start.2 = (f32[3,8,1024]{2,1,0:T(8,128)S(1)}, f32[3,8,1024]{2,1,0:T(8,128)S(1)}, u32[]{:S(2)}, u32[]{:S(2)}) collective-permute-start(f32[3,8,1024]{2,1,0:T(8,128)S(1)} %fusion.1), channel_id=1, source_target_pairs={{0,3},{1,2},{2,1},{3,0},{4,7},{5,6},{6,5},{7,4},{8,11},{9,10},{10,... | collective-permute-start | bytes 294920 | tf_op jit(solution)/shard_map/ppermute | solution.py:468
  5.3 0.0 copy-done.3
  5.3 0.1 collective-permute-start.7
  5.4 1.2 %collective-permute-done.7.refs_6_ = f32[1,16,1024]{2,1,0:T(8,128)S(1)} collective-permute-done((f32[1,16,1024]{2,1,0:T(8,128)S(1)}, f32[1,16,1024]{2,1,0:T(8,128)S(1)}, u32[]{:S(2)}, u32[]{:S(2)}) %collective-permute-start.7) | collective-permute-done | bytes 65568 | tf_op jit(solution)/shard_map/ppermute | solution.py:435
  6.6 0.1 collective-permute-start
  6.7 1.7 %collective-permute-done.2.refs_2_ = f32[3,8,1024]{2,1,0:T(8,128)S(1)} collective-permute-done((f32[3,8,1024]{2,1,0:T(8,128)S(1)}, f32[3,8,1024]{2,1,0:T(8,128)S(1)}, u32[]{:S(2)}, u32[]{:S(2)}) %collective-permute-start.2) | collective-permute-done | bytes 98336 | tf_op jit(solution)/shard_map/ppermute | solution.py:468
  8.4 2.2 %collective-permute-start.1 = (f32[2,16,1024]{2,1,0:T(8,128)}, f32[2,16,1024]{2,1,0:T(8,128)S(1)}, u32[]{:S(2)}, u32[]{:S(2)}) collective-permute-start(f32[2,16,1024]{2,1,0:T(8,128)} %bitcast.10), channel_id=1, source_target_pairs={{0,3},{1,2},{2,1},{3,0},{4,7},{5,6},{6,5},{7,4},{8,11},{9,10},{10,... | collective-permute-start | bytes 393224 | tf_op jit(solution)/shard_map/ppermute | solution.py:471
  10.6 0.0 collective-permute-done.5.refs_4_
  10.6 1.1 %collective-permute-start.3 = (f32[3,8,1024]{2,1,0:T(8,128)S(1)}, f32[3,8,1024]{2,1,0:T(8,128)S(1)}, u32[]{:S(2)}, u32[]{:S(2)}) collective-permute-start(f32[3,8,1024]{2,1,0:T(8,128)S(1)} %collective-permute-done.2.refs_2_), channel_id=1, source_target_pairs={{0,4},{4,0},{8,12},{12,8},{16,20},{20,16},{24,28},{28,24},{1,5},{5... | collective-permute-start | bytes 294920 | tf_op jit(solution)/shard_map/ppermute | solution.py:435
  11.7 0.0 collective-permute-done.6.refs_5_
  11.7 0.0 collective-permute-done.8.refs_7_
  11.7 0.0 copy-done.2
  11.7 0.0 copy-start
  11.7 1.0 %copy-done = bf16[1024,256]{1,0:T(8,128)(2,1)S(1)} copy-done((bf16[1024,256]{1,0:T(8,128)(2,1)S(1)}, bf16[1024,256]{1,0:T(8,128)(2,1)}, u32[]{:S(2)}) %copy-start) | copy-done | bytes 524312
  12.7 0.0 copy-start.4
  12.7 0.9 %copy-done.4 = f32[1,2,16,1024]{3,2,1,0:T(8,128)S(1)} copy-done((f32[1,2,16,1024]{3,2,1,0:T(8,128)S(1)}, f32[1,2,16,1024]{3,2,1,0:T(8,128)}, u32[]{:S(2)}) %copy-start.4) | copy-done | bytes 131096
  13.7 0.0 copy-start.5
  13.7 0.9 %copy-done.5 = f32[1,2,16,1024]{3,2,1,0:T(8,128)S(1)} copy-done((f32[1,2,16,1024]{3,2,1,0:T(8,128)S(1)}, f32[1,2,16,1024]{3,2,1,0:T(8,128)}, u32[]{:S(2)}) %copy-start.5) | copy-done | bytes 131096
  14.6 1.0 %shard_map.76 = (f32[4,8,64,128]{3,2,1,0:T(8,128)S(1)}, f32[3,8,48,128]{3,2,1,0:T(8,128)S(1)}, f32[4,8,56,128]{3,2,1,0:T(8,128)S(1)}, bf16[4,4,48,512]{3,2,1,0:T(8,128)(2,1)S(1)}, bf16[4,4,48,512]{3,2,1,0:T(8,128)(2,1)S(1)}) custom-call(f32[2,16,1024]{2,1,0:T(8,128)S(1)} %bitcast.8, f32[2,16,1024]{2,1,0:T(8,128)S(1)} %bitcast.11, ...), custom_call_target="tpu_custom_call" | custom-call | flops 2850816000 | bytes 11403264 | tf_op jit(solution)/shard_map/pallas_call | solution.py:422
  15.6 0.0 copy-start.1
  15.6 0.0 collective-permute-done.refs_0_
  15.6 0.0 collective-permute-done.1.refs_1_
  15.6 0.0 collective-permute-done.3.refs_3_
  15.7 0.1 collective-permute-start.4
  15.8 0.8 %copy-done.1 = bf16[1024,256]{1,0:T(8,128)(2,1)S(1)} copy-done((bf16[1024,256]{1,0:T(8,128)(2,1)S(1)}, bf16[1024,256]{1,0:T(8,128)(2,1)}, u32[]{:S(2)}) %copy-start.1) | copy-done | bytes 524312
  16.6 0.8 %shard_map.77 = (f32[4,8,64,128]{3,2,1,0:T(8,128)S(1)}, f32[3,8,48,128]{3,2,1,0:T(8,128)S(1)}, f32[4,8,56,128]{3,2,1,0:T(8,128)S(1)}, bf16[4,4,48,512]{3,2,1,0:T(8,128)(2,1)S(1)}, bf16[4,4,48,512]{3,2,1,0:T(8,128)(2,1)S(1)}) custom-call(f32[2,16,1024]{2,1,0:T(8,128)S(1)} %collective-permute-d, ...), custom_call_target="tpu_custom_call", output_to_operand_aliasing={{0}: (4, {}), {1}: (5, {}), {2}: (6, {}), {3}: (7, {}), {4}... | custom-call | flops 2850816000 | bytes 11403264 | tf_op jit(solution)/shard_map/pallas_call | solution.py:422
  17.5 0.0 collective-permute-done.4.refs_0_.refs_1_
  17.5 3.0 %shard_map.78 = (f32[4,8,16,128]{3,2,1,0:T(8,128)S(1)}, f32[4,8,16,128]{3,2,1,0:T(8,128)S(1)}, f32[4,2,4,16,128]{4,3,2,1,0:T(8,128)S(1)}, f32[4,8,56,128]{3,2,1,...) custom-call(f32[4,8,1024]{2,1,0:T(8,128)S(1)} %collective-permute-do, ...), custom_call_target="tpu_custom_call", output_to_operand_aliasing={{3}: (4, {}), {4}: (5, {}), {5}: (6, {})} | custom-call | flops 2424832000 | bytes 9699328 | tf_op jit(solution)/shard_map/pallas_call | solution.py:422
  20.5 1.6 %collective-permute-start.10 = (f32[1,2,4,16,128]{4,3,2,1,0:T(8,128)S(1)}, f32[1,2,4,16,128]{4,3,2,1,0:T(8,128)S(1)}, u32[]{:S(2)}, u32[]{:S(2)}) collective-permute-start(f32[1,2,4,16,128]{4,3,2,1,0:T(8,128)S(1)} %get-tuple-element.53), channel_id=1, source_target_pairs={{0,8},{4,12},{8,0},{12,4},{16,24},{20,28},{24,16},{28,20},{1,9},{5... | collective-permute-start | bytes 196616 | tf_op jit(solution)/shard_map/ppermute | solution.py:435
  22.1 0.8 %collective-permute-start.11 = (f32[1,2,4,16,128]{4,3,2,1,0:T(8,128)S(1)}, f32[1,2,4,16,128]{4,3,2,1,0:T(8,128)S(1)}, u32[]{:S(2)}, u32[]{:S(2)}) collective-permute-start(f32[1,2,4,16,128]{4,3,2,1,0:T(8,128)S(1)} %get-tuple-element.52), channel_id=1, source_target_pairs={{0,12},{4,8},{8,4},{12,0},{16,28},{20,24},{24,20},{28,16},{1,13},{... | collective-permute-start | bytes 196616 | tf_op jit(solution)/shard_map/ppermute | solution.py:435
  22.9 1.1 %collective-permute-start.9 = (f32[1,2,4,16,128]{4,3,2,1,0:T(8,128)S(1)}, f32[1,2,4,16,128]{4,3,2,1,0:T(8,128)S(1)}, u32[]{:S(2)}, u32[]{:S(2)}) collective-permute-start(f32[1,2,4,16,128]{4,3,2,1,0:T(8,128)S(1)} %get-tuple-element.51), channel_id=1, source_target_pairs={{0,4},{4,0},{8,12},{12,8},{16,20},{20,16},{24,28},{28,24},{1,5},{5... | collective-permute-start | bytes 196616 | tf_op jit(solution)/shard_map/ppermute | solution.py:435
  24.1 1.0 %collective-permute-done.10 = f32[1,2,4,16,128]{4,3,2,1,0:T(8,128)S(1)} collective-permute-done((f32[1,2,4,16,128]{4,3,2,1,0:T(8,128)S(1)}, f32[1,2,4,16,128]{4,3,2,1,0:T(8,128)S(1)}, u32[]{:S(2)}, u32[]{:S(2)}) %collective-permute-start.10) | collective-permute-done | bytes 65568 | tf_op jit(solution)/shard_map/ppermute | solution.py:435
  25.0 2.4 %collective-permute-done.11 = f32[1,2,4,16,128]{4,3,2,1,0:T(8,128)S(1)} collective-permute-done((f32[1,2,4,16,128]{4,3,2,1,0:T(8,128)S(1)}, f32[1,2,4,16,128]{4,3,2,1,0:T(8,128)S(1)}, u32[]{:S(2)}, u32[]{:S(2)}) %collective-permute-start.11) | collective-permute-done | bytes 65568 | tf_op jit(solution)/shard_map/ppermute | solution.py:435
  27.4 0.5 %collective-permute-done.9 = f32[1,2,4,16,128]{4,3,2,1,0:T(8,128)S(1)} collective-permute-done((f32[1,2,4,16,128]{4,3,2,1,0:T(8,128)S(1)}, f32[1,2,4,16,128]{4,3,2,1,0:T(8,128)S(1)}, u32[]{:S(2)}, u32[]{:S(2)}) %collective-permute-start.9) | collective-permute-done | bytes 65568 | tf_op jit(solution)/shard_map/ppermute | solution.py:435
  27.9 2.4 %collective-permute-start.12 = (f32[1,2,4,16,128]{4,3,2,1,0:T(8,128)S(1)}, f32[1,2,4,16,128]{4,3,2,1,0:T(8,128)S(1)}, u32[]{:S(2)}, u32[]{:S(2)}) collective-permute-start(f32[1,2,4,16,128]{4,3,2,1,0:T(8,128)S(1)} %add_add_fusion), channel_id=1, source_target_pairs={{0,16},{4,20},{8,24},{12,28},{16,0},{20,4},{24,8},{28,12},{1,17},{... | collective-permute-start | bytes 196616 | tf_op jit(solution)/shard_map/ppermute | solution.py:435
  30.3 3.6 %collective-permute-done.12 = f32[1,2,4,16,128]{4,3,2,1,0:T(8,128)S(1)} collective-permute-done((f32[1,2,4,16,128]{4,3,2,1,0:T(8,128)S(1)}, f32[1,2,4,16,128]{4,3,2,1,0:T(8,128)S(1)}, u32[]{:S(2)}, u32[]{:S(2)}) %collective-permute-start.12) | collective-permute-done | bytes 65568 | tf_op jit(solution)/shard_map/ppermute | solution.py:435
  33.9 0.1 divide_subtract_fusion
  34.0 0.2 collective-permute-start.13
  34.1 1.3 %collective-permute-start.14 = (f32[1,2,4,16,128]{4,3,2,1,0:T(8,128)S(1)}, f32[1,2,4,16,128]{4,3,2,1,0:T(8,128)S(1)}, u32[]{:S(2)}, u32[]{:S(2)}) collective-permute-start(f32[1,2,4,16,128]{4,3,2,1,0:T(8,128)S(1)} %pad_maximum_fusion.1.refs_0_), channel_id=1, source_target_pairs={{0,8},{4,12},{8,0},{12,4},{16,24},{20,28},{24,16},{28,20},{1,9},{5... | collective-permute-start | bytes 196616 | tf_op jit(solution)/shard_map/ppermute | solution.py:435
  35.4 2.1 %collective-permute-start.15 = (f32[1,2,4,16,128]{4,3,2,1,0:T(8,128)S(1)}, f32[1,2,4,16,128]{4,3,2,1,0:T(8,128)S(1)}, u32[]{:S(2)}, u32[]{:S(2)}) collective-permute-start(f32[1,2,4,16,128]{4,3,2,1,0:T(8,128)S(1)} %pad_maximum_fusion.1.refs_0_), channel_id=1, source_target_pairs={{0,12},{4,8},{8,4},{12,0},{16,28},{20,24},{24,20},{28,16},{1,13},{... | collective-permute-start | bytes 196616 | tf_op jit(solution)/shard_map/ppermute | solution.py:435
  37.5 0.8 %collective-permute-done.13.refs_1_ = f32[1,2,4,16,128]{4,3,2,1,0:T(8,128)S(1)} collective-permute-done((f32[1,2,4,16,128]{4,3,2,1,0:T(8,128)S(1)}, f32[1,2,4,16,128]{4,3,2,1,0:T(8,128)S(1)}, u32[]{:S(2)}, u32[]{:S(2)}) %collective-permute-start.13) | collective-permute-done | bytes 65568 | tf_op jit(solution)/shard_map/ppermute | solution.py:435
  38.3 0.1 collective-permute-done.14.refs_2_
  38.4 2.2 %collective-permute-done.15.refs_3_ = f32[1,2,4,16,128]{4,3,2,1,0:T(8,128)S(1)} collective-permute-done((f32[1,2,4,16,128]{4,3,2,1,0:T(8,128)S(1)}, f32[1,2,4,16,128]{4,3,2,1,0:T(8,128)S(1)}, u32[]{:S(2)}, u32[]{:S(2)}) %collective-permute-start.15) | collective-permute-done | bytes 65568 | tf_op jit(solution)/shard_map/ppermute | solution.py:435
  40.6 0.1 shard_map.79
  40.7 0.1 collective-permute-start.16
  40.8 0.5 %collective-permute-start.17 = (f32[8,16,128]{2,1,0:T(8,128)S(1)}, f32[8,16,128]{2,1,0:T(8,128)S(1)}, u32[]{:S(2)}, u32[]{:S(2)}) collective-permute-start(f32[8,16,128]{2,1,0:T(8,128)S(1)} %get-tuple-element.47), channel_id=1, source_target_pairs={{0,1},{1,0},{2,3},{3,2},{4,5},{5,4},{6,7},{7,6},{8,9},{9,8},{10,11... | collective-permute-start | bytes 196616 | tf_op jit(solution)/shard_map/ppermute | solution.py:435
  41.2 1.3 %shard_map.80 = (f32[4,8,16,128]{3,2,1,0:T(8,128)S(1)}, f32[4,16,1024]{2,1,0:T(8,128)}) custom-call(f32[4,8,16,128]{3,2,1,0:T(8,128)S(1)} %get-tuple-element.40.refs_4_.refs_0_, f32[4,8,16,128]{3,2,1,0:T(8,128)S(1)} %get-tuple-element.41.refs_5_.refs_1_, f32[4,8,16,128]{3,2,1,0:T(8,128)S(1)} %get-tuple-element.43.refs_2_, ...), custom_call_target="tpu_custom_call" | custom-call | flops 262144000 | bytes 1048576 | tf_op jit(solution)/shard_map/pallas_call | solution.py:422
  42.6 1.9 %collective-permute-done.16.refs_1_ = f32[8,16,128]{2,1,0:T(8,128)S(1)} collective-permute-done((f32[8,16,128]{2,1,0:T(8,128)S(1)}, f32[8,16,128]{2,1,0:T(8,128)S(1)}, u32[]{:S(2)}, u32[]{:S(2)}) %collective-permute-start.16) | collective-permute-done | bytes 65568 | tf_op jit(solution)/shard_map/ppermute | solution.py:557
  44.4 0.0 collective-permute-done.17.refs_2_
  44.4 0.9 %shard_map.81 = (f32[1,2,16,1024]{3,2,1,0:T(8,128)}, f32[1,2,16,1024]{3,2,1,0:T(8,128)}) custom-call(f32[4,8,16,128]{3,2,1,0:T(8,128)S(1)} %get-tuple-element.45.refs_0_, f32[8,16,128]{2,1,0:T(8,128)S(1)} %collective-permute-done.16.refs_1_, f32[8,16,128]{2,1,0:T(8,128)S(1)} %collective-permute-done.17.refs_2_), custom_call_target="tpu_custom_call" | custom-call | flops 131072000 | bytes 524288 | tf_op jit(solution)/shard_map/pallas_call | solution.py:422
  (6 shorter events, 0.1 us)
Async XLA Ops:
  0.6 9.9 %collective-permute-start.5 = (f32[2,16,1024]{2,1,0:T(8,128)}, f32[2,16,1024]{2,1,0:T(8,128)S(1)}, u32[]{:S(2)}, u32[]{:S(2)}) collective-permute-start(f32[2,16,1024]{2,1,0:T(8,128)} %bitcast.6), channel_id=1, source_target_pairs={{0,1},{1,0},{2,3},{3,2},{4,5},{5,4},{6,7},{7,6},{8,9},{9,8},{10,11... | collective-permute-start | bytes 393224 | tf_op jit(solution)/shard_map/ppermute | solution.py:435
  1.2 10.5 %collective-permute-start.6 = (f32[2,16,1024]{2,1,0:T(8,128)}, f32[2,16,1024]{2,1,0:T(8,128)S(1)}, u32[]{:S(2)}, u32[]{:S(2)}) collective-permute-start(f32[2,16,1024]{2,1,0:T(8,128)} %bitcast.9), channel_id=1, source_target_pairs={{0,1},{1,0},{2,3},{3,2},{4,5},{5,4},{6,7},{7,6},{8,9},{9,8},{10,11... | collective-permute-start | bytes 393224 | tf_op jit(solution)/shard_map/ppermute | solution.py:435
  1.3 10.4 %collective-permute-start.8 = (f32[2,16,1024]{2,1,0:T(8,128)}, f32[2,16,1024]{2,1,0:T(8,128)S(1)}, u32[]{:S(2)}, u32[]{:S(2)}) collective-permute-start(f32[2,16,1024]{2,1,0:T(8,128)} %refs_3_.1), channel_id=1, source_target_pairs={{0,1},{1,0},{2,3},{3,2},{4,5},{5,4},{6,7},{7,6},{8,9},{9,8},{10,11... | collective-permute-start | bytes 393224 | tf_op jit(solution)/shard_map/ppermute | solution.py:435
  1.7 3.6 %copy-start.3 = (f32[16,1024]{1,0:T(8,128)S(1)}, f32[16,1024]{1,0:T(8,128)}, u32[]{:S(2)}) copy-start(f32[16,1024]{1,0:T(8,128)} %param.7) | copy-start | bytes 196612
  1.7 10.0 %copy-start.2 = (f32[2,16,1024]{2,1,0:T(8,128)S(1)}, f32[2,16,1024]{2,1,0:T(8,128)}, u32[]{:S(2)}) copy-start(f32[2,16,1024]{2,1,0:T(8,128)} %refs_3_.1) | copy-start | bytes 393220
  2.7 5.7 %collective-permute-start.2 = (f32[3,8,1024]{2,1,0:T(8,128)S(1)}, f32[3,8,1024]{2,1,0:T(8,128)S(1)}, u32[]{:S(2)}, u32[]{:S(2)}) collective-permute-start(f32[3,8,1024]{2,1,0:T(8,128)S(1)} %fusion.1), channel_id=1, source_target_pairs={{0,3},{1,2},{2,1},{3,0},{4,7},{5,6},{6,5},{7,4},{8,11},{9,10},{10,... | collective-permute-start | bytes 294920 | tf_op jit(solution)/shard_map/ppermute | solution.py:468
  5.3 1.3 %collective-permute-start.7 = (f32[1,16,1024]{2,1,0:T(8,128)S(1)}, f32[1,16,1024]{2,1,0:T(8,128)S(1)}, u32[]{:S(2)}, u32[]{:S(2)}) collective-permute-start(f32[1,16,1024]{2,1,0:T(8,128)S(1)} %bitcast.4), channel_id=1, source_target_pairs={{0,1},{1,0},{2,3},{3,2},{4,5},{5,4},{6,7},{7,6},{8,9},{9,8},{10,11... | collective-permute-start | bytes 196616 | tf_op jit(solution)/shard_map/ppermute | solution.py:435
  6.6 9.0 %collective-permute-start = (f32[2,16,1024]{2,1,0:T(8,128)}, f32[2,16,1024]{2,1,0:T(8,128)S(1)}, u32[]{:S(2)}, u32[]{:S(2)}) collective-permute-start(f32[2,16,1024]{2,1,0:T(8,128)} %bitcast.7), channel_id=1, source_target_pairs={{0,3},{1,2},{2,1},{3,0},{4,7},{5,6},{6,5},{7,4},{8,11},{9,10},{10,... | collective-permute-start | bytes 393224 | tf_op jit(solution)/shard_map/ppermute | solution.py:471
  8.4 7.2 %collective-permute-start.1 = (f32[2,16,1024]{2,1,0:T(8,128)}, f32[2,16,1024]{2,1,0:T(8,128)S(1)}, u32[]{:S(2)}, u32[]{:S(2)}) collective-permute-start(f32[2,16,1024]{2,1,0:T(8,128)} %bitcast.10), channel_id=1, source_target_pairs={{0,3},{1,2},{2,1},{3,0},{4,7},{5,6},{6,5},{7,4},{8,11},{9,10},{10,... | collective-permute-start | bytes 393224 | tf_op jit(solution)/shard_map/ppermute | solution.py:471
  10.6 5.1 %collective-permute-start.3 = (f32[3,8,1024]{2,1,0:T(8,128)S(1)}, f32[3,8,1024]{2,1,0:T(8,128)S(1)}, u32[]{:S(2)}, u32[]{:S(2)}) collective-permute-start(f32[3,8,1024]{2,1,0:T(8,128)S(1)} %collective-permute-done.2.refs_2_), channel_id=1, source_target_pairs={{0,4},{4,0},{8,12},{12,8},{16,20},{20,16},{24,28},{28,24},{1,5},{5... | collective-permute-start | bytes 294920 | tf_op jit(solution)/shard_map/ppermute | solution.py:435
  11.7 1.0 %copy-start = (bf16[1024,256]{1,0:T(8,128)(2,1)S(1)}, bf16[1024,256]{1,0:T(8,128)(2,1)}, u32[]{:S(2)}) copy-start(bf16[1024,256]{1,0:T(8,128)(2,1)} %constant.55.clone.refs_8_.refs_9_.refs_7_.refs_4_) | copy-start | bytes 1572868
  12.7 0.9 %copy-start.4 = (f32[1,2,16,1024]{3,2,1,0:T(8,128)S(1)}, f32[1,2,16,1024]{3,2,1,0:T(8,128)}, u32[]{:S(2)}) copy-start(f32[1,2,16,1024]{3,2,1,0:T(8,128)} %param.5) | copy-start | bytes 393220
  13.7 0.9 %copy-start.5 = (f32[1,2,16,1024]{3,2,1,0:T(8,128)S(1)}, f32[1,2,16,1024]{3,2,1,0:T(8,128)}, u32[]{:S(2)}) copy-start(f32[1,2,16,1024]{3,2,1,0:T(8,128)} %param.6) | copy-start | bytes 393220
  15.6 1.0 %copy-start.1 = (bf16[1024,256]{1,0:T(8,128)(2,1)S(1)}, bf16[1024,256]{1,0:T(8,128)(2,1)}, u32[]{:S(2)}) copy-start(bf16[1024,256]{1,0:T(8,128)(2,1)} %constant.55.clone.refs_8_.refs_9_.refs_7_.refs_4_) | copy-start | bytes 1572868
  15.7 1.7 %collective-permute-start.4 = (f32[4,8,1024]{2,1,0:T(8,128)S(1)}, f32[4,8,1024]{2,1,0:T(8,128)S(1)}, u32[]{:S(2)}, u32[]{:S(2)}) collective-permute-start(f32[4,8,1024]{2,1,0:T(8,128)S(1)} %maximum_maximum_fusion), channel_id=1, source_target_pairs={{0,1},{1,0},{2,3},{3,2},{4,5},{5,4},{6,7},{7,6},{8,9},{9,8},{10,11... | collective-permute-start | bytes 393224 | tf_op jit(solution)/shard_map/ppermute | solution.py:435
  20.5 4.5 %collective-permute-start.10 = (f32[1,2,4,16,128]{4,3,2,1,0:T(8,128)S(1)}, f32[1,2,4,16,128]{4,3,2,1,0:T(8,128)S(1)}, u32[]{:S(2)}, u32[]{:S(2)}) collective-permute-start(f32[1,2,4,16,128]{4,3,2,1,0:T(8,128)S(1)} %get-tuple-element.53), channel_id=1, source_target_pairs={{0,8},{4,12},{8,0},{12,4},{16,24},{20,28},{24,16},{28,20},{1,9},{5... | collective-permute-start | bytes 196616 | tf_op jit(solution)/shard_map/ppermute | solution.py:435
  22.1 5.3 %collective-permute-start.11 = (f32[1,2,4,16,128]{4,3,2,1,0:T(8,128)S(1)}, f32[1,2,4,16,128]{4,3,2,1,0:T(8,128)S(1)}, u32[]{:S(2)}, u32[]{:S(2)}) collective-permute-start(f32[1,2,4,16,128]{4,3,2,1,0:T(8,128)S(1)} %get-tuple-element.52), channel_id=1, source_target_pairs={{0,12},{4,8},{8,4},{12,0},{16,28},{20,24},{24,20},{28,16},{1,13},{... | collective-permute-start | bytes 196616 | tf_op jit(solution)/shard_map/ppermute | solution.py:435
  22.9 5.0 %collective-permute-start.9 = (f32[1,2,4,16,128]{4,3,2,1,0:T(8,128)S(1)}, f32[1,2,4,16,128]{4,3,2,1,0:T(8,128)S(1)}, u32[]{:S(2)}, u32[]{:S(2)}) collective-permute-start(f32[1,2,4,16,128]{4,3,2,1,0:T(8,128)S(1)} %get-tuple-element.51), channel_id=1, source_target_pairs={{0,4},{4,0},{8,12},{12,8},{16,20},{20,16},{24,28},{28,24},{1,5},{5... | collective-permute-start | bytes 196616 | tf_op jit(solution)/shard_map/ppermute | solution.py:435
  27.9 5.9 %collective-permute-start.12 = (f32[1,2,4,16,128]{4,3,2,1,0:T(8,128)S(1)}, f32[1,2,4,16,128]{4,3,2,1,0:T(8,128)S(1)}, u32[]{:S(2)}, u32[]{:S(2)}) collective-permute-start(f32[1,2,4,16,128]{4,3,2,1,0:T(8,128)S(1)} %add_add_fusion), channel_id=1, source_target_pairs={{0,16},{4,20},{8,24},{12,28},{16,0},{20,4},{24,8},{28,12},{1,17},{... | collective-permute-start | bytes 196616 | tf_op jit(solution)/shard_map/ppermute | solution.py:435
  34.0 4.3 %collective-permute-start.13 = (f32[1,2,4,16,128]{4,3,2,1,0:T(8,128)S(1)}, f32[1,2,4,16,128]{4,3,2,1,0:T(8,128)S(1)}, u32[]{:S(2)}, u32[]{:S(2)}) collective-permute-start(f32[1,2,4,16,128]{4,3,2,1,0:T(8,128)S(1)} %pad_maximum_fusion.1.refs_0_), channel_id=1, source_target_pairs={{0,4},{4,0},{8,12},{12,8},{16,20},{20,16},{24,28},{28,24},{1,5},{5... | collective-permute-start | bytes 196616 | tf_op jit(solution)/shard_map/ppermute | solution.py:435
  34.1 4.3 %collective-permute-start.14 = (f32[1,2,4,16,128]{4,3,2,1,0:T(8,128)S(1)}, f32[1,2,4,16,128]{4,3,2,1,0:T(8,128)S(1)}, u32[]{:S(2)}, u32[]{:S(2)}) collective-permute-start(f32[1,2,4,16,128]{4,3,2,1,0:T(8,128)S(1)} %pad_maximum_fusion.1.refs_0_), channel_id=1, source_target_pairs={{0,8},{4,12},{8,0},{12,4},{16,24},{20,28},{24,16},{28,20},{1,9},{5... | collective-permute-start | bytes 196616 | tf_op jit(solution)/shard_map/ppermute | solution.py:435
  35.4 5.2 %collective-permute-start.15 = (f32[1,2,4,16,128]{4,3,2,1,0:T(8,128)S(1)}, f32[1,2,4,16,128]{4,3,2,1,0:T(8,128)S(1)}, u32[]{:S(2)}, u32[]{:S(2)}) collective-permute-start(f32[1,2,4,16,128]{4,3,2,1,0:T(8,128)S(1)} %pad_maximum_fusion.1.refs_0_), channel_id=1, source_target_pairs={{0,12},{4,8},{8,4},{12,0},{16,28},{20,24},{24,20},{28,16},{1,13},{... | collective-permute-start | bytes 196616 | tf_op jit(solution)/shard_map/ppermute | solution.py:435
  40.7 3.8 %collective-permute-start.16 = (f32[8,16,128]{2,1,0:T(8,128)S(1)}, f32[8,16,128]{2,1,0:T(8,128)S(1)}, u32[]{:S(2)}, u32[]{:S(2)}) collective-permute-start(f32[8,16,128]{2,1,0:T(8,128)S(1)} %get-tuple-element.46), channel_id=1, source_target_pairs={{0,3},{1,2},{2,1},{3,0},{4,7},{5,6},{6,5},{7,4},{8,11},{9,10},{10,... | collective-permute-start | bytes 196616 | tf_op jit(solution)/shard_map/ppermute | solution.py:557
  40.8 3.7 %collective-permute-start.17 = (f32[8,16,128]{2,1,0:T(8,128)S(1)}, f32[8,16,128]{2,1,0:T(8,128)S(1)}, u32[]{:S(2)}, u32[]{:S(2)}) collective-permute-start(f32[8,16,128]{2,1,0:T(8,128)S(1)} %get-tuple-element.47), channel_id=1, source_target_pairs={{0,1},{1,0},{2,3},{3,2},{4,5},{5,4},{6,7},{7,6},{8,9},{9,8},{10,11... | collective-permute-start | bytes 196616 | tf_op jit(solution)/shard_map/ppermute | solution.py:435

commit v6 on v5

--- a/solution.py
+++ b/solution.py
@@ -97,16 +97,20 @@
     return [(r, min(size, rows - r)) for r in range(0, rows, size)]
 
 
-def pipeline(steps, planes, w_ref, xys):
+def pipeline(steps, planes, w_ref, xys, together=False):
     def product(s, big):
         _, _, xy_start, rows, hi, lo, _ = steps[s]
         in_plane(big % 4, 1, up16(rows + 2 * xy_start), w_ref, hi, lo, xys[s % 2])
 
-    product(0, 0)
+    if together:
+        src, start, xy_start, rows, hi, lo, store = steps[0]
+        in_plane(0, 4, up16(rows), w_ref, hi, lo, xys[0])
+    else:
+        product(0, 0)
     for s, (src, start, xy_start, rows, hi, lo, store) in enumerate(steps):
         margin = (planes + 32 - rows) // 2
         for i in range(8):
-            if s == 0 and i in (0, 2, 4):
+            if s == 0 and i in (0, 2, 4) and not together:
                 product(0, i // 2 + 1)
             j = (2 * s + i) % 8
             for r, count in chunks(rows):
@@ -197,47 +201,44 @@
     for ref, row in zip(parts, pieces):
         place_rows(ref, 0, row, b0, pd, hi_a, lo_a, row)
     store = stage_store(b0, pd, b1, 0.5 * time_step, hi_b, lo_b)
-    pipeline([(b0, 8, 0, planes + 32, hi_a, lo_a, store)], planes, w_ref, xys)
+    pipeline([(b0, 8, 0, planes + 32, hi_a, lo_a, store)], planes, w_ref, xys, True)
 
 
 def early_kernel(planes, *refs):
-    parts, w_ref = refs[:8], refs[8]
-    b0, pd, b1, hi_b, lo_b, hi_a, lo_a, *xys = refs[9:]
+    own, near, w_ref = refs[:3]
+    b0, pd, b1, hi_b, lo_b, hi_a, lo_a, xy = refs[3:]
     odd = lax.rem(lax.axis_index("grid"), 2)
     base = pl.multiple_of((1 - odd) * planes, 16)
     clear_rows(b0, base)
     clear_rows(b0, pl.multiple_of(base + 2 * planes + 8, 8))
-    for i, ref in enumerate(parts):
-        inner = pl.multiple_of((odd if i < 4 else 1 - odd) * planes, 16)
-        channel = (0, 2, 4, 5)[i % 4]
-        place_rows(ref, channel, pl.multiple_of(base + inner, 16), b0, pd, hi_a, lo_a, inner)
+    for ref, side in ((own, odd), (near, 1 - odd)):
+        inner = pl.multiple_of(side * planes, 16)
+        place_rows(ref, 0, pl.multiple_of(base + inner, 16), b0, pd, hi_a, lo_a, inner)
     store = stage_store(b0, pd, b1, 0.5 * time_step, hi_b, lo_b, base)
-    pipeline([(b0, base + 8, 0, 2 * planes, hi_a, lo_a, store)], planes, w_ref, xys)
+    pipeline([(b0, base + 8, 0, 2 * planes, hi_a, lo_a, store)], planes, w_ref, [xy], True)
 
 
 def late_kernel(planes, *refs):
-    far_u, far_v, mine, other = refs[:4]
-    w_ref = refs[9]
-    b0, pd, b1, hi_b, lo_b, hi_a, lo_a, past, *xys = refs[10:]
+    far, mine, other = refs[:3]
+    w_ref = refs[8]
+    b0, pd, b1, hi_b, lo_b, hi_a, lo_a, past, *xys = refs[9:]
     odd = lax.rem(lax.axis_index("grid"), 2)
     half = lax.rem(lax.axis_index("modes"), 2)
     base = pl.multiple_of(odd * (2 * planes), 16)
     clear_rows(b0, pl.multiple_of(odd * (3 * planes + 8), 8))
-    for ref, channel in ((far_u, 0), (far_v, 2)):
-        place_rows(ref, channel, base, b0, pd, hi_a, lo_a, 0)
+    place_rows(far, 0, base, b0, pd, hi_a, lo_a, 0)
     for ref, which in ((mine, half), (other, 1 - half)):
         row = pl.multiple_of(base + which * (planes // 2), 8)
         place_rows(ref, 4, row, b0, pd, hi_a, lo_a, 0)
     store = stage_store(b0, pd, b1, 0.5 * time_step, hi_b, lo_b, base)
-    pipeline([(b0, base + 8, 0, planes, hi_a, lo_a, store)], planes, w_ref, xys)
+    pipeline([(b0, base + 8, 0, planes, hi_a, lo_a, store)], planes, w_ref, xys, True)
 
     clear_past(past)
     none = jnp.zeros((REACH, LANES), jnp.float32)
     for c in range(4):
-        ref = far_u if c < 2 else far_v
         for j in range(8):
             lanes = slice(j * LANES, (j + 1) * LANES)
-            ahead, behind = ref[c % 2, planes - REACH :, lanes], ref[c % 2, :REACH, lanes]
+            ahead, behind = far[c, planes - REACH :, lanes], far[c, :REACH, lanes]
             past[c, j, 0:REACH, :] = jnp.where(odd == 0, ahead, none)
             past[c, j, 24 : 24 + REACH, :] = jnp.where(odd == 0, none, behind)
     row = pl.multiple_of(planes + odd * (planes - 8), 8)
@@ -443,7 +444,8 @@
     paired = slabs == 4 and planes == 16 and low_bits == 4
     f32, bf16 = jnp.float32, jnp.bfloat16
     weights = jnp.asarray(in_plane_matrix())
-    psi = (u_modes[0], v_modes[0])
+    own = jnp.concatenate([u_modes[0], v_modes[0], potential[None], pairing], axis=0)
+    own = lax.optimization_barrier(own)
     tall = up16(planes + 32)
     state = (4, 8, planes, LANES)
     split = ((4, 4, tall, WINDOW), bf16)
@@ -463,36 +465,24 @@
     if paired:
         part = planes // 2
         upper = lax.rem(lax.axis_index("modes"), 2) == 1
-        frozen = (potential[None], pairing)
-        both = jnp.concatenate(frozen, axis=0)
-        mine = lax.ppermute(
-            jnp.where(upper, both[:, part:], both[:, :part]), "grid", cross
-        )
-        far_u, far_v = [lax.ppermute(x, "grid", cross) for x in psi]
-        near = [exchange_xor(x, "grid", 1, slabs) for x in (*psi, *frozen)]
+        picked = jnp.where(upper, own[4:, part:], own[4:, :part])
+        mine = lax.ppermute(picked, "grid", cross)
+        far = lax.ppermute(own[:4], "grid", cross)
+        near = exchange_xor(own, "grid", 1, slabs)
         other = exchange_xor(mine, "modes", 1, modes)
-        ready = call(
-            functools.partial(early_kernel, planes), buffers, [split, split, product], [*psi, *frozen, *near, weights]
-        )
-        far_u, far_v, other = lax.optimization_barrier((far_u, far_v, other))
-        both = jnp.concatenate(
-            [
-                jnp.concatenate([x[:, :REACH], x[:, planes - REACH :]], axis=1)
-                for x in (far_u, far_v)
-            ],
-            axis=0,
-        )
+        ready = call(functools.partial(early_kernel, planes), buffers, [split, split, product], [own, near, weights])
+        far, other = lax.optimization_barrier((far, other))
+        both = jnp.concatenate([far[:, :REACH], far[:, planes - REACH :]], axis=1)
         lead_far = tail_far = exchange_xor(both, "grid", 1, slabs)
-        far = (REACH, 0)
+        past_rows = (REACH, 0)
         b0, pd, b1, hi, lo = call(
             functools.partial(late_kernel, planes),
             buffers,
             [split, split, past, product],
-            [far_u, far_v, mine, other, *ready, weights],
-            {4 + i: i for i in range(5)},
+            [far, mine, other, *ready, weights],
+            {3 + i: i for i in range(5)},
         )
     else:
-        own = jnp.concatenate([*psi, potential[None], pairing], axis=0)
         pieces, arrays = [16], [own]
         reach, step = 0, 0
         while reach < 5 * REACH:
@@ -509,7 +499,7 @@
                 pieces += [16 - reach - count, 16 + planes + reach]
                 arrays += [before, after]
             else:
-                lead_far, tail_far, far = before, after, (0, 0)
+                lead_far, tail_far, past_rows = before, after, (0, 0)
             reach += count
         b0, pd, b1, hi, lo = call(
             functools.partial(first_kernel, pieces, planes), buffers, [split, split, product], arrays + [weights]
@@ -517,7 +507,7 @@
 
     inputs = [lead_far, tail_far, b0, pd, b1, hi, lo, weights]
     psi1, kin1, sums, *rest = call(
-        functools.partial(stages_kernel, far, planes, low_bits),
+        functools.partial(stages_kernel, past_rows, planes, low_bits),
         [state, state, (4, 2, 4, planes, LANES), b1.shape, split, split],
         [
             ((4, 8, tall + 8, LANES), f32),

time: 45.6 us -> 49.5 us (1.086)
  waiting for transfers between devices: 15.3 us -> 22.9 us
  local copies, waits for them, and re-layouts: 3.75 us -> 0.07 us
    ppermute x3 -> x2, waiting for transfers between devices: 1.75 us -> 7.97 us  [the longest x1 7.97 us: local(): mine = lax.ppermute(picked, 'grid', cross)]
    unnamed x12 -> x2, local copies, waits for them, and re-layouts: 3.71 us -> 0.01 us
    ppermute x14 -> x11, starting transfers between devices: 12.3 us -> 14.7 us  [exchange_xor(): return lax.ppermute(x, axis, [(i, i ^ bits) for i in range(count)])]
    ppermute x3 -> x2, starting transfers between devices: 4.9 us -> 2.56 us  [the longest x1 2.47 us: local(): far = lax.ppermute(own[:4], 'grid', cross)]
    ppermute x14 -> x11, waiting for transfers between devices: 11.6 us -> 13.7 us  [exchange_xor(): return lax.ppermute(x, axis, [(i, i ^ bits) for i in range(count)])]
    concatenate x1 -> x2, other arithmetic: 0.03 us -> 1.13 us  [the longest x1 1.1 us: local(): jnp.concatenate([u_modes[0], v_modes[0], potential[None], pairing], axis=0)]
    select_n x1, other arithmetic: 0.96 us -> 0.01 us  [local(): picked = jnp.where(upper, own[4:, part:], own[4:, :part])]
    ppermute x1, waiting for transfers between devices: 1.88 us -> 1.27 us  [local(): first = lax.ppermute(first, 'grid', cross)]
  transfers between devices with their start and end apart: 18 -> 14, of which waited for: 10 -> 10; matrix products, arithmetic and copies ran while one was open for 2% -> 0% of each run, Pallas kernels for 7% -> 6%
where the time goes in v6:
time: 49.5 us; the launch traced here: 49.3 us
  waiting for transfers between devices  22.9 us (46%)
  starting transfers between devices  17.3 us (35%)
  Pallas kernels  7.04 us (14%)
  other arithmetic  1.23 us (2%)
  between operations  0.78 us (2%)
    ppermute x11, starting transfers between devices, exchange_xor(): return lax.ppermute(x, axis, [(i, i ^ bits) for i in range(count)])  14.7 us
    ppermute x11, waiting for transfers between devices, exchange_xor(): return lax.ppermute(x, axis, [(i, i ^ bits) for i in range(count)])  13.7 us
    ppermute x1, waiting for transfers between devices, local(): mine = lax.ppermute(picked, 'grid', cross)  7.97 us
    pallas_call x6, Pallas kernels, call(): pl.pallas_call(kernel, out_shape=tuple((jax.ShapeDtypeStruct(s, d) for s,...  7.04 us
    ppermute x1, starting transfers between devices, local(): far = lax.ppermute(own[:4], 'grid', cross)  2.47 us
    ppermute x1, waiting for transfers between devices, local(): first = lax.ppermute(first, 'grid', cross)  1.27 us
    concatenate x1, other arithmetic, local(): jnp.concatenate([u_modes[0], v_modes[0], potential[None], pairing], axis=0)  1.1 us
  transfers between devices with their start and end apart: 14, of which 10 were waited for; matrix products, arithmetic and copies ran while one was open for 0% of the time, Pallas kernels for 6%

profile of v6, /device:TPU:0, one launch (start us, length us, event | category | flops | bytes accessed | tf_op | source)
XLA Modules:
  0.0 49.3 jit_solution(2964626886279111466)
XLA Ops:
  0.6 1.1 %pad_maximum_fusion.refs_0_ = f32[7,16,1024]{2,1,0:T(8,128)S(1)} fusion(f32[2,16,1024]{2,1,0:T(8,128)} %param.8, f32[1,16,1024]{2,1,0:T(8,128)} %bitcast.5, f32[2,16,1024]{2,1,0:T(8,128)} %bitcast.3, f32[2,16,1024]{2,1,0:T(8,128)} %bitcast.4), kind=kLoop, calls=%fused_computation | loop fusion | flops 344064 | bytes 917504 | tf_op jit(solution)/shard_map/concatenate | solution.py:447
  1.8 0.0 copy-start
  1.8 2.5 %collective-permute-start = (f32[4,16,1024]{2,1,0:T(8,128)S(1)}, f32[4,16,1024]{2,1,0:T(8,128)S(1)}, u32[]{:S(2)}, u32[]{:S(2)}) collective-permute-start(f32[4,16,1024]{2,1,0:T(8,128)S(1)} %slice.52), channel_id=1, source_target_pairs={{0,3},{1,2},{2,1},{3,0},{4,7},{5,6},{6,5},{7,4},{8,11},{9,10},{10,... | collective-permute-start | bytes 786440 | tf_op jit(solution)/shard_map/ppermute | solution.py:470
  4.3 0.1 collective-permute-start.1
  4.3 0.7 %collective-permute-start.4 = (f32[7,16,1024]{2,1,0:T(8,128)S(1)}, f32[7,16,1024]{2,1,0:T(8,128)S(1)}, u32[]{:S(2)}, u32[]{:S(2)}) collective-permute-start(f32[7,16,1024]{2,1,0:T(8,128)S(1)} %pad_maximum_fusion.refs_0_), channel_id=1, source_target_pairs={{0,1},{1,0},{2,3},{3,2},{4,5},{5,4},{6,7},{7,6},{8,9},{9,8},{10,11... | collective-permute-start | bytes 1376264 | tf_op jit(solution)/shard_map/ppermute | solution.py:436
  5.1 8.0 %collective-permute-done.1.refs_1_ = f32[3,8,1024]{2,1,0:T(8,128)S(1)} collective-permute-done((f32[3,8,1024]{2,1,0:T(8,128)S(1)}, f32[3,8,1024]{2,1,0:T(8,128)S(1)}, u32[]{:S(2)}, u32[]{:S(2)}) %collective-permute-start.1) | collective-permute-done | bytes 98336 | tf_op jit(solution)/shard_map/ppermute | solution.py:469
  13.0 2.4 %collective-permute-start.2 = (f32[3,8,1024]{2,1,0:T(8,128)S(1)}, f32[3,8,1024]{2,1,0:T(8,128)S(1)}, u32[]{:S(2)}, u32[]{:S(2)}) collective-permute-start(f32[3,8,1024]{2,1,0:T(8,128)S(1)} %collective-permute-done.1.refs_1_), channel_id=1, source_target_pairs={{0,4},{4,0},{8,12},{12,8},{16,20},{20,16},{24,28},{28,24},{1,5},{5... | collective-permute-start | bytes 294920 | tf_op jit(solution)/shard_map/ppermute | solution.py:436
  15.5 3.1 %collective-permute-done.2.refs_2_ = f32[3,8,1024]{2,1,0:T(8,128)S(1)} collective-permute-done((f32[3,8,1024]{2,1,0:T(8,128)S(1)}, f32[3,8,1024]{2,1,0:T(8,128)S(1)}, u32[]{:S(2)}, u32[]{:S(2)}) %collective-permute-start.2) | collective-permute-done | bytes 98336 | tf_op jit(solution)/shard_map/ppermute | solution.py:436
  18.6 0.0 collective-permute-done.refs_0_
  18.6 0.1 collective-permute-start.3
  18.7 0.0 collective-permute-done.4.refs_1_
  18.7 0.0 copy-done
  18.7 1.1 %shard_map.76 = (f32[4,8,64,128]{3,2,1,0:T(8,128)S(1)}, f32[3,8,48,128]{3,2,1,0:T(8,128)S(1)}, f32[4,8,56,128]{3,2,1,0:T(8,128)S(1)}, bf16[4,4,48,512]{3,2,1,0:T(8,128)(2,1)S(1)}, bf16[4,4,48,512]{3,2,1,0:T(8,128)(2,1)S(1)}) custom-call(f32[7,16,1024]{2,1,0:T(8,128)S(1)} %pad_maximum_fusion.refs_0_, f32[7,16,1024]{2,1,0:T(8,128)S(1)} %collective-permute-done.4.refs_1_, ...), custom_call_target="tpu_custom_call" | custom-call | flops 2850816000 | bytes 11403264 | tf_op jit(solution)/shard_map/pallas_call | solution.py:423
  19.8 0.7 %shard_map.77 = (f32[4,8,64,128]{3,2,1,0:T(8,128)S(1)}, f32[3,8,48,128]{3,2,1,0:T(8,128)S(1)}, f32[4,8,56,128]{3,2,1,0:T(8,128)S(1)}, bf16[4,4,48,512]{3,2,1,0:T(8,128)(2,1)S(1)}, bf16[4,4,48,512]{3,2,1,0:T(8,128)(2,1)S(1)}) custom-call(f32[4,16,1024]{2,1,0:T(8,128)S(1)} %collective-permute-d, ...), custom_call_target="tpu_custom_call", output_to_operand_aliasing={{0}: (3, {}), {1}: (4, {}), {2}: (5, {}), {3}: (6, {}), {4}... | custom-call | flops 2850816000 | bytes 11403264 | tf_op jit(solution)/shard_map/pallas_call | solution.py:423
  20.5 0.0 collective-permute-done.3.refs_0_.refs_1_
  20.5 3.0 %shard_map.78 = (f32[4,8,16,128]{3,2,1,0:T(8,128)S(1)}, f32[4,8,16,128]{3,2,1,0:T(8,128)S(1)}, f32[4,2,4,16,128]{4,3,2,1,0:T(8,128)S(1)}, f32[4,8,56,128]{3,2,1,...) custom-call(f32[4,8,1024]{2,1,0:T(8,128)S(1)} %collective-permute-do, ...), custom_call_target="tpu_custom_call", output_to_operand_aliasing={{3}: (4, {}), {4}: (5, {}), {5}: (6, {})} | custom-call | flops 2424832000 | bytes 9699328 | tf_op jit(solution)/shard_map/pallas_call | solution.py:423
  23.5 1.8 %collective-permute-start.5 = (f32[1,2,4,16,128]{4,3,2,1,0:T(8,128)S(1)}, f32[1,2,4,16,128]{4,3,2,1,0:T(8,128)S(1)}, u32[]{:S(2)}, u32[]{:S(2)}) collective-permute-start(f32[1,2,4,16,128]{4,3,2,1,0:T(8,128)S(1)} %get-tuple-element.49), channel_id=1, source_target_pairs={{0,4},{4,0},{8,12},{12,8},{16,20},{20,16},{24,28},{28,24},{1,5},{5... | collective-permute-start | bytes 196616 | tf_op jit(solution)/shard_map/ppermute | solution.py:436
  25.3 1.6 %collective-permute-start.6 = (f32[1,2,4,16,128]{4,3,2,1,0:T(8,128)S(1)}, f32[1,2,4,16,128]{4,3,2,1,0:T(8,128)S(1)}, u32[]{:S(2)}, u32[]{:S(2)}) collective-permute-start(f32[1,2,4,16,128]{4,3,2,1,0:T(8,128)S(1)} %get-tuple-element.51), channel_id=1, source_target_pairs={{0,8},{4,12},{8,0},{12,4},{16,24},{20,28},{24,16},{28,20},{1,9},{5... | collective-permute-start | bytes 196616 | tf_op jit(solution)/shard_map/ppermute | solution.py:436
  26.9 0.2 collective-permute-start.7
  27.1 0.9 %collective-permute-done.5 = f32[1,2,4,16,128]{4,3,2,1,0:T(8,128)S(1)} collective-permute-done((f32[1,2,4,16,128]{4,3,2,1,0:T(8,128)S(1)}, f32[1,2,4,16,128]{4,3,2,1,0:T(8,128)S(1)}, u32[]{:S(2)}, u32[]{:S(2)}) %collective-permute-start.5) | collective-permute-done | bytes 65568 | tf_op jit(solution)/shard_map/ppermute | solution.py:436
  28.0 2.0 %collective-permute-done.6 = f32[1,2,4,16,128]{4,3,2,1,0:T(8,128)S(1)} collective-permute-done((f32[1,2,4,16,128]{4,3,2,1,0:T(8,128)S(1)}, f32[1,2,4,16,128]{4,3,2,1,0:T(8,128)S(1)}, u32[]{:S(2)}, u32[]{:S(2)}) %collective-permute-start.6) | collective-permute-done | bytes 65568 | tf_op jit(solution)/shard_map/ppermute | solution.py:436
  29.9 2.1 %collective-permute-done.7 = f32[1,2,4,16,128]{4,3,2,1,0:T(8,128)S(1)} collective-permute-done((f32[1,2,4,16,128]{4,3,2,1,0:T(8,128)S(1)}, f32[1,2,4,16,128]{4,3,2,1,0:T(8,128)S(1)}, u32[]{:S(2)}, u32[]{:S(2)}) %collective-permute-start.7) | collective-permute-done | bytes 65568 | tf_op jit(solution)/shard_map/ppermute | solution.py:436
  32.1 2.7 %collective-permute-start.8 = (f32[1,2,4,16,128]{4,3,2,1,0:T(8,128)S(1)}, f32[1,2,4,16,128]{4,3,2,1,0:T(8,128)S(1)}, u32[]{:S(2)}, u32[]{:S(2)}) collective-permute-start(f32[1,2,4,16,128]{4,3,2,1,0:T(8,128)S(1)} %add_add_fusion), channel_id=1, source_target_pairs={{0,16},{4,20},{8,24},{12,28},{16,0},{20,4},{24,8},{28,12},{1,17},{... | collective-permute-start | bytes 196616 | tf_op jit(solution)/shard_map/ppermute | solution.py:436
  34.8 3.2 %collective-permute-done.8 = f32[1,2,4,16,128]{4,3,2,1,0:T(8,128)S(1)} collective-permute-done((f32[1,2,4,16,128]{4,3,2,1,0:T(8,128)S(1)}, f32[1,2,4,16,128]{4,3,2,1,0:T(8,128)S(1)}, u32[]{:S(2)}, u32[]{:S(2)}) %collective-permute-start.8) | collective-permute-done | bytes 65568 | tf_op jit(solution)/shard_map/ppermute | solution.py:436
  37.9 0.1 divide_subtract_fusion
  38.0 0.1 collective-permute-start.10
  38.1 1.4 %collective-permute-start.11 = (f32[1,2,4,16,128]{4,3,2,1,0:T(8,128)S(1)}, f32[1,2,4,16,128]{4,3,2,1,0:T(8,128)S(1)}, u32[]{:S(2)}, u32[]{:S(2)}) collective-permute-start(f32[1,2,4,16,128]{4,3,2,1,0:T(8,128)S(1)} %pad_maximum_fusion.2.refs_0_), channel_id=1, source_target_pairs={{0,12},{4,8},{8,4},{12,0},{16,28},{20,24},{24,20},{28,16},{1,13},{... | collective-permute-start | bytes 196616 | tf_op jit(solution)/shard_map/ppermute | solution.py:436
  39.5 2.1 %collective-permute-start.9 = (f32[1,2,4,16,128]{4,3,2,1,0:T(8,128)S(1)}, f32[1,2,4,16,128]{4,3,2,1,0:T(8,128)S(1)}, u32[]{:S(2)}, u32[]{:S(2)}) collective-permute-start(f32[1,2,4,16,128]{4,3,2,1,0:T(8,128)S(1)} %pad_maximum_fusion.2.refs_0_), channel_id=1, source_target_pairs={{0,4},{4,0},{8,12},{12,8},{16,20},{20,16},{24,28},{28,24},{1,5},{5... | collective-permute-start | bytes 196616 | tf_op jit(solution)/shard_map/ppermute | solution.py:436
  41.6 0.8 %collective-permute-done.10.refs_2_ = f32[1,2,4,16,128]{4,3,2,1,0:T(8,128)S(1)} collective-permute-done((f32[1,2,4,16,128]{4,3,2,1,0:T(8,128)S(1)}, f32[1,2,4,16,128]{4,3,2,1,0:T(8,128)S(1)}, u32[]{:S(2)}, u32[]{:S(2)}) %collective-permute-start.10) | collective-permute-done | bytes 65568 | tf_op jit(solution)/shard_map/ppermute | solution.py:436
  42.3 1.0 %collective-permute-done.11.refs_3_ = f32[1,2,4,16,128]{4,3,2,1,0:T(8,128)S(1)} collective-permute-done((f32[1,2,4,16,128]{4,3,2,1,0:T(8,128)S(1)}, f32[1,2,4,16,128]{4,3,2,1,0:T(8,128)S(1)}, u32[]{:S(2)}, u32[]{:S(2)}) %collective-permute-start.11) | collective-permute-done | bytes 65568 | tf_op jit(solution)/shard_map/ppermute | solution.py:436
  43.3 0.7 %collective-permute-done.9.refs_1_ = f32[1,2,4,16,128]{4,3,2,1,0:T(8,128)S(1)} collective-permute-done((f32[1,2,4,16,128]{4,3,2,1,0:T(8,128)S(1)}, f32[1,2,4,16,128]{4,3,2,1,0:T(8,128)S(1)}, u32[]{:S(2)}, u32[]{:S(2)}) %collective-permute-start.9) | collective-permute-done | bytes 65568 | tf_op jit(solution)/shard_map/ppermute | solution.py:436
  44.0 0.1 shard_map.79
  44.2 0.1 collective-permute-start.12
  44.2 1.7 %collective-permute-start.13 = (f32[8,16,128]{2,1,0:T(8,128)S(1)}, f32[8,16,128]{2,1,0:T(8,128)S(1)}, u32[]{:S(2)}, u32[]{:S(2)}) collective-permute-start(f32[8,16,128]{2,1,0:T(8,128)S(1)} %get-tuple-element.45), channel_id=1, source_target_pairs={{0,1},{1,0},{2,3},{3,2},{4,5},{5,4},{6,7},{7,6},{8,9},{9,8},{10,11... | collective-permute-start | bytes 196616 | tf_op jit(solution)/shard_map/ppermute | solution.py:436
  45.9 1.3 %shard_map.80 = (f32[4,8,16,128]{3,2,1,0:T(8,128)S(1)}, f32[4,16,1024]{2,1,0:T(8,128)}) custom-call(f32[4,8,16,128]{3,2,1,0:T(8,128)S(1)} %get-tuple-element.38.refs_4_.refs_0_, f32[4,8,16,128]{3,2,1,0:T(8,128)S(1)} %get-tuple-element.39.refs_5_.refs_1_, f32[4,8,16,128]{3,2,1,0:T(8,128)S(1)} %get-tuple-element.41.refs_2_, ...), custom_call_target="tpu_custom_call" | custom-call | flops 262144000 | bytes 1048576 | tf_op jit(solution)/shard_map/pallas_call | solution.py:423
  47.2 1.3 %collective-permute-done.12.refs_1_ = f32[8,16,128]{2,1,0:T(8,128)S(1)} collective-permute-done((f32[8,16,128]{2,1,0:T(8,128)S(1)}, f32[8,16,128]{2,1,0:T(8,128)S(1)}, u32[]{:S(2)}, u32[]{:S(2)}) %collective-permute-start.12) | collective-permute-done | bytes 65568 | tf_op jit(solution)/shard_map/ppermute | solution.py:547
  48.5 0.0 collective-permute-done.13.refs_2_
  48.5 0.9 %shard_map.81 = (f32[1,2,16,1024]{3,2,1,0:T(8,128)}, f32[1,2,16,1024]{3,2,1,0:T(8,128)}) custom-call(f32[4,8,16,128]{3,2,1,0:T(8,128)S(1)} %get-tuple-element.43.refs_0_, f32[8,16,128]{2,1,0:T(8,128)S(1)} %collective-permute-done.12.refs_1_, f32[8,16,128]{2,1,0:T(8,128)S(1)} %collective-permute-done.13.refs_2_), custom_call_target="tpu_custom_call" | custom-call | flops 131072000 | bytes 524288 | tf_op jit(solution)/shard_map/pallas_call | solution.py:423
  (8 shorter events, 0.1 us)
Async XLA Ops:
  1.8 17.0 %copy-start = (bf16[1024,256]{1,0:T(8,128)(2,1)S(1)}, bf16[1024,256]{1,0:T(8,128)(2,1)}, u32[]{:S(2)}) copy-start(bf16[1024,256]{1,0:T(8,128)(2,1)} %constant.55.clone.refs_2_.refs_8_.refs_7_.refs_4_) | copy-start | bytes 1572868
  1.8 16.8 %collective-permute-start = (f32[4,16,1024]{2,1,0:T(8,128)S(1)}, f32[4,16,1024]{2,1,0:T(8,128)S(1)}, u32[]{:S(2)}, u32[]{:S(2)}) collective-permute-start(f32[4,16,1024]{2,1,0:T(8,128)S(1)} %slice.52), channel_id=1, source_target_pairs={{0,3},{1,2},{2,1},{3,0},{4,7},{5,6},{6,5},{7,4},{8,11},{9,10},{10,... | collective-permute-start | bytes 786440 | tf_op jit(solution)/shard_map/ppermute | solution.py:470
  4.3 8.8 %collective-permute-start.1 = (f32[3,8,1024]{2,1,0:T(8,128)S(1)}, f32[3,8,1024]{2,1,0:T(8,128)S(1)}, u32[]{:S(2)}, u32[]{:S(2)}) collective-permute-start(f32[3,8,1024]{2,1,0:T(8,128)S(1)} %slice_select_fusion), channel_id=1, source_target_pairs={{0,3},{1,2},{2,1},{3,0},{4,7},{5,6},{6,5},{7,4},{8,11},{9,10},{10,... | collective-permute-start | bytes 294920 | tf_op jit(solution)/shard_map/ppermute | solution.py:469
  4.3 14.4 %collective-permute-start.4 = (f32[7,16,1024]{2,1,0:T(8,128)S(1)}, f32[7,16,1024]{2,1,0:T(8,128)S(1)}, u32[]{:S(2)}, u32[]{:S(2)}) collective-permute-start(f32[7,16,1024]{2,1,0:T(8,128)S(1)} %pad_maximum_fusion.refs_0_), channel_id=1, source_target_pairs={{0,1},{1,0},{2,3},{3,2},{4,5},{5,4},{6,7},{7,6},{8,9},{9,8},{10,11... | collective-permute-start | bytes 1376264 | tf_op jit(solution)/shard_map/ppermute | solution.py:436
  13.0 5.5 %collective-permute-start.2 = (f32[3,8,1024]{2,1,0:T(8,128)S(1)}, f32[3,8,1024]{2,1,0:T(8,128)S(1)}, u32[]{:S(2)}, u32[]{:S(2)}) collective-permute-start(f32[3,8,1024]{2,1,0:T(8,128)S(1)} %collective-permute-done.1.refs_1_), channel_id=1, source_target_pairs={{0,4},{4,0},{8,12},{12,8},{16,20},{20,16},{24,28},{28,24},{1,5},{5... | collective-permute-start | bytes 294920 | tf_op jit(solution)/shard_map/ppermute | solution.py:436
  18.6 1.9 %collective-permute-start.3 = (f32[4,8,1024]{2,1,0:T(8,128)S(1)}, f32[4,8,1024]{2,1,0:T(8,128)S(1)}, u32[]{:S(2)}, u32[]{:S(2)}) collective-permute-start(f32[4,8,1024]{2,1,0:T(8,128)S(1)} %pad_maximum_fusion.1), channel_id=1, source_target_pairs={{0,1},{1,0},{2,3},{3,2},{4,5},{5,4},{6,7},{7,6},{8,9},{9,8},{10,11... | collective-permute-start | bytes 393224 | tf_op jit(solution)/shard_map/ppermute | solution.py:436
  23.5 4.4 %collective-permute-start.5 = (f32[1,2,4,16,128]{4,3,2,1,0:T(8,128)S(1)}, f32[1,2,4,16,128]{4,3,2,1,0:T(8,128)S(1)}, u32[]{:S(2)}, u32[]{:S(2)}) collective-permute-start(f32[1,2,4,16,128]{4,3,2,1,0:T(8,128)S(1)} %get-tuple-element.49), channel_id=1, source_target_pairs={{0,4},{4,0},{8,12},{12,8},{16,20},{20,16},{24,28},{28,24},{1,5},{5... | collective-permute-start | bytes 196616 | tf_op jit(solution)/shard_map/ppermute | solution.py:436
  25.3 4.6 %collective-permute-start.6 = (f32[1,2,4,16,128]{4,3,2,1,0:T(8,128)S(1)}, f32[1,2,4,16,128]{4,3,2,1,0:T(8,128)S(1)}, u32[]{:S(2)}, u32[]{:S(2)}) collective-permute-start(f32[1,2,4,16,128]{4,3,2,1,0:T(8,128)S(1)} %get-tuple-element.51), channel_id=1, source_target_pairs={{0,8},{4,12},{8,0},{12,4},{16,24},{20,28},{24,16},{28,20},{1,9},{5... | collective-permute-start | bytes 196616 | tf_op jit(solution)/shard_map/ppermute | solution.py:436
  26.9 5.2 %collective-permute-start.7 = (f32[1,2,4,16,128]{4,3,2,1,0:T(8,128)S(1)}, f32[1,2,4,16,128]{4,3,2,1,0:T(8,128)S(1)}, u32[]{:S(2)}, u32[]{:S(2)}) collective-permute-start(f32[1,2,4,16,128]{4,3,2,1,0:T(8,128)S(1)} %get-tuple-element.50), channel_id=1, source_target_pairs={{0,12},{4,8},{8,4},{12,0},{16,28},{20,24},{24,20},{28,16},{1,13},{... | collective-permute-start | bytes 196616 | tf_op jit(solution)/shard_map/ppermute | solution.py:436
  32.1 5.8 %collective-permute-start.8 = (f32[1,2,4,16,128]{4,3,2,1,0:T(8,128)S(1)}, f32[1,2,4,16,128]{4,3,2,1,0:T(8,128)S(1)}, u32[]{:S(2)}, u32[]{:S(2)}) collective-permute-start(f32[1,2,4,16,128]{4,3,2,1,0:T(8,128)S(1)} %add_add_fusion), channel_id=1, source_target_pairs={{0,16},{4,20},{8,24},{12,28},{16,0},{20,4},{24,8},{28,12},{1,17},{... | collective-permute-start | bytes 196616 | tf_op jit(solution)/shard_map/ppermute | solution.py:436
  38.0 4.3 %collective-permute-start.10 = (f32[1,2,4,16,128]{4,3,2,1,0:T(8,128)S(1)}, f32[1,2,4,16,128]{4,3,2,1,0:T(8,128)S(1)}, u32[]{:S(2)}, u32[]{:S(2)}) collective-permute-start(f32[1,2,4,16,128]{4,3,2,1,0:T(8,128)S(1)} %pad_maximum_fusion.2.refs_0_), channel_id=1, source_target_pairs={{0,8},{4,12},{8,0},{12,4},{16,24},{20,28},{24,16},{28,20},{1,9},{5... | collective-permute-start | bytes 196616 | tf_op jit(solution)/shard_map/ppermute | solution.py:436
  38.1 5.3 %collective-permute-start.11 = (f32[1,2,4,16,128]{4,3,2,1,0:T(8,128)S(1)}, f32[1,2,4,16,128]{4,3,2,1,0:T(8,128)S(1)}, u32[]{:S(2)}, u32[]{:S(2)}) collective-permute-start(f32[1,2,4,16,128]{4,3,2,1,0:T(8,128)S(1)} %pad_maximum_fusion.2.refs_0_), channel_id=1, source_target_pairs={{0,12},{4,8},{8,4},{12,0},{16,28},{20,24},{24,20},{28,16},{1,13},{... | collective-permute-start | bytes 196616 | tf_op jit(solution)/shard_map/ppermute | solution.py:436
  39.5 4.6 %collective-permute-start.9 = (f32[1,2,4,16,128]{4,3,2,1,0:T(8,128)S(1)}, f32[1,2,4,16,128]{4,3,2,1,0:T(8,128)S(1)}, u32[]{:S(2)}, u32[]{:S(2)}) collective-permute-start(f32[1,2,4,16,128]{4,3,2,1,0:T(8,128)S(1)} %pad_maximum_fusion.2.refs_0_), channel_id=1, source_target_pairs={{0,4},{4,0},{8,12},{12,8},{16,20},{20,16},{24,28},{28,24},{1,5},{5... | collective-permute-start | bytes 196616 | tf_op jit(solution)/shard_map/ppermute | solution.py:436
  44.2 4.3 %collective-permute-start.12 = (f32[8,16,128]{2,1,0:T(8,128)S(1)}, f32[8,16,128]{2,1,0:T(8,128)S(1)}, u32[]{:S(2)}, u32[]{:S(2)}) collective-permute-start(f32[8,16,128]{2,1,0:T(8,128)S(1)} %get-tuple-element.44), channel_id=1, source_target_pairs={{0,3},{1,2},{2,1},{3,0},{4,7},{5,6},{6,5},{7,4},{8,11},{9,10},{10,... | collective-permute-start | bytes 196616 | tf_op jit(solution)/shard_map/ppermute | solution.py:547
  44.2 4.3 %collective-permute-start.13 = (f32[8,16,128]{2,1,0:T(8,128)S(1)}, f32[8,16,128]{2,1,0:T(8,128)S(1)}, u32[]{:S(2)}, u32[]{:S(2)}) collective-permute-start(f32[8,16,128]{2,1,0:T(8,128)S(1)} %get-tuple-element.45), channel_id=1, source_target_pairs={{0,1},{1,0},{2,3},{3,2},{4,5},{5,4},{6,7},{7,6},{8,9},{9,8},{10,11... | collective-permute-start | bytes 196616 | tf_op jit(solution)/shard_map/ppermute | solution.py:436

commit v7 on v6

--- a/solution.py
+++ b/solution.py
@@ -219,14 +219,21 @@
 
 
 def late_kernel(planes, *refs):
-    far, mine, other = refs[:3]
-    w_ref = refs[8]
-    b0, pd, b1, hi_b, lo_b, hi_a, lo_a, past, *xys = refs[9:]
+    rims, far, mine, other, relayed = refs[:5]
+    w_ref = refs[10]
+    b0, pd, b1, hi_b, lo_b, hi_a, lo_a, past, *xys = refs[11:]
     odd = lax.rem(lax.axis_index("grid"), 2)
     half = lax.rem(lax.axis_index("modes"), 2)
     base = pl.multiple_of(odd * (2 * planes), 16)
     clear_rows(b0, pl.multiple_of(odd * (3 * planes + 8), 8))
-    place_rows(far, 0, base, b0, pd, hi_a, lo_a, 0)
+    for c in range(4):
+        for j in range(8):
+            lanes = slice(j * LANES, (j + 1) * LANES)
+            value = jnp.concatenate(
+                [rims[c, :REACH, lanes], far[c, :, lanes], rims[c, REACH:, lanes]], axis=0
+            )
+            b0[c, j, pl.ds(pl.multiple_of(base + 8, 8), planes), :] = value
+            put_split(value, c, j, 0, hi_a, lo_a)
     for ref, which in ((mine, half), (other, 1 - half)):
         row = pl.multiple_of(base + which * (planes // 2), 8)
         place_rows(ref, 4, row, b0, pd, hi_a, lo_a, 0)
@@ -238,28 +245,34 @@
     for c in range(4):
         for j in range(8):
             lanes = slice(j * LANES, (j + 1) * LANES)
-            ahead, behind = far[c, planes - REACH :, lanes], far[c, :REACH, lanes]
+            ahead, behind = rims[c, REACH:, lanes], rims[c, :REACH, lanes]
             past[c, j, 0:REACH, :] = jnp.where(odd == 0, ahead, none)
             past[c, j, 24 : 24 + REACH, :] = jnp.where(odd == 0, none, behind)
     row = pl.multiple_of(planes + odd * (planes - 8), 8)
     add_share(past, b1, hi_b, lo_b, row, (LEAD, TAIL))
-
-
-def stages_kernel(far, planes, low_bits, *refs):
-    lead_ref, tail_ref, b0, pd = refs[:4]
-    w_ref = refs[7]
-    psi1_ref, kin1_ref, sums_ref, b1, hi_b, lo_b = refs[8:14]
-    b2, b3, b4, hi_a, lo_a, past, *xys = refs[14:]
-    quarter = lax.rem(lax.axis_index("modes"), low_bits)
-
+    add_far_share(past, b1, hi_b, lo_b, planes, relayed, REACH, relayed, 0)
+
+
+def add_far_share(past, b1, hi, lo, planes, lead_ref, lead, tail_ref, tail):
     clear_past(past)
     for c in range(4):
         for j in range(8):
             lanes = slice(j * LANES, (j + 1) * LANES)
-            past[c, j, 0:REACH, :] = lead_ref[c, far[0] : far[0] + REACH, lanes]
-            past[c, j, 24 : 24 + REACH, :] = tail_ref[c, far[1] : far[1] + REACH, lanes]
-    add_share(past, b1, hi_b, lo_b, 0, (LEAD,))
-    add_share(past, b1, hi_b, lo_b, planes + 24, (TAIL,))
+            past[c, j, 0:REACH, :] = lead_ref[c, lead : lead + REACH, lanes]
+            past[c, j, 24 : 24 + REACH, :] = tail_ref[c, tail : tail + REACH, lanes]
+    add_share(past, b1, hi, lo, 0, (LEAD,))
+    add_share(past, b1, hi, lo, planes + 24, (TAIL,))
+
+
+def stages_kernel(ends, planes, low_bits, *refs):
+    n = 2 if ends else 0
+    b0, pd = refs[n : n + 2]
+    w_ref = refs[n + 5]
+    psi1_ref, kin1_ref, sums_ref, b1, hi_b, lo_b = refs[n + 6 : n + 12]
+    b2, b3, b4, hi_a, lo_a, past, *xys = refs[n + 12 :]
+    quarter = lax.rem(lax.axis_index("modes"), low_bits)
+    if ends:
+        add_far_share(past, b1, hi_b, lo_b, planes, refs[0], 0, refs[1], 0)
 
     def last(j, r, count, row, f, near):
         k = derivative(pd, j, row, count, f, near)
@@ -467,20 +480,21 @@
         upper = lax.rem(lax.axis_index("modes"), 2) == 1
         picked = jnp.where(upper, own[4:, part:], own[4:, :part])
         mine = lax.ppermute(picked, "grid", cross)
-        far = lax.ppermute(own[:4], "grid", cross)
+        rims = jnp.concatenate([own[:4, :REACH], own[:4, planes - REACH :]], axis=1)
+        rims = lax.ppermute(rims, "grid", cross)
+        far = lax.ppermute(own[:4, REACH : planes - REACH], "grid", cross)
         near = exchange_xor(own, "grid", 1, slabs)
         other = exchange_xor(mine, "modes", 1, modes)
         ready = call(functools.partial(early_kernel, planes), buffers, [split, split, product], [own, near, weights])
-        far, other = lax.optimization_barrier((far, other))
-        both = jnp.concatenate([far[:, :REACH], far[:, planes - REACH :]], axis=1)
-        lead_far = tail_far = exchange_xor(both, "grid", 1, slabs)
-        past_rows = (REACH, 0)
+        relayed = exchange_xor(rims, "grid", 1, slabs)
+        far, other, relayed = lax.optimization_barrier((far, other, relayed))
+        ends = []
         b0, pd, b1, hi, lo = call(
             functools.partial(late_kernel, planes),
             buffers,
             [split, split, past, product],
-            [far, mine, other, *ready, weights],
-            {3 + i: i for i in range(5)},
+            [rims, far, mine, other, relayed, *ready, weights],
+            {5 + i: i for i in range(5)},
         )
     else:
         pieces, arrays = [16], [own]
@@ -499,15 +513,15 @@
                 pieces += [16 - reach - count, 16 + planes + reach]
                 arrays += [before, after]
             else:
-                lead_far, tail_far, past_rows = before, after, (0, 0)
+                ends = [before, after]
             reach += count
         b0, pd, b1, hi, lo = call(
             functools.partial(first_kernel, pieces, planes), buffers, [split, split, product], arrays + [weights]
         )
 
-    inputs = [lead_far, tail_far, b0, pd, b1, hi, lo, weights]
+    inputs = [*ends, b0, pd, b1, hi, lo, weights]
     psi1, kin1, sums, *rest = call(
-        functools.partial(stages_kernel, past_rows, planes, low_bits),
+        functools.partial(stages_kernel, bool(ends), planes, low_bits),
         [state, state, (4, 2, 4, planes, LANES), b1.shape, split, split],
         [
             ((4, 8, tall + 8, LANES), f32),
@@ -520,7 +534,7 @@
             product,
         ],
         inputs,
-        {4: 3, 5: 4, 6: 5},
+        {len(ends) + 2 + i: 3 + i for i in range(3)},
     )
 
     if low_bits == 4:

time: 49.5 us -> 47.2 us (0.954)
  waiting for transfers between devices: 22.9 us -> 20 us
  starting transfers between devices: 17.3 us -> 17.8 us
    ppermute x1, waiting for transfers between devices: 7.97 us -> 1.63 us  [local(): mine = lax.ppermute(picked, 'grid', cross)]
    ppermute x1 -> x2, waiting for transfers between devices: 0.01 us -> 3.23 us  [the longest x1 1.98 us: local(): rims = lax.ppermute(rims, 'grid', cross)]
    ppermute x1 -> x2, starting transfers between devices: 2.47 us -> 4.44 us  [the longest x1 2.65 us: local(): rims = lax.ppermute(rims, 'grid', cross)]
    ppermute x11, starting transfers between devices: 14.7 us -> 13.2 us  [exchange_xor(): return lax.ppermute(x, axis, [(i, i ^ bits) for i in range(count)])]
  transfers between devices with their start and end apart: 14 -> 15, of which waited for: 10 -> 11; matrix products, arithmetic and copies ran while one was open for 0% -> 0% of each run, Pallas kernels for 6% -> 3%
where the time goes in v7:
time: 47.2 us; the launch traced here: 47.1 us
  waiting for transfers between devices  20 us (42%)
  starting transfers between devices  17.8 us (38%)
  Pallas kernels  7.25 us (15%)
  other arithmetic  1.23 us (3%)
  between operations  0.74 us (2%)
    ppermute x11, waiting for transfers between devices, exchange_xor(): return lax.ppermute(x, axis, [(i, i ^ bits) for i in range(count)])  13.6 us
    ppermute x11, starting transfers between devices, exchange_xor(): return lax.ppermute(x, axis, [(i, i ^ bits) for i in range(count)])  13.2 us
    pallas_call x6, Pallas kernels, call(): pl.pallas_call(kernel, out_shape=tuple((jax.ShapeDtypeStruct(s, d) for s,...  7.25 us
    ppermute x1, starting transfers between devices, local(): rims = lax.ppermute(rims, 'grid', cross)  2.65 us
    ppermute x1, waiting for transfers between devices, local(): rims = lax.ppermute(rims, 'grid', cross)  1.98 us
    ppermute x1, starting transfers between devices, local(): far = lax.ppermute(own[:4, REACH:planes - REACH], 'grid', cross)  1.79 us
    ppermute x1, waiting for transfers between devices, local(): mine = lax.ppermute(picked, 'grid', cross)  1.63 us
    ppermute x1, waiting for transfers between devices, local(): first = lax.ppermute(first, 'grid', cross)  1.51 us
  transfers between devices with their start and end apart: 15, of which 11 were waited for; matrix products, arithmetic and copies ran while one was open for 0% of the time, Pallas kernels for 3%

profile of v7, /device:TPU:0, one launch (start us, length us, event | category | flops | bytes accessed | tf_op | source)
XLA Modules:
  0.0 47.1 jit_solution(13947885557196599490)
XLA Ops:
  0.6 1.1 %pad_maximum_fusion.refs_0_ = f32[7,16,1024]{2,1,0:T(8,128)S(1)} fusion(f32[2,16,1024]{2,1,0:T(8,128)} %param.8, f32[1,16,1024]{2,1,0:T(8,128)} %bitcast.5, f32[2,16,1024]{2,1,0:T(8,128)} %bitcast.3, f32[2,16,1024]{2,1,0:T(8,128)} %bitcast.4), kind=kLoop, calls=%fused_computation | loop fusion | flops 344064 | bytes 917504 | tf_op jit(solution)/shard_map/concatenate | solution.py:460
  1.7 0.0 copy-start
  1.7 0.6 %collective-permute-start.5 = (f32[7,16,1024]{2,1,0:T(8,128)S(1)}, f32[7,16,1024]{2,1,0:T(8,128)S(1)}, u32[]{:S(2)}, u32[]{:S(2)}) collective-permute-start(f32[7,16,1024]{2,1,0:T(8,128)S(1)} %pad_maximum_fusion.refs_0_), channel_id=1, source_target_pairs={{0,1},{1,0},{2,3},{3,2},{4,5},{5,4},{6,7},{7,6},{8,9},{9,8},{10,11... | collective-permute-start | bytes 1376264 | tf_op jit(solution)/shard_map/ppermute | solution.py:449
  2.4 2.7 %collective-permute-start = (f32[4,8,1024]{2,1,0:T(8,128)S(1)}, f32[4,8,1024]{2,1,0:T(8,128)S(1)}, u32[]{:S(2)}, u32[]{:S(2)}) collective-permute-start(f32[4,8,1024]{2,1,0:T(8,128)S(1)} %pad_maximum_fusion.1), channel_id=1, source_target_pairs={{0,3},{1,2},{2,1},{3,0},{4,7},{5,6},{6,5},{7,4},{8,11},{9,10},{10,... | collective-permute-start | bytes 393224 | tf_op jit(solution)/shard_map/ppermute | solution.py:484
  5.0 0.1 collective-permute-start.2
  5.1 1.8 %collective-permute-start.1 = (f32[4,8,1024]{2,1,0:T(8,128)S(1)}, f32[4,8,1024]{2,1,0:T(8,128)S(1)}, u32[]{:S(2)}, u32[]{:S(2)}) collective-permute-start(f32[4,8,1024]{2,1,0:T(8,128)S(1)} %slice.54), channel_id=1, source_target_pairs={{0,3},{1,2},{2,1},{3,0},{4,7},{5,6},{6,5},{7,4},{8,11},{9,10},{10,... | collective-permute-start | bytes 393224 | tf_op jit(solution)/shard_map/ppermute | solution.py:485
  6.9 2.0 %collective-permute-done.refs_0_ = f32[4,8,1024]{2,1,0:T(8,128)S(1)} collective-permute-done((f32[4,8,1024]{2,1,0:T(8,128)S(1)}, f32[4,8,1024]{2,1,0:T(8,128)S(1)}, u32[]{:S(2)}, u32[]{:S(2)}) %collective-permute-start) | collective-permute-done | bytes 131104 | tf_op jit(solution)/shard_map/ppermute | solution.py:484
  8.9 0.5 %collective-permute-start.4 = (f32[4,8,1024]{2,1,0:T(8,128)S(1)}, f32[4,8,1024]{2,1,0:T(8,128)S(1)}, u32[]{:S(2)}, u32[]{:S(2)}) collective-permute-start(f32[4,8,1024]{2,1,0:T(8,128)S(1)} %collective-permute-done.refs_0_), channel_id=1, source_target_pairs={{0,1},{1,0},{2,3},{3,2},{4,5},{5,4},{6,7},{7,6},{8,9},{9,8},{10,11... | collective-permute-start | bytes 393224 | tf_op jit(solution)/shard_map/ppermute | solution.py:449
  9.4 1.6 %collective-permute-done.2.refs_2_ = f32[3,8,1024]{2,1,0:T(8,128)S(1)} collective-permute-done((f32[3,8,1024]{2,1,0:T(8,128)S(1)}, f32[3,8,1024]{2,1,0:T(8,128)S(1)}, u32[]{:S(2)}, u32[]{:S(2)}) %collective-permute-start.2) | collective-permute-done | bytes 98336 | tf_op jit(solution)/shard_map/ppermute | solution.py:482
  11.0 1.5 %collective-permute-start.3 = (f32[3,8,1024]{2,1,0:T(8,128)S(1)}, f32[3,8,1024]{2,1,0:T(8,128)S(1)}, u32[]{:S(2)}, u32[]{:S(2)}) collective-permute-start(f32[3,8,1024]{2,1,0:T(8,128)S(1)} %collective-permute-done.2.refs_2_), channel_id=1, source_target_pairs={{0,4},{4,0},{8,12},{12,8},{16,20},{20,16},{24,28},{28,24},{1,5},{5... | collective-permute-start | bytes 294920 | tf_op jit(solution)/shard_map/ppermute | solution.py:449
  12.5 1.3 %collective-permute-done.1.refs_1_ = f32[4,8,1024]{2,1,0:T(8,128)S(1)} collective-permute-done((f32[4,8,1024]{2,1,0:T(8,128)S(1)}, f32[4,8,1024]{2,1,0:T(8,128)S(1)}, u32[]{:S(2)}, u32[]{:S(2)}) %collective-permute-start.1) | collective-permute-done | bytes 131104 | tf_op jit(solution)/shard_map/ppermute | solution.py:485
  13.8 2.8 %collective-permute-done.3.refs_3_ = f32[3,8,1024]{2,1,0:T(8,128)S(1)} collective-permute-done((f32[3,8,1024]{2,1,0:T(8,128)S(1)}, f32[3,8,1024]{2,1,0:T(8,128)S(1)}, u32[]{:S(2)}, u32[]{:S(2)}) %collective-permute-start.3) | collective-permute-done | bytes 98336 | tf_op jit(solution)/shard_map/ppermute | solution.py:449
  16.6 0.0 collective-permute-done.4.refs_4_
  16.6 0.0 collective-permute-done.5.refs_1_
  16.6 0.0 copy-done
  16.6 1.1 %shard_map.76 = (f32[4,8,64,128]{3,2,1,0:T(8,128)S(1)}, f32[3,8,48,128]{3,2,1,0:T(8,128)S(1)}, f32[4,8,56,128]{3,2,1,0:T(8,128)S(1)}, bf16[4,4,48,512]{3,2,1,0:T(8,128)(2,1)S(1)}, bf16[4,4,48,512]{3,2,1,0:T(8,128)(2,1)S(1)}) custom-call(f32[7,16,1024]{2,1,0:T(8,128)S(1)} %pad_maximum_fusion.refs_0_, f32[7,16,1024]{2,1,0:T(8,128)S(1)} %collective-permute-done.5.refs_1_, ...), custom_call_target="tpu_custom_call" | custom-call | flops 2850816000 | bytes 11403264 | tf_op jit(solution)/shard_map/pallas_call | solution.py:436
  17.7 0.9 %shard_map.77 = (f32[4,8,64,128]{3,2,1,0:T(8,128)S(1)}, f32[3,8,48,128]{3,2,1,0:T(8,128)S(1)}, f32[4,8,56,128]{3,2,1,0:T(8,128)S(1)}, bf16[4,4,48,512]{3,2,1,0:T(8,128)(2,1)S(1)}, bf16[4,4,48,512]{3,2,1,0:T(8,128)(2,1)S(1)}) custom-call(f32[4,8,1024]{2,1,0:T(8,128)S(1)} %collective-permute-do, ...), custom_call_target="tpu_custom_call", output_to_operand_aliasing={{0}: (5, {}), {1}: (6, {}), {2}: (7, {}), {3}: (8, {}), {4}... | custom-call | flops 2850816000 | bytes 11403264 | tf_op jit(solution)/shard_map/pallas_call | solution.py:436
  18.6 2.9 %shard_map.78 = (f32[4,8,16,128]{3,2,1,0:T(8,128)S(1)}, f32[4,8,16,128]{3,2,1,0:T(8,128)S(1)}, f32[4,2,4,16,128]{4,3,2,1,0:T(8,128)S(1)}, f32[4,8,56,128]{3,2,1,...) custom-call(f32[4,8,64,128]{3,2,1,0:T(8,128)S(1)} %get-tuple-element, ...), custom_call_target="tpu_custom_call", output_to_operand_aliasing={{3}: (2, {}), {4}: (3, {}), {5}: (4, {})} | custom-call | flops 2424832000 | bytes 9699328 | tf_op jit(solution)/shard_map/pallas_call | solution.py:436
  21.6 1.5 %collective-permute-start.6 = (f32[1,2,4,16,128]{4,3,2,1,0:T(8,128)S(1)}, f32[1,2,4,16,128]{4,3,2,1,0:T(8,128)S(1)}, u32[]{:S(2)}, u32[]{:S(2)}) collective-permute-start(f32[1,2,4,16,128]{4,3,2,1,0:T(8,128)S(1)} %get-tuple-element.53), channel_id=1, source_target_pairs={{0,4},{4,0},{8,12},{12,8},{16,20},{20,16},{24,28},{28,24},{1,5},{5... | collective-permute-start | bytes 196616 | tf_op jit(solution)/shard_map/ppermute | solution.py:449
  23.2 1.5 %collective-permute-start.8 = (f32[1,2,4,16,128]{4,3,2,1,0:T(8,128)S(1)}, f32[1,2,4,16,128]{4,3,2,1,0:T(8,128)S(1)}, u32[]{:S(2)}, u32[]{:S(2)}) collective-permute-start(f32[1,2,4,16,128]{4,3,2,1,0:T(8,128)S(1)} %get-tuple-element.54), channel_id=1, source_target_pairs={{0,12},{4,8},{8,4},{12,0},{16,28},{20,24},{24,20},{28,16},{1,13},{... | collective-permute-start | bytes 196616 | tf_op jit(solution)/shard_map/ppermute | solution.py:449
  24.7 0.5 %collective-permute-start.7 = (f32[1,2,4,16,128]{4,3,2,1,0:T(8,128)S(1)}, f32[1,2,4,16,128]{4,3,2,1,0:T(8,128)S(1)}, u32[]{:S(2)}, u32[]{:S(2)}) collective-permute-start(f32[1,2,4,16,128]{4,3,2,1,0:T(8,128)S(1)} %get-tuple-element.55), channel_id=1, source_target_pairs={{0,8},{4,12},{8,0},{12,4},{16,24},{20,28},{24,16},{28,20},{1,9},{5... | collective-permute-start | bytes 196616 | tf_op jit(solution)/shard_map/ppermute | solution.py:449
  25.2 0.8 %collective-permute-done.6 = f32[1,2,4,16,128]{4,3,2,1,0:T(8,128)S(1)} collective-permute-done((f32[1,2,4,16,128]{4,3,2,1,0:T(8,128)S(1)}, f32[1,2,4,16,128]{4,3,2,1,0:T(8,128)S(1)}, u32[]{:S(2)}, u32[]{:S(2)}) %collective-permute-start.6) | collective-permute-done | bytes 65568 | tf_op jit(solution)/shard_map/ppermute | solution.py:449
  25.9 3.0 %collective-permute-done.8 = f32[1,2,4,16,128]{4,3,2,1,0:T(8,128)S(1)} collective-permute-done((f32[1,2,4,16,128]{4,3,2,1,0:T(8,128)S(1)}, f32[1,2,4,16,128]{4,3,2,1,0:T(8,128)S(1)}, u32[]{:S(2)}, u32[]{:S(2)}) %collective-permute-start.8) | collective-permute-done | bytes 65568 | tf_op jit(solution)/shard_map/ppermute | solution.py:449
  29.0 0.0 collective-permute-done.7
  29.0 2.7 %collective-permute-start.9 = (f32[1,2,4,16,128]{4,3,2,1,0:T(8,128)S(1)}, f32[1,2,4,16,128]{4,3,2,1,0:T(8,128)S(1)}, u32[]{:S(2)}, u32[]{:S(2)}) collective-permute-start(f32[1,2,4,16,128]{4,3,2,1,0:T(8,128)S(1)} %add_add_fusion), channel_id=1, source_target_pairs={{0,16},{4,20},{8,24},{12,28},{16,0},{20,4},{24,8},{28,12},{1,17},{... | collective-permute-start | bytes 196616 | tf_op jit(solution)/shard_map/ppermute | solution.py:449
  31.7 3.3 %collective-permute-done.9 = f32[1,2,4,16,128]{4,3,2,1,0:T(8,128)S(1)} collective-permute-done((f32[1,2,4,16,128]{4,3,2,1,0:T(8,128)S(1)}, f32[1,2,4,16,128]{4,3,2,1,0:T(8,128)S(1)}, u32[]{:S(2)}, u32[]{:S(2)}) %collective-permute-start.9) | collective-permute-done | bytes 65568 | tf_op jit(solution)/shard_map/ppermute | solution.py:449
  34.9 0.1 divide_subtract_fusion
  35.0 1.2 %collective-permute-start.12 = (f32[1,2,4,16,128]{4,3,2,1,0:T(8,128)S(1)}, f32[1,2,4,16,128]{4,3,2,1,0:T(8,128)S(1)}, u32[]{:S(2)}, u32[]{:S(2)}) collective-permute-start(f32[1,2,4,16,128]{4,3,2,1,0:T(8,128)S(1)} %pad_maximum_fusion.2.refs_0_), channel_id=1, source_target_pairs={{0,12},{4,8},{8,4},{12,0},{16,28},{20,24},{24,20},{28,16},{1,13},{... | collective-permute-start | bytes 196616 | tf_op jit(solution)/shard_map/ppermute | solution.py:449
  36.3 1.8 %collective-permute-start.11 = (f32[1,2,4,16,128]{4,3,2,1,0:T(8,128)S(1)}, f32[1,2,4,16,128]{4,3,2,1,0:T(8,128)S(1)}, u32[]{:S(2)}, u32[]{:S(2)}) collective-permute-start(f32[1,2,4,16,128]{4,3,2,1,0:T(8,128)S(1)} %pad_maximum_fusion.2.refs_0_), channel_id=1, source_target_pairs={{0,8},{4,12},{8,0},{12,4},{16,24},{20,28},{24,16},{28,20},{1,9},{5... | collective-permute-start | bytes 196616 | tf_op jit(solution)/shard_map/ppermute | solution.py:449
  38.0 0.6 %collective-permute-start.10 = (f32[1,2,4,16,128]{4,3,2,1,0:T(8,128)S(1)}, f32[1,2,4,16,128]{4,3,2,1,0:T(8,128)S(1)}, u32[]{:S(2)}, u32[]{:S(2)}) collective-permute-start(f32[1,2,4,16,128]{4,3,2,1,0:T(8,128)S(1)} %pad_maximum_fusion.2.refs_0_), channel_id=1, source_target_pairs={{0,4},{4,0},{8,12},{12,8},{16,20},{20,16},{24,28},{28,24},{1,5},{5... | collective-permute-start | bytes 196616 | tf_op jit(solution)/shard_map/ppermute | solution.py:449
  38.6 1.7 %collective-permute-done.12.refs_3_ = f32[1,2,4,16,128]{4,3,2,1,0:T(8,128)S(1)} collective-permute-done((f32[1,2,4,16,128]{4,3,2,1,0:T(8,128)S(1)}, f32[1,2,4,16,128]{4,3,2,1,0:T(8,128)S(1)}, u32[]{:S(2)}, u32[]{:S(2)}) %collective-permute-start.12) | collective-permute-done | bytes 65568 | tf_op jit(solution)/shard_map/ppermute | solution.py:449
  40.3 0.7 %collective-permute-done.11.refs_2_ = f32[1,2,4,16,128]{4,3,2,1,0:T(8,128)S(1)} collective-permute-done((f32[1,2,4,16,128]{4,3,2,1,0:T(8,128)S(1)}, f32[1,2,4,16,128]{4,3,2,1,0:T(8,128)S(1)}, u32[]{:S(2)}, u32[]{:S(2)}) %collective-permute-start.11) | collective-permute-done | bytes 65568 | tf_op jit(solution)/shard_map/ppermute | solution.py:449
  41.0 1.3 %collective-permute-done.10.refs_1_ = f32[1,2,4,16,128]{4,3,2,1,0:T(8,128)S(1)} collective-permute-done((f32[1,2,4,16,128]{4,3,2,1,0:T(8,128)S(1)}, f32[1,2,4,16,128]{4,3,2,1,0:T(8,128)S(1)}, u32[]{:S(2)}, u32[]{:S(2)}) %collective-permute-start.10) | collective-permute-done | bytes 65568 | tf_op jit(solution)/shard_map/ppermute | solution.py:449
  42.3 0.1 shard_map.79
  42.4 0.1 collective-permute-start.13
  42.5 0.9 %collective-permute-start.14 = (f32[8,16,128]{2,1,0:T(8,128)S(1)}, f32[8,16,128]{2,1,0:T(8,128)S(1)}, u32[]{:S(2)}, u32[]{:S(2)}) collective-permute-start(f32[8,16,128]{2,1,0:T(8,128)S(1)} %get-tuple-element.47), channel_id=1, source_target_pairs={{0,1},{1,0},{2,3},{3,2},{4,5},{5,4},{6,7},{7,6},{8,9},{9,8},{10,11... | collective-permute-start | bytes 196616 | tf_op jit(solution)/shard_map/ppermute | solution.py:449
  43.4 1.3 %shard_map.80 = (f32[4,8,16,128]{3,2,1,0:T(8,128)S(1)}, f32[4,16,1024]{2,1,0:T(8,128)}) custom-call(f32[4,8,16,128]{3,2,1,0:T(8,128)S(1)} %get-tuple-element.40.refs_4_.refs_0_, f32[4,8,16,128]{3,2,1,0:T(8,128)S(1)} %get-tuple-element.41.refs_5_.refs_1_, f32[4,8,16,128]{3,2,1,0:T(8,128)S(1)} %get-tuple-element.43.refs_2_, ...), custom_call_target="tpu_custom_call" | custom-call | flops 262144000 | bytes 1048576 | tf_op jit(solution)/shard_map/pallas_call | solution.py:436
  44.7 1.5 %collective-permute-done.13.refs_1_ = f32[8,16,128]{2,1,0:T(8,128)S(1)} collective-permute-done((f32[8,16,128]{2,1,0:T(8,128)S(1)}, f32[8,16,128]{2,1,0:T(8,128)S(1)}, u32[]{:S(2)}, u32[]{:S(2)}) %collective-permute-start.13) | collective-permute-done | bytes 65568 | tf_op jit(solution)/shard_map/ppermute | solution.py:561
  46.2 0.0 collective-permute-done.14.refs_2_
  46.2 0.9 %shard_map.81 = (f32[1,2,16,1024]{3,2,1,0:T(8,128)}, f32[1,2,16,1024]{3,2,1,0:T(8,128)}) custom-call(f32[4,8,16,128]{3,2,1,0:T(8,128)S(1)} %get-tuple-element.45.refs_0_, f32[8,16,128]{2,1,0:T(8,128)S(1)} %collective-permute-done.13.refs_1_, f32[8,16,128]{2,1,0:T(8,128)S(1)} %collective-permute-done.14.refs_2_), custom_call_target="tpu_custom_call" | custom-call | flops 131072000 | bytes 524288 | tf_op jit(solution)/shard_map/pallas_call | solution.py:436
  (8 shorter events, 0.1 us)
Async XLA Ops:
  1.7 14.9 %copy-start = (bf16[1024,256]{1,0:T(8,128)(2,1)S(1)}, bf16[1024,256]{1,0:T(8,128)(2,1)}, u32[]{:S(2)}) copy-start(bf16[1024,256]{1,0:T(8,128)(2,1)} %constant.55.clone.refs_2_.refs_10_.refs_5_.refs_4_) | copy-start | bytes 1572868
  1.7 14.9 %collective-permute-start.5 = (f32[7,16,1024]{2,1,0:T(8,128)S(1)}, f32[7,16,1024]{2,1,0:T(8,128)S(1)}, u32[]{:S(2)}, u32[]{:S(2)}) collective-permute-start(f32[7,16,1024]{2,1,0:T(8,128)S(1)} %pad_maximum_fusion.refs_0_), channel_id=1, source_target_pairs={{0,1},{1,0},{2,3},{3,2},{4,5},{5,4},{6,7},{7,6},{8,9},{9,8},{10,11... | collective-permute-start | bytes 1376264 | tf_op jit(solution)/shard_map/ppermute | solution.py:449
  2.4 6.5 %collective-permute-start = (f32[4,8,1024]{2,1,0:T(8,128)S(1)}, f32[4,8,1024]{2,1,0:T(8,128)S(1)}, u32[]{:S(2)}, u32[]{:S(2)}) collective-permute-start(f32[4,8,1024]{2,1,0:T(8,128)S(1)} %pad_maximum_fusion.1), channel_id=1, source_target_pairs={{0,3},{1,2},{2,1},{3,0},{4,7},{5,6},{6,5},{7,4},{8,11},{9,10},{10,... | collective-permute-start | bytes 393224 | tf_op jit(solution)/shard_map/ppermute | solution.py:484
  5.0 6.0 %collective-permute-start.2 = (f32[3,8,1024]{2,1,0:T(8,128)S(1)}, f32[3,8,1024]{2,1,0:T(8,128)S(1)}, u32[]{:S(2)}, u32[]{:S(2)}) collective-permute-start(f32[3,8,1024]{2,1,0:T(8,128)S(1)} %slice_select_fusion), channel_id=1, source_target_pairs={{0,3},{1,2},{2,1},{3,0},{4,7},{5,6},{6,5},{7,4},{8,11},{9,10},{10,... | collective-permute-start | bytes 294920 | tf_op jit(solution)/shard_map/ppermute | solution.py:482
  5.1 8.6 %collective-permute-start.1 = (f32[4,8,1024]{2,1,0:T(8,128)S(1)}, f32[4,8,1024]{2,1,0:T(8,128)S(1)}, u32[]{:S(2)}, u32[]{:S(2)}) collective-permute-start(f32[4,8,1024]{2,1,0:T(8,128)S(1)} %slice.54), channel_id=1, source_target_pairs={{0,3},{1,2},{2,1},{3,0},{4,7},{5,6},{6,5},{7,4},{8,11},{9,10},{10,... | collective-permute-start | bytes 393224 | tf_op jit(solution)/shard_map/ppermute | solution.py:485
  8.9 7.7 %collective-permute-start.4 = (f32[4,8,1024]{2,1,0:T(8,128)S(1)}, f32[4,8,1024]{2,1,0:T(8,128)S(1)}, u32[]{:S(2)}, u32[]{:S(2)}) collective-permute-start(f32[4,8,1024]{2,1,0:T(8,128)S(1)} %collective-permute-done.refs_0_), channel_id=1, source_target_pairs={{0,1},{1,0},{2,3},{3,2},{4,5},{5,4},{6,7},{7,6},{8,9},{9,8},{10,11... | collective-permute-start | bytes 393224 | tf_op jit(solution)/shard_map/ppermute | solution.py:449
  11.0 5.6 %collective-permute-start.3 = (f32[3,8,1024]{2,1,0:T(8,128)S(1)}, f32[3,8,1024]{2,1,0:T(8,128)S(1)}, u32[]{:S(2)}, u32[]{:S(2)}) collective-permute-start(f32[3,8,1024]{2,1,0:T(8,128)S(1)} %collective-permute-done.2.refs_2_), channel_id=1, source_target_pairs={{0,4},{4,0},{8,12},{12,8},{16,20},{20,16},{24,28},{28,24},{1,5},{5... | collective-permute-start | bytes 294920 | tf_op jit(solution)/shard_map/ppermute | solution.py:449
  21.6 4.3 %collective-permute-start.6 = (f32[1,2,4,16,128]{4,3,2,1,0:T(8,128)S(1)}, f32[1,2,4,16,128]{4,3,2,1,0:T(8,128)S(1)}, u32[]{:S(2)}, u32[]{:S(2)}) collective-permute-start(f32[1,2,4,16,128]{4,3,2,1,0:T(8,128)S(1)} %get-tuple-element.53), channel_id=1, source_target_pairs={{0,4},{4,0},{8,12},{12,8},{16,20},{20,16},{24,28},{28,24},{1,5},{5... | collective-permute-start | bytes 196616 | tf_op jit(solution)/shard_map/ppermute | solution.py:449
  23.2 5.8 %collective-permute-start.8 = (f32[1,2,4,16,128]{4,3,2,1,0:T(8,128)S(1)}, f32[1,2,4,16,128]{4,3,2,1,0:T(8,128)S(1)}, u32[]{:S(2)}, u32[]{:S(2)}) collective-permute-start(f32[1,2,4,16,128]{4,3,2,1,0:T(8,128)S(1)} %get-tuple-element.54), channel_id=1, source_target_pairs={{0,12},{4,8},{8,4},{12,0},{16,28},{20,24},{24,20},{28,16},{1,13},{... | collective-permute-start | bytes 196616 | tf_op jit(solution)/shard_map/ppermute | solution.py:449
  24.7 4.3 %collective-permute-start.7 = (f32[1,2,4,16,128]{4,3,2,1,0:T(8,128)S(1)}, f32[1,2,4,16,128]{4,3,2,1,0:T(8,128)S(1)}, u32[]{:S(2)}, u32[]{:S(2)}) collective-permute-start(f32[1,2,4,16,128]{4,3,2,1,0:T(8,128)S(1)} %get-tuple-element.55), channel_id=1, source_target_pairs={{0,8},{4,12},{8,0},{12,4},{16,24},{20,28},{24,16},{28,20},{1,9},{5... | collective-permute-start | bytes 196616 | tf_op jit(solution)/shard_map/ppermute | solution.py:449
  29.0 5.9 %collective-permute-start.9 = (f32[1,2,4,16,128]{4,3,2,1,0:T(8,128)S(1)}, f32[1,2,4,16,128]{4,3,2,1,0:T(8,128)S(1)}, u32[]{:S(2)}, u32[]{:S(2)}) collective-permute-start(f32[1,2,4,16,128]{4,3,2,1,0:T(8,128)S(1)} %add_add_fusion), channel_id=1, source_target_pairs={{0,16},{4,20},{8,24},{12,28},{16,0},{20,4},{24,8},{28,12},{1,17},{... | collective-permute-start | bytes 196616 | tf_op jit(solution)/shard_map/ppermute | solution.py:449
  35.0 5.2 %collective-permute-start.12 = (f32[1,2,4,16,128]{4,3,2,1,0:T(8,128)S(1)}, f32[1,2,4,16,128]{4,3,2,1,0:T(8,128)S(1)}, u32[]{:S(2)}, u32[]{:S(2)}) collective-permute-start(f32[1,2,4,16,128]{4,3,2,1,0:T(8,128)S(1)} %pad_maximum_fusion.2.refs_0_), channel_id=1, source_target_pairs={{0,12},{4,8},{8,4},{12,0},{16,28},{20,24},{24,20},{28,16},{1,13},{... | collective-permute-start | bytes 196616 | tf_op jit(solution)/shard_map/ppermute | solution.py:449
  36.3 4.7 %collective-permute-start.11 = (f32[1,2,4,16,128]{4,3,2,1,0:T(8,128)S(1)}, f32[1,2,4,16,128]{4,3,2,1,0:T(8,128)S(1)}, u32[]{:S(2)}, u32[]{:S(2)}) collective-permute-start(f32[1,2,4,16,128]{4,3,2,1,0:T(8,128)S(1)} %pad_maximum_fusion.2.refs_0_), channel_id=1, source_target_pairs={{0,8},{4,12},{8,0},{12,4},{16,24},{20,28},{24,16},{28,20},{1,9},{5... | collective-permute-start | bytes 196616 | tf_op jit(solution)/shard_map/ppermute | solution.py:449
  38.0 4.3 %collective-permute-start.10 = (f32[1,2,4,16,128]{4,3,2,1,0:T(8,128)S(1)}, f32[1,2,4,16,128]{4,3,2,1,0:T(8,128)S(1)}, u32[]{:S(2)}, u32[]{:S(2)}) collective-permute-start(f32[1,2,4,16,128]{4,3,2,1,0:T(8,128)S(1)} %pad_maximum_fusion.2.refs_0_), channel_id=1, source_target_pairs={{0,4},{4,0},{8,12},{12,8},{16,20},{20,16},{24,28},{28,24},{1,5},{5... | collective-permute-start | bytes 196616 | tf_op jit(solution)/shard_map/ppermute | solution.py:449
  42.4 3.8 %collective-permute-start.13 = (f32[8,16,128]{2,1,0:T(8,128)S(1)}, f32[8,16,128]{2,1,0:T(8,128)S(1)}, u32[]{:S(2)}, u32[]{:S(2)}) collective-permute-start(f32[8,16,128]{2,1,0:T(8,128)S(1)} %get-tuple-element.46), channel_id=1, source_target_pairs={{0,3},{1,2},{2,1},{3,0},{4,7},{5,6},{6,5},{7,4},{8,11},{9,10},{10,... | collective-permute-start | bytes 196616 | tf_op jit(solution)/shard_map/ppermute | solution.py:561
  42.5 3.7 %collective-permute-start.14 = (f32[8,16,128]{2,1,0:T(8,128)S(1)}, f32[8,16,128]{2,1,0:T(8,128)S(1)}, u32[]{:S(2)}, u32[]{:S(2)}) collective-permute-start(f32[8,16,128]{2,1,0:T(8,128)S(1)} %get-tuple-element.47), channel_id=1, source_target_pairs={{0,1},{1,0},{2,3},{3,2},{4,5},{5,4},{6,7},{7,6},{8,9},{9,8},{10,11... | collective-permute-start | bytes 196616 | tf_op jit(solution)/shard_map/ppermute | solution.py:449

commit v8 on v7

--- a/solution.py
+++ b/solution.py
@@ -540,7 +540,8 @@
     if low_bits == 4:
         total = sums[0:1]
         for k in (1, 2, 3):
-            total = total + exchange_xor(sums[k : k + 1], "modes", k, modes)
+            got = exchange_xor(sums[k : k + 1], "modes", k, modes)
+            total = total + got
     else:
         total = sums
     bits = low_bits
@@ -548,7 +549,9 @@
         total = total + exchange_xor(total, "modes", bits, modes)
         bits *= 2
     quarter = potentials(total, float(u_modes.shape[0] * modes))
-    got = [quarter] + [exchange_xor(quarter, "modes", k, modes) for k in range(1, low_bits)]
+    got = [quarter]
+    for k in range(1, low_bits):
+        got.append(exchange_xor(quarter, "modes", k, modes))
 
     edge = (8, 4 * REACH, LANES)
     mid, first, second, fields_flat = call(

time: 47.2 us -> 47.2 us (level)
  no operation moved by 1% of the time
where the time goes in v8:
time: 47.2 us; the launch traced here: 47.1 us
  waiting for transfers between devices  20 us (42%)
  starting transfers between devices  17.8 us (38%)
  Pallas kernels  7.25 us (15%)
  other arithmetic  1.23 us (3%)
  between operations  0.74 us (2%)
    ppermute x11, waiting for transfers between devices, exchange_xor(): return lax.ppermute(x, axis, [(i, i ^ bits) for i in range(count)])  13.6 us
    ppermute x11, starting transfers between devices, exchange_xor(): return lax.ppermute(x, axis, [(i, i ^ bits) for i in range(count)])  13.2 us
    pallas_call x6, Pallas kernels, call(): pl.pallas_call(kernel, out_shape=tuple((jax.ShapeDtypeStruct(s, d) for s,...  7.25 us
    ppermute x1, starting transfers between devices, local(): rims = lax.ppermute(rims, 'grid', cross)  2.65 us
    ppermute x1, waiting for transfers between devices, local(): rims = lax.ppermute(rims, 'grid', cross)  1.98 us
    ppermute x1, starting transfers between devices, local(): far = lax.ppermute(own[:4, REACH:planes - REACH], 'grid', cross)  1.79 us
    ppermute x1, waiting for transfers between devices, local(): mine = lax.ppermute(picked, 'grid', cross)  1.63 us
    ppermute x1, waiting for transfers between devices, local(): first = lax.ppermute(first, 'grid', cross)  1.51 us
  transfers between devices with their start and end apart: 15, of which 11 were waited for; matrix products, arithmetic and copies ran while one was open for 0% of the time, Pallas kernels for 3%

profile of v8, /device:TPU:0, one launch (start us, length us, event | category | flops | bytes accessed | tf_op | source)
XLA Modules:
  0.0 47.1 jit_solution(13947885557196599490)
XLA Ops:
  0.6 1.1 %pad_maximum_fusion.refs_0_ = f32[7,16,1024]{2,1,0:T(8,128)S(1)} fusion(f32[2,16,1024]{2,1,0:T(8,128)} %param.8, f32[1,16,1024]{2,1,0:T(8,128)} %bitcast.5, f32[2,16,1024]{2,1,0:T(8,128)} %bitcast.3, f32[2,16,1024]{2,1,0:T(8,128)} %bitcast.4), kind=kLoop, calls=%fused_computation | loop fusion | flops 344064 | bytes 917504 | tf_op jit(solution)/shard_map/concatenate | solution.py:460
  1.7 0.0 copy-start
  1.7 0.6 %collective-permute-start.5 = (f32[7,16,1024]{2,1,0:T(8,128)S(1)}, f32[7,16,1024]{2,1,0:T(8,128)S(1)}, u32[]{:S(2)}, u32[]{:S(2)}) collective-permute-start(f32[7,16,1024]{2,1,0:T(8,128)S(1)} %pad_maximum_fusion.refs_0_), channel_id=1, source_target_pairs={{0,1},{1,0},{2,3},{3,2},{4,5},{5,4},{6,7},{7,6},{8,9},{9,8},{10,11... | collective-permute-start | bytes 1376264 | tf_op jit(solution)/shard_map/ppermute | solution.py:449
  2.4 2.7 %collective-permute-start = (f32[4,8,1024]{2,1,0:T(8,128)S(1)}, f32[4,8,1024]{2,1,0:T(8,128)S(1)}, u32[]{:S(2)}, u32[]{:S(2)}) collective-permute-start(f32[4,8,1024]{2,1,0:T(8,128)S(1)} %pad_maximum_fusion.1), channel_id=1, source_target_pairs={{0,3},{1,2},{2,1},{3,0},{4,7},{5,6},{6,5},{7,4},{8,11},{9,10},{10,... | collective-permute-start | bytes 393224 | tf_op jit(solution)/shard_map/ppermute | solution.py:484
  5.0 0.1 collective-permute-start.2
  5.1 1.8 %collective-permute-start.1 = (f32[4,8,1024]{2,1,0:T(8,128)S(1)}, f32[4,8,1024]{2,1,0:T(8,128)S(1)}, u32[]{:S(2)}, u32[]{:S(2)}) collective-permute-start(f32[4,8,1024]{2,1,0:T(8,128)S(1)} %slice.54), channel_id=1, source_target_pairs={{0,3},{1,2},{2,1},{3,0},{4,7},{5,6},{6,5},{7,4},{8,11},{9,10},{10,... | collective-permute-start | bytes 393224 | tf_op jit(solution)/shard_map/ppermute | solution.py:485
  6.9 2.0 %collective-permute-done.refs_0_ = f32[4,8,1024]{2,1,0:T(8,128)S(1)} collective-permute-done((f32[4,8,1024]{2,1,0:T(8,128)S(1)}, f32[4,8,1024]{2,1,0:T(8,128)S(1)}, u32[]{:S(2)}, u32[]{:S(2)}) %collective-permute-start) | collective-permute-done | bytes 131104 | tf_op jit(solution)/shard_map/ppermute | solution.py:484
  8.9 0.5 %collective-permute-start.4 = (f32[4,8,1024]{2,1,0:T(8,128)S(1)}, f32[4,8,1024]{2,1,0:T(8,128)S(1)}, u32[]{:S(2)}, u32[]{:S(2)}) collective-permute-start(f32[4,8,1024]{2,1,0:T(8,128)S(1)} %collective-permute-done.refs_0_), channel_id=1, source_target_pairs={{0,1},{1,0},{2,3},{3,2},{4,5},{5,4},{6,7},{7,6},{8,9},{9,8},{10,11... | collective-permute-start | bytes 393224 | tf_op jit(solution)/shard_map/ppermute | solution.py:449
  9.4 1.6 %collective-permute-done.2.refs_2_ = f32[3,8,1024]{2,1,0:T(8,128)S(1)} collective-permute-done((f32[3,8,1024]{2,1,0:T(8,128)S(1)}, f32[3,8,1024]{2,1,0:T(8,128)S(1)}, u32[]{:S(2)}, u32[]{:S(2)}) %collective-permute-start.2) | collective-permute-done | bytes 98336 | tf_op jit(solution)/shard_map/ppermute | solution.py:482
  11.0 1.5 %collective-permute-start.3 = (f32[3,8,1024]{2,1,0:T(8,128)S(1)}, f32[3,8,1024]{2,1,0:T(8,128)S(1)}, u32[]{:S(2)}, u32[]{:S(2)}) collective-permute-start(f32[3,8,1024]{2,1,0:T(8,128)S(1)} %collective-permute-done.2.refs_2_), channel_id=1, source_target_pairs={{0,4},{4,0},{8,12},{12,8},{16,20},{20,16},{24,28},{28,24},{1,5},{5... | collective-permute-start | bytes 294920 | tf_op jit(solution)/shard_map/ppermute | solution.py:449
  12.5 1.3 %collective-permute-done.1.refs_1_ = f32[4,8,1024]{2,1,0:T(8,128)S(1)} collective-permute-done((f32[4,8,1024]{2,1,0:T(8,128)S(1)}, f32[4,8,1024]{2,1,0:T(8,128)S(1)}, u32[]{:S(2)}, u32[]{:S(2)}) %collective-permute-start.1) | collective-permute-done | bytes 131104 | tf_op jit(solution)/shard_map/ppermute | solution.py:485
  13.8 2.8 %collective-permute-done.3.refs_3_ = f32[3,8,1024]{2,1,0:T(8,128)S(1)} collective-permute-done((f32[3,8,1024]{2,1,0:T(8,128)S(1)}, f32[3,8,1024]{2,1,0:T(8,128)S(1)}, u32[]{:S(2)}, u32[]{:S(2)}) %collective-permute-start.3) | collective-permute-done | bytes 98336 | tf_op jit(solution)/shard_map/ppermute | solution.py:449
  16.6 0.0 collective-permute-done.4.refs_4_
  16.6 0.0 collective-permute-done.5.refs_1_
  16.6 0.0 copy-done
  16.6 1.1 %shard_map.76 = (f32[4,8,64,128]{3,2,1,0:T(8,128)S(1)}, f32[3,8,48,128]{3,2,1,0:T(8,128)S(1)}, f32[4,8,56,128]{3,2,1,0:T(8,128)S(1)}, bf16[4,4,48,512]{3,2,1,0:T(8,128)(2,1)S(1)}, bf16[4,4,48,512]{3,2,1,0:T(8,128)(2,1)S(1)}) custom-call(f32[7,16,1024]{2,1,0:T(8,128)S(1)} %pad_maximum_fusion.refs_0_, f32[7,16,1024]{2,1,0:T(8,128)S(1)} %collective-permute-done.5.refs_1_, ...), custom_call_target="tpu_custom_call" | custom-call | flops 2850816000 | bytes 11403264 | tf_op jit(solution)/shard_map/pallas_call | solution.py:436
  17.7 0.9 %shard_map.77 = (f32[4,8,64,128]{3,2,1,0:T(8,128)S(1)}, f32[3,8,48,128]{3,2,1,0:T(8,128)S(1)}, f32[4,8,56,128]{3,2,1,0:T(8,128)S(1)}, bf16[4,4,48,512]{3,2,1,0:T(8,128)(2,1)S(1)}, bf16[4,4,48,512]{3,2,1,0:T(8,128)(2,1)S(1)}) custom-call(f32[4,8,1024]{2,1,0:T(8,128)S(1)} %collective-permute-do, ...), custom_call_target="tpu_custom_call", output_to_operand_aliasing={{0}: (5, {}), {1}: (6, {}), {2}: (7, {}), {3}: (8, {}), {4}... | custom-call | flops 2850816000 | bytes 11403264 | tf_op jit(solution)/shard_map/pallas_call | solution.py:436
  18.6 2.9 %shard_map.78 = (f32[4,8,16,128]{3,2,1,0:T(8,128)S(1)}, f32[4,8,16,128]{3,2,1,0:T(8,128)S(1)}, f32[4,2,4,16,128]{4,3,2,1,0:T(8,128)S(1)}, f32[4,8,56,128]{3,2,1,...) custom-call(f32[4,8,64,128]{3,2,1,0:T(8,128)S(1)} %get-tuple-element, ...), custom_call_target="tpu_custom_call", output_to_operand_aliasing={{3}: (2, {}), {4}: (3, {}), {5}: (4, {})} | custom-call | flops 2424832000 | bytes 9699328 | tf_op jit(solution)/shard_map/pallas_call | solution.py:436
  21.6 1.5 %collective-permute-start.6 = (f32[1,2,4,16,128]{4,3,2,1,0:T(8,128)S(1)}, f32[1,2,4,16,128]{4,3,2,1,0:T(8,128)S(1)}, u32[]{:S(2)}, u32[]{:S(2)}) collective-permute-start(f32[1,2,4,16,128]{4,3,2,1,0:T(8,128)S(1)} %get-tuple-element.53), channel_id=1, source_target_pairs={{0,4},{4,0},{8,12},{12,8},{16,20},{20,16},{24,28},{28,24},{1,5},{5... | collective-permute-start | bytes 196616 | tf_op jit(solution)/shard_map/ppermute | solution.py:449
  23.2 1.5 %collective-permute-start.8 = (f32[1,2,4,16,128]{4,3,2,1,0:T(8,128)S(1)}, f32[1,2,4,16,128]{4,3,2,1,0:T(8,128)S(1)}, u32[]{:S(2)}, u32[]{:S(2)}) collective-permute-start(f32[1,2,4,16,128]{4,3,2,1,0:T(8,128)S(1)} %get-tuple-element.54), channel_id=1, source_target_pairs={{0,12},{4,8},{8,4},{12,0},{16,28},{20,24},{24,20},{28,16},{1,13},{... | collective-permute-start | bytes 196616 | tf_op jit(solution)/shard_map/ppermute | solution.py:449
  24.7 0.5 %collective-permute-start.7 = (f32[1,2,4,16,128]{4,3,2,1,0:T(8,128)S(1)}, f32[1,2,4,16,128]{4,3,2,1,0:T(8,128)S(1)}, u32[]{:S(2)}, u32[]{:S(2)}) collective-permute-start(f32[1,2,4,16,128]{4,3,2,1,0:T(8,128)S(1)} %get-tuple-element.55), channel_id=1, source_target_pairs={{0,8},{4,12},{8,0},{12,4},{16,24},{20,28},{24,16},{28,20},{1,9},{5... | collective-permute-start | bytes 196616 | tf_op jit(solution)/shard_map/ppermute | solution.py:449
  25.2 0.8 %collective-permute-done.6 = f32[1,2,4,16,128]{4,3,2,1,0:T(8,128)S(1)} collective-permute-done((f32[1,2,4,16,128]{4,3,2,1,0:T(8,128)S(1)}, f32[1,2,4,16,128]{4,3,2,1,0:T(8,128)S(1)}, u32[]{:S(2)}, u32[]{:S(2)}) %collective-permute-start.6) | collective-permute-done | bytes 65568 | tf_op jit(solution)/shard_map/ppermute | solution.py:449
  25.9 3.0 %collective-permute-done.8 = f32[1,2,4,16,128]{4,3,2,1,0:T(8,128)S(1)} collective-permute-done((f32[1,2,4,16,128]{4,3,2,1,0:T(8,128)S(1)}, f32[1,2,4,16,128]{4,3,2,1,0:T(8,128)S(1)}, u32[]{:S(2)}, u32[]{:S(2)}) %collective-permute-start.8) | collective-permute-done | bytes 65568 | tf_op jit(solution)/shard_map/ppermute | solution.py:449
  29.0 0.0 collective-permute-done.7
  29.0 2.7 %collective-permute-start.9 = (f32[1,2,4,16,128]{4,3,2,1,0:T(8,128)S(1)}, f32[1,2,4,16,128]{4,3,2,1,0:T(8,128)S(1)}, u32[]{:S(2)}, u32[]{:S(2)}) collective-permute-start(f32[1,2,4,16,128]{4,3,2,1,0:T(8,128)S(1)} %add_add_fusion), channel_id=1, source_target_pairs={{0,16},{4,20},{8,24},{12,28},{16,0},{20,4},{24,8},{28,12},{1,17},{... | collective-permute-start | bytes 196616 | tf_op jit(solution)/shard_map/ppermute | solution.py:449
  31.7 3.3 %collective-permute-done.9 = f32[1,2,4,16,128]{4,3,2,1,0:T(8,128)S(1)} collective-permute-done((f32[1,2,4,16,128]{4,3,2,1,0:T(8,128)S(1)}, f32[1,2,4,16,128]{4,3,2,1,0:T(8,128)S(1)}, u32[]{:S(2)}, u32[]{:S(2)}) %collective-permute-start.9) | collective-permute-done | bytes 65568 | tf_op jit(solution)/shard_map/ppermute | solution.py:449
  34.9 0.1 divide_subtract_fusion
  35.0 1.2 %collective-permute-start.12 = (f32[1,2,4,16,128]{4,3,2,1,0:T(8,128)S(1)}, f32[1,2,4,16,128]{4,3,2,1,0:T(8,128)S(1)}, u32[]{:S(2)}, u32[]{:S(2)}) collective-permute-start(f32[1,2,4,16,128]{4,3,2,1,0:T(8,128)S(1)} %pad_maximum_fusion.2.refs_0_), channel_id=1, source_target_pairs={{0,12},{4,8},{8,4},{12,0},{16,28},{20,24},{24,20},{28,16},{1,13},{... | collective-permute-start | bytes 196616 | tf_op jit(solution)/shard_map/ppermute | solution.py:449
  36.3 1.8 %collective-permute-start.11 = (f32[1,2,4,16,128]{4,3,2,1,0:T(8,128)S(1)}, f32[1,2,4,16,128]{4,3,2,1,0:T(8,128)S(1)}, u32[]{:S(2)}, u32[]{:S(2)}) collective-permute-start(f32[1,2,4,16,128]{4,3,2,1,0:T(8,128)S(1)} %pad_maximum_fusion.2.refs_0_), channel_id=1, source_target_pairs={{0,8},{4,12},{8,0},{12,4},{16,24},{20,28},{24,16},{28,20},{1,9},{5... | collective-permute-start | bytes 196616 | tf_op jit(solution)/shard_map/ppermute | solution.py:449
  38.0 0.6 %collective-permute-start.10 = (f32[1,2,4,16,128]{4,3,2,1,0:T(8,128)S(1)}, f32[1,2,4,16,128]{4,3,2,1,0:T(8,128)S(1)}, u32[]{:S(2)}, u32[]{:S(2)}) collective-permute-start(f32[1,2,4,16,128]{4,3,2,1,0:T(8,128)S(1)} %pad_maximum_fusion.2.refs_0_), channel_id=1, source_target_pairs={{0,4},{4,0},{8,12},{12,8},{16,20},{20,16},{24,28},{28,24},{1,5},{5... | collective-permute-start | bytes 196616 | tf_op jit(solution)/shard_map/ppermute | solution.py:449
  38.6 1.7 %collective-permute-done.12.refs_3_ = f32[1,2,4,16,128]{4,3,2,1,0:T(8,128)S(1)} collective-permute-done((f32[1,2,4,16,128]{4,3,2,1,0:T(8,128)S(1)}, f32[1,2,4,16,128]{4,3,2,1,0:T(8,128)S(1)}, u32[]{:S(2)}, u32[]{:S(2)}) %collective-permute-start.12) | collective-permute-done | bytes 65568 | tf_op jit(solution)/shard_map/ppermute | solution.py:449
  40.3 0.7 %collective-permute-done.11.refs_2_ = f32[1,2,4,16,128]{4,3,2,1,0:T(8,128)S(1)} collective-permute-done((f32[1,2,4,16,128]{4,3,2,1,0:T(8,128)S(1)}, f32[1,2,4,16,128]{4,3,2,1,0:T(8,128)S(1)}, u32[]{:S(2)}, u32[]{:S(2)}) %collective-permute-start.11) | collective-permute-done | bytes 65568 | tf_op jit(solution)/shard_map/ppermute | solution.py:449
  41.0 1.3 %collective-permute-done.10.refs_1_ = f32[1,2,4,16,128]{4,3,2,1,0:T(8,128)S(1)} collective-permute-done((f32[1,2,4,16,128]{4,3,2,1,0:T(8,128)S(1)}, f32[1,2,4,16,128]{4,3,2,1,0:T(8,128)S(1)}, u32[]{:S(2)}, u32[]{:S(2)}) %collective-permute-start.10) | collective-permute-done | bytes 65568 | tf_op jit(solution)/shard_map/ppermute | solution.py:449
  42.3 0.1 shard_map.79
  42.4 0.1 collective-permute-start.13
  42.5 0.9 %collective-permute-start.14 = (f32[8,16,128]{2,1,0:T(8,128)S(1)}, f32[8,16,128]{2,1,0:T(8,128)S(1)}, u32[]{:S(2)}, u32[]{:S(2)}) collective-permute-start(f32[8,16,128]{2,1,0:T(8,128)S(1)} %get-tuple-element.47), channel_id=1, source_target_pairs={{0,1},{1,0},{2,3},{3,2},{4,5},{5,4},{6,7},{7,6},{8,9},{9,8},{10,11... | collective-permute-start | bytes 196616 | tf_op jit(solution)/shard_map/ppermute | solution.py:449
  43.4 1.3 %shard_map.80 = (f32[4,8,16,128]{3,2,1,0:T(8,128)S(1)}, f32[4,16,1024]{2,1,0:T(8,128)}) custom-call(f32[4,8,16,128]{3,2,1,0:T(8,128)S(1)} %get-tuple-element.40.refs_4_.refs_0_, f32[4,8,16,128]{3,2,1,0:T(8,128)S(1)} %get-tuple-element.41.refs_5_.refs_1_, f32[4,8,16,128]{3,2,1,0:T(8,128)S(1)} %get-tuple-element.43.refs_2_, ...), custom_call_target="tpu_custom_call" | custom-call | flops 262144000 | bytes 1048576 | tf_op jit(solution)/shard_map/pallas_call | solution.py:436
  44.7 1.5 %collective-permute-done.13.refs_1_ = f32[8,16,128]{2,1,0:T(8,128)S(1)} collective-permute-done((f32[8,16,128]{2,1,0:T(8,128)S(1)}, f32[8,16,128]{2,1,0:T(8,128)S(1)}, u32[]{:S(2)}, u32[]{:S(2)}) %collective-permute-start.13) | collective-permute-done | bytes 65568 | tf_op jit(solution)/shard_map/ppermute | solution.py:564
  46.2 0.0 collective-permute-done.14.refs_2_
  46.2 0.9 %shard_map.81 = (f32[1,2,16,1024]{3,2,1,0:T(8,128)}, f32[1,2,16,1024]{3,2,1,0:T(8,128)}) custom-call(f32[4,8,16,128]{3,2,1,0:T(8,128)S(1)} %get-tuple-element.45.refs_0_, f32[8,16,128]{2,1,0:T(8,128)S(1)} %collective-permute-done.13.refs_1_, f32[8,16,128]{2,1,0:T(8,128)S(1)} %collective-permute-done.14.refs_2_), custom_call_target="tpu_custom_call" | custom-call | flops 131072000 | bytes 524288 | tf_op jit(solution)/shard_map/pallas_call | solution.py:436
  (8 shorter events, 0.1 us)
Async XLA Ops:
  1.7 14.9 %copy-start = (bf16[1024,256]{1,0:T(8,128)(2,1)S(1)}, bf16[1024,256]{1,0:T(8,128)(2,1)}, u32[]{:S(2)}) copy-start(bf16[1024,256]{1,0:T(8,128)(2,1)} %constant.55.clone.refs_2_.refs_10_.refs_5_.refs_4_) | copy-start | bytes 1572868
  1.7 14.9 %collective-permute-start.5 = (f32[7,16,1024]{2,1,0:T(8,128)S(1)}, f32[7,16,1024]{2,1,0:T(8,128)S(1)}, u32[]{:S(2)}, u32[]{:S(2)}) collective-permute-start(f32[7,16,1024]{2,1,0:T(8,128)S(1)} %pad_maximum_fusion.refs_0_), channel_id=1, source_target_pairs={{0,1},{1,0},{2,3},{3,2},{4,5},{5,4},{6,7},{7,6},{8,9},{9,8},{10,11... | collective-permute-start | bytes 1376264 | tf_op jit(solution)/shard_map/ppermute | solution.py:449
  2.4 6.5 %collective-permute-start = (f32[4,8,1024]{2,1,0:T(8,128)S(1)}, f32[4,8,1024]{2,1,0:T(8,128)S(1)}, u32[]{:S(2)}, u32[]{:S(2)}) collective-permute-start(f32[4,8,1024]{2,1,0:T(8,128)S(1)} %pad_maximum_fusion.1), channel_id=1, source_target_pairs={{0,3},{1,2},{2,1},{3,0},{4,7},{5,6},{6,5},{7,4},{8,11},{9,10},{10,... | collective-permute-start | bytes 393224 | tf_op jit(solution)/shard_map/ppermute | solution.py:484
  5.0 6.0 %collective-permute-start.2 = (f32[3,8,1024]{2,1,0:T(8,128)S(1)}, f32[3,8,1024]{2,1,0:T(8,128)S(1)}, u32[]{:S(2)}, u32[]{:S(2)}) collective-permute-start(f32[3,8,1024]{2,1,0:T(8,128)S(1)} %slice_select_fusion), channel_id=1, source_target_pairs={{0,3},{1,2},{2,1},{3,0},{4,7},{5,6},{6,5},{7,4},{8,11},{9,10},{10,... | collective-permute-start | bytes 294920 | tf_op jit(solution)/shard_map/ppermute | solution.py:482
  5.1 8.6 %collective-permute-start.1 = (f32[4,8,1024]{2,1,0:T(8,128)S(1)}, f32[4,8,1024]{2,1,0:T(8,128)S(1)}, u32[]{:S(2)}, u32[]{:S(2)}) collective-permute-start(f32[4,8,1024]{2,1,0:T(8,128)S(1)} %slice.54), channel_id=1, source_target_pairs={{0,3},{1,2},{2,1},{3,0},{4,7},{5,6},{6,5},{7,4},{8,11},{9,10},{10,... | collective-permute-start | bytes 393224 | tf_op jit(solution)/shard_map/ppermute | solution.py:485
  8.9 7.7 %collective-permute-start.4 = (f32[4,8,1024]{2,1,0:T(8,128)S(1)}, f32[4,8,1024]{2,1,0:T(8,128)S(1)}, u32[]{:S(2)}, u32[]{:S(2)}) collective-permute-start(f32[4,8,1024]{2,1,0:T(8,128)S(1)} %collective-permute-done.refs_0_), channel_id=1, source_target_pairs={{0,1},{1,0},{2,3},{3,2},{4,5},{5,4},{6,7},{7,6},{8,9},{9,8},{10,11... | collective-permute-start | bytes 393224 | tf_op jit(solution)/shard_map/ppermute | solution.py:449
  11.0 5.6 %collective-permute-start.3 = (f32[3,8,1024]{2,1,0:T(8,128)S(1)}, f32[3,8,1024]{2,1,0:T(8,128)S(1)}, u32[]{:S(2)}, u32[]{:S(2)}) collective-permute-start(f32[3,8,1024]{2,1,0:T(8,128)S(1)} %collective-permute-done.2.refs_2_), channel_id=1, source_target_pairs={{0,4},{4,0},{8,12},{12,8},{16,20},{20,16},{24,28},{28,24},{1,5},{5... | collective-permute-start | bytes 294920 | tf_op jit(solution)/shard_map/ppermute | solution.py:449
  21.6 4.3 %collective-permute-start.6 = (f32[1,2,4,16,128]{4,3,2,1,0:T(8,128)S(1)}, f32[1,2,4,16,128]{4,3,2,1,0:T(8,128)S(1)}, u32[]{:S(2)}, u32[]{:S(2)}) collective-permute-start(f32[1,2,4,16,128]{4,3,2,1,0:T(8,128)S(1)} %get-tuple-element.53), channel_id=1, source_target_pairs={{0,4},{4,0},{8,12},{12,8},{16,20},{20,16},{24,28},{28,24},{1,5},{5... | collective-permute-start | bytes 196616 | tf_op jit(solution)/shard_map/ppermute | solution.py:449
  23.2 5.8 %collective-permute-start.8 = (f32[1,2,4,16,128]{4,3,2,1,0:T(8,128)S(1)}, f32[1,2,4,16,128]{4,3,2,1,0:T(8,128)S(1)}, u32[]{:S(2)}, u32[]{:S(2)}) collective-permute-start(f32[1,2,4,16,128]{4,3,2,1,0:T(8,128)S(1)} %get-tuple-element.54), channel_id=1, source_target_pairs={{0,12},{4,8},{8,4},{12,0},{16,28},{20,24},{24,20},{28,16},{1,13},{... | collective-permute-start | bytes 196616 | tf_op jit(solution)/shard_map/ppermute | solution.py:449
  24.7 4.3 %collective-permute-start.7 = (f32[1,2,4,16,128]{4,3,2,1,0:T(8,128)S(1)}, f32[1,2,4,16,128]{4,3,2,1,0:T(8,128)S(1)}, u32[]{:S(2)}, u32[]{:S(2)}) collective-permute-start(f32[1,2,4,16,128]{4,3,2,1,0:T(8,128)S(1)} %get-tuple-element.55), channel_id=1, source_target_pairs={{0,8},{4,12},{8,0},{12,4},{16,24},{20,28},{24,16},{28,20},{1,9},{5... | collective-permute-start | bytes 196616 | tf_op jit(solution)/shard_map/ppermute | solution.py:449
  29.0 5.9 %collective-permute-start.9 = (f32[1,2,4,16,128]{4,3,2,1,0:T(8,128)S(1)}, f32[1,2,4,16,128]{4,3,2,1,0:T(8,128)S(1)}, u32[]{:S(2)}, u32[]{:S(2)}) collective-permute-start(f32[1,2,4,16,128]{4,3,2,1,0:T(8,128)S(1)} %add_add_fusion), channel_id=1, source_target_pairs={{0,16},{4,20},{8,24},{12,28},{16,0},{20,4},{24,8},{28,12},{1,17},{... | collective-permute-start | bytes 196616 | tf_op jit(solution)/shard_map/ppermute | solution.py:449
  35.0 5.2 %collective-permute-start.12 = (f32[1,2,4,16,128]{4,3,2,1,0:T(8,128)S(1)}, f32[1,2,4,16,128]{4,3,2,1,0:T(8,128)S(1)}, u32[]{:S(2)}, u32[]{:S(2)}) collective-permute-start(f32[1,2,4,16,128]{4,3,2,1,0:T(8,128)S(1)} %pad_maximum_fusion.2.refs_0_), channel_id=1, source_target_pairs={{0,12},{4,8},{8,4},{12,0},{16,28},{20,24},{24,20},{28,16},{1,13},{... | collective-permute-start | bytes 196616 | tf_op jit(solution)/shard_map/ppermute | solution.py:449
  36.3 4.7 %collective-permute-start.11 = (f32[1,2,4,16,128]{4,3,2,1,0:T(8,128)S(1)}, f32[1,2,4,16,128]{4,3,2,1,0:T(8,128)S(1)}, u32[]{:S(2)}, u32[]{:S(2)}) collective-permute-start(f32[1,2,4,16,128]{4,3,2,1,0:T(8,128)S(1)} %pad_maximum_fusion.2.refs_0_), channel_id=1, source_target_pairs={{0,8},{4,12},{8,0},{12,4},{16,24},{20,28},{24,16},{28,20},{1,9},{5... | collective-permute-start | bytes 196616 | tf_op jit(solution)/shard_map/ppermute | solution.py:449
  38.0 4.3 %collective-permute-start.10 = (f32[1,2,4,16,128]{4,3,2,1,0:T(8,128)S(1)}, f32[1,2,4,16,128]{4,3,2,1,0:T(8,128)S(1)}, u32[]{:S(2)}, u32[]{:S(2)}) collective-permute-start(f32[1,2,4,16,128]{4,3,2,1,0:T(8,128)S(1)} %pad_maximum_fusion.2.refs_0_), channel_id=1, source_target_pairs={{0,4},{4,0},{8,12},{12,8},{16,20},{20,16},{24,28},{28,24},{1,5},{5... | collective-permute-start | bytes 196616 | tf_op jit(solution)/shard_map/ppermute | solution.py:449
  42.4 3.8 %collective-permute-start.13 = (f32[8,16,128]{2,1,0:T(8,128)S(1)}, f32[8,16,128]{2,1,0:T(8,128)S(1)}, u32[]{:S(2)}, u32[]{:S(2)}) collective-permute-start(f32[8,16,128]{2,1,0:T(8,128)S(1)} %get-tuple-element.46), channel_id=1, source_target_pairs={{0,3},{1,2},{2,1},{3,0},{4,7},{5,6},{6,5},{7,4},{8,11},{9,10},{10,... | collective-permute-start | bytes 196616 | tf_op jit(solution)/shard_map/ppermute | solution.py:564
  42.5 3.7 %collective-permute-start.14 = (f32[8,16,128]{2,1,0:T(8,128)S(1)}, f32[8,16,128]{2,1,0:T(8,128)S(1)}, u32[]{:S(2)}, u32[]{:S(2)}) collective-permute-start(f32[8,16,128]{2,1,0:T(8,128)S(1)} %get-tuple-element.47), channel_id=1, source_target_pairs={{0,1},{1,0},{2,3},{3,2},{4,5},{5,4},{6,7},{7,6},{8,9},{9,8},{10,11... | collective-permute-start | bytes 196616 | tf_op jit(solution)/shard_map/ppermute | solution.py:449

commit v9 on v8

--- a/solution.py
+++ b/solution.py
@@ -241,15 +241,15 @@
     pipeline([(b0, base + 8, 0, planes, hi_a, lo_a, store)], planes, w_ref, xys, True)
 
     clear_past(past)
-    none = jnp.zeros((REACH, LANES), jnp.float32)
     for c in range(4):
         for j in range(8):
             lanes = slice(j * LANES, (j + 1) * LANES)
             ahead, behind = rims[c, REACH:, lanes], rims[c, :REACH, lanes]
-            past[c, j, 0:REACH, :] = jnp.where(odd == 0, ahead, none)
-            past[c, j, 24 : 24 + REACH, :] = jnp.where(odd == 0, none, behind)
+            past[c, j, 0:REACH, :] = ahead
+            past[c, j, 24 : 24 + REACH, :] = behind
     row = pl.multiple_of(planes + odd * (planes - 8), 8)
-    add_share(past, b1, hi_b, lo_b, row, (LEAD, TAIL))
+    side = (LEAD[0] + odd * (TAIL[0] - LEAD[0]), 2 * odd - 1)
+    add_share(past, b1, hi_b, lo_b, row, (side,))
     add_far_share(past, b1, hi_b, lo_b, planes, relayed, REACH, relayed, 0)
 
 

time: 47.2 us -> 47.1 us (level)
  no operation moved by 1% of the time
where the time goes in v9:
time: 47.1 us; the launch traced here: 47 us
  waiting for transfers between devices  20 us (42%)
  starting transfers between devices  17.8 us (38%)
  Pallas kernels  7.16 us (15%)
  other arithmetic  1.23 us (3%)
  between operations  0.74 us (2%)
    ppermute x11, waiting for transfers between devices, exchange_xor(): return lax.ppermute(x, axis, [(i, i ^ bits) for i in range(count)])  13.6 us
    ppermute x11, starting transfers between devices, exchange_xor(): return lax.ppermute(x, axis, [(i, i ^ bits) for i in range(count)])  13.2 us
    pallas_call x6, Pallas kernels, call(): pl.pallas_call(kernel, out_shape=tuple((jax.ShapeDtypeStruct(s, d) for s,...  7.16 us
    ppermute x1, starting transfers between devices, local(): rims = lax.ppermute(rims, 'grid', cross)  2.65 us
    ppermute x1, waiting for transfers between devices, local(): rims = lax.ppermute(rims, 'grid', cross)  1.98 us
    ppermute x1, starting transfers between devices, local(): far = lax.ppermute(own[:4, REACH:planes - REACH], 'grid', cross)  1.79 us
    ppermute x1, waiting for transfers between devices, local(): mine = lax.ppermute(picked, 'grid', cross)  1.63 us
    ppermute x1, waiting for transfers between devices, local(): first = lax.ppermute(first, 'grid', cross)  1.51 us
  transfers between devices with their start and end apart: 15, of which 11 were waited for; matrix products, arithmetic and copies ran while one was open for 0% of the time, Pallas kernels for 3%

profile of v9, /device:TPU:0, one launch (start us, length us, event | category | flops | bytes accessed | tf_op | source)
XLA Modules:
  0.0 47.0 jit_solution(6273910112212443492)
XLA Ops:
  0.6 1.1 %pad_maximum_fusion.refs_0_ = f32[7,16,1024]{2,1,0:T(8,128)S(1)} fusion(f32[2,16,1024]{2,1,0:T(8,128)} %param.8, f32[1,16,1024]{2,1,0:T(8,128)} %bitcast.5, f32[2,16,1024]{2,1,0:T(8,128)} %bitcast.3, f32[2,16,1024]{2,1,0:T(8,128)} %bitcast.4), kind=kLoop, calls=%fused_computation | loop fusion | flops 344064 | bytes 917504 | tf_op jit(solution)/shard_map/concatenate | solution.py:460
  1.7 0.0 copy-start
  1.7 0.6 %collective-permute-start.5 = (f32[7,16,1024]{2,1,0:T(8,128)S(1)}, f32[7,16,1024]{2,1,0:T(8,128)S(1)}, u32[]{:S(2)}, u32[]{:S(2)}) collective-permute-start(f32[7,16,1024]{2,1,0:T(8,128)S(1)} %pad_maximum_fusion.refs_0_), channel_id=1, source_target_pairs={{0,1},{1,0},{2,3},{3,2},{4,5},{5,4},{6,7},{7,6},{8,9},{9,8},{10,11... | collective-permute-start | bytes 1376264 | tf_op jit(solution)/shard_map/ppermute | solution.py:449
  2.4 2.7 %collective-permute-start = (f32[4,8,1024]{2,1,0:T(8,128)S(1)}, f32[4,8,1024]{2,1,0:T(8,128)S(1)}, u32[]{:S(2)}, u32[]{:S(2)}) collective-permute-start(f32[4,8,1024]{2,1,0:T(8,128)S(1)} %pad_maximum_fusion.1), channel_id=1, source_target_pairs={{0,3},{1,2},{2,1},{3,0},{4,7},{5,6},{6,5},{7,4},{8,11},{9,10},{10,... | collective-permute-start | bytes 393224 | tf_op jit(solution)/shard_map/ppermute | solution.py:484
  5.0 0.1 collective-permute-start.2
  5.1 1.8 %collective-permute-start.1 = (f32[4,8,1024]{2,1,0:T(8,128)S(1)}, f32[4,8,1024]{2,1,0:T(8,128)S(1)}, u32[]{:S(2)}, u32[]{:S(2)}) collective-permute-start(f32[4,8,1024]{2,1,0:T(8,128)S(1)} %slice.54), channel_id=1, source_target_pairs={{0,3},{1,2},{2,1},{3,0},{4,7},{5,6},{6,5},{7,4},{8,11},{9,10},{10,... | collective-permute-start | bytes 393224 | tf_op jit(solution)/shard_map/ppermute | solution.py:485
  6.9 2.0 %collective-permute-done.refs_0_ = f32[4,8,1024]{2,1,0:T(8,128)S(1)} collective-permute-done((f32[4,8,1024]{2,1,0:T(8,128)S(1)}, f32[4,8,1024]{2,1,0:T(8,128)S(1)}, u32[]{:S(2)}, u32[]{:S(2)}) %collective-permute-start) | collective-permute-done | bytes 131104 | tf_op jit(solution)/shard_map/ppermute | solution.py:484
  8.9 0.5 %collective-permute-start.4 = (f32[4,8,1024]{2,1,0:T(8,128)S(1)}, f32[4,8,1024]{2,1,0:T(8,128)S(1)}, u32[]{:S(2)}, u32[]{:S(2)}) collective-permute-start(f32[4,8,1024]{2,1,0:T(8,128)S(1)} %collective-permute-done.refs_0_), channel_id=1, source_target_pairs={{0,1},{1,0},{2,3},{3,2},{4,5},{5,4},{6,7},{7,6},{8,9},{9,8},{10,11... | collective-permute-start | bytes 393224 | tf_op jit(solution)/shard_map/ppermute | solution.py:449
  9.4 1.6 %collective-permute-done.2.refs_2_ = f32[3,8,1024]{2,1,0:T(8,128)S(1)} collective-permute-done((f32[3,8,1024]{2,1,0:T(8,128)S(1)}, f32[3,8,1024]{2,1,0:T(8,128)S(1)}, u32[]{:S(2)}, u32[]{:S(2)}) %collective-permute-start.2) | collective-permute-done | bytes 98336 | tf_op jit(solution)/shard_map/ppermute | solution.py:482
  11.0 1.5 %collective-permute-start.3 = (f32[3,8,1024]{2,1,0:T(8,128)S(1)}, f32[3,8,1024]{2,1,0:T(8,128)S(1)}, u32[]{:S(2)}, u32[]{:S(2)}) collective-permute-start(f32[3,8,1024]{2,1,0:T(8,128)S(1)} %collective-permute-done.2.refs_2_), channel_id=1, source_target_pairs={{0,4},{4,0},{8,12},{12,8},{16,20},{20,16},{24,28},{28,24},{1,5},{5... | collective-permute-start | bytes 294920 | tf_op jit(solution)/shard_map/ppermute | solution.py:449
  12.5 1.3 %collective-permute-done.1.refs_1_ = f32[4,8,1024]{2,1,0:T(8,128)S(1)} collective-permute-done((f32[4,8,1024]{2,1,0:T(8,128)S(1)}, f32[4,8,1024]{2,1,0:T(8,128)S(1)}, u32[]{:S(2)}, u32[]{:S(2)}) %collective-permute-start.1) | collective-permute-done | bytes 131104 | tf_op jit(solution)/shard_map/ppermute | solution.py:485
  13.8 2.8 %collective-permute-done.3.refs_3_ = f32[3,8,1024]{2,1,0:T(8,128)S(1)} collective-permute-done((f32[3,8,1024]{2,1,0:T(8,128)S(1)}, f32[3,8,1024]{2,1,0:T(8,128)S(1)}, u32[]{:S(2)}, u32[]{:S(2)}) %collective-permute-start.3) | collective-permute-done | bytes 98336 | tf_op jit(solution)/shard_map/ppermute | solution.py:449
  16.6 0.0 collective-permute-done.4.refs_4_
  16.6 0.0 collective-permute-done.5.refs_1_
  16.6 0.0 copy-done
  16.6 1.1 %shard_map.76 = (f32[4,8,64,128]{3,2,1,0:T(8,128)S(1)}, f32[3,8,48,128]{3,2,1,0:T(8,128)S(1)}, f32[4,8,56,128]{3,2,1,0:T(8,128)S(1)}, bf16[4,4,48,512]{3,2,1,0:T(8,128)(2,1)S(1)}, bf16[4,4,48,512]{3,2,1,0:T(8,128)(2,1)S(1)}) custom-call(f32[7,16,1024]{2,1,0:T(8,128)S(1)} %pad_maximum_fusion.refs_0_, f32[7,16,1024]{2,1,0:T(8,128)S(1)} %collective-permute-done.5.refs_1_, ...), custom_call_target="tpu_custom_call" | custom-call | flops 2850816000 | bytes 11403264 | tf_op jit(solution)/shard_map/pallas_call | solution.py:436
  17.7 0.8 %shard_map.77 = (f32[4,8,64,128]{3,2,1,0:T(8,128)S(1)}, f32[3,8,48,128]{3,2,1,0:T(8,128)S(1)}, f32[4,8,56,128]{3,2,1,0:T(8,128)S(1)}, bf16[4,4,48,512]{3,2,1,0:T(8,128)(2,1)S(1)}, bf16[4,4,48,512]{3,2,1,0:T(8,128)(2,1)S(1)}) custom-call(f32[4,8,1024]{2,1,0:T(8,128)S(1)} %collective-permute-do, ...), custom_call_target="tpu_custom_call", output_to_operand_aliasing={{0}: (5, {}), {1}: (6, {}), {2}: (7, {}), {3}: (8, {}), {4}... | custom-call | flops 2850816000 | bytes 11403264 | tf_op jit(solution)/shard_map/pallas_call | solution.py:436
  18.6 2.9 %shard_map.78 = (f32[4,8,16,128]{3,2,1,0:T(8,128)S(1)}, f32[4,8,16,128]{3,2,1,0:T(8,128)S(1)}, f32[4,2,4,16,128]{4,3,2,1,0:T(8,128)S(1)}, f32[4,8,56,128]{3,2,1,...) custom-call(f32[4,8,64,128]{3,2,1,0:T(8,128)S(1)} %get-tuple-element, ...), custom_call_target="tpu_custom_call", output_to_operand_aliasing={{3}: (2, {}), {4}: (3, {}), {5}: (4, {})} | custom-call | flops 2424832000 | bytes 9699328 | tf_op jit(solution)/shard_map/pallas_call | solution.py:436
  21.5 1.5 %collective-permute-start.6 = (f32[1,2,4,16,128]{4,3,2,1,0:T(8,128)S(1)}, f32[1,2,4,16,128]{4,3,2,1,0:T(8,128)S(1)}, u32[]{:S(2)}, u32[]{:S(2)}) collective-permute-start(f32[1,2,4,16,128]{4,3,2,1,0:T(8,128)S(1)} %get-tuple-element.53), channel_id=1, source_target_pairs={{0,4},{4,0},{8,12},{12,8},{16,20},{20,16},{24,28},{28,24},{1,5},{5... | collective-permute-start | bytes 196616 | tf_op jit(solution)/shard_map/ppermute | solution.py:449
  23.1 1.5 %collective-permute-start.8 = (f32[1,2,4,16,128]{4,3,2,1,0:T(8,128)S(1)}, f32[1,2,4,16,128]{4,3,2,1,0:T(8,128)S(1)}, u32[]{:S(2)}, u32[]{:S(2)}) collective-permute-start(f32[1,2,4,16,128]{4,3,2,1,0:T(8,128)S(1)} %get-tuple-element.54), channel_id=1, source_target_pairs={{0,12},{4,8},{8,4},{12,0},{16,28},{20,24},{24,20},{28,16},{1,13},{... | collective-permute-start | bytes 196616 | tf_op jit(solution)/shard_map/ppermute | solution.py:449
  24.6 0.5 %collective-permute-start.7 = (f32[1,2,4,16,128]{4,3,2,1,0:T(8,128)S(1)}, f32[1,2,4,16,128]{4,3,2,1,0:T(8,128)S(1)}, u32[]{:S(2)}, u32[]{:S(2)}) collective-permute-start(f32[1,2,4,16,128]{4,3,2,1,0:T(8,128)S(1)} %get-tuple-element.55), channel_id=1, source_target_pairs={{0,8},{4,12},{8,0},{12,4},{16,24},{20,28},{24,16},{28,20},{1,9},{5... | collective-permute-start | bytes 196616 | tf_op jit(solution)/shard_map/ppermute | solution.py:449
  25.1 0.8 %collective-permute-done.6 = f32[1,2,4,16,128]{4,3,2,1,0:T(8,128)S(1)} collective-permute-done((f32[1,2,4,16,128]{4,3,2,1,0:T(8,128)S(1)}, f32[1,2,4,16,128]{4,3,2,1,0:T(8,128)S(1)}, u32[]{:S(2)}, u32[]{:S(2)}) %collective-permute-start.6) | collective-permute-done | bytes 65568 | tf_op jit(solution)/shard_map/ppermute | solution.py:449
  25.9 3.0 %collective-permute-done.8 = f32[1,2,4,16,128]{4,3,2,1,0:T(8,128)S(1)} collective-permute-done((f32[1,2,4,16,128]{4,3,2,1,0:T(8,128)S(1)}, f32[1,2,4,16,128]{4,3,2,1,0:T(8,128)S(1)}, u32[]{:S(2)}, u32[]{:S(2)}) %collective-permute-start.8) | collective-permute-done | bytes 65568 | tf_op jit(solution)/shard_map/ppermute | solution.py:449
  28.9 0.0 collective-permute-done.7
  28.9 2.6 %collective-permute-start.9 = (f32[1,2,4,16,128]{4,3,2,1,0:T(8,128)S(1)}, f32[1,2,4,16,128]{4,3,2,1,0:T(8,128)S(1)}, u32[]{:S(2)}, u32[]{:S(2)}) collective-permute-start(f32[1,2,4,16,128]{4,3,2,1,0:T(8,128)S(1)} %add_add_fusion), channel_id=1, source_target_pairs={{0,16},{4,20},{8,24},{12,28},{16,0},{20,4},{24,8},{28,12},{1,17},{... | collective-permute-start | bytes 196616 | tf_op jit(solution)/shard_map/ppermute | solution.py:449
  31.5 3.3 %collective-permute-done.9 = f32[1,2,4,16,128]{4,3,2,1,0:T(8,128)S(1)} collective-permute-done((f32[1,2,4,16,128]{4,3,2,1,0:T(8,128)S(1)}, f32[1,2,4,16,128]{4,3,2,1,0:T(8,128)S(1)}, u32[]{:S(2)}, u32[]{:S(2)}) %collective-permute-start.9) | collective-permute-done | bytes 65568 | tf_op jit(solution)/shard_map/ppermute | solution.py:449
  34.8 0.1 divide_subtract_fusion
  34.9 1.3 %collective-permute-start.12 = (f32[1,2,4,16,128]{4,3,2,1,0:T(8,128)S(1)}, f32[1,2,4,16,128]{4,3,2,1,0:T(8,128)S(1)}, u32[]{:S(2)}, u32[]{:S(2)}) collective-permute-start(f32[1,2,4,16,128]{4,3,2,1,0:T(8,128)S(1)} %pad_maximum_fusion.2.refs_0_), channel_id=1, source_target_pairs={{0,12},{4,8},{8,4},{12,0},{16,28},{20,24},{24,20},{28,16},{1,13},{... | collective-permute-start | bytes 196616 | tf_op jit(solution)/shard_map/ppermute | solution.py:449
  36.2 1.7 %collective-permute-start.11 = (f32[1,2,4,16,128]{4,3,2,1,0:T(8,128)S(1)}, f32[1,2,4,16,128]{4,3,2,1,0:T(8,128)S(1)}, u32[]{:S(2)}, u32[]{:S(2)}) collective-permute-start(f32[1,2,4,16,128]{4,3,2,1,0:T(8,128)S(1)} %pad_maximum_fusion.2.refs_0_), channel_id=1, source_target_pairs={{0,8},{4,12},{8,0},{12,4},{16,24},{20,28},{24,16},{28,20},{1,9},{5... | collective-permute-start | bytes 196616 | tf_op jit(solution)/shard_map/ppermute | solution.py:449
  37.9 0.5 %collective-permute-start.10 = (f32[1,2,4,16,128]{4,3,2,1,0:T(8,128)S(1)}, f32[1,2,4,16,128]{4,3,2,1,0:T(8,128)S(1)}, u32[]{:S(2)}, u32[]{:S(2)}) collective-permute-start(f32[1,2,4,16,128]{4,3,2,1,0:T(8,128)S(1)} %pad_maximum_fusion.2.refs_0_), channel_id=1, source_target_pairs={{0,4},{4,0},{8,12},{12,8},{16,20},{20,16},{24,28},{28,24},{1,5},{5... | collective-permute-start | bytes 196616 | tf_op jit(solution)/shard_map/ppermute | solution.py:449
  38.5 1.7 %collective-permute-done.12.refs_3_ = f32[1,2,4,16,128]{4,3,2,1,0:T(8,128)S(1)} collective-permute-done((f32[1,2,4,16,128]{4,3,2,1,0:T(8,128)S(1)}, f32[1,2,4,16,128]{4,3,2,1,0:T(8,128)S(1)}, u32[]{:S(2)}, u32[]{:S(2)}) %collective-permute-start.12) | collective-permute-done | bytes 65568 | tf_op jit(solution)/shard_map/ppermute | solution.py:449
  40.2 0.7 %collective-permute-done.11.refs_2_ = f32[1,2,4,16,128]{4,3,2,1,0:T(8,128)S(1)} collective-permute-done((f32[1,2,4,16,128]{4,3,2,1,0:T(8,128)S(1)}, f32[1,2,4,16,128]{4,3,2,1,0:T(8,128)S(1)}, u32[]{:S(2)}, u32[]{:S(2)}) %collective-permute-start.11) | collective-permute-done | bytes 65568 | tf_op jit(solution)/shard_map/ppermute | solution.py:449
  40.9 1.3 %collective-permute-done.10.refs_1_ = f32[1,2,4,16,128]{4,3,2,1,0:T(8,128)S(1)} collective-permute-done((f32[1,2,4,16,128]{4,3,2,1,0:T(8,128)S(1)}, f32[1,2,4,16,128]{4,3,2,1,0:T(8,128)S(1)}, u32[]{:S(2)}, u32[]{:S(2)}) %collective-permute-start.10) | collective-permute-done | bytes 65568 | tf_op jit(solution)/shard_map/ppermute | solution.py:449
  42.2 0.1 shard_map.79
  42.3 0.1 collective-permute-start.13
  42.4 0.9 %collective-permute-start.14 = (f32[8,16,128]{2,1,0:T(8,128)S(1)}, f32[8,16,128]{2,1,0:T(8,128)S(1)}, u32[]{:S(2)}, u32[]{:S(2)}) collective-permute-start(f32[8,16,128]{2,1,0:T(8,128)S(1)} %get-tuple-element.47), channel_id=1, source_target_pairs={{0,1},{1,0},{2,3},{3,2},{4,5},{5,4},{6,7},{7,6},{8,9},{9,8},{10,11... | collective-permute-start | bytes 196616 | tf_op jit(solution)/shard_map/ppermute | solution.py:449
  43.3 1.3 %shard_map.80 = (f32[4,8,16,128]{3,2,1,0:T(8,128)S(1)}, f32[4,16,1024]{2,1,0:T(8,128)}) custom-call(f32[4,8,16,128]{3,2,1,0:T(8,128)S(1)} %get-tuple-element.40.refs_4_.refs_0_, f32[4,8,16,128]{3,2,1,0:T(8,128)S(1)} %get-tuple-element.41.refs_5_.refs_1_, f32[4,8,16,128]{3,2,1,0:T(8,128)S(1)} %get-tuple-element.43.refs_2_, ...), custom_call_target="tpu_custom_call" | custom-call | flops 262144000 | bytes 1048576 | tf_op jit(solution)/shard_map/pallas_call | solution.py:436
  44.6 1.5 %collective-permute-done.13.refs_1_ = f32[8,16,128]{2,1,0:T(8,128)S(1)} collective-permute-done((f32[8,16,128]{2,1,0:T(8,128)S(1)}, f32[8,16,128]{2,1,0:T(8,128)S(1)}, u32[]{:S(2)}, u32[]{:S(2)}) %collective-permute-start.13) | collective-permute-done | bytes 65568 | tf_op jit(solution)/shard_map/ppermute | solution.py:564
  46.1 0.0 collective-permute-done.14.refs_2_
  46.1 0.9 %shard_map.81 = (f32[1,2,16,1024]{3,2,1,0:T(8,128)}, f32[1,2,16,1024]{3,2,1,0:T(8,128)}) custom-call(f32[4,8,16,128]{3,2,1,0:T(8,128)S(1)} %get-tuple-element.45.refs_0_, f32[8,16,128]{2,1,0:T(8,128)S(1)} %collective-permute-done.13.refs_1_, f32[8,16,128]{2,1,0:T(8,128)S(1)} %collective-permute-done.14.refs_2_), custom_call_target="tpu_custom_call" | custom-call | flops 131072000 | bytes 524288 | tf_op jit(solution)/shard_map/pallas_call | solution.py:436
  (8 shorter events, 0.1 us)
Async XLA Ops:
  1.7 14.9 %copy-start = (bf16[1024,256]{1,0:T(8,128)(2,1)S(1)}, bf16[1024,256]{1,0:T(8,128)(2,1)}, u32[]{:S(2)}) copy-start(bf16[1024,256]{1,0:T(8,128)(2,1)} %constant.55.clone.refs_2_.refs_10_.refs_5_.refs_4_) | copy-start | bytes 1572868
  1.7 14.9 %collective-permute-start.5 = (f32[7,16,1024]{2,1,0:T(8,128)S(1)}, f32[7,16,1024]{2,1,0:T(8,128)S(1)}, u32[]{:S(2)}, u32[]{:S(2)}) collective-permute-start(f32[7,16,1024]{2,1,0:T(8,128)S(1)} %pad_maximum_fusion.refs_0_), channel_id=1, source_target_pairs={{0,1},{1,0},{2,3},{3,2},{4,5},{5,4},{6,7},{7,6},{8,9},{9,8},{10,11... | collective-permute-start | bytes 1376264 | tf_op jit(solution)/shard_map/ppermute | solution.py:449
  2.4 6.5 %collective-permute-start = (f32[4,8,1024]{2,1,0:T(8,128)S(1)}, f32[4,8,1024]{2,1,0:T(8,128)S(1)}, u32[]{:S(2)}, u32[]{:S(2)}) collective-permute-start(f32[4,8,1024]{2,1,0:T(8,128)S(1)} %pad_maximum_fusion.1), channel_id=1, source_target_pairs={{0,3},{1,2},{2,1},{3,0},{4,7},{5,6},{6,5},{7,4},{8,11},{9,10},{10,... | collective-permute-start | bytes 393224 | tf_op jit(solution)/shard_map/ppermute | solution.py:484
  5.0 6.0 %collective-permute-start.2 = (f32[3,8,1024]{2,1,0:T(8,128)S(1)}, f32[3,8,1024]{2,1,0:T(8,128)S(1)}, u32[]{:S(2)}, u32[]{:S(2)}) collective-permute-start(f32[3,8,1024]{2,1,0:T(8,128)S(1)} %slice_select_fusion), channel_id=1, source_target_pairs={{0,3},{1,2},{2,1},{3,0},{4,7},{5,6},{6,5},{7,4},{8,11},{9,10},{10,... | collective-permute-start | bytes 294920 | tf_op jit(solution)/shard_map/ppermute | solution.py:482
  5.1 8.6 %collective-permute-start.1 = (f32[4,8,1024]{2,1,0:T(8,128)S(1)}, f32[4,8,1024]{2,1,0:T(8,128)S(1)}, u32[]{:S(2)}, u32[]{:S(2)}) collective-permute-start(f32[4,8,1024]{2,1,0:T(8,128)S(1)} %slice.54), channel_id=1, source_target_pairs={{0,3},{1,2},{2,1},{3,0},{4,7},{5,6},{6,5},{7,4},{8,11},{9,10},{10,... | collective-permute-start | bytes 393224 | tf_op jit(solution)/shard_map/ppermute | solution.py:485
  8.9 7.7 %collective-permute-start.4 = (f32[4,8,1024]{2,1,0:T(8,128)S(1)}, f32[4,8,1024]{2,1,0:T(8,128)S(1)}, u32[]{:S(2)}, u32[]{:S(2)}) collective-permute-start(f32[4,8,1024]{2,1,0:T(8,128)S(1)} %collective-permute-done.refs_0_), channel_id=1, source_target_pairs={{0,1},{1,0},{2,3},{3,2},{4,5},{5,4},{6,7},{7,6},{8,9},{9,8},{10,11... | collective-permute-start | bytes 393224 | tf_op jit(solution)/shard_map/ppermute | solution.py:449
  11.0 5.6 %collective-permute-start.3 = (f32[3,8,1024]{2,1,0:T(8,128)S(1)}, f32[3,8,1024]{2,1,0:T(8,128)S(1)}, u32[]{:S(2)}, u32[]{:S(2)}) collective-permute-start(f32[3,8,1024]{2,1,0:T(8,128)S(1)} %collective-permute-done.2.refs_2_), channel_id=1, source_target_pairs={{0,4},{4,0},{8,12},{12,8},{16,20},{20,16},{24,28},{28,24},{1,5},{5... | collective-permute-start | bytes 294920 | tf_op jit(solution)/shard_map/ppermute | solution.py:449
  21.5 4.3 %collective-permute-start.6 = (f32[1,2,4,16,128]{4,3,2,1,0:T(8,128)S(1)}, f32[1,2,4,16,128]{4,3,2,1,0:T(8,128)S(1)}, u32[]{:S(2)}, u32[]{:S(2)}) collective-permute-start(f32[1,2,4,16,128]{4,3,2,1,0:T(8,128)S(1)} %get-tuple-element.53), channel_id=1, source_target_pairs={{0,4},{4,0},{8,12},{12,8},{16,20},{20,16},{24,28},{28,24},{1,5},{5... | collective-permute-start | bytes 196616 | tf_op jit(solution)/shard_map/ppermute | solution.py:449
  23.1 5.8 %collective-permute-start.8 = (f32[1,2,4,16,128]{4,3,2,1,0:T(8,128)S(1)}, f32[1,2,4,16,128]{4,3,2,1,0:T(8,128)S(1)}, u32[]{:S(2)}, u32[]{:S(2)}) collective-permute-start(f32[1,2,4,16,128]{4,3,2,1,0:T(8,128)S(1)} %get-tuple-element.54), channel_id=1, source_target_pairs={{0,12},{4,8},{8,4},{12,0},{16,28},{20,24},{24,20},{28,16},{1,13},{... | collective-permute-start | bytes 196616 | tf_op jit(solution)/shard_map/ppermute | solution.py:449
  24.6 4.3 %collective-permute-start.7 = (f32[1,2,4,16,128]{4,3,2,1,0:T(8,128)S(1)}, f32[1,2,4,16,128]{4,3,2,1,0:T(8,128)S(1)}, u32[]{:S(2)}, u32[]{:S(2)}) collective-permute-start(f32[1,2,4,16,128]{4,3,2,1,0:T(8,128)S(1)} %get-tuple-element.55), channel_id=1, source_target_pairs={{0,8},{4,12},{8,0},{12,4},{16,24},{20,28},{24,16},{28,20},{1,9},{5... | collective-permute-start | bytes 196616 | tf_op jit(solution)/shard_map/ppermute | solution.py:449
  28.9 5.9 %collective-permute-start.9 = (f32[1,2,4,16,128]{4,3,2,1,0:T(8,128)S(1)}, f32[1,2,4,16,128]{4,3,2,1,0:T(8,128)S(1)}, u32[]{:S(2)}, u32[]{:S(2)}) collective-permute-start(f32[1,2,4,16,128]{4,3,2,1,0:T(8,128)S(1)} %add_add_fusion), channel_id=1, source_target_pairs={{0,16},{4,20},{8,24},{12,28},{16,0},{20,4},{24,8},{28,12},{1,17},{... | collective-permute-start | bytes 196616 | tf_op jit(solution)/shard_map/ppermute | solution.py:449
  34.9 5.2 %collective-permute-start.12 = (f32[1,2,4,16,128]{4,3,2,1,0:T(8,128)S(1)}, f32[1,2,4,16,128]{4,3,2,1,0:T(8,128)S(1)}, u32[]{:S(2)}, u32[]{:S(2)}) collective-permute-start(f32[1,2,4,16,128]{4,3,2,1,0:T(8,128)S(1)} %pad_maximum_fusion.2.refs_0_), channel_id=1, source_target_pairs={{0,12},{4,8},{8,4},{12,0},{16,28},{20,24},{24,20},{28,16},{1,13},{... | collective-permute-start | bytes 196616 | tf_op jit(solution)/shard_map/ppermute | solution.py:449
  36.2 4.7 %collective-permute-start.11 = (f32[1,2,4,16,128]{4,3,2,1,0:T(8,128)S(1)}, f32[1,2,4,16,128]{4,3,2,1,0:T(8,128)S(1)}, u32[]{:S(2)}, u32[]{:S(2)}) collective-permute-start(f32[1,2,4,16,128]{4,3,2,1,0:T(8,128)S(1)} %pad_maximum_fusion.2.refs_0_), channel_id=1, source_target_pairs={{0,8},{4,12},{8,0},{12,4},{16,24},{20,28},{24,16},{28,20},{1,9},{5... | collective-permute-start | bytes 196616 | tf_op jit(solution)/shard_map/ppermute | solution.py:449
  37.9 4.3 %collective-permute-start.10 = (f32[1,2,4,16,128]{4,3,2,1,0:T(8,128)S(1)}, f32[1,2,4,16,128]{4,3,2,1,0:T(8,128)S(1)}, u32[]{:S(2)}, u32[]{:S(2)}) collective-permute-start(f32[1,2,4,16,128]{4,3,2,1,0:T(8,128)S(1)} %pad_maximum_fusion.2.refs_0_), channel_id=1, source_target_pairs={{0,4},{4,0},{8,12},{12,8},{16,20},{20,16},{24,28},{28,24},{1,5},{5... | collective-permute-start | bytes 196616 | tf_op jit(solution)/shard_map/ppermute | solution.py:449
  42.3 3.8 %collective-permute-start.13 = (f32[8,16,128]{2,1,0:T(8,128)S(1)}, f32[8,16,128]{2,1,0:T(8,128)S(1)}, u32[]{:S(2)}, u32[]{:S(2)}) collective-permute-start(f32[8,16,128]{2,1,0:T(8,128)S(1)} %get-tuple-element.46), channel_id=1, source_target_pairs={{0,3},{1,2},{2,1},{3,0},{4,7},{5,6},{6,5},{7,4},{8,11},{9,10},{10,... | collective-permute-start | bytes 196616 | tf_op jit(solution)/shard_map/ppermute | solution.py:564
  42.4 3.7 %collective-permute-start.14 = (f32[8,16,128]{2,1,0:T(8,128)S(1)}, f32[8,16,128]{2,1,0:T(8,128)S(1)}, u32[]{:S(2)}, u32[]{:S(2)}) collective-permute-start(f32[8,16,128]{2,1,0:T(8,128)S(1)} %get-tuple-element.47), channel_id=1, source_target_pairs={{0,1},{1,0},{2,3},{3,2},{4,5},{5,4},{6,7},{7,6},{8,9},{9,8},{10,11... | collective-permute-start | bytes 196616 | tf_op jit(solution)/shard_map/ppermute | solution.py:449
